TPU v7x, 32 devices: a whole 2x2x4 slice. The times are simulated.
32 devices in a mesh: seq: 4 (over y, x), vocab: 8 (over z, core).
Axes of the slice: x: 2, y: 2, z: 4, core: 2. Of those that a mesh axis runs over, the one named last changes fastest.
Arguments:
- tokens: int32 [2, 8, 1024], P(None, 'vocab', 'seq'), may hold values from 0 to 4095
- source: int32 [2, 8, 1024], P(None, 'vocab', 'seq'), may hold values from 0 to 4095
- segments: int32 [2, 8, 1024], P(None, 'vocab', 'seq'), may hold values from 0 to 7, never falling along the last dimension, each value on 1 to 512 neighbouring positions
- loss_rows: int32 [2, 8, 128], P(None, 'vocab', 'seq'), may hold values from 0 to 255
- targets: int32 [2, 8, 128], P(None, 'vocab', 'seq'), may hold values from 0 to 4095
- exit_depth: int32 [2, 8, 128], P(None, 'vocab', 'seq'), may hold values from 0 to 1
- qkv_weight: float32 [5, 512, 1536], P(None, 'vocab'), may hold values from -0.25 to 0.25
- out_weight: float32 [5, 512, 512], P(None, 'vocab'), may hold values from -1 to 1
- up_weight: float32 [3, 512, 2048], P(None, 'vocab'), may hold values from -0.25 to 0.25
- down_weight: float32 [3, 2048, 512], P(None, 'vocab'), may hold values from -0.125 to 0.125
- norm_gains: float32 [11, 512], P(None, 'vocab'), may hold values from 0.5 to 1.5
- embed_table: float32 [4096, 512], P('vocab'), may hold values from -0.25 to 0.25
- qkv_first: float32 [5, 512, 1536], P(None, 'vocab'), may hold values from -1.9073486e-06 to 1.9073486e-06
- out_first: float32 [5, 512, 512], P(None, 'vocab'), may hold values from -1.9073486e-06 to 1.9073486e-06
- up_first: float32 [3, 512, 2048], P(None, 'vocab'), may hold values from -1.9073486e-06 to 1.9073486e-06
- down_first: float32 [3, 2048, 512], P(None, 'vocab'), may hold values from -1.9073486e-06 to 1.9073486e-06
- gains_first: float32 [11, 512], P(None, 'vocab'), may hold values from -1.9073486e-06 to 1.9073486e-06
- table_first: float32 [4096, 512], P('vocab'), may hold values from -1.9073486e-06 to 1.9073486e-06
- qkv_second: float32 [5, 512, 1536], P(None, 'vocab'), may hold values from 3.6664634e-15 to 5.8663415e-14
- out_second: float32 [5, 512, 512], P(None, 'vocab'), may hold values from 3.6664634e-15 to 5.8663415e-14
- up_second: float32 [3, 512, 2048], P(None, 'vocab'), may hold values from 3.6664634e-15 to 5.8663415e-14
- down_second: float32 [3, 2048, 512], P(None, 'vocab'), may hold values from 3.6664634e-15 to 5.8663415e-14
- gains_second: float32 [11, 512], P(None, 'vocab'), may hold values from 3.6664634e-15 to 5.8663415e-14
- table_second: float32 [4096, 512], P('vocab'), may hold values from 3.6664634e-15 to 5.8663415e-14
Outputs:
- loss_total: float32 [], replicated
- grad_norm: float32 [], replicated
- new_qkv: float32 [5, 512, 1536], P(None, 'vocab')
- new_out: float32 [5, 512, 512], P(None, 'vocab')
- new_up: float32 [3, 512, 2048], P(None, 'vocab')
- new_down: float32 [3, 2048, 512], P(None, 'vocab')
- gains_grad: float32 [11, 512], P(None, 'vocab')
- new_table: float32 [4096, 512], P('vocab')
- new_qkv_first: float32 [5, 512, 1536], P(None, 'vocab')
- new_out_first: float32 [5, 512, 512], P(None, 'vocab')
- new_up_first: float32 [3, 512, 2048], P(None, 'vocab')
- new_down_first: float32 [3, 2048, 512], P(None, 'vocab')
- new_gains_first: float32 [11, 512], P(None, 'vocab')
- new_table_first: float32 [4096, 512], P('vocab')
- new_qkv_second: float32 [5, 512, 1536], P(None, 'vocab')
- new_out_second: float32 [5, 512, 512], P(None, 'vocab')
- new_up_second: float32 [3, 512, 2048], P(None, 'vocab')
- new_down_second: float32 [3, 2048, 512], P(None, 'vocab')
- new_gains_second: float32 [11, 512], P(None, 'vocab')
- new_table_second: float32 [4096, 512], P('vocab')
All inputs are finite; a program needn't handle non-finite values.
Results may differ from a plain program's by a relative error of at most 0.0078.
The roundings to bfloat16 on the way count: a program that leaves them out, or rounds other values in their place, can miss the bound.
Values may be sent and summed in bfloat16 or wider, within the bound.
No kernel may reach another device: no remote copies, remote signals or barrier semaphores. Data moves between devices by JAX's collectives and lax.ppermute only.
A program may use at most 768 MiB of HBM per device.

v0:
```python
import math

import jax
import jax.numpy as jnp
from jax import lax
from jax.sharding import PartitionSpec as P

HEADS = 8
HEAD = 64
ENC = 1
LAYERS = 2
MICRO = 2


NORM_EPS = 1e-06
CLIP_NORM = 0.01
LEARN_RATE = 0.05
BETA_ONE = 0.9
BETA_TWO = 0.999
ADAM_EPS = 1e-08
WEIGHT_DECAY = 0.01
ADAM_STEP = 10
LOGIT_SCALE = 4.0
NEGATIVE = -1e30


def merged(array, axis, combine):
    everything = jax.tree.map(lambda part: lax.all_gather(part, axis), array)
    initial = jax.tree.map(lambda part: part[0], everything)

    def lap(k, so_far):
        return combine(so_far, jax.tree.map(lambda part: part[k], everything))

    return lax.fori_loop(1, lax.axis_size(axis), lap, initial)


def normalize(v, g):
    return v * lax.rsqrt(jnp.mean(v * v, axis=-1, keepdims=True) + NORM_EPS) * g


def norm_back(v, g, cotangent):
    _, pullback = jax.vjp(normalize, v, g)
    return pullback(cotangent)


def product(a, b):
    return jnp.dot(a, b, preferred_element_type=jnp.float32)


def outer_sum(a, b):
    return lax.dot_general(a, b, (((0,), (0,)), ((), ())), preferred_element_type=jnp.float32)


def against_rows(a, b):
    return lax.dot_general(a, b, (((1,), (1,)), ((), ())), preferred_element_type=jnp.float32)


def split_heads(v):
    return v.reshape(v.shape[0], HEADS, HEAD)


def score_block(queries, keys, allowed):
    scores = jnp.einsum(
        "qhd,khd->hqk", queries, keys, preferred_element_type=jnp.float32
    ) * HEAD ** (-0.5)
    return jnp.where(allowed[None], scores, NEGATIVE)


def combine_stats(first, later):
    top = jnp.maximum(first[0], later[0])
    return (
        top,
        first[1] * jnp.exp(first[0] - top) + later[1] * jnp.exp(later[0] - top),
        first[2] + later[2],
    )


def adam_update(master, first, second, grad):
    first = BETA_ONE * first + (1.0 - BETA_ONE) * grad
    second = BETA_TWO * second + (1.0 - BETA_TWO) * grad * grad
    fixed_first = first / (1.0 - BETA_ONE**ADAM_STEP)
    fixed_second = second / (1.0 - BETA_TWO**ADAM_STEP)
    master = master - LEARN_RATE * (
        fixed_first / (jnp.sqrt(fixed_second) + ADAM_EPS) + WEIGHT_DECAY * master
    )
    return (master, first, second)


def attend_forward(queries, keys_local, values_local, mask):
    n = queries.shape[0]
    keys_all, values_all = (
        lax.all_gather(keys_local, "seq", axis=0, tiled=True),
        lax.all_gather(values_local, "seq", axis=0, tiled=True),
    )
    scores = score_block(queries, split_heads(keys_all), mask)
    top = jnp.max(scores, axis=-1, keepdims=True)
    expo = jnp.exp(scores - top)
    denom = jnp.sum(expo, axis=-1, keepdims=True)
    probs = (expo / denom).astype(jnp.bfloat16)
    lse = top + jnp.log(denom)
    attended = (
        jnp.einsum(
            "hqk,khd->qhd", probs, split_heads(values_all), preferred_element_type=jnp.float32
        )
        .reshape(n, -1)
        .astype(jnp.bfloat16)
    )
    return (attended, (keys_all, values_all, lse))


def attend_backward(queries, saved, mask, wout, grad_low):
    n = queries.shape[0]
    keys_all, values_all, lse = saved
    width = keys_all.shape[1]
    keys = split_heads(keys_all)
    values = split_heads(values_all)
    probs = jnp.exp(score_block(queries, keys, mask) - lse)
    probs_low = probs.astype(jnp.bfloat16)
    attended = (
        jnp.einsum("hqk,khd->qhd", probs_low, values, preferred_element_type=jnp.float32)
        .reshape(n, width)
        .astype(jnp.bfloat16)
    )
    grad_wout = outer_sum(attended, grad_low)
    grad_att = split_heads(against_rows(grad_low, wout).astype(jnp.bfloat16))
    grad_values = jnp.einsum(
        "hqk,qhd->khd", probs_low, grad_att, preferred_element_type=jnp.float32
    )
    grad_probs = jnp.einsum("qhd,khd->hqk", grad_att, values, preferred_element_type=jnp.float32)
    grad_scores = (
        probs * (grad_probs - jnp.sum(probs * grad_probs, axis=-1, keepdims=True))
    ).astype(jnp.bfloat16)
    grad_queries = jnp.einsum(
        "hqk,khd->qhd", grad_scores, keys, preferred_element_type=jnp.float32
    ) * HEAD ** (-0.5)
    grad_keys = jnp.einsum(
        "hqk,qhd->khd", grad_scores, queries, preferred_element_type=jnp.float32
    ) * HEAD ** (-0.5)
    grad_key_own, grad_value_own = (
        lax.psum_scatter(grad_keys.reshape(-1, width), "seq", scatter_dimension=0, tiled=True),
        lax.psum_scatter(grad_values.reshape(-1, width), "seq", scatter_dimension=0, tiled=True),
    )
    return (grad_queries.reshape(n, width), grad_key_own, grad_value_own, grad_wout)


def self_inputs(x, wqkv, gain):
    normed = normalize(x, gain).astype(jnp.bfloat16)
    return (normed, product(normed, wqkv).astype(jnp.bfloat16))


def self_forward(x, wqkv, wout, gain, mask):
    width = x.shape[1]
    normed, packed = self_inputs(x, wqkv, gain)
    attended, saved = attend_forward(
        split_heads(packed[:, :width]), packed[:, width : 2 * width], packed[:, 2 * width :], mask
    )
    return (x + product(attended, wout), saved)


def self_backward(x, saved, wqkv, wout, gain, mask, grad_out):
    width = x.shape[1]
    normed, packed = self_inputs(x, wqkv, gain)
    grad_low = grad_out.astype(jnp.bfloat16)
    grad_q, grad_k, grad_v, grad_wout = attend_backward(
        split_heads(packed[:, :width]), saved, mask, wout, grad_low
    )
    grad_packed = jnp.concatenate([grad_q, grad_k, grad_v], axis=1).astype(jnp.bfloat16)
    grad_wqkv = outer_sum(normed, grad_packed)
    grad_in, grad_gain = norm_back(x, gain, against_rows(grad_packed, wqkv))
    return (grad_out + grad_in, grad_wqkv, grad_wout, grad_gain)


def cross_inputs(x, wqkv, gain):
    width = x.shape[1]
    normed = normalize(x, gain).astype(jnp.bfloat16)
    return (normed, product(normed, wqkv[:, :width]).astype(jnp.bfloat16))


def cross_forward(x, memory, wqkv, wout, gain, mask):
    width = x.shape[1]
    normed, queries = cross_inputs(x, wqkv, gain)
    pair = product(memory, wqkv[:, width:]).astype(jnp.bfloat16)
    attended, saved = attend_forward(split_heads(queries), pair[:, :width], pair[:, width:], mask)
    return (x + product(attended, wout), saved)


def cross_backward(x, memory, saved, wqkv, wout, gain, mask, grad_out):
    width = x.shape[1]
    normed, queries = cross_inputs(x, wqkv, gain)
    grad_low = grad_out.astype(jnp.bfloat16)
    grad_q, grad_k, grad_v, grad_wout = attend_backward(
        split_heads(queries), saved, mask, wout, grad_low
    )
    grad_q_low = grad_q.astype(jnp.bfloat16)
    grad_pair = jnp.concatenate([grad_k, grad_v], axis=1).astype(jnp.bfloat16)
    grad_wqkv = jnp.concatenate(
        [outer_sum(normed, grad_q_low), outer_sum(memory, grad_pair)], axis=1
    )
    grad_memory = against_rows(grad_pair, wqkv[:, width:])
    grad_in, grad_gain = norm_back(x, gain, against_rows(grad_q_low, wqkv[:, :width]))
    return (grad_out + grad_in, grad_memory, grad_wqkv, grad_wout, grad_gain)


def ffn_inputs(x, wup, gain):
    normed = normalize(x, gain).astype(jnp.bfloat16)
    return (normed, product(normed, wup))


def ffn_forward(x, wup, wdown, gain):
    normed, hidden = ffn_inputs(x, wup, gain)
    return x + product(jnp.maximum(hidden, 0.0).astype(jnp.bfloat16), wdown)


def ffn_backward(x, wup, wdown, gain, grad_out):
    normed, hidden = ffn_inputs(x, wup, gain)
    relu_low = jnp.maximum(hidden, 0.0).astype(jnp.bfloat16)
    grad_low = grad_out.astype(jnp.bfloat16)
    grad_down = outer_sum(relu_low, grad_low)
    grad_relu = against_rows(grad_low, wdown)
    grad_hidden = jnp.where(hidden > 0.0, grad_relu, 0.0).astype(jnp.bfloat16)
    grad_up = outer_sum(normed, grad_hidden)
    grad_in, grad_gain = norm_back(x, gain, against_rows(grad_hidden, wup))
    return (grad_out + grad_in, grad_up, grad_down, grad_gain)


def layer_forward(x, parts, gains, self_mask, cross_mask, memory):
    inputs = [x]
    saved = []
    x, kept = self_forward(x, parts[0], parts[1], gains[0], self_mask)
    saved.append(kept)
    inputs.append(x)
    if memory is not None:
        x, kept = cross_forward(x, memory, parts[2], parts[3], gains[1], cross_mask)
        saved.append(kept)
        inputs.append(x)
    x = ffn_forward(x, parts[4], parts[5], gains[-1])
    return (x, (inputs, saved))


def layer_backward(parts, gains, kept, self_mask, cross_mask, memory, grad):
    inputs, saved = kept
    grad, grad_up, grad_down, gain_ffn = ffn_backward(
        inputs[-1], parts[4], parts[5], gains[-1], grad
    )
    extra = None
    if memory is not None:
        grad, grad_memory, grad_cross_qkv, grad_cross_out, gain_cross = cross_backward(
            inputs[1], memory, saved[1], parts[2], parts[3], gains[1], cross_mask, grad
        )
        extra = (grad_memory, grad_cross_qkv, grad_cross_out, gain_cross)
    grad, grad_qkv, grad_out_proj, gain_self = self_backward(
        inputs[0], saved[0], parts[0], parts[1], gains[0], self_mask, grad
    )
    return (grad, (grad_qkv, grad_out_proj, grad_up, grad_down, gain_self, gain_ffn), extra)


def shards(
    tokens,
    source,
    segments,
    loss_rows,
    targets,
    exit_depth,
    qkv_weight,
    out_weight,
    up_weight,
    down_weight,
    norm_gains,
    embed_table,
    qkv_first,
    out_first,
    up_first,
    down_first,
    gains_first,
    table_first,
    qkv_second,
    out_second,
    up_second,
    down_second,
    gains_second,
    table_second,
):
    seq_count = lax.axis_size("seq")
    vocab_count = lax.axis_size("vocab")
    seq_index = lax.axis_index("seq")
    vocab_index = lax.axis_index("vocab")
    tok_dev = tokens.shape[2]
    loss_dev = targets.shape[2]
    voc_dev = embed_table.shape[0]
    width = embed_table.shape[1]
    gain_count = norm_gains.shape[0]
    length = tok_dev * seq_count
    root_width = math.sqrt(width)
    table_low = embed_table.astype(jnp.bfloat16)
    table_whole = lax.all_gather(table_low, "vocab", axis=0, tiled=True)
    seen_targets, seen_depth, seen_segments = (
        lax.all_gather(targets, ("seq", "vocab"), axis=1, tiled=True),
        lax.all_gather(exit_depth, ("seq", "vocab"), axis=1, tiled=True),
        lax.all_gather(segments, ("seq", "vocab"), axis=1, tiled=True),
    )
    reach_local = jnp.stack(
        [
            jnp.sum((seen_depth >= layer_id).astype(jnp.float32), axis=(1, 2))
            for layer_id in range(LAYERS)
        ],
        axis=1,
    )
    reach = jnp.maximum(reach_local, 1.0)
    my_targets = lax.dynamic_index_in_dim(
        seen_targets.reshape(MICRO, seq_count, vocab_count, loss_dev), seq_index, 1, False
    )
    my_depth = lax.dynamic_index_in_dim(
        seen_depth.reshape(MICRO, seq_count, vocab_count, loss_dev), seq_index, 1, False
    )
    key_segments = lax.dynamic_index_in_dim(
        seen_segments.reshape(MICRO, seq_count, vocab_count, tok_dev), vocab_index, 2, False
    ).reshape(MICRO, length)
    places = seq_index * tok_dev + jnp.arange(tok_dev)
    key_places = jnp.arange(length)
    layer_ids = jnp.arange(LAYERS)
    weights = None
    owned_total = None
    table_total = jnp.zeros((voc_dev, width), jnp.float32)
    logit_table_grad = jnp.zeros((voc_dev, width), jnp.float32)
    loss_part = jnp.zeros((), jnp.float32)
    for micro in range(MICRO):
        weights = (
            lax.all_gather(qkv_weight.astype(jnp.bfloat16), "vocab", axis=1, tiled=True),
            lax.all_gather(out_weight.astype(jnp.bfloat16), "vocab", axis=1, tiled=True),
            lax.all_gather(up_weight.astype(jnp.bfloat16), "vocab", axis=1, tiled=True),
            lax.all_gather(down_weight.astype(jnp.bfloat16), "vocab", axis=1, tiled=True),
            lax.all_gather(norm_gains.astype(jnp.bfloat16), "vocab", axis=1, tiled=True),
        )
        gains_full = weights[4].astype(jnp.float32)

        def encoder_parts(enc_id):
            return (
                (
                    weights[0][enc_id],
                    weights[1][enc_id],
                    None,
                    None,
                    weights[2][enc_id],
                    weights[3][enc_id],
                ),
                (gains_full[2 * enc_id], gains_full[2 * enc_id + 1]),
            )

        def decoder_parts(layer_id):
            slot = ENC + 2 * layer_id
            base = 2 * ENC + 1 + 4 * layer_id
            return (
                (
                    weights[0][slot],
                    weights[1][slot],
                    weights[0][slot + 1],
                    weights[1][slot + 1],
                    weights[2][ENC + layer_id],
                    weights[3][ENC + layer_id],
                ),
                (gains_full[base], gains_full[base + 1], gains_full[base + 2]),
            )

        target_ids = tokens[micro, 0]
        source_ids = source[micro, 0]
        same = segments[micro, 0][:, None] == key_segments[micro][None, :]
        allowed = same & (places[:, None] >= key_places[None, :])
        local_rows = loss_rows[micro, 0]
        enc_states = [table_whole[source_ids].astype(jnp.float32) * root_width]
        enc_id = 0
        parts, gains = encoder_parts(enc_id)
        x_next, kept = layer_forward(enc_states[-1], parts, gains, same, same, None)
        enc_states.append(x_next)
        enc_saved = [kept]
        final_gain = gains_full[2 * ENC]
        memory = normalize(enc_states[-1], final_gain).astype(jnp.bfloat16)
        states = [table_whole[target_ids].astype(jnp.float32) * root_width]
        saved_list = []
        for layer_id in range(LAYERS):
            parts, gains = decoder_parts(layer_id)
            x_next, kept = layer_forward(states[-1], parts, gains, allowed, same, memory)
            states.append(x_next)
            saved_list.append(kept)
        exit_gains = [gains_full[2 * ENC + 4 + 4 * layer_id] for layer_id in range(LAYERS)]
        exit_local = jnp.stack(
            [
                normalize(states[layer_id + 1][local_rows], exit_gains[layer_id])
                for layer_id in range(LAYERS)
            ]
        ).astype(jnp.bfloat16)
        exit_all = lax.all_gather(exit_local, "vocab", axis=1, tiled=True)
        logits = (
            jnp.einsum("lrd,vd->lrv", exit_all, table_low, preferred_element_type=jnp.float32)
            * LOGIT_SCALE
        )
        wanted = my_targets[micro].reshape(-1) - vocab_index * voc_dev
        onehot = (jnp.arange(voc_dev)[None, :] == wanted[:, None]).astype(jnp.float32)
        picked = jnp.sum(logits * onehot[None], axis=-1)
        top = jnp.max(logits, axis=-1)
        sums = jnp.sum(jnp.exp(logits - top[..., None]), axis=-1)
        top, sums, picked = merged((top, sums, picked), "vocab", combine_stats)
        lse = top + jnp.log(sums)
        shares = (
            (my_depth[micro].reshape(-1)[None, :] >= layer_ids[:, None]).astype(jnp.float32)
            / reach[micro][:, None]
            / MICRO
        )
        loss_part = loss_part + jnp.sum((lse - picked) * shares)
        grad_logits = (
            (jnp.exp(logits - lse[..., None]) - onehot[None]) * shares[..., None] * LOGIT_SCALE
        ).astype(jnp.bfloat16)
        logit_table_grad = logit_table_grad + jnp.einsum(
            "lrv,lrd->vd", grad_logits, exit_all, preferred_element_type=jnp.float32
        )
        grad_exit_part = jnp.einsum(
            "lrv,vd->lrd", grad_logits, table_low, preferred_element_type=jnp.float32
        )
        grad_exits = lax.psum_scatter(grad_exit_part, "vocab", scatter_dimension=1, tiled=True)
        qkv_parts = [None] * (ENC + 2 * LAYERS)
        out_parts = [None] * (ENC + 2 * LAYERS)
        up_parts = [None] * (ENC + LAYERS)
        down_parts = [None] * (ENC + LAYERS)
        gain_parts = [None] * gain_count
        grad_x = jnp.zeros((tok_dev, width), jnp.float32)
        grad_memory = jnp.zeros((tok_dev, width), jnp.float32)
        for layer_id in reversed(range(LAYERS)):
            slot = ENC + 2 * layer_id
            base = 2 * ENC + 1 + 4 * layer_id
            grad_rows, gain_exit = norm_back(
                states[layer_id + 1][local_rows], exit_gains[layer_id], grad_exits[layer_id]
            )
            grad_x = grad_x.at[local_rows].add(grad_rows)
            parts, gains = decoder_parts(layer_id)
            grad_x, own, extra = layer_backward(
                parts, gains, saved_list[layer_id], allowed, same, memory, grad_x
            )
            grad_memory = grad_memory + extra[0]
            qkv_parts[slot], out_parts[slot] = (own[0], own[1])
            qkv_parts[slot + 1], out_parts[slot + 1] = (extra[1], extra[2])
            up_parts[ENC + layer_id], down_parts[ENC + layer_id] = (own[2], own[3])
            gain_parts[base], gain_parts[base + 1], gain_parts[base + 2], gain_parts[base + 3] = (
                own[4],
                extra[3],
                own[5],
                gain_exit,
            )
        grad_enc, gain_parts[2 * ENC] = norm_back(enc_states[-1], final_gain, grad_memory)
        for enc_id in reversed(range(ENC)):
            parts, gains = encoder_parts(enc_id)
            grad_enc, own, _ = layer_backward(
                parts, gains, enc_saved[enc_id], same, same, None, grad_enc
            )
            qkv_parts[enc_id], out_parts[enc_id], up_parts[enc_id], down_parts[enc_id] = (
                own[0],
                own[1],
                own[2],
                own[3],
            )
            gain_parts[2 * enc_id], gain_parts[2 * enc_id + 1] = (own[4], own[5])
        stacked = (
            jnp.stack(qkv_parts),
            jnp.stack(out_parts),
            jnp.stack(up_parts),
            jnp.stack(down_parts),
            jnp.stack(gain_parts),
        )
        token_ids = jnp.concatenate([target_ids, source_ids])
        token_grads = (jnp.concatenate([grad_x, grad_enc]) * root_width).astype(jnp.bfloat16)
        owned = (
            lax.psum_scatter(stacked[0], "vocab", scatter_dimension=1, tiled=True),
            lax.psum_scatter(stacked[1], "vocab", scatter_dimension=1, tiled=True),
            lax.psum_scatter(stacked[2], "vocab", scatter_dimension=1, tiled=True),
            lax.psum_scatter(stacked[3], "vocab", scatter_dimension=1, tiled=True),
            lax.psum_scatter(stacked[4], "vocab", scatter_dimension=1, tiled=True),
        )
        start = jnp.int32(0)
        count = voc_dev * lax.axis_size("vocab")
        inside = (token_ids >= start) & (token_ids < start + count)
        local = jnp.where(inside, token_ids, count)
        table_part = lax.psum_scatter(
            jax.ops.segment_sum(token_grads.astype(jnp.float32), local, num_segments=count + 1)[
                :count
            ],
            "vocab",
            scatter_dimension=0,
            tiled=True,
        )
        owned, table_part = (tuple(owned), table_part)
        owned_total = (
            owned if owned_total is None else tuple((a + b for a, b in zip(owned_total, owned)))
        )
        table_total = table_total + table_part
    table_grad = table_total + logit_table_grad
    summed = lax.psum(
        (
            owned_total[0],
            owned_total[1],
            owned_total[2],
            owned_total[3],
            owned_total[4],
            table_grad,
            loss_part,
        ),
        "seq",
    )
    gradients = summed[:6]
    loss_total = summed[6]
    squares = sum((jnp.sum(grad * grad) for grad in gradients))
    grad_norm = jnp.sqrt(lax.psum(squares, "vocab"))
    clip_factor = CLIP_NORM / jnp.maximum(grad_norm, CLIP_NORM)
    masters = (qkv_weight, out_weight, up_weight, down_weight, norm_gains, embed_table)
    firsts = (qkv_first, out_first, up_first, down_first, gains_first, table_first)
    seconds = (qkv_second, out_second, up_second, down_second, gains_second, table_second)
    results = [
        adam_update(masters[i], firsts[i], seconds[i], gradients[i] * clip_factor) for i in range(6)
    ]
    gains_grad = gradients[4] * clip_factor
    return (
        loss_total,
        grad_norm,
        results[0][0],
        results[1][0],
        results[2][0],
        results[3][0],
        gains_grad,
        results[5][0],
        results[0][1],
        results[1][1],
        results[2][1],
        results[3][1],
        results[4][1],
        results[5][1],
        results[0][2],
        results[1][2],
        results[2][2],
        results[3][2],
        results[4][2],
        results[5][2],
    )


def solution(mesh):
    placed = (
        P(None, "vocab", "seq"),
        P(None, "vocab", "seq"),
        P(None, "vocab", "seq"),
        P(None, "vocab", "seq"),
        P(None, "vocab", "seq"),
        P(None, "vocab", "seq"),
        P(None, "vocab", None),
        P(None, "vocab", None),
        P(None, "vocab", None),
        P(None, "vocab", None),
        P(None, "vocab"),
        P("vocab", None),
        P(None, "vocab", None),
        P(None, "vocab", None),
        P(None, "vocab", None),
        P(None, "vocab", None),
        P(None, "vocab"),
        P("vocab", None),
        P(None, "vocab", None),
        P(None, "vocab", None),
        P(None, "vocab", None),
        P(None, "vocab", None),
        P(None, "vocab"),
        P("vocab", None),
    )
    return jax.shard_map(
        shards,
        mesh=mesh,
        in_specs=placed,
        out_specs=(
            P(),
            P(),
            P(None, "vocab", None),
            P(None, "vocab", None),
            P(None, "vocab", None),
            P(None, "vocab", None),
            P(None, "vocab"),
            P("vocab", None),
            P(None, "vocab", None),
            P(None, "vocab", None),
            P(None, "vocab", None),
            P(None, "vocab", None),
            P(None, "vocab"),
            P("vocab", None),
            P(None, "vocab", None),
            P(None, "vocab", None),
            P(None, "vocab", None),
            P(None, "vocab", None),
            P(None, "vocab"),
            P("vocab", None),
        ),
        check_vma=False,
    )
```

profile of v0, /device:TPU:0, one launch (start us, length us, event | category | flops | bytes accessed | tf_op | source)
XLA Modules:
  0.0 2760.0 jit_solution(13271640131451688009)
XLA Ops:
  28.8 31.6 %all-gather.39.cloned.1.call-done = bf16[4096,512]{1,0:T(8,128)(2,1)} async-done(((bf16[512,512]{1,0:T(8,128)(2,1)}), bf16[4096,512]{1,0:T(8,128)(2,1)}) %all-gather.39.cloned.1.call-update) | async-done | bytes 4194320 | tf_op jit(solution)/shard_map/all_gather | solution.py:295
  65.1 74.1 %all-gather.41.cloned.1.call-done = bf16[5,512,1536]{2,1,0:T(8,128)(2,1)} async-done(((bf16[5,64,1536]{2,1,0:T(8,128)(2,1)}), bf16[5,512,1536]{2,1,0:T(8,128)(2,1)}) %all-gather.41.cloned.1.call-update) | async-done | bytes 7864336 | tf_op jit(solution)/shard_map/all_gather | solution.py:328
  170.8 39.5 %all_gather.138 = s32[2,32,256]{2,0,1:T(2,128)S(1)} all-gather(s32[2,1,256]{2,0,1:T(2,128)S(1)} %copy.239), channel_id=1, replica_groups=mesh['seq'=4,'vocab'=8] {'seq','vocab'}, dimensions={1}, use_global_device_ids=true | all-gather | bytes 67584 | tf_op jit(solution)/shard_map/all_gather | solution.py:299
  234.0 26.4 all-gather.51.cloned.1.call-done
  298.2 58.2 %all-gather.53.cloned.1.call-done = bf16[3,512,2048]{2,1,0:T(8,128)(2,1)} async-done(((bf16[3,64,2048]{2,1,0:T(8,128)(2,1)}), bf16[3,512,2048]{2,1,0:T(8,128)(2,1)}) %all-gather.53.cloned.1.call-update) | async-done | bytes 6291472 | tf_op jit(solution)/shard_map/all_gather | solution.py:330
  358.8 63.3 %all-gather.55.cloned.1.call-done = bf16[3,2048,512]{2,1,0:T(8,128)(2,1)} async-done(((bf16[3,256,512]{2,1,0:T(8,128)(2,1)}), bf16[3,2048,512]{2,1,0:T(8,128)(2,1)}) %all-gather.55.cloned.1.call-update) | async-done | bytes 6291472 | tf_op jit(solution)/shard_map/all_gather | solution.py:331
  438.0 39.2 %all_gather.159 = s32[2,32,32]{2,0,1:T(2,128)S(1)} all-gather(s32[2,1,32]{2,0,1:T(2,128)S(1)} %bitcast.1093), channel_id=1, replica_groups=mesh['seq'=4,'vocab'=8] {'seq','vocab'}, dimensions={1}, use_global_device_ids=true | all-gather | bytes 8448 | tf_op jit(solution)/shard_map/all_gather | solution.py:298
  477.2 36.7 %all_gather.156 = s32[2,32,32]{2,0,1:T(2,128)S(1)} all-gather(s32[2,1,32]{2,0,1:T(2,128)S(1)} %bitcast.1094), channel_id=1, replica_groups=mesh['seq'=4,'vocab'=8] {'seq','vocab'}, dimensions={1}, use_global_device_ids=true | all-gather | bytes 8448 | tf_op jit(solution)/shard_map/all_gather | solution.py:297
  682.9 25.9 all-gather.87.cloned.1.call-done
  711.1 26.1 all-gather.65.cloned.1.call-done
  739.4 26.2 all-gather.67.cloned.1.call-done
  767.9 26.8 all-gather.83.cloned.1.call-done
  1059.7 32.9 %reduce-scatter.31.cloned.1.call-done = f32[2,32,512]{2,1,0:T(8,128)} async-done(((f32[2,256,512]{2,1,0:T(8,128)}), f32[2,32,512]{2,1,0:T(8,128)}) %reduce-scatter.31.cloned.1.call-update) | async-done | bytes 131088 | tf_op jit(solution)/shard_map/reduce_scatter | solution.py:418
  1227.5 34.2 %reduce-scatter.61.cloned.1.call-done = f32[256,512]{0,1:T(8,128)} async-done(((f32[1024,512]{0,1:T(8,128)}), f32[256,512]{0,1:T(8,128)}) %reduce-scatter.61.cloned.1.call-update) | async-done | bytes 524304 | tf_op jit(solution)/shard_map/reduce_scatter | solution.py:141
  1262.8 37.4 %reduce-scatter.59.cloned.1.call-done = f32[256,512]{0,1:T(8,128)} async-done(((f32[1024,512]{0,1:T(8,128)}), f32[256,512]{0,1:T(8,128)}) %reduce-scatter.59.cloned.1.call-update) | async-done | bytes 524304 | tf_op jit(solution)/shard_map/reduce_scatter | solution.py:140
  1418.4 35.0 %reduce-scatter.55.cloned.1.call-done = f32[256,512]{0,1:T(8,128)} async-done(((f32[1024,512]{0,1:T(8,128)}), f32[256,512]{0,1:T(8,128)}) %reduce-scatter.55.cloned.1.call-update) | async-done | bytes 524304 | tf_op jit(solution)/shard_map/reduce_scatter | solution.py:140
  1469.0 22.3 reduce-scatter.43.cloned.1.call-done
  1492.4 37.2 %reduce-scatter.41.cloned.1.call-done = f32[256,512]{0,1:T(8,128)} async-done(((f32[1024,512]{0,1:T(8,128)}), f32[256,512]{0,1:T(8,128)}) %reduce-scatter.41.cloned.1.call-update) | async-done | bytes 524304 | tf_op jit(solution)/shard_map/reduce_scatter | solution.py:140
  1530.8 37.1 %reduce-scatter.65.cloned.1.call-done = f32[256,512]{0,1:T(8,128)} async-done(((f32[1024,512]{0,1:T(8,128)}), f32[256,512]{0,1:T(8,128)}) %reduce-scatter.65.cloned.1.call-update) | async-done | bytes 524304 | tf_op jit(solution)/shard_map/reduce_scatter | solution.py:141
  1569.0 37.2 %reduce-scatter.63.cloned.1.call-done = f32[256,512]{0,1:T(8,128)} async-done(((f32[1024,512]{0,1:T(8,128)}), f32[256,512]{0,1:T(8,128)}) %reduce-scatter.63.cloned.1.call-update) | async-done | bytes 524304 | tf_op jit(solution)/shard_map/reduce_scatter | solution.py:140
  1684.7 36.4 %reduce-scatter.51.cloned.1.call-done = f32[256,512]{0,1:T(8,128)} async-done(((f32[1024,512]{0,1:T(8,128)}), f32[256,512]{0,1:T(8,128)}) %reduce-scatter.51.cloned.1.call-update) | async-done | bytes 524304 | tf_op jit(solution)/shard_map/reduce_scatter | solution.py:141
  1722.8 36.5 %reduce-scatter.49.cloned.1.call-done = f32[256,512]{0,1:T(8,128)} async-done(((f32[1024,512]{0,1:T(8,128)}), f32[256,512]{0,1:T(8,128)}) %reduce-scatter.49.cloned.1.call-update) | async-done | bytes 524304 | tf_op jit(solution)/shard_map/reduce_scatter | solution.py:140
  1771.7 25.8 reduce-scatter.69.cloned.1.call-done
  1799.3 36.5 %reduce-scatter.67.cloned.1.call-done = f32[256,512]{0,1:T(8,128)} async-done(((f32[1024,512]{0,1:T(8,128)}), f32[256,512]{0,1:T(8,128)}) %reduce-scatter.67.cloned.1.call-update) | async-done | bytes 524304 | tf_op jit(solution)/shard_map/reduce_scatter | solution.py:140
  1837.6 36.3 %reduce-scatter.47.cloned.1.call-done = f32[256,512]{0,1:T(8,128)} async-done(((f32[1024,512]{0,1:T(8,128)}), f32[256,512]{0,1:T(8,128)}) %reduce-scatter.47.cloned.1.call-update) | async-done | bytes 524304 | tf_op jit(solution)/shard_map/reduce_scatter | solution.py:141
  1875.7 36.6 %reduce-scatter.45.cloned.1.call-done = f32[256,512]{0,1:T(8,128)} async-done(((f32[1024,512]{0,1:T(8,128)}), f32[256,512]{0,1:T(8,128)}) %reduce-scatter.45.cloned.1.call-update) | async-done | bytes 524304 | tf_op jit(solution)/shard_map/reduce_scatter | solution.py:140
  2052.6 45.0 %reduce-scatter.77.cloned.1.call-done = f32[5,64,512]{2,1,0:T(8,128)} async-done(((f32[5,512,512]{2,1,0:T(8,128)}), f32[5,64,512]{2,1,0:T(8,128)}) %reduce-scatter.77.cloned.1.call-update) | async-done | bytes 655376 | tf_op jit(solution)/shard_map/reduce_scatter | solution.py:471
  2097.7 129.9 %reduce-scatter.79.cloned.1.call-done = f32[3,64,2048]{2,1,0:T(8,128)} async-done(((f32[3,512,2048]{2,1,0:T(8,128)}), f32[3,64,2048]{2,1,0:T(8,128)}) %reduce-scatter.79.cloned.1.call-update) | async-done | bytes 1572880 | tf_op jit(solution)/shard_map/reduce_scatter | solution.py:472
  2227.6 129.8 %reduce-scatter.81.cloned.1.call-done = f32[3,256,512]{2,1,0:T(8,128)} async-done(((f32[3,2048,512]{2,1,0:T(8,128)}), f32[3,256,512]{2,1,0:T(8,128)}) %reduce-scatter.81.cloned.1.call-update) | async-done | bytes 1572880 | tf_op jit(solution)/shard_map/reduce_scatter | solution.py:473
  2357.3 159.6 %reduce-scatter.75.cloned.1.call-done = f32[5,64,1536]{2,1,0:T(8,128)} async-done(((f32[5,512,1536]{2,1,0:T(8,128)}), f32[5,64,1536]{2,1,0:T(8,128)}) %reduce-scatter.75.cloned.1.call-update) | async-done | bytes 1966096 | tf_op jit(solution)/shard_map/reduce_scatter | solution.py:470
  2518.4 30.0 %reduce-scatter.85.cloned.1.call-done = f32[64,11]{1,0:T(8,128)} async-done(((f32[512,11]{1,0:T(8,128)}), f32[64,11]{1,0:T(8,128)}) %reduce-scatter.85.cloned.1.call-update) | async-done | bytes 2832
  2560.5 140.1 %all-reduce.4.cloned.1.call-done = (f32[5,64,1536]{2,1,0:T(8,128)}, f32[5,64,512]{2,1,0:T(8,128)}, f32[3,64,2048]{2,1,0:T(8,128)}, f32[3,256,512]{2,1,0:T(8,128)}, f32[512,512]{1,0:T(8,128)}) async-done(((f32[5,64,1536]{2,1,0:T(8,128)}, f32[5,64,512]{2,1,0:T(8,128)}, f32[3,64,2048]{2,1,0:T(8,128)}, f32[3,256,512]{2,1,0:T(8,128)}, f32[512,512]{1,0:T(8,128)}), (f32[5,64,1536]{2,1,0:T(8,128)}, ...) | async-done | bytes 6815760 | tf_op jit(solution)/shard_map/psum | solution.py:494
  (1704 shorter events, 1146.1 us)
Async XLA Ops:
  153.4 268.6 %all-gather.55.cloned.1.call-start = ((), (), s32[]{:S(2)}) async-start(), calls=%async_computation.36 | async-start | bytes 7077888 | tf_op jit(solution)/shard_map/all_gather | solution.py:331
  154.5 364.3 %all-gather.71.cloned.1.call-start = ((), (), s32[]{:S(2)}) async-start(), calls=%async_computation.44 | async-start | bytes 1310720 | tf_op jit(solution)/shard_map/all_gather | solution.py:92
  162.2 363.0 %all-gather.69.cloned.1.call-start = ((), (), s32[]{:S(2)}) async-start(), calls=%async_computation.43 | async-start | bytes 1310720 | tf_op jit(solution)/shard_map/all_gather | solution.py:93
  162.9 378.8 %all-gather.45.cloned.1.call-start = ((), (), s32[]{:S(2)}) async-start(), calls=%async_computation.31 | async-start | bytes 1310720 | tf_op jit(solution)/shard_map/all_gather | solution.py:92
  170.7 380.1 %all-gather.43.cloned.1.call-start = ((), (), s32[]{:S(2)}) async-start(), calls=%async_computation.30 | async-start | bytes 1310720 | tf_op jit(solution)/shard_map/all_gather | solution.py:93
  212.9 352.3 %all-gather.79.cloned.1.call-start = ((), (), s32[]{:S(2)}) async-start(), calls=%async_computation.48 | async-start | bytes 1310720 | tf_op jit(solution)/shard_map/all_gather | solution.py:92
  436.6 243.8 %all-gather.85.cloned.1.call-start = ((), (), s32[]{:S(2)}) async-start(), calls=%async_computation.51 | async-start | bytes 1310720 | tf_op jit(solution)/shard_map/all_gather | solution.py:93
  438.0 270.8 %all-gather.87.cloned.1.call-start = ((), (), s32[]{:S(2)}) async-start(), calls=%async_computation.52 | async-start | bytes 1310720 | tf_op jit(solution)/shard_map/all_gather | solution.py:92
  518.7 218.4 %all-gather.65.cloned.1.call-start = ((), (), s32[]{:S(2)}) async-start(), calls=%async_computation.41 | async-start | bytes 1310720 | tf_op jit(solution)/shard_map/all_gather | solution.py:93
  537.8 227.9 %all-gather.67.cloned.1.call-start = ((), (), s32[]{:S(2)}) async-start(), calls=%async_computation.42 | async-start | bytes 1310720 | tf_op jit(solution)/shard_map/all_gather | solution.py:92
  550.7 244.0 %all-gather.83.cloned.1.call-start = ((), (), s32[]{:S(2)}) async-start(), calls=%async_computation.50 | async-start | bytes 1310720 | tf_op jit(solution)/shard_map/all_gather | solution.py:92
  622.2 231.2 %all-gather.63.cloned.1.call-start = ((), (), s32[]{:S(2)}) async-start(), calls=%async_computation.40 | async-start | bytes 1310720 | tf_op jit(solution)/shard_map/all_gather | solution.py:92
  678.9 380.7 %reduce-scatter.53.cloned.1.call-start = ((), (), s32[]{:S(2)}) async-start(), calls=%async_computation.64 | async-start | bytes 1179648 | tf_op jit(solution)/shard_map/reduce_scatter | solution.py:418
  1189.4 224.6 %reduce-scatter.35.cloned.1.call-start = ((), (), s32[]{:S(2)}) async-start(), calls=%async_computation.55 | async-start | bytes 2621440 | tf_op jit(solution)/shard_map/reduce_scatter | solution.py:141
  1195.7 219.6 %reduce-scatter.33.cloned.1.call-start = ((), (), s32[]{:S(2)}) async-start(), calls=%async_computation.54 | async-start | bytes 2621440 | tf_op jit(solution)/shard_map/reduce_scatter | solution.py:140
  1206.9 246.4 %reduce-scatter.55.cloned.1.call-start = ((), (), s32[]{:S(2)}) async-start(), calls=%async_computation.65 | async-start | bytes 2621440 | tf_op jit(solution)/shard_map/reduce_scatter | solution.py:140
  1216.6 274.8 %reduce-scatter.43.cloned.1.call-start = ((), (), s32[]{:S(2)}) async-start(), calls=%async_computation.59 | async-start | bytes 2621440 | tf_op jit(solution)/shard_map/reduce_scatter | solution.py:141
  1350.7 217.2 %reduce-scatter.65.cloned.1.call-start = ((), (), s32[]{:S(2)}) async-start(), calls=%async_computation.70 | async-start | bytes 2621440 | tf_op jit(solution)/shard_map/reduce_scatter | solution.py:141
  1359.4 246.8 %reduce-scatter.63.cloned.1.call-start = ((), (), s32[]{:S(2)}) async-start(), calls=%async_computation.69 | async-start | bytes 2621440 | tf_op jit(solution)/shard_map/reduce_scatter | solution.py:140
  1374.0 300.7 %reduce-scatter.73.cloned.1.call-start = ((), (), s32[]{:S(2)}) async-start(), calls=%async_computation.74 | async-start | bytes 2621440 | tf_op jit(solution)/shard_map/reduce_scatter | solution.py:141
  1392.7 290.2 %reduce-scatter.71.cloned.1.call-start = ((), (), s32[]{:S(2)}) async-start(), calls=%async_computation.73 | async-start | bytes 2621440 | tf_op jit(solution)/shard_map/reduce_scatter | solution.py:140
  1406.9 314.1 %reduce-scatter.51.cloned.1.call-start = ((), (), s32[]{:S(2)}) async-start(), calls=%async_computation.63 | async-start | bytes 2621440 | tf_op jit(solution)/shard_map/reduce_scatter | solution.py:141
  1413.7 345.7 %reduce-scatter.49.cloned.1.call-start = ((), (), s32[]{:S(2)}) async-start(), calls=%async_computation.62 | async-start | bytes 2621440 | tf_op jit(solution)/shard_map/reduce_scatter | solution.py:140
  1469.0 328.6 %reduce-scatter.69.cloned.1.call-start = ((), (), s32[]{:S(2)}) async-start(), calls=%async_computation.72 | async-start | bytes 2621440 | tf_op jit(solution)/shard_map/reduce_scatter | solution.py:141
  1643.4 230.5 %reduce-scatter.47.cloned.1.call-start = ((), (), s32[]{:S(2)}) async-start(), calls=%async_computation.61 | async-start | bytes 2621440 | tf_op jit(solution)/shard_map/reduce_scatter | solution.py:141
  1653.1 259.1 %reduce-scatter.45.cloned.1.call-start = ((), (), s32[]{:S(2)}) async-start(), calls=%async_computation.60 | async-start | bytes 2621440 | tf_op jit(solution)/shard_map/reduce_scatter | solution.py:140
  1667.5 382.5 %reduce-scatter.83.cloned.1.call-start = ((), (), s32[]{:S(2)}) async-start(), calls=%async_computation.79 | async-start | bytes 9437184 | tf_op jit(solution)/shard_map/reduce_scatter | solution.py:480
  1986.2 241.4 %reduce-scatter.79.cloned.1.call-start = ((), (), s32[]{:S(2)}) async-start(), calls=%async_computation.77 | async-start | bytes 14155776 | tf_op jit(solution)/shard_map/reduce_scatter | solution.py:472
  2002.9 354.4 %reduce-scatter.81.cloned.1.call-start = ((), (), s32[]{:S(2)}) async-start(), calls=%async_computation.78 | async-start | bytes 14155776 | tf_op jit(solution)/shard_map/reduce_scatter | solution.py:473
  2019.8 497.1 %reduce-scatter.75.cloned.1.call-start = ((), (), s32[]{:S(2)}) async-start(), calls=%async_computation.75 | async-start | bytes 17694720 | tf_op jit(solution)/shard_map/reduce_scatter | solution.py:470
  2047.2 501.2 %reduce-scatter.85.cloned.1.call-start = ((), (), s32[]{:S(2)}) async-start(), calls=%async_computation.80 | async-start | bytes 294912
  2049.9 650.7 %all-reduce.4.cloned.1.call-start = ((), (), s32[]{:S(2)}) async-start(), calls=%async_computation.81 | async-start | bytes 13631488 | tf_op jit(solution)/shard_map/psum | solution.py:494
  (567 other events, 16086.9 us)
Sparse Core Ops, SparseCore 0:
  10.2 50.1 all-gather.38
  62.6 76.5 all-gather.40
  198.6 33.9 all-gather.46
  291.7 64.6 all-gather.52
  358.6 63.3 all-gather.54
  1061.8 30.7 reduce-scatter.30
  1151.6 33.6 reduce-scatter.38
  1188.5 35.1 reduce-scatter.36
  1226.5 35.1 reduce-scatter.60
  1265.0 35.1 reduce-scatter.58
  1303.2 35.1 reduce-scatter.34
  1341.5 35.1 reduce-scatter.32
  1379.7 35.1 reduce-scatter.56
  1418.1 35.1 reduce-scatter.54
  1456.2 35.1 reduce-scatter.42
  1494.5 35.1 reduce-scatter.40
  1532.7 35.1 reduce-scatter.64
  1570.9 35.1 reduce-scatter.62
  1609.2 35.1 reduce-scatter.72
  1647.6 35.2 reduce-scatter.70
  1685.8 35.1 reduce-scatter.50
  1724.1 35.1 reduce-scatter.48
  1762.3 35.1 reduce-scatter.68
  1800.7 35.1 reduce-scatter.66
  1838.7 35.1 reduce-scatter.46
  1877.0 35.1 reduce-scatter.44
  1947.6 89.5 reduce-scatter.82
  2039.3 58.2 reduce-scatter.76
  2099.9 127.5 reduce-scatter.78
  2229.7 127.5 reduce-scatter.80
  2359.6 157.2 reduce-scatter.74
  2553.8 146.7 all-reduce.3
  (22 shorter events, 585.9 us)
where the time goes:
time: 2770 us; the launch traced here: 2760 us
  waiting for transfers between devices  1610 us (58%)
  matrix products  439 us (16%)
  blocking collectives  265 us (10%)
  other arithmetic  227 us (8%)
  local copies, waits for them, and re-layouts  185 us (7%)
  between operations  29.3 us (1%)
    reduce_scatter x10, waiting for transfers between devices, attend_backward(): lax.psum_scatter(grad_keys.reshape(-1, width), 'seq', scatter_dimension=0...  269 us
    reduce_scatter x10, waiting for transfers between devices, attend_backward(): lax.psum_scatter(grad_values.reshape(-1, width), 'seq', scatter_dimension...  192 us
    reduce_scatter x1, waiting for transfers between devices, shards(): lax.psum_scatter(stacked[0], 'vocab', scatter_dimension=1, tiled=True)  160 us
    psum x1, waiting for transfers between devices, shards(): lax.psum((owned_total[0], owned_total[1], owned_total[2], owned_total[3],...  140 us
    reduce_scatter x1, waiting for transfers between devices, shards(): lax.psum_scatter(stacked[2], 'vocab', scatter_dimension=1, tiled=True)  130 us
    reduce_scatter x1, waiting for transfers between devices, shards(): lax.psum_scatter(stacked[3], 'vocab', scatter_dimension=1, tiled=True)  130 us
    all_gather x10, waiting for transfers between devices, attend_forward(): lax.all_gather(keys_local, 'seq', axis=0, tiled=True)  118 us
    all_gather x10, waiting for transfers between devices, attend_forward(): lax.all_gather(values_local, 'seq', axis=0, tiled=True)  116 us
  transfers between devices with their start and end apart: 54, of which 40 were waited for; matrix products, arithmetic and copies ran while one was open for 22% of the time, Pallas kernels for 0%

commit v1 on v0

v1 whole, which is shorter than its diff:
```python
import functools
import math

import jax
import jax.numpy as jnp
from jax import lax
from jax.experimental import pallas as pl
from jax.experimental.pallas import tpu as pltpu
from jax.sharding import Mesh
from jax.sharding import PartitionSpec as P

HEADS = 8
HEAD = 64
ENC = 1
LAYERS = 2
MICRO = 2
COL = 512

NORM_EPS = 1e-06
CLIP_NORM = 0.01
LEARN_RATE = 0.05
BETA_ONE = 0.9
BETA_TWO = 0.999
ADAM_EPS = 1e-08
WEIGHT_DECAY = 0.01
ADAM_STEP = 10
LOGIT_SCALE = 4.0
NEGATIVE = -1e30

PLANE = ("sy", "sx")
LINE = ("z", "c")

BUCKETS = (
    (("table", 0, "blk"), ("qkv", 0, "row"), ("out", 0, "row")),
    (("up", 0, "row"), ("down", 0, "blk"), ("qkv", 1, "row"), ("out", 1, "row")),
    (("qkv", 2, "row"), ("out", 2, "row"), ("up", 1, "row"), ("down", 1, "blk")),
    (
        ("qkv", 3, "row"),
        ("out", 3, "row"),
        ("qkv", 4, "row"),
        ("out", 4, "row"),
        ("up", 2, "row"),
        ("down", 2, "blk"),
    ),
)


def flip(x, axis, bit=1):
    if isinstance(axis, tuple):
        n = math.prod(lax.axis_size(a) for a in axis)
    else:
        n = lax.axis_size(axis)
    return lax.ppermute(x, axis, [(i, i ^ bit) for i in range(n)])


def bits(axis):
    n = lax.axis_size(axis)
    return [1 << k for k in range(n.bit_length() - 1)]


def all_sum(x):
    for axis in ("c", "sx", "sy", "z"):
        for bit in bits(axis):
            x = x + flip(x, axis, bit)
    return x


def doubling(x, axes):
    x = x[None]
    for axis in axes:
        for bit in bits(axis):
            x = jnp.concatenate([x, flip(x, axis, bit)], axis=0)
    return x


def normalize(v, g):
    return v * lax.rsqrt(jnp.mean(v * v, axis=-1, keepdims=True) + NORM_EPS) * g


def norm_back(v, g, cotangent):
    _, pullback = jax.vjp(normalize, v, g)
    return pullback(cotangent)


def product(a, b):
    return jnp.dot(a, b, preferred_element_type=jnp.float32)


def outer_sum(a, b):
    return lax.dot_general(a, b, (((0,), (0,)), ((), ())), preferred_element_type=jnp.float32)


def against_rows(a, b):
    return lax.dot_general(a, b, (((1,), (1,)), ((), ())), preferred_element_type=jnp.float32)


def split_heads(v):
    return v.reshape(v.shape[0], HEADS, HEAD)


def low(v):
    return v.astype(jnp.bfloat16)


def wide(v):
    return v.astype(jnp.float32)


def adam_update(master, first, second, grad):
    first = BETA_ONE * first + (1.0 - BETA_ONE) * grad
    second = BETA_TWO * second + (1.0 - BETA_TWO) * grad * grad
    fixed_first = first / (1.0 - BETA_ONE**ADAM_STEP)
    fixed_second = second / (1.0 - BETA_TWO**ADAM_STEP)
    master = master - LEARN_RATE * (
        fixed_first / (jnp.sqrt(fixed_second) + ADAM_EPS) + WEIGHT_DECAY * master
    )
    return (master, first, second)


def owned_blocks(array, kind, unit):
    if kind == "row":
        rows, columns = array.shape
        return array.reshape(rows, columns // COL, COL).transpose(1, 0, 2)
    rows = array.shape[0]
    per = rows // (4 * unit)
    return array.reshape(4, per, unit, COL).transpose(1, 0, 2, 3).reshape(per, 4 * unit, COL)


def block_counts(entries, shard_shapes, unit):
    counts = []
    for name, _, kind in entries:
        rows, columns = shard_shapes[name]
        counts.append(columns // COL if kind == "row" else rows // (4 * unit))
    return counts


def natural_shape(kind, count, unit, owners):
    if kind == "row":
        return (count, owners * 4 * unit, COL)
    return (owners, 4, count, unit, COL)


def scatter_kernel(plan, unit, half, me_ref, *refs):
    pieces, outs, sem = refs[:12], refs[12:-1], refs[-1]
    c, z, s = me_ref[0], me_ref[1], me_ref[2]

    def put(out, kind, owner, part, rows, source):
        if kind == "row":
            start = pl.multiple_of(owner * (4 * unit) + part * unit, unit)
            target = outs[out].at[:, pl.ds(start, rows), :]
        else:
            target = outs[out].at[owner, part]
        pltpu.make_async_copy(source, target, sem.at[out]).start()

    for c_rel in range(2):
        shard, mine, from_x, from_y, diag_x, diag_y = pieces[6 * c_rel : 6 * c_rel + 6]
        for z_rel in range(4):
            owner = (z ^ z_rel) * 2 + (c ^ c_rel)
            for out, (kind, first, count) in enumerate(plan):
                last = first + count
                if z_rel == 0:
                    if kind == "row":
                        put(out, kind, owner, 0, 4 * unit, shard.at[first:last])
                    else:
                        for part in range(4):
                            rows = pl.ds(part * unit, unit)
                            put(out, kind, owner, part, unit, shard.at[first:last, rows, :])
                    continue
                i = z_rel - 1
                put(out, kind, owner, s, unit, mine.at[i, first:last])
                put(out, kind, owner, s ^ 1, unit, from_x.at[i, first:last])
                put(out, kind, owner, s ^ 2, unit, from_y.at[i, first:last])
                for piece, low_k, high_k in ((diag_x, 0, half), (diag_y, half, 2 * half)):
                    a, b = max(first, low_k), min(last, high_k)
                    if a >= b:
                        continue
                    source = piece.at[i, a - low_k : b - low_k]
                    part = s ^ 3
                    if kind == "row":
                        start = pl.multiple_of(owner * (4 * unit) + part * unit, unit)
                        target = outs[out].at[a - first : b - first, pl.ds(start, unit), :]
                    else:
                        target = outs[out].at[owner, part, a - first : b - first]
                    pltpu.make_async_copy(source, target, sem.at[out]).start()
    for out in range(len(plan)):
        pltpu.make_async_copy(outs[out], outs[out], sem.at[out]).wait()


def collect_kernel(plan, unit, me_ref, *refs):
    grads, keep, send, sem = refs[: len(plan)], refs[len(plan)], refs[len(plan) + 1], refs[-1]
    c, z, s = me_ref[0], me_ref[1], me_ref[2]
    for c_rel, out in ((0, keep), (1, send)):
        for z_rel in range(4):
            owner = (z ^ z_rel) * 2 + (c ^ c_rel)
            for s_rel in range(4):
                part = s ^ s_rel
                for grad, (kind, first, count) in zip(grads, plan):
                    if kind == "row":
                        start = pl.multiple_of(owner * (4 * unit) + part * unit, unit)
                        source = grad.at[:, pl.ds(start, unit), :]
                    else:
                        source = grad.at[owner, part]
                    target = out.at[z_rel, s_rel // 2, s_rel % 2, first : first + count]
                    pltpu.make_async_copy(source, target, sem.at[c_rel]).start()
    for c_rel, out in ((0, keep), (1, send)):
        pltpu.make_async_copy(out, out, sem.at[c_rel]).wait()


ANY = pl.BlockSpec(memory_space=pl.ANY)
SCALAR = pl.BlockSpec(memory_space=pltpu.SMEM)


def gather_bucket(me, shard, kinds, counts, unit, owners):
    total = sum(counts)
    starts = [sum(counts[:i]) for i in range(len(counts))]
    half = total // 2
    s = me[2]
    part = lax.dynamic_slice_in_dim(shard, s * unit, unit, axis=1)
    mine = jnp.stack([flip(part, "z", bit) for bit in (1, 2, 3)])
    from_x = flip(mine, "sx")
    from_y = flip(mine, "sy")
    diag_x = flip(from_x[:, :half], "sy")
    diag_y = flip(from_y[:, half:], "sx")
    held = (shard, mine, from_x, from_y, diag_x, diag_y)
    other = tuple(flip(piece, "c") for piece in held)
    plan = tuple(zip(kinds, starts, counts))
    return pl.pallas_call(
        functools.partial(scatter_kernel, plan, unit, half),
        out_shape=[
            jax.ShapeDtypeStruct(natural_shape(kind, count, unit, owners), jnp.bfloat16)
            for kind, count in zip(kinds, counts)
        ],
        in_specs=[SCALAR] + [ANY] * 12,
        out_specs=[ANY] * len(plan),
        scratch_shapes=[pltpu.SemaphoreType.DMA((len(plan),))],
        name="place_weights",
    )(me, *held, *other)


def reduce_bucket(me, grads, kinds, counts, unit):
    total = sum(counts)
    starts = [sum(counts[:i]) for i in range(len(counts))]
    half = total // 2
    plan = tuple(zip(kinds, starts, counts))
    shape = jax.ShapeDtypeStruct((4, 2, 2, total, unit, COL), jnp.bfloat16)
    keep, send = pl.pallas_call(
        functools.partial(collect_kernel, plan, unit),
        out_shape=[shape, shape],
        in_specs=[SCALAR] + [ANY] * len(plan),
        out_specs=[ANY, ANY],
        scratch_shapes=[pltpu.SemaphoreType.DMA((2,))],
        name="collect_gradients",
    )(me, *grads)
    chip = wide(keep) + wide(flip(send, "c"))
    got_a = flip(low(chip[:, :, 1, :half]), "sx")
    got_b = flip(low(chip[:, 1, :, half:]), "sy")
    pair_a = chip[:, :, 0, :half] + wide(got_a)
    pair_b = chip[:, 0, :, half:] + wide(got_b)
    got_a = flip(low(pair_a[:, 1]), "sy")
    got_b = flip(low(pair_b[:, 1]), "sx")
    plane_a = pair_a[:, 0] + wide(got_a)
    plane_b = pair_b[:, 0] + wide(got_b)
    plane = jnp.concatenate([plane_a, plane_b], axis=1)
    whole = plane[0]
    for bit in (1, 2, 3):
        whole = whole + wide(flip(low(plane[bit]), "z", bit))
    return whole


def share_rows(me, whole):
    own = low(whole)
    parts = jnp.stack([own, flip(own, "sx"), flip(own, "sy"), flip(own, PLANE, 3)])
    order = jnp.arange(4) ^ me[2]
    return jnp.concatenate(
        [lax.dynamic_index_in_dim(parts, order[i], 0, keepdims=True) for i in range(4)], axis=0
    )


def owned_natural(parts, kind):
    if kind == "row":
        four, count, unit, _ = parts.shape
        return parts.transpose(0, 2, 1, 3).reshape(four * unit, count * COL)
    return parts.reshape(-1, COL)


def exchange(pair):
    return flip(pair, "c")


def score_block(queries, keys, allowed):
    scores = jnp.einsum(
        "qhd,khd->hqk", queries, keys, preferred_element_type=jnp.float32
    ) * HEAD ** (-0.5)
    return jnp.where(allowed[None], scores, NEGATIVE)


def attend_forward(queries, keys_local, values_local, mask):
    n = queries.shape[0]
    other = exchange(jnp.stack([keys_local, values_local]))
    keys_all = jnp.concatenate([keys_local, other[0]])
    values_all = jnp.concatenate([values_local, other[1]])
    scores = score_block(split_heads(queries), split_heads(keys_all), mask)
    top = jnp.max(scores, axis=-1, keepdims=True)
    expo = jnp.exp(scores - top)
    denom = jnp.sum(expo, axis=-1, keepdims=True)
    probs = (expo / denom).astype(jnp.bfloat16)
    lse = top + jnp.log(denom)
    attended = (
        jnp.einsum(
            "hqk,khd->qhd", probs, split_heads(values_all), preferred_element_type=jnp.float32
        )
        .reshape(n, -1)
        .astype(jnp.bfloat16)
    )
    return (attended, (queries, keys_all, values_all, lse, attended))


def attend_backward(saved, mask, grad_att):
    queries, keys_all, values_all, lse, _ = saved
    n, width = queries.shape
    queries = split_heads(queries)
    keys = split_heads(keys_all)
    values = split_heads(values_all)
    probs = jnp.exp(score_block(queries, keys, mask) - lse)
    probs_low = probs.astype(jnp.bfloat16)
    grad_att = split_heads(grad_att)
    grad_values = jnp.einsum(
        "hqk,qhd->khd", probs_low, grad_att, preferred_element_type=jnp.float32
    )
    grad_probs = jnp.einsum("qhd,khd->hqk", grad_att, values, preferred_element_type=jnp.float32)
    grad_scores = (
        probs * (grad_probs - jnp.sum(probs * grad_probs, axis=-1, keepdims=True))
    ).astype(jnp.bfloat16)
    grad_queries = jnp.einsum(
        "hqk,khd->qhd", grad_scores, keys, preferred_element_type=jnp.float32
    ) * HEAD ** (-0.5)
    grad_keys = jnp.einsum(
        "hqk,qhd->khd", grad_scores, queries, preferred_element_type=jnp.float32
    ) * HEAD ** (-0.5)
    both = jnp.stack([grad_keys.reshape(-1, width), grad_values.reshape(-1, width)])
    both = both[:, :n] + exchange(both[:, n:])
    return (low(grad_queries.reshape(n, width)), low(both[0]), low(both[1]))


def self_forward(x, wqkv, wout, gain, mask):
    normed = low(normalize(x, gain))
    q, k, v = (low(product(normed, wqkv[i])) for i in range(3))
    attended, saved = attend_forward(q, k, v, mask)
    return (x + product(attended, wout[0]), (x, normed, saved))


def self_backward(kept, wqkv, wout, gain, mask, grad_out):
    x, normed, saved = kept
    grad_low = low(grad_out)
    grad_wout = low(outer_sum(saved[4], grad_low))[None]
    parts = attend_backward(saved, mask, low(against_rows(grad_low, wout[0])))
    grad_wqkv = jnp.stack([low(outer_sum(normed, part)) for part in parts])
    back = sum(against_rows(part, wqkv[i]) for i, part in enumerate(parts))
    grad_in, grad_gain = norm_back(x, gain, back)
    return (grad_out + grad_in, grad_wqkv, grad_wout, grad_gain)


def cross_forward(x, memory, wqkv, wout, gain, mask):
    normed = low(normalize(x, gain))
    q = low(product(normed, wqkv[0]))
    k, v = (low(product(memory, wqkv[i])) for i in (1, 2))
    attended, saved = attend_forward(q, k, v, mask)
    return (x + product(attended, wout[0]), (x, normed, saved))


def cross_backward(kept, memory, wqkv, wout, gain, mask, grad_out):
    x, normed, saved = kept
    grad_low = low(grad_out)
    grad_wout = low(outer_sum(saved[4], grad_low))[None]
    grad_q, grad_k, grad_v = attend_backward(saved, mask, low(against_rows(grad_low, wout[0])))
    grad_wqkv = jnp.stack(
        [
            low(outer_sum(normed, grad_q)),
            low(outer_sum(memory, grad_k)),
            low(outer_sum(memory, grad_v)),
        ]
    )
    grad_memory = against_rows(grad_k, wqkv[1]) + against_rows(grad_v, wqkv[2])
    grad_in, grad_gain = norm_back(x, gain, against_rows(grad_q, wqkv[0]))
    return (grad_out + grad_in, grad_memory, grad_wqkv, grad_wout, grad_gain)


def ffn_forward(x, wup, wdown, gain):
    normed = low(normalize(x, gain))
    hidden = [low(jnp.maximum(product(normed, wup[i]), 0.0)) for i in range(wup.shape[0])]
    y = x + sum(product(r, wdown[i]) for i, r in enumerate(hidden))
    return (y, (x, normed, hidden))


def ffn_backward(kept, wup, wdown, gain, grad_out):
    x, normed, hidden = kept
    grad_low = low(grad_out)
    grad_down = jnp.stack([low(outer_sum(r, grad_low)) for r in hidden])
    grad_hidden = [
        low(jnp.where(r > 0.0, against_rows(grad_low, wdown[i]), 0.0))
        for i, r in enumerate(hidden)
    ]
    grad_up = jnp.stack([low(outer_sum(normed, g)) for g in grad_hidden])
    back = sum(against_rows(g, wup[i]) for i, g in enumerate(grad_hidden))
    grad_in, grad_gain = norm_back(x, gain, back)
    return (grad_out + grad_in, grad_up, grad_down, grad_gain)


def shards(
    tokens,
    source,
    segments,
    loss_rows,
    targets,
    exit_depth,
    qkv_weight,
    out_weight,
    up_weight,
    down_weight,
    norm_gains,
    embed_table,
    qkv_first,
    out_first,
    up_first,
    down_first,
    gains_first,
    table_first,
    qkv_second,
    out_second,
    up_second,
    down_second,
    gains_second,
    table_second,
):
    sy, sx = lax.axis_index("sy"), lax.axis_index("sx")
    z, c = lax.axis_index("z"), lax.axis_index("c")
    s = sy * 2 + sx
    me = jnp.stack([c, z, s]).astype(jnp.int32)
    owners = lax.axis_size("z") * 2
    tok_dev = tokens.shape[2]
    loss_dev = targets.shape[2]
    voc_dev, width = embed_table.shape
    gain_count, gain_dev = norm_gains.shape
    vocabulary = voc_dev * owners
    root_width = math.sqrt(width)
    half_row = 2 * tok_dev
    unit = qkv_weight.shape[1] // 4
    fast = lax.axis_size("z") == 4 and unit % 16 == 0

    shard_of = {
        "table": embed_table[None],
        "qkv": qkv_weight,
        "out": out_weight,
        "up": up_weight,
        "down": down_weight,
    }
    shard_shapes = {name: array.shape[1:] for name, array in shard_of.items()}
    weights = {}
    for entries in BUCKETS:
        kinds = [kind for _, _, kind in entries]
        counts = block_counts(entries, shard_shapes, unit)
        shard = jnp.concatenate(
            [owned_blocks(low(shard_of[name][i]), kind, unit) for name, i, kind in entries]
        )
        if fast:
            outs = gather_bucket(me, shard, kinds, counts, unit, owners)
        else:
            everything = lax.all_gather(shard, LINE)
            outs = []
            first = 0
            for kind, count in zip(kinds, counts):
                piece = everything[:, first : first + count]
                first += count
                if kind == "row":
                    outs.append(piece.transpose(1, 0, 2, 3).reshape(count, -1, COL))
                else:
                    outs.append(
                        piece.reshape(owners, count, 4, unit, COL).transpose(0, 2, 1, 3, 4)
                    )
        for (name, i, kind), out in zip(entries, outs):
            weights[name, i] = out.reshape(-1, COL, COL) if kind == "blk" else out
    table = weights["table", 0].reshape(vocabulary, width)

    numbers = jnp.concatenate(
        [array[:, 0] for array in (tokens, source, segments, loss_rows, targets, exit_depth)],
        axis=1,
    )
    plane = doubling(numbers, ("c", "sx", "sy")).reshape(2, 2, 2, MICRO, -1)
    depths_seen = plane[..., 3 * tok_dev + 2 * loss_dev :]
    reached = jnp.stack(
        [
            jnp.sum((depths_seen >= layer_id).astype(jnp.float32), axis=(0, 1, 2, 4))
            for layer_id in range(LAYERS)
        ],
        axis=1,
    )
    small = jnp.concatenate([norm_gains.reshape(-1), reached.reshape(-1)])
    small = doubling(small, ("c", "z"))
    reach = jnp.maximum(
        jnp.sum(small[::2, gain_count * gain_dev :], axis=0).reshape(MICRO, LAYERS), 1.0
    )
    reach = lax.dynamic_index_in_dim(reach, sy, 0, False)
    gains_seen = small[:, : gain_count * gain_dev].reshape(owners, gain_count, gain_dev)
    order = jnp.arange(owners)
    rel = ((order // 2) ^ z) * 2 + ((order % 2) ^ c)
    gains_full = gains_seen[rel].transpose(1, 0, 2).reshape(gain_count, width)
    gains_full = wide(low(gains_full))

    row = lax.dynamic_index_in_dim(plane, sx ^ c, 2, False)
    row = lax.dynamic_index_in_dim(row, sy, 2, False).reshape(4, -1)
    row = row[jnp.arange(4) ^ s]
    mine = lax.dynamic_slice_in_dim(row, 2 * c, 2, 0)
    theirs = lax.dynamic_slice_in_dim(row, 2 * (1 - c), 2, 0)
    target_ids = mine[:, :tok_dev].reshape(-1)
    source_ids = mine[:, tok_dev : 2 * tok_dev].reshape(-1)
    sentence = mine[:, 2 * tok_dev : 3 * tok_dev].reshape(-1)
    other_sentence = theirs[:, 2 * tok_dev : 3 * tok_dev].reshape(-1)
    rest = 3 * tok_dev
    places = (
        mine[:, rest : rest + loss_dev] + (jnp.arange(2, dtype=jnp.int32) * tok_dev)[:, None]
    ).reshape(-1)
    wanted = mine[:, rest + loss_dev : rest + 2 * loss_dev].reshape(-1)
    depth = mine[:, rest + 2 * loss_dev :].reshape(-1)
    key_sentence = jnp.concatenate([sentence, other_sentence])
    spots = c * half_row + jnp.arange(half_row)
    key_spots = jnp.concatenate([spots, (1 - c) * half_row + jnp.arange(half_row)])
    same = sentence[:, None] == key_sentence[None, :]
    allowed = same & (spots[:, None] >= key_spots[None, :])

    looked_up = table[jnp.concatenate([source_ids, target_ids])].astype(jnp.float32) * root_width
    xe = looked_up[:half_row]
    x = looked_up[half_row:]
    xe, kept_enc_self = self_forward(
        xe, weights["qkv", 0], weights["out", 0], gains_full[0], same
    )
    xe, kept_enc_ffn = ffn_forward(xe, weights["up", 0], weights["down", 0], gains_full[1])
    final_gain = gains_full[2 * ENC]
    memory = low(normalize(xe, final_gain))
    kept = []
    states = []
    for layer_id in range(LAYERS):
        base = 2 * ENC + 1 + 4 * layer_id
        slot = ENC + 2 * layer_id
        x, kept_self = self_forward(
            x, weights["qkv", slot], weights["out", slot], gains_full[base], allowed
        )
        x, kept_cross = cross_forward(
            x,
            memory,
            weights["qkv", slot + 1],
            weights["out", slot + 1],
            gains_full[base + 1],
            same,
        )
        x, kept_ffn = ffn_forward(
            x, weights["up", ENC + layer_id], weights["down", ENC + layer_id], gains_full[base + 2]
        )
        kept.append((kept_self, kept_cross, kept_ffn))
        states.append(x)

    pick = (places[:, None] == jnp.arange(half_row)[None, :]).astype(jnp.bfloat16)
    exit_gains = [gains_full[2 * ENC + 4 + 4 * layer_id] for layer_id in range(LAYERS)]
    exits = jnp.concatenate(
        [low(product(pick, low(normalize(states[i], exit_gains[i])))) for i in range(LAYERS)]
    )
    logits = against_rows(exits, table) * LOGIT_SCALE
    wanted_all = jnp.concatenate([wanted] * LAYERS)
    hit = jnp.arange(vocabulary)[None, :] == wanted_all[:, None]
    picked = jnp.sum(jnp.where(hit, logits, 0.0), axis=-1)
    top = jnp.max(logits, axis=-1)
    lse = top + jnp.log(jnp.sum(jnp.exp(logits - top[:, None]), axis=-1))
    shares = jnp.concatenate(
        [(depth >= i).astype(jnp.float32) / reach[i] / MICRO for i in range(LAYERS)]
    )
    loss_part = jnp.sum((lse - picked) * shares)
    grad_logits = low(
        (jnp.exp(logits - lse[:, None]) - hit.astype(jnp.float32))
        * shares[:, None]
        * LOGIT_SCALE
    )
    grad_exits = product(grad_logits, table)
    table_grad = outer_sum(grad_logits, exits)

    grads = {}
    gain_parts = [None] * gain_count
    grad_x = None
    grad_memory = None
    for layer_id in reversed(range(LAYERS)):
        slot = ENC + 2 * layer_id
        base = 2 * ENC + 1 + 4 * layer_id
        count = places.shape[0]
        grad_rows = lax.dot_general(
            wide(pick),
            grad_exits[layer_id * count : (layer_id + 1) * count],
            (((0,), (0,)), ((), ())),
            precision=lax.Precision.HIGHEST,
            preferred_element_type=jnp.float32,
        )
        grad_here, gain_parts[base + 3] = norm_back(
            states[layer_id], exit_gains[layer_id], grad_rows
        )
        grad_x = grad_here if grad_x is None else grad_x + grad_here
        kept_self, kept_cross, kept_ffn = kept[layer_id]
        up, down = ("up", ENC + layer_id), ("down", ENC + layer_id)
        grad_x, grads[up], grads[down], gain_parts[base + 2] = ffn_backward(
            kept_ffn, weights[up], weights[down], gains_full[base + 2], grad_x
        )
        qkv, out = ("qkv", slot + 1), ("out", slot + 1)
        grad_x, more, grads[qkv], grads[out], gain_parts[base + 1] = cross_backward(
            kept_cross, memory, weights[qkv], weights[out], gains_full[base + 1], same, grad_x
        )
        grad_memory = more if grad_memory is None else grad_memory + more
        qkv, out = ("qkv", slot), ("out", slot)
        grad_x, grads[qkv], grads[out], gain_parts[base] = self_backward(
            kept_self, weights[qkv], weights[out], gains_full[base], allowed, grad_x
        )
    grad_enc, gain_parts[2 * ENC] = norm_back(xe, final_gain, grad_memory)
    up, down, qkv, out = ("up", 0), ("down", 0), ("qkv", 0), ("out", 0)
    grad_enc, grads[up], grads[down], gain_parts[1] = ffn_backward(
        kept_enc_ffn, weights[up], weights[down], gains_full[1], grad_enc
    )
    grad_enc, grads[qkv], grads[out], gain_parts[0] = self_backward(
        kept_enc_self, weights[qkv], weights[out], gains_full[0], same, grad_enc
    )
    token_ids = jnp.concatenate([source_ids, target_ids])
    token_grads = low(jnp.concatenate([grad_enc, grad_x]) * root_width)
    looked = (token_ids[:, None] == jnp.arange(vocabulary)[None, :]).astype(jnp.bfloat16)
    table_grad = low(table_grad + outer_sum(looked, token_grads))
    grads["table", 0] = table_grad

    shape_of = {}
    reduced = {}
    squares = jnp.zeros((), jnp.float32)
    for entries in reversed(BUCKETS):
        kinds = [kind for _, _, kind in entries]
        counts = block_counts(entries, shard_shapes, unit)
        own = [
            grads[name, i].reshape(natural_shape(kind, count, unit, owners))
            for (name, i, kind), count in zip(entries, counts)
        ]
        if fast:
            whole = reduce_bucket(me, own, kinds, counts, unit)
            squares = squares + jnp.sum(whole * whole)
            parts = share_rows(me, whole)
        else:
            parts = []
            for array, kind in zip(own, kinds):
                if kind == "row":
                    array = array.reshape(array.shape[0], owners, 4, unit, COL)
                    array = array.transpose(1, 2, 0, 3, 4)
                parts.append(array)
            total = jnp.concatenate([wide(part) for part in parts], axis=2)
            total = lax.psum_scatter(total, LINE, scatter_dimension=0, tiled=True)
            parts = lax.psum(total, PLANE)[0]
            squares = squares + jnp.sum(parts * parts) / 4.0
        first = 0
        for (name, i, kind), count in zip(entries, counts):
            reduced[name, i] = owned_natural(parts[:, first : first + count], kind)
            first += count
    gain_grad = jnp.stack(gain_parts)
    small = all_sum(jnp.concatenate([gain_grad.reshape(-1), loss_part[None]]))
    loss_total = small[-1]
    gain_grad = small[:-1].reshape(gain_count, width)
    squares = all_sum(squares) + jnp.sum(gain_grad * gain_grad)
    grad_norm = jnp.sqrt(squares)
    clip_factor = CLIP_NORM / jnp.maximum(grad_norm, CLIP_NORM)

    def stacked(name, n):
        return wide(jnp.stack([reduced[name, i] for i in range(n)]))

    gradients = (
        stacked("qkv", ENC + 2 * LAYERS),
        stacked("out", ENC + 2 * LAYERS),
        stacked("up", ENC + LAYERS),
        stacked("down", ENC + LAYERS),
        lax.dynamic_slice_in_dim(gain_grad, (2 * z + c) * gain_dev, gain_dev, 1),
        wide(reduced["table", 0]),
    )
    masters = (qkv_weight, out_weight, up_weight, down_weight, norm_gains, embed_table)
    firsts = (qkv_first, out_first, up_first, down_first, gains_first, table_first)
    seconds = (qkv_second, out_second, up_second, down_second, gains_second, table_second)
    results = [
        adam_update(masters[i], firsts[i], seconds[i], gradients[i] * clip_factor) for i in range(6)
    ]
    gains_grad = gradients[4] * clip_factor
    return (
        loss_total,
        grad_norm,
        results[0][0],
        results[1][0],
        results[2][0],
        results[3][0],
        gains_grad,
        results[5][0],
        results[0][1],
        results[1][1],
        results[2][1],
        results[3][1],
        results[4][1],
        results[5][1],
        results[0][2],
        results[1][2],
        results[2][2],
        results[3][2],
        results[4][2],
        results[5][2],
    )


def solution(mesh):
    seq, vocab = mesh.devices.shape
    fine = Mesh(mesh.devices.reshape(2, seq // 2, vocab // 2, 2), ("sy", "sx", "z", "c"))
    ints = P(None, LINE, PLANE)
    block = P(None, LINE, None)
    gains = P(None, LINE)
    rows = P(LINE, None)
    arrays = (block, block, block, block, gains, rows)
    return jax.shard_map(
        shards,
        mesh=fine,
        in_specs=(ints,) * 6 + arrays * 3,
        out_specs=(P(), P(), block, block, block, block, gains, rows) + arrays * 2,
        check_vma=False,
    )
```

time: 2770 us -> 2620 us (0.946)
  Pallas kernels: 0 us -> 1670 us
  waiting for transfers between devices: 1610 us -> 160 us
  blocking collectives: 265 us -> 0 us
  matrix products: 439 us -> 291 us
  starting transfers between devices: 4.13 us -> 125 us
  local copies, waits for them, and re-layouts: 185 us -> 134 us
    pallas_call x0 -> x8, Pallas kernels: none -> 1670 us  [the longest x4 833 us: reduce_bucket(): pl.pallas_call(functools.partial(collect_kernel, plan, unit), out_shape=[...]
    reduce_scatter x27 -> x0, waiting for transfers between devices: 977 us -> none  [the longest x10 269 us: attend_backward(): lax.psum_scatter(grad_keys.reshape(-1, width), 'seq', scatter_dimension=0...]
    all_gather x25 -> x0, waiting for transfers between devices: 461 us -> none  [the longest x10 118 us: attend_forward(): lax.all_gather(keys_local, 'seq', axis=0, tiled=True)]
    all_gather x12 -> x0, blocking collectives: 237 us -> none  [the longest x6 76.4 us: merged(): everything = jax.tree.map(lambda part: lax.all_gather(part, axis), array)]
    ppermute x0 -> x122, waiting for transfers between devices: none -> 160 us  [flip(): return lax.ppermute(x, axis, [(i, i ^ bit) for i in range(n)])]
    psum x1 -> x0, waiting for transfers between devices: 140 us -> none  [shards(): lax.psum((owned_total[0], owned_total[1], owned_total[2], owned_total[3],...]
    ppermute x0 -> x122, starting transfers between devices: none -> 125 us  [flip(): return lax.ppermute(x, axis, [(i, i ^ bit) for i in range(n)])]
    all_gather x20 -> x0, local copies, waits for them, and re-layouts: 42.8 us -> none  [the longest x10 21.5 us: attend_forward(): lax.all_gather(values_local, 'seq', axis=0, tiled=True)]
  transfers between devices with their start and end apart: 54 -> 122, of which waited for: 40 -> 37; matrix products, arithmetic and copies ran while one was open for 22% -> 13% of each run, Pallas kernels for 0% -> 54%
where the time goes in v1:
time: 2620 us; the launch traced here: 2610 us
  Pallas kernels  1670 us (64%)
  matrix products  291 us (11%)
  other arithmetic  210 us (8%)
  waiting for transfers between devices  160 us (6%)
  local copies, waits for them, and re-layouts  134 us (5%)
  starting transfers between devices  125 us (5%)
    pallas_call x4, Pallas kernels, reduce_bucket(): pl.pallas_call(functools.partial(collect_kernel, plan, unit), out_shape=[...  833 us
    pallas_call x4, Pallas kernels, gather_bucket(): pl.pallas_call(functools.partial(scatter_kernel, plan, unit, half), out_s...  833 us
    ppermute x122, waiting for transfers between devices, flip(): return lax.ppermute(x, axis, [(i, i ^ bit) for i in range(n)])  160 us
    ppermute x122, starting transfers between devices, flip(): return lax.ppermute(x, axis, [(i, i ^ bit) for i in range(n)])  125 us
    convert_element_type x5, other arithmetic, attend_backward(): grad_scores = (probs * (grad_probs - jnp.sum(probs * grad_probs, axis=-1,...  57.9 us
    dot_general x46, matrix products, outer_sum(): lax.dot_general(a, b, (((0,), (0,)), ((), ())), preferred_element_type=jn...  54.2 us
  transfers between devices with their start and end apart: 122, of which 37 were waited for; matrix products, arithmetic and copies ran while one was open for 13% of the time, Pallas kernels for 54%

profile of v1, /device:TPU:0, one launch (start us, length us, event | category | flops | bytes accessed | tf_op | source)
XLA Modules:
  0.0 2609.2 jit_solution(16870215663601307431)
XLA Ops:
  59.6 11.6 collective-permute-done.22
  71.3 7.9 collective-permute-start.20
  84.7 7.0 collective-permute-done.20
  94.6 9.6 collective-permute-done.49
  114.0 6.9 collective-permute-done.24.refs_3_
  127.6 20.6 collective-permute-done.38.refs_3_
  177.4 192.4 %place_weights.4 = (bf16[8,4,8,16,512]{4,3,2,1,0:T(8,128)(2,1)}, bf16[3,512,512]{2,1,0:T(8,128)(2,1)}, bf16[1,512,512]{2,1,0:T(8,128)(2,1)}) custom-call(s32[3]{0:T(128)} %pad_add_fusion.6.me_ref, bf16[12,64,512]{2,1,0:T(8,128)(2,1)} %copy-done.109, bf16[3,12,16,512]{3,2,1,0:T(8,128)(2,1)} %copy-done.124, ...), custom_call_target="tpu_custom_call" | custom-call | tf_op jit(solution)/shard_map/place_weights/pallas_call | solution.py:227
  369.7 6.9 gather_fusion.1
  385.7 192.4 %place_weights.5 = (bf16[4,512,512]{2,1,0:T(8,128)(2,1)}, bf16[8,4,4,16,512]{4,3,2,1,0:T(8,128)(2,1)}, bf16[3,512,512]{2,1,0:T(8,128)(2,1)}, bf16[1,512,512]{2,1,0:T(8,128)(2,1)}) custom-call(s32[3]{0:T(128)} %pad_add_fusion.6.me_ref, bf16[12,64,512]{2,1,0:T(8,128)(2,1)} %pad_maximum_fusion.39.refs_0_, bf16[3,12,16,512]{3,2,1,0:T(8,128)(2,1)} %pad_maximum_fusion.69.refs_1_, ...), custom_call_target="tpu_custom_call" | custom-call | tf_op jit(solution)/shard_map/place_weights/pallas_call | solution.py:227
  595.9 192.4 %place_weights.6 = (bf16[3,512,512]{2,1,0:T(8,128)(2,1)}, bf16[1,512,512]{2,1,0:T(8,128)(2,1)}, bf16[4,512,512]{2,1,0:T(8,128)(2,1)}, bf16[8,4,4,16,512]{4,3,2,1,0:T(8,128)(2,1)}) custom-call(s32[3]{0:T(128)} %pad_add_fusion.6.me_ref, bf16[12,64,512]{2,1,0:T(8,128)(2,1)} %pad_maximum_fusion.40.refs_0_, bf16[3,12,16,512]{3,2,1,0:T(8,128)(2,1)} %pad_maximum_fusion.70.refs_1_, ...), custom_call_target="tpu_custom_call" | custom-call | tf_op jit(solution)/shard_map/place_weights/pallas_call | solution.py:227
  795.5 256.0 %place_weights.7 = (bf16[3,512,512]{2,1,0:T(8,128)(2,1)}, bf16[1,512,512]{2,1,0:T(8,128)(2,1)}, bf16[3,512,512]{2,1,0:T(8,128)(2,1)}, bf16[1,512,512]{2,1,0:T(8,...) custom-call(s32[3]{0:T(128)} %pad_add_fusion.6.me_ref, ...), custom_call_target="tpu_custom_call" | custom-call | tf_op jit(solution)/shard_map/place_weights/pallas_call | solution.py:227
  1144.9 8.2 fusion.465
  1153.0 7.7 fusion.5
  1160.8 7.6 fusion.93
  1199.3 8.6 fusion.17
  1207.9 12.1 multiply_reduce_fusion.4
  1220.0 15.5 multiply_convert_fusion.4
  1257.1 9.8 multiply_reduce_fusion.3
  1270.3 8.0 multiply_convert_fusion.3
  1336.1 9.6 multiply_reduce_fusion.2
  1345.8 10.4 multiply_convert_fusion.2
  1377.5 9.8 multiply_reduce_fusion
  1391.5 256.0 %collect_gradients.4 = (bf16[4,2,2,16,16,512]{5,4,3,2,1,0:T(8,128)(2,1)}, bf16[4,2,2,16,16,512]{5,4,3,2,1,0:T(8,128)(2,1)}) custom-call(s32[3]{0:T(128)} %pad_add_fusion.6.me_ref, bf16[3,512,512]{2,1,0:T(8,128)(2,1)} %pad_maximum_fusion.15.refs_0_, bf16[1,512,512]{2,1,0:T(8,128)(2,1)} %fusion.101.refs_1_, bf16[3,512,512]{2,1,0:T(8,128)(2,1)} %pad_maximum_fusion.16.refs_2_, ...), custom_call_target="tpu_custom_call" | custom-call | tf_op jit(solution)/shard_map/collect_gradients/pallas_call | solution.py:246
  1649.6 12.2 multiply_convert_fusion
  1698.8 9.9 multiply_reduce_fusion.1
  1711.4 192.5 %collect_gradients.5 = (bf16[4,2,2,12,16,512]{5,4,3,2,1,0:T(8,128)(2,1)}, bf16[4,2,2,12,16,512]{5,4,3,2,1,0:T(8,128)(2,1)}) custom-call(s32[3]{0:T(128)} %pad_add_fusion.6.me_ref, bf16[3,512,512]{2,1,0:T(8,128)(2,1)} %pad_maximum_fusion.17.refs_0_, bf16[1,512,512]{2,1,0:T(8,128)(2,1)} %fusion.117.refs_1_, bf16[4,512,512]{2,1,0:T(8,128)(2,1)} %pad_maximum_fusion.8.refs_2_, ...), custom_call_target="tpu_custom_call" | custom-call | tf_op jit(solution)/shard_map/collect_gradients/pallas_call | solution.py:246
  1904.2 11.8 multiply_convert_fusion.1
  1936.4 192.5 %collect_gradients.6 = (bf16[4,2,2,12,16,512]{5,4,3,2,1,0:T(8,128)(2,1)}, bf16[4,2,2,12,16,512]{5,4,3,2,1,0:T(8,128)(2,1)}) custom-call(s32[3]{0:T(128)} %pad_add_fusion.6.me_ref, bf16[4,512,512]{2,1,0:T(8,128)(2,1)} %pad_maximum_fusion.10.refs_0_, bf16[8,4,4,16,512]{4,3,2,1,0:T(8,128)(2,1)} %bitcast.993, bf16[3,512,512]{2,1,0:T(8,128)(2,1)} %pad_maximum_fusion.18.refs_2_, ...), custom_call_target="tpu_custom_call" | custom-call | tf_op jit(solution)/shard_map/collect_gradients/pallas_call | solution.py:246
  2179.2 192.4 %collect_gradients.7 = (bf16[4,2,2,12,16,512]{5,4,3,2,1,0:T(8,128)(2,1)}, bf16[4,2,2,12,16,512]{5,4,3,2,1,0:T(8,128)(2,1)}) custom-call(s32[3]{0:T(128)} %pad_add_fusion.6.me_ref, bf16[8,4,8,16,512]{4,3,2,1,0:T(8,128)(2,1)} %bitcast.991, bf16[3,512,512]{2,1,0:T(8,128)(2,1)} %pad_maximum_fusion.19.refs_1_, bf16[1,512,512]{2,1,0:T(8,128)(2,1)} %fusion.141.refs_2_), custom_call_target="tpu_custom_call" | custom-call | tf_op jit(solution)/shard_map/collect_gradients/pallas_call | solution.py:246
  2399.0 6.8 collective-permute-done.78
  2420.7 8.9 collective-permute-done.92
  2479.9 7.9 collective-permute-done.87
  (1522 shorter events, 683.6 us)
Async XLA Ops:
  13.9 41.2 %collective-permute-start.36 = (bf16[12,16,512]{2,1,0:T(8,128)(2,1)}, bf16[12,16,512]{2,1,0:T(8,128)(2,1)}, u32[]{:S(2)}, u32[]{:S(2)}) collective-permute-start(bf16[12,16,512]{2,1,0:T(8,128)(2,1)} %constant_dynamic-slice_fusion.19), channel_id=1, source_target_pairs={{0,6},{2,4},{4,2},{6,0},{1,7},{3,5},{5,3},{7,1},{8,14},{10,12},{12... | collective-permute-start | bytes 589832 | tf_op jit(solution)/shard_map/ppermute | solution.py:53
  19.0 37.0 %collective-permute-start.35 = (bf16[12,16,512]{2,1,0:T(8,128)(2,1)}, bf16[12,16,512]{2,1,0:T(8,128)(2,1)}, u32[]{:S(2)}, u32[]{:S(2)}) collective-permute-start(bf16[12,16,512]{2,1,0:T(8,128)(2,1)} %constant_dynamic-slice_fusion.19), channel_id=1, source_target_pairs={{0,4},{2,6},{4,0},{6,2},{1,5},{3,7},{5,1},{7,3},{8,12},{10,14},{12... | collective-permute-start | bytes 589832 | tf_op jit(solution)/shard_map/ppermute | solution.py:53
  19.0 40.7 %collective-permute-start.34 = (bf16[12,16,512]{2,1,0:T(8,128)(2,1)}, bf16[12,16,512]{2,1,0:T(8,128)(2,1)}, u32[]{:S(2)}, u32[]{:S(2)}) collective-permute-start(bf16[12,16,512]{2,1,0:T(8,128)(2,1)} %constant_dynamic-slice_fusion.19), channel_id=1, source_target_pairs={{0,2},{2,0},{4,6},{6,4},{1,3},{3,1},{5,7},{7,5},{8,10},{10,8},{12,... | collective-permute-start | bytes 589832 | tf_op jit(solution)/shard_map/ppermute | solution.py:53
  20.9 58.3 %collective-permute-start.2 = (bf16[12,16,512]{2,1,0:T(8,128)(2,1)}, bf16[12,16,512]{2,1,0:T(8,128)(2,1)}, u32[]{:S(2)}, u32[]{:S(2)}) collective-permute-start(bf16[12,16,512]{2,1,0:T(8,128)(2,1)} %constant_dynamic-slice_fusion.21), channel_id=1, source_target_pairs={{0,6},{2,4},{4,2},{6,0},{1,7},{3,5},{5,3},{7,1},{8,14},{10,12},{12... | collective-permute-start | bytes 589832 | tf_op jit(solution)/shard_map/ppermute | solution.py:53
  109.8 40.4 %collective-permute-start.7 = (bf16[12,64,512]{2,1,0:T(8,128)(2,1)S(1)}, bf16[12,64,512]{2,1,0:T(8,128)(2,1)}, u32[]{:S(2)}, u32[]{:S(2)}) collective-permute-start(bf16[12,64,512]{2,1,0:T(8,128)(2,1)S(1)} %pad_maximum_fusion.37.refs_0_), channel_id=1, source_target_pairs={{0,1},{1,0},{2,3},{3,2},{4,5},{5,4},{6,7},{7,6},{8,9},{9,8},{10,11... | collective-permute-start | bytes 2359304 | tf_op jit(solution)/shard_map/ppermute | solution.py:53
  109.9 40.3 %collective-permute-start.52 = (bf16[3,16,16,512]{3,2,1,0:T(8,128)(2,1)}, bf16[3,16,16,512]{3,2,1,0:T(8,128)(2,1)}, u32[]{:S(2)}, u32[]{:S(2)}) collective-permute-start(bf16[3,16,16,512]{3,2,1,0:T(8,128)(2,1)} %pad_maximum_fusion.38.refs_1_), channel_id=1, source_target_pairs={{0,16},{16,0},{1,17},{17,1},{2,18},{18,2},{3,19},{19,3},{4,20},{20... | collective-permute-start | bytes 2359304 | tf_op jit(solution)/shard_map/ppermute | solution.py:53
  163.6 216.3 %collective-permute-start.27 = (bf16[12,64,512]{2,1,0:T(8,128)(2,1)}, bf16[12,64,512]{2,1,0:T(8,128)(2,1)}, u32[]{:S(2)}, u32[]{:S(2)}) collective-permute-start(bf16[12,64,512]{2,1,0:T(8,128)(2,1)} %pad_maximum_fusion.39.refs_0_), channel_id=1, source_target_pairs={{0,1},{1,0},{2,3},{3,2},{4,5},{5,4},{6,7},{7,6},{8,9},{9,8},{10,11... | collective-permute-start | bytes 2359304 | tf_op jit(solution)/shard_map/ppermute | solution.py:53
  174.7 205.0 %collective-permute-start.28 = (bf16[3,12,16,512]{3,2,1,0:T(8,128)(2,1)}, bf16[3,12,16,512]{3,2,1,0:T(8,128)(2,1)}, u32[]{:S(2)}, u32[]{:S(2)}) collective-permute-start(bf16[3,12,16,512]{3,2,1,0:T(8,128)(2,1)} %pad_maximum_fusion.69.refs_1_), channel_id=1, source_target_pairs={{0,1},{1,0},{2,3},{3,2},{4,5},{5,4},{6,7},{7,6},{8,9},{9,8},{10,11... | collective-permute-start | bytes 1769480 | tf_op jit(solution)/shard_map/ppermute | solution.py:53
  175.3 205.0 %collective-permute-start.25 = (bf16[3,6,16,512]{3,2,1,0:T(8,128)(2,1)}, bf16[3,6,16,512]{3,2,1,0:T(8,128)(2,1)}, u32[]{:S(2)}, u32[]{:S(2)}) collective-permute-start(bf16[3,6,16,512]{3,2,1,0:T(8,128)(2,1)} %slice.921), channel_id=1, source_target_pairs={{0,16},{16,0},{1,17},{17,1},{2,18},{18,2},{3,19},{19,3},{4,20},{20... | collective-permute-start | bytes 884744 | tf_op jit(solution)/shard_map/ppermute | solution.py:53
  176.8 205.1 %collective-permute-start.30 = (bf16[3,12,16,512]{3,2,1,0:T(8,128)(2,1)}, bf16[3,12,16,512]{3,2,1,0:T(8,128)(2,1)}, u32[]{:S(2)}, u32[]{:S(2)}) collective-permute-start(bf16[3,12,16,512]{3,2,1,0:T(8,128)(2,1)} %collective-permute-done.24.refs_3_), channel_id=1, source_target_pairs={{0,1},{1,0},{2,3},{3,2},{4,5},{5,4},{6,7},{7,6},{8,9},{9,8},{10,11... | collective-permute-start | bytes 1769480 | tf_op jit(solution)/shard_map/ppermute | solution.py:53
  176.8 204.6 %collective-permute-start.32 = (bf16[3,6,16,512]{3,2,1,0:T(8,128)(2,1)S(1)}, bf16[3,6,16,512]{3,2,1,0:T(8,128)(2,1)}, u32[]{:S(2)}, u32[]{:S(2)}) collective-permute-start(bf16[3,6,16,512]{3,2,1,0:T(8,128)(2,1)S(1)} %collective-permute-done.26.refs_5_), channel_id=1, source_target_pairs={{0,1},{1,0},{2,3},{3,2},{4,5},{5,4},{6,7},{7,6},{8,9},{9,8},{10,11... | collective-permute-start | bytes 884744 | tf_op jit(solution)/shard_map/ppermute | solution.py:53
  379.8 198.4 %collective-permute-start.42 = (bf16[3,12,16,512]{3,2,1,0:T(8,128)(2,1)}, bf16[3,12,16,512]{3,2,1,0:T(8,128)(2,1)}, u32[]{:S(2)}, u32[]{:S(2)}) collective-permute-start(bf16[3,12,16,512]{3,2,1,0:T(8,128)(2,1)} %pad_maximum_fusion.70.refs_1_), channel_id=1, source_target_pairs={{0,1},{1,0},{2,3},{3,2},{4,5},{5,4},{6,7},{7,6},{8,9},{9,8},{10,11... | collective-permute-start | bytes 1769480 | tf_op jit(solution)/shard_map/ppermute | solution.py:53
  381.5 199.7 %collective-permute-start.41 = (bf16[12,64,512]{2,1,0:T(8,128)(2,1)}, bf16[12,64,512]{2,1,0:T(8,128)(2,1)}, u32[]{:S(2)}, u32[]{:S(2)}) collective-permute-start(bf16[12,64,512]{2,1,0:T(8,128)(2,1)} %pad_maximum_fusion.40.refs_0_), channel_id=1, source_target_pairs={{0,1},{1,0},{2,3},{3,2},{4,5},{5,4},{6,7},{7,6},{8,9},{9,8},{10,11... | collective-permute-start | bytes 2359304 | tf_op jit(solution)/shard_map/ppermute | solution.py:53
  381.9 199.3 %collective-permute-start.56 = (bf16[3,16,16,512]{3,2,1,0:T(8,128)(2,1)}, bf16[3,16,16,512]{3,2,1,0:T(8,128)(2,1)}, u32[]{:S(2)}, u32[]{:S(2)}) collective-permute-start(bf16[3,16,16,512]{3,2,1,0:T(8,128)(2,1)} %pad_maximum_fusion.38.refs_1_), channel_id=1, source_target_pairs={{0,1},{1,0},{2,3},{3,2},{4,5},{5,4},{6,7},{7,6},{8,9},{9,8},{10,11... | collective-permute-start | bytes 2359304 | tf_op jit(solution)/shard_map/ppermute | solution.py:53
  383.3 207.0 %collective-permute-start.55 = (bf16[16,64,512]{2,1,0:T(8,128)(2,1)}, bf16[16,64,512]{2,1,0:T(8,128)(2,1)}, u32[]{:S(2)}, u32[]{:S(2)}) collective-permute-start(bf16[16,64,512]{2,1,0:T(8,128)(2,1)} %constant_dynamic-update-slice_fusion.2.refs_0_), channel_id=1, source_target_pairs={{0,1},{1,0},{2,3},{3,2},{4,5},{5,4},{6,7},{7,6},{8,9},{9,8},{10,11... | collective-permute-start | bytes 3145736 | tf_op jit(solution)/shard_map/ppermute | solution.py:53
  385.1 199.1 %collective-permute-start.40 = (bf16[3,6,16,512]{3,2,1,0:T(8,128)(2,1)}, bf16[3,6,16,512]{3,2,1,0:T(8,128)(2,1)}, u32[]{:S(2)}, u32[]{:S(2)}) collective-permute-start(bf16[3,6,16,512]{3,2,1,0:T(8,128)(2,1)} %slice.933), channel_id=1, source_target_pairs={{0,8},{8,0},{1,9},{9,1},{2,10},{10,2},{3,11},{11,3},{4,12},{12,4},... | collective-permute-start | bytes 884744 | tf_op jit(solution)/shard_map/ppermute | solution.py:53
  590.3 201.0 %collective-permute-start.54 = (bf16[3,8,16,512]{3,2,1,0:T(8,128)(2,1)}, bf16[3,8,16,512]{3,2,1,0:T(8,128)(2,1)S(1)}, u32[]{:S(2)}, u32[]{:S(2)}) collective-permute-start(bf16[3,8,16,512]{3,2,1,0:T(8,128)(2,1)} %slice.914), channel_id=1, source_target_pairs={{0,8},{8,0},{1,9},{9,1},{2,10},{10,2},{3,11},{11,3},{4,12},{12,4},... | collective-permute-start | bytes 1179656 | tf_op jit(solution)/shard_map/ppermute | solution.py:53
  591.8 199.7 %collective-permute-start.53 = (bf16[3,8,16,512]{3,2,1,0:T(8,128)(2,1)}, bf16[3,8,16,512]{3,2,1,0:T(8,128)(2,1)}, u32[]{:S(2)}, u32[]{:S(2)}) collective-permute-start(bf16[3,8,16,512]{3,2,1,0:T(8,128)(2,1)} %slice.913), channel_id=1, source_target_pairs={{0,16},{16,0},{1,17},{17,1},{2,18},{18,2},{3,19},{19,3},{4,20},{20... | collective-permute-start | bytes 1179656 | tf_op jit(solution)/shard_map/ppermute | solution.py:53
  592.4 203.1 %collective-permute-start.58 = (bf16[3,16,16,512]{3,2,1,0:T(8,128)(2,1)}, bf16[3,16,16,512]{3,2,1,0:T(8,128)(2,1)}, u32[]{:S(2)}, u32[]{:S(2)}) collective-permute-start(bf16[3,16,16,512]{3,2,1,0:T(8,128)(2,1)} %collective-permute-done.52.refs_3_), channel_id=1, source_target_pairs={{0,1},{1,0},{2,3},{3,2},{4,5},{5,4},{6,7},{7,6},{8,9},{9,8},{10,11... | collective-permute-start | bytes 2359304 | tf_op jit(solution)/shard_map/ppermute | solution.py:53
  592.6 202.9 %collective-permute-start.57 = (bf16[3,16,16,512]{3,2,1,0:T(8,128)(2,1)}, bf16[3,16,16,512]{3,2,1,0:T(8,128)(2,1)}, u32[]{:S(2)}, u32[]{:S(2)}) collective-permute-start(bf16[3,16,16,512]{3,2,1,0:T(8,128)(2,1)} %collective-permute-done.51.refs_2_), channel_id=1, source_target_pairs={{0,1},{1,0},{2,3},{3,2},{4,5},{5,4},{6,7},{7,6},{8,9},{9,8},{10,11... | collective-permute-start | bytes 2359304 | tf_op jit(solution)/shard_map/ppermute | solution.py:53
  593.3 461.2 %collective-permute-start.19 = (bf16[2,512,512]{1,2,0:T(8,128)(2,1)}, bf16[2,512,512]{1,2,0:T(8,128)(2,1)}, u32[]{:S(2)}, u32[]{:S(2)}) collective-permute-start(bf16[2,512,512]{1,2,0:T(8,128)(2,1)} %pad_maximum_fusion.20), channel_id=1, source_target_pairs={{0,1},{1,0},{2,3},{3,2},{4,5},{5,4},{6,7},{7,6},{8,9},{9,8},{10,11... | collective-permute-start | bytes 3145736 | tf_op jit(solution)/shard_map/ppermute | solution.py:53
  795.3 287.3 %collective-permute-start.33 = (bf16[2,512,512]{1,2,0:T(8,128)(2,1)}, bf16[2,512,512]{1,2,0:T(8,128)(2,1)}, u32[]{:S(2)}, u32[]{:S(2)}) collective-permute-start(bf16[2,512,512]{1,2,0:T(8,128)(2,1)} %pad_maximum_fusion.22), channel_id=1, source_target_pairs={{0,1},{1,0},{2,3},{3,2},{4,5},{5,4},{6,7},{7,6},{8,9},{9,8},{10,11... | collective-permute-start | bytes 3145736 | tf_op jit(solution)/shard_map/ppermute | solution.py:53
  1079.8 49.3 %collective-permute-start.62 = (bf16[2,512,512]{1,2,0:T(8,128)(2,1)}, bf16[2,512,512]{1,2,0:T(8,128)(2,1)}, u32[]{:S(2)}, u32[]{:S(2)}) collective-permute-start(bf16[2,512,512]{1,2,0:T(8,128)(2,1)} %pad_maximum_fusion.32), channel_id=1, source_target_pairs={{0,1},{1,0},{2,3},{3,2},{4,5},{5,4},{6,7},{7,6},{8,9},{9,8},{10,11... | collective-permute-start | bytes 3145736 | tf_op jit(solution)/shard_map/ppermute | solution.py:53
  1647.5 484.3 %collective-permute-start.73 = (bf16[4,2,2,16,16,512]{5,4,3,2,1,0:T(8,128)(2,1)}, bf16[4,2,2,16,16,512]{5,4,3,2,1,0:T(8,128)(2,1)}, u32[]{:S(2)}, u32[]{:S(2)}) collective-permute-start(bf16[4,2,2,16,16,512]{5,4,3,2,1,0:T(8,128)(2,1)} %get-tuple-element.63), channel_id=1, source_target_pairs={{0,1},{1,0},{2,3},{3,2},{4,5},{5,4},{6,7},{7,6},{8,9},{9,8},{10,11... | collective-permute-start | bytes 12582920 | tf_op jit(solution)/shard_map/ppermute | solution.py:53
  1665.5 262.0 %collective-permute-start.67 = (f32[2,512,512]{1,2,0:T(8,128)}, f32[2,512,512]{1,2,0:T(8,128)}, u32[]{:S(2)}, u32[]{:S(2)}) collective-permute-start(f32[2,512,512]{1,2,0:T(8,128)} %pad_maximum_fusion.1), channel_id=1, source_target_pairs={{0,1},{1,0},{2,3},{3,2},{4,5},{5,4},{6,7},{7,6},{8,9},{9,8},{10,11... | collective-permute-start | bytes 6291464 | tf_op jit(solution)/shard_map/ppermute | solution.py:53
  1903.9 477.3 %collective-permute-start.81 = (bf16[4,2,2,12,16,512]{5,4,3,2,1,0:T(8,128)(2,1)}, bf16[4,2,2,12,16,512]{5,4,3,2,1,0:T(8,128)(2,1)}, u32[]{:S(2)}, u32[]{:S(2)}) collective-permute-start(bf16[4,2,2,12,16,512]{5,4,3,2,1,0:T(8,128)(2,1)} %get-tuple-element.65), channel_id=1, source_target_pairs={{0,1},{1,0},{2,3},{3,2},{4,5},{5,4},{6,7},{7,6},{8,9},{9,8},{10,11... | collective-permute-start | bytes 9437192 | tf_op jit(solution)/shard_map/ppermute | solution.py:53
  1919.3 223.1 %collective-permute-start.66 = (f32[2,512,512]{1,2,0:T(8,128)}, f32[2,512,512]{1,2,0:T(8,128)}, u32[]{:S(2)}, u32[]{:S(2)}) collective-permute-start(f32[2,512,512]{1,2,0:T(8,128)} %pad_maximum_fusion.2), channel_id=1, source_target_pairs={{0,1},{1,0},{2,3},{3,2},{4,5},{5,4},{6,7},{7,6},{8,9},{9,8},{10,11... | collective-permute-start | bytes 6291464 | tf_op jit(solution)/shard_map/ppermute | solution.py:53
  2128.9 257.4 %collective-permute-start.89 = (bf16[4,2,2,12,16,512]{5,4,3,2,1,0:T(8,128)(2,1)}, bf16[4,2,2,12,16,512]{5,4,3,2,1,0:T(8,128)(2,1)}, u32[]{:S(2)}, u32[]{:S(2)}) collective-permute-start(bf16[4,2,2,12,16,512]{5,4,3,2,1,0:T(8,128)(2,1)} %get-tuple-element.67), channel_id=1, source_target_pairs={{0,1},{1,0},{2,3},{3,2},{4,5},{5,4},{6,7},{7,6},{8,9},{9,8},{10,11... | collective-permute-start | bytes 9437192 | tf_op jit(solution)/shard_map/ppermute | solution.py:53
  2138.8 234.5 %collective-permute-start.76 = (bf16[4,2,8,16,512]{4,3,2,0,1:T(8,128)(2,1)}, bf16[4,2,8,16,512]{4,3,2,0,1:T(8,128)(2,1)}, u32[]{:S(2)}, u32[]{:S(2)}) collective-permute-start(bf16[4,2,8,16,512]{4,3,2,0,1:T(8,128)(2,1)} %slice_bitcast_fusion.9), channel_id=1, source_target_pairs={{0,16},{16,0},{1,17},{17,1},{2,18},{18,2},{3,19},{19,3},{4,20},{20... | collective-permute-start | bytes 3145736 | tf_op jit(solution)/shard_map/ppermute | solution.py:53
  2141.9 235.3 %collective-permute-start.74 = (bf16[4,2,8,16,512]{4,3,2,0,1:T(8,128)(2,1)}, bf16[4,2,8,16,512]{4,3,2,0,1:T(8,128)(2,1)}, u32[]{:S(2)}, u32[]{:S(2)}) collective-permute-start(bf16[4,2,8,16,512]{4,3,2,0,1:T(8,128)(2,1)} %slice_bitcast_fusion.11), channel_id=1, source_target_pairs={{0,8},{8,0},{1,9},{9,1},{2,10},{10,2},{3,11},{11,3},{4,12},{12,4},... | collective-permute-start | bytes 3145736 | tf_op jit(solution)/shard_map/ppermute | solution.py:53
  2176.9 194.7 %collective-permute-start.72 = (f32[5633]{0:T(1024)S(1)}, f32[5633]{0:T(1024)S(1)}, u32[]{:S(2)}, u32[]{:S(2)}) collective-permute-start(f32[5633]{0:T(1024)S(1)} %add.764), channel_id=1, source_target_pairs={{0,4},{2,6},{4,0},{6,2},{1,5},{3,7},{5,1},{7,3},{8,12},{10,14},{12... | collective-permute-start | bytes 67604 | tf_op jit(solution)/shard_map/ppermute | solution.py:53
  2405.8 96.2 %collective-permute-start.97 = (bf16[4,2,2,12,16,512]{5,4,3,2,1,0:T(8,128)(2,1)}, bf16[4,2,2,12,16,512]{5,4,3,2,1,0:T(8,128)(2,1)}, u32[]{:S(2)}, u32[]{:S(2)}) collective-permute-start(bf16[4,2,2,12,16,512]{5,4,3,2,1,0:T(8,128)(2,1)} %get-tuple-element.69), channel_id=1, source_target_pairs={{0,1},{1,0},{2,3},{3,2},{4,5},{5,4},{6,7},{7,6},{8,9},{9,8},{10,11... | collective-permute-start | bytes 9437192 | tf_op jit(solution)/shard_map/ppermute | solution.py:53
  (489 other events, 9585.1 us)

commit v2 on v1

--- a/solution.py
+++ b/solution.py
@@ -207,6 +207,7 @@
 
 
 ANY = pl.BlockSpec(memory_space=pl.ANY)
+ONCHIP = pl.BlockSpec(memory_space=pltpu.VMEM)
 SCALAR = pl.BlockSpec(memory_space=pltpu.SMEM)
 
 
@@ -231,7 +232,7 @@
             for kind, count in zip(kinds, counts)
         ],
         in_specs=[SCALAR] + [ANY] * 12,
-        out_specs=[ANY] * len(plan),
+        out_specs=[ONCHIP] * len(plan),
         scratch_shapes=[pltpu.SemaphoreType.DMA((len(plan),))],
         name="place_weights",
     )(me, *held, *other)
@@ -247,7 +248,7 @@
         functools.partial(collect_kernel, plan, unit),
         out_shape=[shape, shape],
         in_specs=[SCALAR] + [ANY] * len(plan),
-        out_specs=[ANY, ANY],
+        out_specs=[ONCHIP, ONCHIP],
         scratch_shapes=[pltpu.SemaphoreType.DMA((2,))],
         name="collect_gradients",
     )(me, *grads)
@@ -283,96 +284,309 @@
     return parts.reshape(-1, COL)
 
 
-def exchange(pair):
-    return flip(pair, "c")
-
-
-def score_block(queries, keys, allowed):
-    scores = jnp.einsum(
-        "qhd,khd->hqk", queries, keys, preferred_element_type=jnp.float32
-    ) * HEAD ** (-0.5)
-    return jnp.where(allowed[None], scores, NEGATIVE)
-
-
-def attend_forward(queries, keys_local, values_local, mask):
-    n = queries.shape[0]
-    other = exchange(jnp.stack([keys_local, values_local]))
-    keys_all = jnp.concatenate([keys_local, other[0]])
-    values_all = jnp.concatenate([values_local, other[1]])
-    scores = score_block(split_heads(queries), split_heads(keys_all), mask)
-    top = jnp.max(scores, axis=-1, keepdims=True)
-    expo = jnp.exp(scores - top)
-    denom = jnp.sum(expo, axis=-1, keepdims=True)
-    probs = (expo / denom).astype(jnp.bfloat16)
-    lse = top + jnp.log(denom)
-    attended = (
-        jnp.einsum(
-            "hqk,khd->qhd", probs, split_heads(values_all), preferred_element_type=jnp.float32
-        )
-        .reshape(n, -1)
-        .astype(jnp.bfloat16)
-    )
-    return (attended, (queries, keys_all, values_all, lse, attended))
-
-
-def attend_backward(saved, mask, grad_att):
-    queries, keys_all, values_all, lse, _ = saved
-    n, width = queries.shape
-    queries = split_heads(queries)
-    keys = split_heads(keys_all)
-    values = split_heads(values_all)
-    probs = jnp.exp(score_block(queries, keys, mask) - lse)
-    probs_low = probs.astype(jnp.bfloat16)
-    grad_att = split_heads(grad_att)
-    grad_values = jnp.einsum(
-        "hqk,qhd->khd", probs_low, grad_att, preferred_element_type=jnp.float32
-    )
-    grad_probs = jnp.einsum("qhd,khd->hqk", grad_att, values, preferred_element_type=jnp.float32)
-    grad_scores = (
-        probs * (grad_probs - jnp.sum(probs * grad_probs, axis=-1, keepdims=True))
-    ).astype(jnp.bfloat16)
-    grad_queries = jnp.einsum(
-        "hqk,khd->qhd", grad_scores, keys, preferred_element_type=jnp.float32
-    ) * HEAD ** (-0.5)
-    grad_keys = jnp.einsum(
-        "hqk,qhd->khd", grad_scores, queries, preferred_element_type=jnp.float32
-    ) * HEAD ** (-0.5)
-    both = jnp.stack([grad_keys.reshape(-1, width), grad_values.reshape(-1, width)])
-    both = both[:, :n] + exchange(both[:, n:])
-    return (low(grad_queries.reshape(n, width)), low(both[0]), low(both[1]))
-
-
-def self_forward(x, wqkv, wout, gain, mask):
+BQ = 128
+NT = (((1,), (1,)), ((), ()))
+TN = (((0,), (0,)), ((), ()))
+NN = (((1,), (0,)), ((), ()))
+
+
+def dot32(a, b, dims):
+    return lax.dot_general(a, b, dims, preferred_element_type=jnp.float32)
+
+
+def load_halves(own, other, whole, sem):
+    half = whole.shape[0] // 2
+    copies = [
+        pltpu.make_async_copy(own, whole.at[pl.ds(0, half)], sem.at[0]),
+        pltpu.make_async_copy(other, whole.at[pl.ds(half, half)], sem.at[1]),
+    ]
+    for copy in copies:
+        copy.start()
+    return copies
+
+
+def pair_rows(block, scale=None):
+    lane = lax.broadcasted_iota(jnp.int32, block.shape, 1)
+    zero = jnp.zeros_like(block)
+    if scale is not None:
+        block = block * jnp.asarray(scale, block.dtype)
+    return jnp.concatenate(
+        [jnp.where(lane < HEAD, block, zero), jnp.where(lane < HEAD, zero, block)], axis=0
+    )
+
+
+def pair_lanes(stacked):
+    rows = stacked.shape[0] // 2
+    lane = lax.broadcasted_iota(jnp.int32, (rows, 2 * HEAD), 1)
+    return jnp.where(lane < HEAD, stacked[:rows], stacked[rows:])
+
+
+def attend_kernel(
+    causal, act, q_seg, k_seg, q_pos, k_pos, q, k_own, k_oth, v_own, v_oth, o, lse,
+    k_all, v_all, scores, queries, top, total, acc, sem_k, sem_v,
+):
+    pairs = q.shape[1] // (2 * HEAD)
+    blocks = q.shape[0] // BQ
+    chunks = k_all.shape[0] // BQ
+    waits = load_halves(k_own, k_oth, k_all, sem_k) + load_halves(v_own, v_oth, v_all, sem_v)
+    for copy in waits:
+        copy.wait()
+
+    def one_block(b, _):
+        rows = pl.ds(pl.multiple_of(b * BQ, BQ), BQ)
+        for h in range(pairs):
+            queries[h] = pair_rows(q[rows, h * 128 : h * 128 + 128], HEAD ** (-0.5))
+        top[...] = jnp.full_like(top, NEGATIVE)
+        total[...] = jnp.zeros_like(total)
+        acc[...] = jnp.zeros_like(acc)
+
+        def first(j, _):
+            @pl.when(act[b * chunks + j] > 0)
+            def _():
+                keys = pl.ds(pl.multiple_of(j * BQ, BQ), BQ)
+                open_ = q_seg[rows, :] == k_seg[0:1, keys]
+                if causal:
+                    open_ = open_ & (q_pos[rows, :] >= k_pos[0:1, keys])
+                open_ = jnp.concatenate([open_, open_], axis=0)
+                for h in range(pairs):
+                    s = dot32(queries[h], k_all[keys, h * 128 : h * 128 + 128], NT)
+                    s = jnp.where(open_, s, NEGATIVE)
+                    scores[h, j] = s
+                    top[h] = jnp.maximum(top[h], s)
+
+            return 0
+
+        lax.fori_loop(0, chunks, first, 0)
+        for h in range(pairs):
+            top[h] = jnp.broadcast_to(jnp.max(top[h], axis=1, keepdims=True), top.shape[1:])
+
+        def second(j, _):
+            @pl.when(act[b * chunks + j] > 0)
+            def _():
+                keys = pl.ds(pl.multiple_of(j * BQ, BQ), BQ)
+                for h in range(pairs):
+                    e = jnp.exp(scores[h, j] - top[h])
+                    total[h] = total[h] + e
+                    acc[h] = acc[h] + dot32(
+                        e.astype(jnp.bfloat16), v_all[keys, h * 128 : h * 128 + 128], NN
+                    )
+
+            return 0
+
+        lax.fori_loop(0, chunks, second, 0)
+        for h in range(pairs):
+            denom = jnp.broadcast_to(
+                jnp.sum(total[h], axis=1, keepdims=True), total.shape[1:]
+            )
+            o[rows, h * 128 : h * 128 + 128] = pair_lanes(acc[h] / denom).astype(o.dtype)
+            line = (top[h] + jnp.log(denom)).T[0:1]
+            lse[2 * h : 2 * h + 1, rows] = line[:, :BQ]
+            lse[2 * h + 1 : 2 * h + 2, rows] = line[:, BQ:]
+        return 0
+
+    lax.fori_loop(0, blocks, one_block, 0)
+
+
+def attend_back_kernel(
+    causal, act, k_seg, q_seg, k_pos, q_pos, q, k_own, k_oth, v_own, v_oth, o, grad, lse,
+    grad_q, grad_own, grad_oth,
+    k_all, v_all, queries, grads, deltas, grad_queries, sem_k, sem_v,
+):
+    pairs = q.shape[1] // (2 * HEAD)
+    blocks = q.shape[0] // BQ
+    chunks = k_all.shape[0] // BQ
+    waits = load_halves(k_own, k_oth, k_all, sem_k) + load_halves(v_own, v_oth, v_all, sem_v)
+    grad_own[...] = jnp.zeros_like(grad_own)
+    grad_oth[...] = jnp.zeros_like(grad_oth)
+    head_of = lax.broadcasted_iota(jnp.int32, (HEADS, q.shape[1]), 1) // HEAD
+    ones = (head_of == lax.broadcasted_iota(jnp.int32, head_of.shape, 0)).astype(jnp.float32)
+    deltas[...] = lax.dot_general(
+        ones,
+        o[...].astype(jnp.float32) * grad[...].astype(jnp.float32),
+        NT,
+        precision=lax.Precision.HIGHEST,
+        preferred_element_type=jnp.float32,
+    )
+    for copy in waits:
+        copy.wait()
+
+    def one_block(b, _):
+        rows = pl.ds(pl.multiple_of(b * BQ, BQ), BQ)
+        for h in range(pairs):
+            queries[h] = pair_rows(q[rows, h * 128 : h * 128 + 128], HEAD ** (-0.5))
+            grads[h] = pair_rows(grad[rows, h * 128 : h * 128 + 128])
+        grad_queries[...] = jnp.zeros_like(grad_queries)
+
+        def both_heads(ref, h):
+            return jnp.concatenate([ref[2 * h : 2 * h + 1, rows], ref[2 * h + 1 : 2 * h + 2, rows]], axis=1)
+
+        def one_chunk(j, target, local):
+            keys = pl.ds(pl.multiple_of(j * BQ, BQ), BQ)
+            own_keys = pl.ds(pl.multiple_of(local * BQ, BQ), BQ)
+            open_ = k_seg[keys, :] == q_seg[0:1, rows]
+            if causal:
+                open_ = open_ & (k_pos[keys, :] <= q_pos[0:1, rows])
+            open_ = jnp.concatenate([open_, open_], axis=1)
+            for h in range(pairs):
+                lanes = slice(h * 128, h * 128 + 128)
+                k, v = k_all[keys, lanes], v_all[keys, lanes]
+                s = jnp.where(open_, dot32(k, queries[h], NT), NEGATIVE)
+                p = jnp.exp(s - both_heads(lse, h))
+                ds = p * (dot32(v, grads[h], NT) - both_heads(deltas, h))
+                p = p.astype(jnp.bfloat16)
+                ds = ds.astype(jnp.bfloat16)
+                target[0, own_keys, lanes] += dot32(ds, queries[h], NN)
+                target[1, own_keys, lanes] += dot32(p, grads[h], NN)
+                grad_queries[h] += dot32(ds, k, TN)
+
+        def own_chunk(j, _):
+            @pl.when(act[b * chunks + j] > 0)
+            def _():
+                one_chunk(j, grad_own, j)
+
+            return 0
+
+        def oth_chunk(j, _):
+            @pl.when(act[b * chunks + j] > 0)
+            def _():
+                one_chunk(j, grad_oth, j - chunks // 2)
+
+            return 0
+
+        lax.fori_loop(0, chunks // 2, own_chunk, 0)
+        lax.fori_loop(chunks // 2, chunks, oth_chunk, 0)
+        for h in range(pairs):
+            grad_q[rows, h * 128 : h * 128 + 128] = (
+                pair_lanes(grad_queries[h]) * HEAD ** (-0.5)
+            ).astype(grad_q.dtype)
+        return 0
+
+    lax.fori_loop(0, blocks, one_block, 0)
+
+
+def attend_masks(sentence, other, spots, other_spots):
+    n = sentence.shape[0]
+    seg = jnp.concatenate([sentence, other])
+    pos = jnp.concatenate([spots, other_spots])
+
+    def down(v):
+        return jnp.broadcast_to(v[:, None], (v.shape[0], BQ))
+
+    def across(v):
+        return jnp.broadcast_to(v[None, :], (8, v.shape[0]))
+
+    blocks = sentence.reshape(-1, BQ)
+    keys = seg.reshape(-1, BQ)
+    live = (blocks.min(1)[:, None] <= keys.max(1)[None, :]) & (
+        blocks.max(1)[:, None] >= keys.min(1)[None, :]
+    )
+    early = spots.reshape(-1, BQ).max(1)[:, None] >= pos.reshape(-1, BQ).min(1)[None, :]
+    return {
+        "forward": (down(sentence), across(seg), down(spots), across(pos)),
+        "backward": (down(seg), across(sentence), down(pos), across(spots)),
+        False: live.astype(jnp.int32).reshape(-1),
+        True: (live & early).astype(jnp.int32).reshape(-1),
+    }
+
+
+def attend(masks, causal, q, k, v, k_oth, v_oth):
+    n, width = q.shape
+    pairs = width // (2 * HEAD)
+    chunks = 2 * n // BQ
+    return pl.pallas_call(
+        functools.partial(attend_kernel, causal),
+        out_shape=[
+            jax.ShapeDtypeStruct((n, width), jnp.bfloat16),
+            jax.ShapeDtypeStruct((HEADS, n), jnp.float32),
+        ],
+        in_specs=[SCALAR] + [ONCHIP] * 5 + [ANY] * 4,
+        out_specs=[ONCHIP, ONCHIP],
+        scratch_shapes=[
+            pltpu.VMEM((2 * n, width), jnp.bfloat16),
+            pltpu.VMEM((2 * n, width), jnp.bfloat16),
+            pltpu.VMEM((pairs, chunks, 2 * BQ, BQ), jnp.float32),
+            pltpu.VMEM((pairs, 2 * BQ, 128), jnp.bfloat16),
+            pltpu.VMEM((pairs, 2 * BQ, 128), jnp.float32),
+            pltpu.VMEM((pairs, 2 * BQ, 128), jnp.float32),
+            pltpu.VMEM((pairs, 2 * BQ, 128), jnp.float32),
+            pltpu.SemaphoreType.DMA((2,)),
+            pltpu.SemaphoreType.DMA((2,)),
+        ],
+        name="attend",
+    )(masks[causal], *masks["forward"], q, k, k_oth, v, v_oth)
+
+
+def attend_back(masks, causal, q, k, v, k_oth, v_oth, o, lse, grad):
+    n, width = q.shape
+    pairs = width // (2 * HEAD)
+    return pl.pallas_call(
+        functools.partial(attend_back_kernel, causal),
+        out_shape=[
+            jax.ShapeDtypeStruct((n, width), jnp.bfloat16),
+            jax.ShapeDtypeStruct((2, n, width), jnp.float32),
+            jax.ShapeDtypeStruct((2, n, width), jnp.float32),
+        ],
+        in_specs=[SCALAR] + [ONCHIP] * 5 + [ANY] * 4 + [ONCHIP] * 3,
+        out_specs=[ONCHIP] * 3,
+        scratch_shapes=[
+            pltpu.VMEM((2 * n, width), jnp.bfloat16),
+            pltpu.VMEM((2 * n, width), jnp.bfloat16),
+            pltpu.VMEM((pairs, 2 * BQ, 128), jnp.bfloat16),
+            pltpu.VMEM((pairs, 2 * BQ, 128), jnp.bfloat16),
+            pltpu.VMEM((HEADS, n), jnp.float32),
+            pltpu.VMEM((pairs, 2 * BQ, 128), jnp.float32),
+            pltpu.SemaphoreType.DMA((2,)),
+            pltpu.SemaphoreType.DMA((2,)),
+        ],
+        name="attend_back",
+    )(masks[causal], *masks["backward"], q, k, k_oth, v, v_oth, o, grad, lse)
+
+
+def attend_forward(masks, causal, q, k, v):
+    other = flip(jnp.stack([k, v]), "c")
+    o, lse = attend(masks, causal, q, k, v, other[0], other[1])
+    return (o, (q, k, v, other[0], other[1], o, lse))
+
+
+def attend_backward(saved, masks, causal, grad):
+    grad_q, own, other = attend_back(masks, causal, *saved, grad)
+    both = own + flip(other, "c")
+    return (grad_q, low(both[0]), low(both[1]))
+
+
+def self_forward(x, wqkv, wout, gain, masks, causal):
     normed = low(normalize(x, gain))
     q, k, v = (low(product(normed, wqkv[i])) for i in range(3))
-    attended, saved = attend_forward(q, k, v, mask)
+    attended, saved = attend_forward(masks, causal, q, k, v)
     return (x + product(attended, wout[0]), (x, normed, saved))
 
 
-def self_backward(kept, wqkv, wout, gain, mask, grad_out):
+def self_backward(kept, wqkv, wout, gain, masks, causal, grad_out):
     x, normed, saved = kept
     grad_low = low(grad_out)
-    grad_wout = low(outer_sum(saved[4], grad_low))[None]
-    parts = attend_backward(saved, mask, low(against_rows(grad_low, wout[0])))
+    grad_wout = low(outer_sum(saved[5], grad_low))[None]
+    parts = attend_backward(saved, masks, causal, low(against_rows(grad_low, wout[0])))
     grad_wqkv = jnp.stack([low(outer_sum(normed, part)) for part in parts])
     back = sum(against_rows(part, wqkv[i]) for i, part in enumerate(parts))
     grad_in, grad_gain = norm_back(x, gain, back)
     return (grad_out + grad_in, grad_wqkv, grad_wout, grad_gain)
 
 
-def cross_forward(x, memory, wqkv, wout, gain, mask):
+def cross_forward(x, memory, wqkv, wout, gain, masks):
     normed = low(normalize(x, gain))
     q = low(product(normed, wqkv[0]))
     k, v = (low(product(memory, wqkv[i])) for i in (1, 2))
-    attended, saved = attend_forward(q, k, v, mask)
+    attended, saved = attend_forward(masks, False, q, k, v)
     return (x + product(attended, wout[0]), (x, normed, saved))
 
 
-def cross_backward(kept, memory, wqkv, wout, gain, mask, grad_out):
+def cross_backward(kept, memory, wqkv, wout, gain, masks, grad_out):
     x, normed, saved = kept
     grad_low = low(grad_out)
-    grad_wout = low(outer_sum(saved[4], grad_low))[None]
-    grad_q, grad_k, grad_v = attend_backward(saved, mask, low(against_rows(grad_low, wout[0])))
+    grad_wout = low(outer_sum(saved[5], grad_low))[None]
+    grad_q, grad_k, grad_v = attend_backward(
+        saved, masks, False, low(against_rows(grad_low, wout[0]))
+    )
     grad_wqkv = jnp.stack(
         [
             low(outer_sum(normed, grad_q)),
@@ -521,17 +735,15 @@
     ).reshape(-1)
     wanted = mine[:, rest + loss_dev : rest + 2 * loss_dev].reshape(-1)
     depth = mine[:, rest + 2 * loss_dev :].reshape(-1)
-    key_sentence = jnp.concatenate([sentence, other_sentence])
     spots = c * half_row + jnp.arange(half_row)
-    key_spots = jnp.concatenate([spots, (1 - c) * half_row + jnp.arange(half_row)])
-    same = sentence[:, None] == key_sentence[None, :]
-    allowed = same & (spots[:, None] >= key_spots[None, :])
+    other_spots = (1 - c) * half_row + jnp.arange(half_row)
+    masks = attend_masks(sentence, other_sentence, spots, other_spots)
 
     looked_up = table[jnp.concatenate([source_ids, target_ids])].astype(jnp.float32) * root_width
     xe = looked_up[:half_row]
     x = looked_up[half_row:]
     xe, kept_enc_self = self_forward(
-        xe, weights["qkv", 0], weights["out", 0], gains_full[0], same
+        xe, weights["qkv", 0], weights["out", 0], gains_full[0], masks, False
     )
     xe, kept_enc_ffn = ffn_forward(xe, weights["up", 0], weights["down", 0], gains_full[1])
     final_gain = gains_full[2 * ENC]
@@ -542,7 +754,7 @@
         base = 2 * ENC + 1 + 4 * layer_id
         slot = ENC + 2 * layer_id
         x, kept_self = self_forward(
-            x, weights["qkv", slot], weights["out", slot], gains_full[base], allowed
+            x, weights["qkv", slot], weights["out", slot], gains_full[base], masks, True
         )
         x, kept_cross = cross_forward(
             x,
@@ -550,7 +762,7 @@
             weights["qkv", slot + 1],
             weights["out", slot + 1],
             gains_full[base + 1],
-            same,
+            masks,
         )
         x, kept_ffn = ffn_forward(
             x, weights["up", ENC + layer_id], weights["down", ENC + layer_id], gains_full[base + 2]
@@ -607,12 +819,12 @@
         )
         qkv, out = ("qkv", slot + 1), ("out", slot + 1)
         grad_x, more, grads[qkv], grads[out], gain_parts[base + 1] = cross_backward(
-            kept_cross, memory, weights[qkv], weights[out], gains_full[base + 1], same, grad_x
+            kept_cross, memory, weights[qkv], weights[out], gains_full[base + 1], masks, grad_x
         )
         grad_memory = more if grad_memory is None else grad_memory + more
         qkv, out = ("qkv", slot), ("out", slot)
         grad_x, grads[qkv], grads[out], gain_parts[base] = self_backward(
-            kept_self, weights[qkv], weights[out], gains_full[base], allowed, grad_x
+            kept_self, weights[qkv], weights[out], gains_full[base], masks, True, grad_x
         )
     grad_enc, gain_parts[2 * ENC] = norm_back(xe, final_gain, grad_memory)
     up, down, qkv, out = ("up", 0), ("down", 0), ("qkv", 0), ("out", 0)
@@ -620,7 +832,7 @@
         kept_enc_ffn, weights[up], weights[down], gains_full[1], grad_enc
     )
     grad_enc, grads[qkv], grads[out], gain_parts[0] = self_backward(
-        kept_enc_self, weights[qkv], weights[out], gains_full[0], same, grad_enc
+        kept_enc_self, weights[qkv], weights[out], gains_full[0], masks, False, grad_enc
     )
     token_ids = jnp.concatenate([source_ids, target_ids])
     token_grads = low(jnp.concatenate([grad_enc, grad_x]) * root_width)

time: 2620 us -> 954 us (0.36)
  Pallas kernels: 1670 us -> 228 us
  matrix products: 291 us -> 134 us
  other arithmetic: 210 us -> 111 us
    pallas_call x4, Pallas kernels: 833 us -> 26.1 us  [reduce_bucket(): pl.pallas_call(functools.partial(collect_kernel, plan, unit), out_shape=[...]
    pallas_call x4, Pallas kernels: 833 us -> 25.9 us  [gather_bucket(): pl.pallas_call(functools.partial(scatter_kernel, plan, unit, half), out_s...]
    pallas_call x0 -> x10, Pallas kernels: none -> 176 us  [the longest x5 108 us: attend_back(): pl.pallas_call(functools.partial(attend_back_kernel, causal), out_shape=[...]
    dot_general x30 -> x0, matrix products: 164 us -> none  [the longest x5 51.3 us: attend_backward(): jnp.einsum('qhd,khd->hqk', grad_att, values, preferred_element_type=jnp.f...]
    convert_element_type x5 -> x2, other arithmetic: 57.9 us -> 0.15 us  [the longest x1 0.08 us: attend_masks(): live.astype(jnp.int32).reshape(-1)]
  transfers between devices with their start and end apart: 122 -> 122, of which waited for: 37 -> 38; matrix products, arithmetic and copies ran while one was open for 13% -> 29% of each run, Pallas kernels for 54% -> 13%
where the time goes in v2:
time: 954 us; the launch traced here: 942 us
  Pallas kernels  228 us (24%)
  waiting for transfers between devices  162 us (17%)
  starting transfers between devices  149 us (16%)
  local copies, waits for them, and re-layouts  135 us (14%)
  matrix products  134 us (14%)
  other arithmetic  111 us (12%)
  between operations  23 us (2%)
    ppermute x122, waiting for transfers between devices, flip(): return lax.ppermute(x, axis, [(i, i ^ bit) for i in range(n)])  162 us
    ppermute x122, starting transfers between devices, flip(): return lax.ppermute(x, axis, [(i, i ^ bit) for i in range(n)])  149 us
    pallas_call x5, Pallas kernels, attend_back(): pl.pallas_call(functools.partial(attend_back_kernel, causal), out_shape=[...  108 us
    pallas_call x5, Pallas kernels, attend(): pl.pallas_call(functools.partial(attend_kernel, causal), out_shape=[jax.S...  67.7 us
    dot_general x46, matrix products, outer_sum(): lax.dot_general(a, b, (((0,), (0,)), ((), ())), preferred_element_type=jn...  54.7 us
    unnamed x703, local copies, waits for them, and re-layouts  42.4 us
    dot_general x47, matrix products, product(): return jnp.dot(a, b, preferred_element_type=jnp.float32)  42.2 us
    dot_general x45, matrix products, against_rows(): lax.dot_general(a, b, (((1,), (1,)), ((), ())), preferred_element_type=jn...  34.7 us
  transfers between devices with their start and end apart: 122, of which 38 were waited for; matrix products, arithmetic and copies ran while one was open for 29% of the time, Pallas kernels for 13%

profile of v2, /device:TPU:0, one launch (start us, length us, event | category | flops | bytes accessed | tf_op | source)
XLA Modules:
  0.0 942.1 jit_solution(410266749221166203)
XLA Ops:
  56.6 14.0 %collective-permute-done.18 = f32[4,708]{1,0:T(4,128)S(1)} collective-permute-done((f32[4,708]{1,0:T(4,128)S(1)}, f32[4,708]{1,0:T(4,128)S(1)}, u32[]{:S(2)}, u32[]{:S(2)}) %collective-permute-start.18) | collective-permute-done | bytes 11360 | tf_op jit(solution)/shard_map/ppermute | solution.py:53
  81.1 6.3 collective-permute-done.20
  89.8 8.3 collective-permute-start.48
  125.4 5.6 collective-permute-done.38.refs_3_
  136.8 11.1 %collective-permute-done.52.refs_3_ = bf16[3,16,16,512]{3,2,1,0:T(8,128)(2,1)} collective-permute-done((bf16[3,16,16,512]{3,2,1,0:T(8,128)(2,1)}, bf16[3,16,16,512]{3,2,1,0:T(8,128)(2,1)}, u32[]{:S(2)}, u32[]{:S(2)}) %collective-permute-start.52) | collective-permute-done | bytes 786464 | tf_op jit(solution)/shard_map/ppermute | solution.py:53
  149.9 8.9 collective-permute-done.6.refs_5_
  176.7 6.2 place_weights.4
  182.8 6.9 gather_fusion.1
  197.9 6.1 place_weights.5
  224.0 6.2 place_weights.6
  237.8 7.5 place_weights.7
  250.6 15.4 %attend.5 = (bf16[512,512]{1,0:T(8,128)(2,1)}, f32[8,512]{1,0:T(8,128)}) custom-call(s32[32]{0:T(128)} %reshape.767.act, s32[512,128]{1,0:T(8,128)} %broadcast_in_dim.77.q_seg, s32[8,1024]{1,0:T(8,128)} %broadcast_in_dim.78.k_seg, s32[512,128]{1,0:T(8,128)} %broadcast_in_dim.79.q_pos, s32[8,1024]{1,0:T(8,128)} %broadcast_in_dim.80.k_pos, ...), custom_call_target="tpu_custom_call" | custom-call | tf_op jit(solution)/shard_map/attend/pallas_call | solution.py:496
  280.6 10.8 %attend.6 = (bf16[512,512]{1,0:T(8,128)(2,1)}, f32[8,512]{1,0:T(8,128)}) custom-call(s32[32]{0:T(128)} %reshape.768.act, s32[512,128]{1,0:T(8,128)} %broadcast_in_dim.77.q_seg, s32[8,1024]{1,0:T(8,128)} %broadcast_in_dim.78.k_seg, s32[512,128]{1,0:T(8,128)} %broadcast_in_dim.79.q_pos, s32[8,1024]{1,0:T(8,128)} %broadcast_in_dim.80.k_pos, ...), custom_call_target="tpu_custom_call" | custom-call | tf_op jit(solution)/shard_map/attend/pallas_call | solution.py:496
  298.1 15.6 %attend.7 = (bf16[512,512]{1,0:T(8,128)(2,1)}, f32[8,512]{1,0:T(8,128)}) custom-call(s32[32]{0:T(128)} %reshape.767.act, s32[512,128]{1,0:T(8,128)} %broadcast_in_dim.77.q_seg, s32[8,1024]{1,0:T(8,128)} %broadcast_in_dim.78.k_seg, s32[512,128]{1,0:T(8,128)} %broadcast_in_dim.79.q_pos, s32[8,1024]{1,0:T(8,128)} %broadcast_in_dim.80.k_pos, ...), custom_call_target="tpu_custom_call" | custom-call | tf_op jit(solution)/shard_map/attend/pallas_call | solution.py:496
  331.5 10.7 %attend.8 = (bf16[512,512]{1,0:T(8,128)(2,1)}, f32[8,512]{1,0:T(8,128)}) custom-call(s32[32]{0:T(128)} %reshape.768.act, s32[512,128]{1,0:T(8,128)} %broadcast_in_dim.77.q_seg, s32[8,1024]{1,0:T(8,128)} %broadcast_in_dim.78.k_seg, s32[512,128]{1,0:T(8,128)} %broadcast_in_dim.79.q_pos, s32[8,1024]{1,0:T(8,128)} %broadcast_in_dim.80.k_pos, ...), custom_call_target="tpu_custom_call" | custom-call | tf_op jit(solution)/shard_map/attend/pallas_call | solution.py:496
  347.3 15.3 %attend.9 = (bf16[512,512]{1,0:T(8,128)(2,1)}, f32[8,512]{1,0:T(8,128)}) custom-call(s32[32]{0:T(128)} %reshape.767.act, s32[512,128]{1,0:T(8,128)} %broadcast_in_dim.77.q_seg, s32[8,1024]{1,0:T(8,128)} %broadcast_in_dim.78.k_seg, s32[512,128]{1,0:T(8,128)} %broadcast_in_dim.79.q_pos, s32[8,1024]{1,0:T(8,128)} %broadcast_in_dim.80.k_pos, ...), custom_call_target="tpu_custom_call" | custom-call | tf_op jit(solution)/shard_map/attend/pallas_call | solution.py:496
  392.1 25.9 %attend_back.5 = (bf16[512,512]{1,0:T(8,128)(2,1)}, f32[2,512,512]{2,1,0:T(8,128)}, f32[2,512,512]{2,1,0:T(8,128)}) custom-call(s32[32]{0:T(128)} %reshape.767.act, s32[1024,128]{1,0:T(8,128)} %broadcast_in_dim.72.k_seg, s32[8,512]{1,0:T(8,128)} %broadcast_in_dim.73.q_seg, s32[1024,128]{1,0:T(8,128)} %broadcast_in_dim.74.k_pos, ...), custom_call_target="tpu_custom_call" | custom-call | tf_op jit(solution)/shard_map/attend_back/pallas_call | solution.py:522
  423.5 15.1 %attend_back.6 = (bf16[512,512]{1,0:T(8,128)(2,1)}, f32[2,512,512]{2,1,0:T(8,128)}, f32[2,512,512]{2,1,0:T(8,128)}) custom-call(s32[32]{0:T(128)} %reshape.768.act, s32[1024,128]{1,0:T(8,128)} %broadcast_in_dim.72.k_seg, s32[8,512]{1,0:T(8,128)} %broadcast_in_dim.73.q_seg, s32[1024,128]{1,0:T(8,128)} %broadcast_in_dim.74.k_pos, ...), custom_call_target="tpu_custom_call" | custom-call | tf_op jit(solution)/shard_map/attend_back/pallas_call | solution.py:522
  484.8 26.1 %attend_back.7 = (bf16[512,512]{1,0:T(8,128)(2,1)}, f32[2,512,512]{2,1,0:T(8,128)}, f32[2,512,512]{2,1,0:T(8,128)}) custom-call(s32[32]{0:T(128)} %reshape.767.act, s32[1024,128]{1,0:T(8,128)} %broadcast_in_dim.72.k_seg, s32[8,512]{1,0:T(8,128)} %broadcast_in_dim.73.q_seg, s32[1024,128]{1,0:T(8,128)} %broadcast_in_dim.74.k_pos, ...), custom_call_target="tpu_custom_call" | custom-call | tf_op jit(solution)/shard_map/attend_back/pallas_call | solution.py:522
  515.5 15.1 %attend_back.9 = (bf16[512,512]{1,0:T(8,128)(2,1)}, f32[2,512,512]{2,1,0:T(8,128)}, f32[2,512,512]{2,1,0:T(8,128)}) custom-call(s32[32]{0:T(128)} %reshape.768.act, s32[1024,128]{1,0:T(8,128)} %broadcast_in_dim.72.k_seg, s32[8,512]{1,0:T(8,128)} %broadcast_in_dim.73.q_seg, s32[1024,128]{1,0:T(8,128)} %broadcast_in_dim.74.k_pos, ...), custom_call_target="tpu_custom_call" | custom-call | tf_op jit(solution)/shard_map/attend_back/pallas_call | solution.py:522
  538.4 7.5 collect_gradients.4
  575.2 25.9 %attend_back.8 = (bf16[512,512]{1,0:T(8,128)(2,1)}, f32[2,512,512]{2,1,0:T(8,128)}, f32[2,512,512]{2,1,0:T(8,128)}) custom-call(s32[32]{0:T(128)} %reshape.767.act, s32[1024,128]{1,0:T(8,128)} %broadcast_in_dim.72.k_seg, s32[8,512]{1,0:T(8,128)} %broadcast_in_dim.73.q_seg, s32[1024,128]{1,0:T(8,128)} %broadcast_in_dim.74.k_pos, ...), custom_call_target="tpu_custom_call" | custom-call | tf_op jit(solution)/shard_map/attend_back/pallas_call | solution.py:522
  613.7 6.1 collect_gradients.6
  627.6 6.3 collect_gradients.5
  643.6 6.3 collective-permute-start.76
  680.9 10.5 %collective-permute-start.71 = (f32[5633]{0:T(1024)S(1)}, f32[5633]{0:T(1024)S(1)}, u32[]{:S(2)}, u32[]{:S(2)}) collective-permute-start(f32[5633]{0:T(1024)S(1)} %add.740), channel_id=1, source_target_pairs={{0,2},{2,0},{4,6},{6,4},{1,3},{3,1},{5,7},{7,5},{8,10},{10,8},{12,... | collective-permute-start | bytes 67604 | tf_op jit(solution)/shard_map/ppermute | solution.py:53
  695.3 6.2 collect_gradients.7
  729.4 6.6 collective-permute-done.78
  738.1 6.2 collective-permute-done.79
  751.0 7.9 collective-permute-done.84
  810.1 8.4 collective-permute-done.95
  848.1 6.1 collective-permute-done.100
  (1380 shorter events, 578.0 us)
Async XLA Ops:
  10.0 41.0 %collective-permute-start.2 = (bf16[12,16,512]{2,1,0:T(8,128)(2,1)}, bf16[12,16,512]{2,1,0:T(8,128)(2,1)S(1)}, u32[]{:S(2)}, u32[]{:S(2)}) collective-permute-start(bf16[12,16,512]{2,1,0:T(8,128)(2,1)} %constant_dynamic-slice_fusion.21), channel_id=1, source_target_pairs={{0,6},{2,4},{4,2},{6,0},{1,7},{3,5},{5,3},{7,1},{8,14},{10,12},{12... | collective-permute-start | bytes 589832 | tf_op jit(solution)/shard_map/ppermute | solution.py:53
  15.0 36.7 %collective-permute-start.1 = (bf16[12,16,512]{2,1,0:T(8,128)(2,1)}, bf16[12,16,512]{2,1,0:T(8,128)(2,1)}, u32[]{:S(2)}, u32[]{:S(2)}) collective-permute-start(bf16[12,16,512]{2,1,0:T(8,128)(2,1)} %constant_dynamic-slice_fusion.21), channel_id=1, source_target_pairs={{0,4},{2,6},{4,0},{6,2},{1,5},{3,7},{5,1},{7,3},{8,12},{10,14},{12... | collective-permute-start | bytes 589832 | tf_op jit(solution)/shard_map/ppermute | solution.py:53
  15.0 40.3 %collective-permute-start = (bf16[12,16,512]{2,1,0:T(8,128)(2,1)}, bf16[12,16,512]{2,1,0:T(8,128)(2,1)}, u32[]{:S(2)}, u32[]{:S(2)}) collective-permute-start(bf16[12,16,512]{2,1,0:T(8,128)(2,1)} %constant_dynamic-slice_fusion.21), channel_id=1, source_target_pairs={{0,2},{2,0},{4,6},{6,4},{1,3},{3,1},{5,7},{7,5},{8,10},{10,8},{12,... | collective-permute-start | bytes 589832 | tf_op jit(solution)/shard_map/ppermute | solution.py:53
  20.2 50.4 %collective-permute-start.36 = (bf16[12,16,512]{2,1,0:T(8,128)(2,1)S(1)}, bf16[12,16,512]{2,1,0:T(8,128)(2,1)S(1)}, u32[]{:S(2)}, u32[]{:S(2)}) collective-permute-start(bf16[12,16,512]{2,1,0:T(8,128)(2,1)S(1)} %constant_dynamic-slice_fusion.19), channel_id=1, source_target_pairs={{0,6},{2,4},{4,2},{6,0},{1,7},{3,5},{5,3},{7,1},{8,14},{10,12},{12... | collective-permute-start | bytes 589832 | tf_op jit(solution)/shard_map/ppermute | solution.py:53
  75.0 26.9 %collective-permute-start.49 = (bf16[16,16,512]{2,1,0:T(8,128)(2,1)S(1)}, bf16[16,16,512]{2,1,0:T(8,128)(2,1)S(1)}, u32[]{:S(2)}, u32[]{:S(2)}) collective-permute-start(bf16[16,16,512]{2,1,0:T(8,128)(2,1)S(1)} %constant_dynamic-slice_fusion.18), channel_id=1, source_target_pairs={{0,4},{2,6},{4,0},{6,2},{1,5},{3,7},{5,1},{7,3},{8,12},{10,14},{12... | collective-permute-start | bytes 786440 | tf_op jit(solution)/shard_map/ppermute | solution.py:53
  75.0 34.0 %collective-permute-start.8 = (bf16[3,12,16,512]{3,2,1,0:T(8,128)(2,1)S(1)}, bf16[3,12,16,512]{3,2,1,0:T(8,128)(2,1)}, u32[]{:S(2)}, u32[]{:S(2)}) collective-permute-start(bf16[3,12,16,512]{3,2,1,0:T(8,128)(2,1)S(1)} %pad_maximum_fusion.33.refs_1_), channel_id=1, source_target_pairs={{0,1},{1,0},{2,3},{3,2},{4,5},{5,4},{6,7},{7,6},{8,9},{9,8},{10,11... | collective-permute-start | bytes 1769480 | tf_op jit(solution)/shard_map/ppermute | solution.py:53
  80.6 30.9 %collective-permute-start.4 = (bf16[3,12,16,512]{3,2,1,0:T(8,128)(2,1)S(1)}, bf16[3,12,16,512]{3,2,1,0:T(8,128)(2,1)S(1)}, u32[]{:S(2)}, u32[]{:S(2)}) collective-permute-start(bf16[3,12,16,512]{3,2,1,0:T(8,128)(2,1)S(1)} %pad_maximum_fusion.33.refs_1_), channel_id=1, source_target_pairs={{0,16},{16,0},{1,17},{17,1},{2,18},{18,2},{3,19},{19,3},{4,20},{20... | collective-permute-start | bytes 1769480 | tf_op jit(solution)/shard_map/ppermute | solution.py:53
  111.6 36.3 %collective-permute-start.52 = (bf16[3,16,16,512]{3,2,1,0:T(8,128)(2,1)}, bf16[3,16,16,512]{3,2,1,0:T(8,128)(2,1)}, u32[]{:S(2)}, u32[]{:S(2)}) collective-permute-start(bf16[3,16,16,512]{3,2,1,0:T(8,128)(2,1)} %pad_maximum_fusion.25.refs_1_), channel_id=1, source_target_pairs={{0,16},{16,0},{1,17},{17,1},{2,18},{18,2},{3,19},{19,3},{4,20},{20... | collective-permute-start | bytes 2359304 | tf_op jit(solution)/shard_map/ppermute | solution.py:53
  124.1 37.3 %collective-permute-start.51 = (bf16[3,16,16,512]{3,2,1,0:T(8,128)(2,1)}, bf16[3,16,16,512]{3,2,1,0:T(8,128)(2,1)}, u32[]{:S(2)}, u32[]{:S(2)}) collective-permute-start(bf16[3,16,16,512]{3,2,1,0:T(8,128)(2,1)} %pad_maximum_fusion.25.refs_1_), channel_id=1, source_target_pairs={{0,8},{8,0},{1,9},{9,1},{2,10},{10,2},{3,11},{11,3},{4,12},{12,4},... | collective-permute-start | bytes 2359304 | tf_op jit(solution)/shard_map/ppermute | solution.py:53
  130.9 27.8 %collective-permute-start.6 = (bf16[3,6,16,512]{3,2,1,0:T(8,128)(2,1)}, bf16[3,6,16,512]{3,2,1,0:T(8,128)(2,1)S(1)}, u32[]{:S(2)}, u32[]{:S(2)}) collective-permute-start(bf16[3,6,16,512]{3,2,1,0:T(8,128)(2,1)} %slice.871), channel_id=1, source_target_pairs={{0,8},{8,0},{1,9},{9,1},{2,10},{10,2},{3,11},{11,3},{4,12},{12,4},... | collective-permute-start | bytes 884744 | tf_op jit(solution)/shard_map/ppermute | solution.py:53
  136.8 37.0 %collective-permute-start.10 = (bf16[3,12,16,512]{3,2,1,0:T(8,128)(2,1)}, bf16[3,12,16,512]{3,2,1,0:T(8,128)(2,1)S(1)}, u32[]{:S(2)}, u32[]{:S(2)}) collective-permute-start(bf16[3,12,16,512]{3,2,1,0:T(8,128)(2,1)} %copy-done.216), channel_id=1, source_target_pairs={{0,1},{1,0},{2,3},{3,2},{4,5},{5,4},{6,7},{7,6},{8,9},{9,8},{10,11... | collective-permute-start | bytes 1769480 | tf_op jit(solution)/shard_map/ppermute | solution.py:53
  147.9 27.9 %collective-permute-start.9 = (bf16[3,12,16,512]{3,2,1,0:T(8,128)(2,1)}, bf16[3,12,16,512]{3,2,1,0:T(8,128)(2,1)S(1)}, u32[]{:S(2)}, u32[]{:S(2)}) collective-permute-start(bf16[3,12,16,512]{3,2,1,0:T(8,128)(2,1)} %collective-permute-done.3.refs_2_), channel_id=1, source_target_pairs={{0,1},{1,0},{2,3},{3,2},{4,5},{5,4},{6,7},{7,6},{8,9},{9,8},{10,11... | collective-permute-start | bytes 1769480 | tf_op jit(solution)/shard_map/ppermute | solution.py:53
  161.5 30.6 %collective-permute-start.27 = (bf16[12,64,512]{2,1,0:T(8,128)(2,1)}, bf16[12,64,512]{2,1,0:T(8,128)(2,1)}, u32[]{:S(2)}, u32[]{:S(2)}) collective-permute-start(bf16[12,64,512]{2,1,0:T(8,128)(2,1)} %pad_maximum_fusion.23.refs_0_), channel_id=1, source_target_pairs={{0,1},{1,0},{2,3},{3,2},{4,5},{5,4},{6,7},{7,6},{8,9},{9,8},{10,11... | collective-permute-start | bytes 2359304 | tf_op jit(solution)/shard_map/ppermute | solution.py:53
  161.5 29.3 %collective-permute-start.28 = (bf16[3,12,16,512]{3,2,1,0:T(8,128)(2,1)}, bf16[3,12,16,512]{3,2,1,0:T(8,128)(2,1)}, u32[]{:S(2)}, u32[]{:S(2)}) collective-permute-start(bf16[3,12,16,512]{3,2,1,0:T(8,128)(2,1)} %pad_maximum_fusion.34.refs_1_), channel_id=1, source_target_pairs={{0,1},{1,0},{2,3},{3,2},{4,5},{5,4},{6,7},{7,6},{8,9},{9,8},{10,11... | collective-permute-start | bytes 1769480 | tf_op jit(solution)/shard_map/ppermute | solution.py:53
  216.4 29.0 %collective-permute-start.19 = (bf16[2,512,512]{2,1,0:T(8,128)(2,1)}, bf16[2,512,512]{2,1,0:T(8,128)(2,1)}, u32[]{:S(2)}, u32[]{:S(2)}) collective-permute-start(bf16[2,512,512]{2,1,0:T(8,128)(2,1)} %pad_maximum_fusion.15), channel_id=1, source_target_pairs={{0,1},{1,0},{2,3},{3,2},{4,5},{5,4},{6,7},{7,6},{8,9},{9,8},{10,11... | collective-permute-start | bytes 3145736 | tf_op jit(solution)/shard_map/ppermute | solution.py:53
  237.4 40.9 %collective-permute-start.33 = (bf16[2,512,512]{2,1,0:T(8,128)(2,1)}, bf16[2,512,512]{2,1,0:T(8,128)(2,1)}, u32[]{:S(2)}, u32[]{:S(2)}) collective-permute-start(bf16[2,512,512]{2,1,0:T(8,128)(2,1)} %pad_maximum_fusion.16), channel_id=1, source_target_pairs={{0,1},{1,0},{2,3},{3,2},{4,5},{5,4},{6,7},{7,6},{8,9},{9,8},{10,11... | collective-permute-start | bytes 3145736 | tf_op jit(solution)/shard_map/ppermute | solution.py:53
  278.2 49.9 %collective-permute-start.62 = (bf16[2,512,512]{2,1,0:T(8,128)(2,1)}, bf16[2,512,512]{2,1,0:T(8,128)(2,1)}, u32[]{:S(2)}, u32[]{:S(2)}) collective-permute-start(bf16[2,512,512]{2,1,0:T(8,128)(2,1)} %pad_maximum_fusion.19), channel_id=1, source_target_pairs={{0,1},{1,0},{2,3},{3,2},{4,5},{5,4},{6,7},{7,6},{8,9},{9,8},{10,11... | collective-permute-start | bytes 3145736 | tf_op jit(solution)/shard_map/ppermute | solution.py:53
  445.7 29.4 %collective-permute-start.63 = (f32[2,512,512]{2,1,0:T(8,128)}, f32[2,512,512]{2,1,0:T(8,128)S(1)}, u32[]{:S(2)}, u32[]{:S(2)}) collective-permute-start(f32[2,512,512]{2,1,0:T(8,128)} %get-tuple-element.94), channel_id=1, source_target_pairs={{0,1},{1,0},{2,3},{3,2},{4,5},{5,4},{6,7},{7,6},{8,9},{9,8},{10,11... | collective-permute-start | bytes 6291464 | tf_op jit(solution)/shard_map/ppermute | solution.py:53
  530.6 70.5 %collective-permute-start.67 = (f32[2,512,512]{2,1,0:T(8,128)}, f32[2,512,512]{2,1,0:T(8,128)}, u32[]{:S(2)}, u32[]{:S(2)}) collective-permute-start(f32[2,512,512]{2,1,0:T(8,128)} %get-tuple-element.111), channel_id=1, source_target_pairs={{0,1},{1,0},{2,3},{3,2},{4,5},{5,4},{6,7},{7,6},{8,9},{9,8},{10,11... | collective-permute-start | bytes 6291464 | tf_op jit(solution)/shard_map/ppermute | solution.py:53
  534.3 25.3 %collective-permute-start.65 = (f32[2,512,512]{2,1,0:T(8,128)}, f32[2,512,512]{2,1,0:T(8,128)}, u32[]{:S(2)}, u32[]{:S(2)}) collective-permute-start(f32[2,512,512]{2,1,0:T(8,128)} %get-tuple-element.102), channel_id=1, source_target_pairs={{0,1},{1,0},{2,3},{3,2},{4,5},{5,4},{6,7},{7,6},{8,9},{9,8},{10,11... | collective-permute-start | bytes 6291464 | tf_op jit(solution)/shard_map/ppermute | solution.py:53
  545.9 90.8 %collective-permute-start.73 = (bf16[4,2,2,16,16,512]{5,4,3,2,1,0:T(8,128)(2,1)}, bf16[4,2,2,16,16,512]{5,4,3,2,1,0:T(8,128)(2,1)}, u32[]{:S(2)}, u32[]{:S(2)}) collective-permute-start(bf16[4,2,2,16,16,512]{5,4,3,2,1,0:T(8,128)(2,1)} %get-tuple-element.113), channel_id=1, source_target_pairs={{0,1},{1,0},{2,3},{3,2},{4,5},{5,4},{6,7},{7,6},{8,9},{9,8},{10,11... | collective-permute-start | bytes 12582920 | tf_op jit(solution)/shard_map/ppermute | solution.py:53
  601.1 50.6 %collective-permute-start.66 = (f32[2,512,512]{2,1,0:T(8,128)}, f32[2,512,512]{2,1,0:T(8,128)}, u32[]{:S(2)}, u32[]{:S(2)}) collective-permute-start(f32[2,512,512]{2,1,0:T(8,128)} %get-tuple-element.106), channel_id=1, source_target_pairs={{0,1},{1,0},{2,3},{3,2},{4,5},{5,4},{6,7},{7,6},{8,9},{9,8},{10,11... | collective-permute-start | bytes 6291464 | tf_op jit(solution)/shard_map/ppermute | solution.py:53
  619.8 90.9 %collective-permute-start.89 = (bf16[4,2,2,12,16,512]{5,4,3,2,1,0:T(8,128)(2,1)}, bf16[4,2,2,12,16,512]{5,4,3,2,1,0:T(8,128)(2,1)}, u32[]{:S(2)}, u32[]{:S(2)}) collective-permute-start(bf16[4,2,2,12,16,512]{5,4,3,2,1,0:T(8,128)(2,1)} %get-tuple-element.117), channel_id=1, source_target_pairs={{0,1},{1,0},{2,3},{3,2},{4,5},{5,4},{6,7},{7,6},{8,9},{9,8},{10,11... | collective-permute-start | bytes 9437192 | tf_op jit(solution)/shard_map/ppermute | solution.py:53
  633.9 82.0 %collective-permute-start.81 = (bf16[4,2,2,12,16,512]{5,4,3,2,1,0:T(8,128)(2,1)}, bf16[4,2,2,12,16,512]{5,4,3,2,1,0:T(8,128)(2,1)}, u32[]{:S(2)}, u32[]{:S(2)}) collective-permute-start(bf16[4,2,2,12,16,512]{5,4,3,2,1,0:T(8,128)(2,1)} %get-tuple-element.115), channel_id=1, source_target_pairs={{0,1},{1,0},{2,3},{3,2},{4,5},{5,4},{6,7},{7,6},{8,9},{9,8},{10,11... | collective-permute-start | bytes 9437192 | tf_op jit(solution)/shard_map/ppermute | solution.py:53
  643.6 59.6 %collective-permute-start.76 = (bf16[4,2,8,16,512]{4,3,2,0,1:T(8,128)(2,1)}, bf16[4,2,8,16,512]{4,3,2,0,1:T(8,128)(2,1)}, u32[]{:S(2)}, u32[]{:S(2)}) collective-permute-start(bf16[4,2,8,16,512]{4,3,2,0,1:T(8,128)(2,1)} %slice_bitcast_fusion.9), channel_id=1, source_target_pairs={{0,16},{16,0},{1,17},{17,1},{2,18},{18,2},{3,19},{19,3},{4,20},{20... | collective-permute-start | bytes 3145736 | tf_op jit(solution)/shard_map/ppermute | solution.py:53
  651.1 56.2 %collective-permute-start.74 = (bf16[4,2,8,16,512]{4,3,2,0,1:T(8,128)(2,1)}, bf16[4,2,8,16,512]{4,3,2,0,1:T(8,128)(2,1)}, u32[]{:S(2)}, u32[]{:S(2)}) collective-permute-start(bf16[4,2,8,16,512]{4,3,2,0,1:T(8,128)(2,1)} %slice_bitcast_fusion.11), channel_id=1, source_target_pairs={{0,8},{8,0},{1,9},{9,1},{2,10},{10,2},{3,11},{11,3},{4,12},{12,4},... | collective-permute-start | bytes 3145736 | tf_op jit(solution)/shard_map/ppermute | solution.py:53
  714.2 31.7 %collective-permute-start.92 = (bf16[4,2,6,16,512]{4,3,2,0,1:T(8,128)(2,1)S(1)}, bf16[4,2,6,16,512]{4,3,2,0,1:T(8,128)(2,1)S(1)}, u32[]{:S(2)}, u32[]{:S(2)}) collective-permute-start(bf16[4,2,6,16,512]{4,3,2,0,1:T(8,128)(2,1)S(1)} %slice_bitcast_fusion.17), channel_id=1, source_target_pairs={{0,16},{16,0},{1,17},{17,1},{2,18},{18,2},{3,19},{19,3},{4,20},{20... | collective-permute-start | bytes 2359304 | tf_op jit(solution)/shard_map/ppermute | solution.py:53
  715.4 32.3 %collective-permute-start.90 = (bf16[4,2,6,16,512]{4,3,2,0,1:T(8,128)(2,1)S(1)}, bf16[4,2,6,16,512]{4,3,2,0,1:T(8,128)(2,1)S(1)}, u32[]{:S(2)}, u32[]{:S(2)}) collective-permute-start(bf16[4,2,6,16,512]{4,3,2,0,1:T(8,128)(2,1)S(1)} %slice_bitcast_fusion.19), channel_id=1, source_target_pairs={{0,8},{8,0},{1,9},{9,1},{2,10},{10,2},{3,11},{11,3},{4,12},{12,4},... | collective-permute-start | bytes 2359304 | tf_op jit(solution)/shard_map/ppermute | solution.py:53
  736.1 97.4 %collective-permute-start.97 = (bf16[4,2,2,12,16,512]{5,4,3,2,1,0:T(8,128)(2,1)}, bf16[4,2,2,12,16,512]{5,4,3,2,1,0:T(8,128)(2,1)}, u32[]{:S(2)}, u32[]{:S(2)}) collective-permute-start(bf16[4,2,2,12,16,512]{5,4,3,2,1,0:T(8,128)(2,1)} %get-tuple-element.119), channel_id=1, source_target_pairs={{0,1},{1,0},{2,3},{3,2},{4,5},{5,4},{6,7},{7,6},{8,9},{9,8},{10,11... | collective-permute-start | bytes 9437192 | tf_op jit(solution)/shard_map/ppermute | solution.py:53
  891.4 35.5 %collective-permute-start.112 = (bf16[12,16,512]{2,1,0:T(8,128)(2,1)}, bf16[12,16,512]{2,1,0:T(8,128)(2,1)}, u32[]{:S(2)}, u32[]{:S(2)}) collective-permute-start(bf16[12,16,512]{2,1,0:T(8,128)(2,1)} %get-tuple-element.190), channel_id=1, source_target_pairs={{0,24},{8,16},{16,8},{24,0},{1,25},{9,17},{17,9},{25,1},{2,26},{10... | collective-permute-start | bytes 589832 | tf_op jit(solution)/shard_map/ppermute | solution.py:53
  893.0 33.8 %collective-permute-start.111 = (bf16[12,16,512]{2,1,0:T(8,128)(2,1)}, bf16[12,16,512]{2,1,0:T(8,128)(2,1)}, u32[]{:S(2)}, u32[]{:S(2)}) collective-permute-start(bf16[12,16,512]{2,1,0:T(8,128)(2,1)} %get-tuple-element.190), channel_id=1, source_target_pairs={{0,16},{16,0},{1,17},{17,1},{2,18},{18,2},{3,19},{19,3},{4,20},{20... | collective-permute-start | bytes 589832 | tf_op jit(solution)/shard_map/ppermute | solution.py:53
  894.5 32.3 %collective-permute-start.110 = (bf16[12,16,512]{2,1,0:T(8,128)(2,1)}, bf16[12,16,512]{2,1,0:T(8,128)(2,1)}, u32[]{:S(2)}, u32[]{:S(2)}) collective-permute-start(bf16[12,16,512]{2,1,0:T(8,128)(2,1)} %get-tuple-element.190), channel_id=1, source_target_pairs={{0,8},{8,0},{1,9},{9,1},{2,10},{10,2},{3,11},{11,3},{4,12},{12,4},... | collective-permute-start | bytes 589832 | tf_op jit(solution)/shard_map/ppermute | solution.py:53
  (429 other events, 3349.8 us)

commit v3 on v2

v3 whole, which is shorter than its diff:
```python
import functools
import math

import jax
import jax.numpy as jnp
from jax import lax
from jax.experimental import pallas as pl
from jax.experimental.pallas import tpu as pltpu
from jax.sharding import Mesh
from jax.sharding import PartitionSpec as P

HEADS = 8
HEAD = 64
ENC = 1
LAYERS = 2
MICRO = 2
COL = 512

NORM_EPS = 1e-06
CLIP_NORM = 0.01
LEARN_RATE = 0.05
BETA_ONE = 0.9
BETA_TWO = 0.999
ADAM_EPS = 1e-08
WEIGHT_DECAY = 0.01
ADAM_STEP = 10
LOGIT_SCALE = 4.0
NEGATIVE = -1e30

PLANE = ("sy", "sx")
LINE = ("z", "c")

TABLE = ("table", 0, "blk")


def attention_parts(i):
    return (("qkv", i, "row"), ("out", i, "row"))


def feed_parts(i):
    return (("up", i, "row"), ("down", i, "blk"))


GATHERED = (
    (TABLE,) + attention_parts(0),
    feed_parts(0),
    attention_parts(1) + attention_parts(2) + feed_parts(1),
    attention_parts(3) + attention_parts(4) + feed_parts(2),
)
REDUCED = (
    feed_parts(2),
    attention_parts(3) + attention_parts(4) + feed_parts(1),
    attention_parts(1) + attention_parts(2),
    feed_parts(0),
    (TABLE,) + attention_parts(0),
)


def flip(x, axis, bit=1):
    if isinstance(axis, tuple):
        n = math.prod(lax.axis_size(a) for a in axis)
    else:
        n = lax.axis_size(axis)
    return lax.ppermute(x, axis, [(i, i ^ bit) for i in range(n)])


def bits(axis):
    n = lax.axis_size(axis)
    return [1 << k for k in range(n.bit_length() - 1)]


def gathered(x, axis):
    if isinstance(axis, tuple) or lax.axis_size(axis) <= 4:
        n = 4 if isinstance(axis, tuple) else lax.axis_size(axis)
        return jnp.stack([x] + [flip(x, axis, r) for r in range(1, n)])
    x = x[None]
    for bit in bits(axis):
        x = jnp.concatenate([x, flip(x, axis, bit)], axis=0)
    return x


def in_order(blocks, index):
    n = blocks.shape[0]
    return jnp.concatenate(
        [lax.dynamic_index_in_dim(blocks, i ^ index, 0, keepdims=True) for i in range(n)]
    )


def all_sum(x):
    for axis in ("c", "sx", "sy", "z"):
        for bit in bits(axis):
            x = x + flip(x, axis, bit)
    return x


def hold(carry, things):
    return lax.optimization_barrier((carry, things))


def step(carry, *movers):
    for mover in movers:
        carry, (mover.held, mover.arrived) = hold(carry, (mover.held, mover.arrived))
        leaving = next(mover.stages)
        carry, (arrays, mover.held) = hold(carry, ([array for array, _ in leaving], mover.held))
        mover.arrived = [
            flip(array, *route)
            if route
            else lax.psum_scatter(array, PLANE + ("z",), scatter_dimension=0, tiled=True)
            for array, (_, route) in zip(arrays, leaving)
        ]
    return carry


class Mover:
    def __init__(self):
        self.held = []
        self.arrived = []


def normalize(v, g):
    return v * lax.rsqrt(jnp.mean(v * v, axis=-1, keepdims=True) + NORM_EPS) * g


def norm_back(v, g, cotangent):
    _, pullback = jax.vjp(normalize, v, g)
    return pullback(cotangent)


def product(a, b):
    return jnp.dot(a, b, preferred_element_type=jnp.float32)


def outer_sum(a, b):
    return lax.dot_general(a, b, (((0,), (0,)), ((), ())), preferred_element_type=jnp.float32)


def against_rows(a, b):
    return lax.dot_general(a, b, (((1,), (1,)), ((), ())), preferred_element_type=jnp.float32)


def split_heads(v):
    return v.reshape(v.shape[0], HEADS, HEAD)


def low(v):
    return v.astype(jnp.bfloat16)


def wide(v):
    return v.astype(jnp.float32)


def adam_update(master, first, second, grad):
    first = BETA_ONE * first + (1.0 - BETA_ONE) * grad
    second = BETA_TWO * second + (1.0 - BETA_TWO) * grad * grad
    fixed_first = first / (1.0 - BETA_ONE**ADAM_STEP)
    fixed_second = second / (1.0 - BETA_TWO**ADAM_STEP)
    master = master - LEARN_RATE * (
        fixed_first / (jnp.sqrt(fixed_second) + ADAM_EPS) + WEIGHT_DECAY * master
    )
    return (master, first, second)


def owned_blocks(array, kind, unit):
    if kind == "row":
        rows, columns = array.shape
        return array.reshape(rows, columns // COL, COL).transpose(1, 0, 2)
    rows = array.shape[0]
    per = rows // (4 * unit)
    return array.reshape(4, per, unit, COL).transpose(1, 0, 2, 3).reshape(per, 4 * unit, COL)


def quarter_blocks(array, kind, unit, s):
    size = array.shape[0] // 4
    array = lax.dynamic_slice_in_dim(array, s * size, size, axis=0)
    if kind == "row":
        return low(array).reshape(unit, -1, COL).transpose(1, 0, 2)
    return low(array).reshape(-1, unit, COL)


def block_counts(entries, shard_shapes, unit):
    counts = []
    for name, _, kind in entries:
        rows, columns = shard_shapes[name]
        counts.append(columns // COL if kind == "row" else rows // (4 * unit))
    return counts


def natural_shape(kind, count, unit, owners):
    if kind == "row":
        return (count, owners * 4 * unit, COL)
    return (owners, 4, count, unit, COL)


def scatter_kernel(plan, unit, me_ref, *refs):
    pieces, outs, sem = refs[:10], refs[10:-1], refs[-1]
    c, z, s = me_ref[0], me_ref[1], me_ref[2]

    def put(out, kind, owner, part, rows, source):
        if kind == "row":
            start = pl.multiple_of(owner * (4 * unit) + part * unit, unit)
            target = outs[out].at[:, pl.ds(start, rows), :]
        else:
            target = outs[out].at[owner, part]
        pltpu.make_async_copy(source, target, sem.at[out]).start()

    for c_rel in range(2):
        shard, *quarters = pieces[5 * c_rel : 5 * c_rel + 5]
        for z_rel in range(4):
            owner = (z ^ z_rel) * 2 + (c ^ c_rel)
            for out, (kind, first, count) in enumerate(plan):
                last = first + count
                if z_rel == 0:
                    if kind == "row":
                        put(out, kind, owner, 0, 4 * unit, shard.at[first:last])
                    else:
                        for part in range(4):
                            rows = pl.ds(part * unit, unit)
                            put(out, kind, owner, part, unit, shard.at[first:last, rows, :])
                else:
                    for s_rel, quarter in enumerate(quarters):
                        put(out, kind, owner, s ^ s_rel, unit, quarter.at[z_rel - 1, first:last])
    for out in range(len(plan)):
        pltpu.make_async_copy(outs[out], outs[out], sem.at[out]).wait()


def collect_kernel(plan, unit, ordered, me_ref, *refs):
    grads, keep, send, sem = refs[: len(plan)], refs[len(plan)], refs[len(plan) + 1], refs[-1]
    c, z, s = me_ref[0], me_ref[1], me_ref[2]
    for c_rel, out in ((0, keep), (1, send)):
        for z_rel in range(4):
            owner = (z ^ z_rel) * 2 + (c ^ c_rel)
            for s_rel in range(4):
                part = s ^ s_rel
                for grad, (kind, first, count) in zip(grads, plan):
                    if kind == "row":
                        start = pl.multiple_of(owner * (4 * unit) + part * unit, unit)
                        source = grad.at[:, pl.ds(start, unit), :]
                    else:
                        source = grad.at[owner, part]
                    place = (part, z ^ z_rel) if ordered else (s_rel, z_rel)
                    target = out.at[*place, first : first + count]
                    pltpu.make_async_copy(source, target, sem.at[c_rel]).start()
    for c_rel, out in ((0, keep), (1, send)):
        pltpu.make_async_copy(out, out, sem.at[c_rel]).wait()


LIGHT = pl.CostEstimate(flops=1, bytes_accessed=1, transcendentals=0)
ANY = pl.BlockSpec(memory_space=pl.ANY)
ONCHIP = pl.BlockSpec(memory_space=pltpu.VMEM)
SCALAR = pl.BlockSpec(memory_space=pltpu.SMEM)


def gather_stages(mover, me, shard, kinds, counts, unit, owners):
    starts = [sum(counts[:i]) for i in range(len(counts))]
    mover.held = [shard]
    part = lax.dynamic_slice_in_dim(shard, me[2] * unit, unit, axis=1)
    yield [(part, ("z", bit)) for bit in (1, 2, 3)]
    mine = jnp.stack(mover.arrived)
    mover.held.append(mine)
    yield [(mine, (PLANE, bit)) for bit in (1, 2, 3)]
    mover.held += mover.arrived
    yield [(piece, ("c",)) for piece in mover.held]
    plan = tuple(zip(kinds, starts, counts))
    mover.result = pl.pallas_call(
        functools.partial(scatter_kernel, plan, unit),
        out_shape=[
            jax.ShapeDtypeStruct(natural_shape(kind, count, unit, owners), jnp.bfloat16)
            for kind, count in zip(kinds, counts)
        ],
        in_specs=[SCALAR] + [ANY] * 10,
        out_specs=[ONCHIP] * len(plan),
        scratch_shapes=[pltpu.SemaphoreType.DMA((len(plan),))],
        cost_estimate=LIGHT,
        name="place_weights",
    )(me, *mover.held, *mover.arrived)
    mover.held = []
    yield []


def unpack_kernel(plan, pieces, *refs):
    outs, sem = refs[:-1], refs[-1]
    for out, (kind, first, count) in enumerate(plan):
        for part in range(4):
            if kind == "blk":
                source = pieces.at[part, :, first : first + count]
                pltpu.make_async_copy(source, outs[out].at[:, part], sem.at[out]).start()
                continue
            for k in range(count):
                source = pieces.at[part, :, first + k]
                pltpu.make_async_copy(source, outs[out].at[k, :, part], sem.at[out]).start()
    for out in range(len(plan)):
        pltpu.make_async_copy(outs[out], outs[out], sem.at[out]).wait()


def unpack(pieces, kinds, counts, unit, owners):
    starts = [sum(counts[:i]) for i in range(len(counts))]
    shapes = [
        (count, owners, 4, unit, COL) if kind == "row" else (owners, 4, count, unit, COL)
        for kind, count in zip(kinds, counts)
    ]
    placed = pl.pallas_call(
        functools.partial(unpack_kernel, tuple(zip(kinds, starts, counts))),
        out_shape=[jax.ShapeDtypeStruct(shape, jnp.bfloat16) for shape in shapes],
        in_specs=[ANY],
        out_specs=[ONCHIP] * len(shapes),
        scratch_shapes=[pltpu.SemaphoreType.DMA((len(shapes),))],
        cost_estimate=LIGHT,
        name="place_gathered",
    )(pieces)
    return [
        out.reshape(count, -1, COL) if kind == "row" else out
        for out, kind, count in zip(placed, kinds, counts)
    ]


def added(arrays):
    total = wide(arrays[0])
    for array in arrays[1:]:
        total = total + wide(array)
    return total


def collect(me, grads, kinds, counts, unit, ordered):
    starts = [sum(counts[:i]) for i in range(len(counts))]
    plan = tuple(zip(kinds, starts, counts))
    shape = jax.ShapeDtypeStruct((4, 4, sum(counts), unit, COL), jnp.bfloat16)
    return pl.pallas_call(
        functools.partial(collect_kernel, plan, unit, ordered),
        out_shape=[shape, shape],
        in_specs=[SCALAR] + [ANY] * len(plan),
        out_specs=[ONCHIP, ONCHIP],
        scratch_shapes=[pltpu.SemaphoreType.DMA((2,))],
        cost_estimate=LIGHT,
        name="collect_gradients",
    )(me, *grads)


def long_reduce_stages(mover, me, grads, kinds, counts, unit):
    keep, send = collect(me, grads, kinds, counts, unit, True)
    mover.held = [keep]
    yield [(send, ("c",))]
    chip = low(added(mover.held + mover.arrived))
    mover.held = []
    yield [(chip.reshape(16, *chip.shape[2:]), None)]
    own = mover.arrived[0][0]
    mover.squares = jnp.sum(wide(own) * wide(own))
    mover.held = [own]
    yield [(own, (PLANE, bit)) for bit in (1, 2, 3)]
    mover.result = mover.held + mover.arrived
    mover.held = []
    yield []


def reduce_stages(mover, me, grads, kinds, counts, unit):
    total = sum(counts)
    keep, send = collect(me, grads, kinds, counts, unit, False)
    mover.held = [keep]
    half = total // 2
    yield [(send, ("c",))]
    mover.held = [a.reshape(2, 2, *a.shape[1:]) for a in mover.held + mover.arrived]
    yield [
        (low(added([a[:, 1, :, :half] for a in mover.held])), ("sx",)),
        (low(added([a[1, :, :, half:] for a in mover.held])), ("sy",)),
    ]
    mover.held += mover.arrived

    def sides():
        both, (come_x, come_y) = mover.held[:2], mover.held[2:4]
        return (
            [a[:, 0, :, :half] for a in both] + [come_x],
            [a[0, :, :, half:] for a in both] + [come_y],
        )

    left, right = sides()
    yield [(low(added([a[1] for a in left])), ("sy",)), (low(added([a[1] for a in right])), ("sx",))]
    mover.held += mover.arrived

    def plane(bit):
        left, right = sides()
        left = [a[0, bit] for a in left] + [mover.held[4][bit]]
        right = [a[0, bit] for a in right] + [mover.held[5][bit]]
        return jnp.concatenate([added(left), added(right)], axis=0)

    yield [(low(plane(bit)), ("z", bit)) for bit in (1, 2, 3)]
    own = plane(0)
    mover.arrived.insert(0, own)
    whole = added(mover.arrived)
    mover.squares = jnp.sum(whole * whole)
    mover.held = [low(whole)]
    yield [(mover.held[0], (PLANE, bit)) for bit in (1, 2, 3)]
    mover.result = mover.held + mover.arrived
    mover.held = []
    yield []


def settle_kernel(sizes, plan, unit, me_ref, *refs):
    buckets, outs, sem = refs[:sizes], refs[sizes:-1], refs[-1]
    s = me_ref[2]
    for bucket, first, count, kind, out, i in plan:
        for s_rel in range(4):
            source = buckets[4 * bucket + s_rel]
            part = s ^ s_rel
            if kind == "blk":
                for k in range(count):
                    start = pl.multiple_of((part * count + k) * unit, unit)
                    target = outs[out].at[i, pl.ds(start, unit), :]
                    pltpu.make_async_copy(source.at[first + k], target, sem.at[out]).start()
                continue
            rows = pl.ds(pl.multiple_of(part * unit, unit), unit)
            for k in range(count):
                target = outs[out].at[i, rows, k * COL : k * COL + COL]
                pltpu.make_async_copy(source.at[first + k], target, sem.at[out]).start()
    for out, ref in enumerate(outs):
        pltpu.make_async_copy(ref, ref, sem.at[out]).wait()


def owned_natural(parts, kind):
    if kind == "row":
        four, count, unit, _ = parts.shape
        return parts.transpose(0, 2, 1, 3).reshape(four * unit, count * COL)
    return parts.reshape(-1, COL)


BQ = 128
CK = 256
CF = 256
NT = (((1,), (1,)), ((), ()))
TN = (((0,), (0,)), ((), ()))
NN = (((1,), (0,)), ((), ()))


def dot32(a, b, dims):
    return lax.dot_general(a, b, dims, preferred_element_type=jnp.float32)


def load_halves(own, other, whole, sem):
    half = whole.shape[0] // 2
    copies = [
        pltpu.make_async_copy(own, whole.at[pl.ds(0, half)], sem.at[0]),
        pltpu.make_async_copy(other, whole.at[pl.ds(half, half)], sem.at[1]),
    ]
    for copy in copies:
        copy.start()
    return copies


def pair_rows(block, scale=None):
    lane = lax.broadcasted_iota(jnp.int32, block.shape, 1)
    zero = jnp.zeros_like(block)
    if scale is not None:
        block = block * jnp.asarray(scale, block.dtype)
    return jnp.concatenate(
        [jnp.where(lane < HEAD, block, zero), jnp.where(lane < HEAD, zero, block)], axis=0
    )


def pair_lanes(stacked):
    rows = stacked.shape[0] // 2
    lane = lax.broadcasted_iota(jnp.int32, (rows, 2 * HEAD), 1)
    return jnp.where(lane < HEAD, stacked[:rows], stacked[rows:])


def open_to(act, bounds, rows, j, chunks):
    half = chunks // 2
    base = jnp.where(j < half, act[0] + j * CK, act[1] + (j - half) * CK)
    spot = base + lax.broadcasted_iota(jnp.int32, (CK, BQ), 0)
    open_ = (spot >= bounds[0:1, rows]) & (spot <= bounds[1:2, rows])
    return jnp.concatenate([open_, open_], axis=1)


def attend_kernel(
    act, bounds, q, kv_own, kv_oth, o, lse,
    k_all, v_all, scores, queries, top, total, acc, sem_k, sem_v,
):
    pairs = q.shape[1] // (2 * HEAD)
    blocks = q.shape[0] // BQ
    chunks = k_all.shape[0] // CF
    half = chunks // 2
    waits = load_halves(kv_own.at[0], kv_oth.at[0], k_all, sem_k)
    waits += load_halves(kv_own.at[1], kv_oth.at[1], v_all, sem_v)
    for copy in waits:
        copy.wait()
    square = lax.broadcasted_iota(jnp.int32, (BQ, BQ), 0)
    along = lax.broadcasted_iota(jnp.int32, (BQ, BQ), 1)

    def one_block(b, _):
        rows = pl.ds(pl.multiple_of(b * BQ, BQ), BQ)
        for h in range(pairs):
            queries[h] = pair_rows(q[rows, h * 128 : h * 128 + 128], HEAD ** (-0.5))
        top[...] = jnp.full_like(top, NEGATIVE)
        total[...] = jnp.zeros_like(total)
        acc[...] = jnp.zeros_like(acc)
        least = jnp.broadcast_to(bounds[0:1, rows], (BQ, BQ)).T
        most = jnp.broadcast_to(bounds[1:2, rows], (BQ, BQ)).T

        def first(j, _):
            @pl.when(act[2 + b * chunks + j] > 0)
            def _():
                keys = pl.ds(pl.multiple_of(j * CF, CF), CF)
                base = jnp.where(j < half, act[0] + j * CF, act[1] + (j - half) * CF)
                open_ = []
                for part in range(CF // 128):
                    spot = base + part * 128 + along
                    one = (spot >= least) & (spot <= most)
                    open_.append(jnp.concatenate([one, one], axis=0))
                for h in range(pairs):
                    s = dot32(queries[h], k_all[keys, h * 128 : h * 128 + 128], NT)
                    best = top[h]
                    for part, one in enumerate(open_):
                        t = jnp.where(one, s[:, part * 128 : part * 128 + 128], NEGATIVE)
                        scores[h, j, :, part * 128 : part * 128 + 128] = t
                        best = jnp.maximum(best, t)
                    top[h] = best

            return 0

        lax.fori_loop(0, chunks, first, 0)
        for h in range(pairs):
            top[h] = jnp.broadcast_to(jnp.max(top[h], axis=1, keepdims=True), top.shape[1:])

        def second(j, _):
            @pl.when(act[2 + b * chunks + j] > 0)
            def _():
                keys = pl.ds(pl.multiple_of(j * CF, CF), CF)
                for h in range(pairs):
                    parts = []
                    more = total[h]
                    for part in range(CF // 128):
                        e = jnp.exp(scores[h, j, :, part * 128 : part * 128 + 128] - top[h])
                        more = more + e
                        parts.append(e.astype(jnp.bfloat16))
                    total[h] = more
                    e = parts[0] if len(parts) == 1 else jnp.concatenate(parts, axis=1)
                    acc[h] = acc[h] + dot32(e, v_all[keys, h * 128 : h * 128 + 128], NN)

            return 0

        lax.fori_loop(0, chunks, second, 0)
        for h in range(pairs):
            denom = jnp.broadcast_to(
                jnp.sum(total[h], axis=1, keepdims=True), total.shape[1:]
            )
            o[rows, h * 128 : h * 128 + 128] = pair_lanes(acc[h] / denom).astype(o.dtype)
            level = top[h] + jnp.log(denom)
            for part in range(2):
                own = jnp.where(square == along, level[part * BQ : part * BQ + BQ], 0.0)
                lse[b, h, :, part * BQ : part * BQ + BQ] = jnp.sum(own, axis=0, keepdims=True)
        return 0

    lax.fori_loop(0, blocks, one_block, 0)


def attend_back_kernel(
    act, bounds, q, kv_own, kv_oth, o, lse, grad,
    grad_q, grad_own, grad_oth,
    k_all, v_all, k_turned, queries, grads, delta, grad_queries, sem_k, sem_v,
):
    pairs = q.shape[1] // (2 * HEAD)
    blocks = q.shape[0] // BQ
    chunks = k_all.shape[0] // CK
    waits = load_halves(kv_own.at[0], kv_oth.at[0], k_all, sem_k)
    waits += load_halves(kv_own.at[1], kv_oth.at[1], v_all, sem_v)
    grad_own[...] = jnp.zeros_like(grad_own)
    grad_oth[...] = jnp.zeros_like(grad_oth)
    for copy in waits:
        copy.wait()

    def turn(j, _):
        for h in range(pairs):
            for part in range(CK // 128):
                keys = pl.ds(pl.multiple_of(j * CK + part * 128, 128), 128)
                k_turned[j, h, :, part * 128 : part * 128 + 128] = k_all[
                    keys, h * 128 : h * 128 + 128
                ].T
        return 0

    lax.fori_loop(0, chunks, turn, 0)

    def one_block(b, _):
        rows = pl.ds(pl.multiple_of(b * BQ, BQ), BQ)
        for h in range(pairs):
            lanes = slice(h * 128, h * 128 + 128)
            queries[h] = pair_rows(q[rows, lanes], HEAD ** (-0.5))
            grads[h] = pair_rows(grad[rows, lanes])
            both = (o[rows, lanes].astype(jnp.float32) * grad[rows, lanes].astype(jnp.float32)).T
            delta[h] = jnp.concatenate(
                [
                    jnp.sum(both[:HEAD], axis=0, keepdims=True),
                    jnp.sum(both[HEAD:], axis=0, keepdims=True),
                ],
                axis=1,
            )
        grad_queries[...] = jnp.zeros_like(grad_queries)

        def one_chunk(j, target, local):
            keys = pl.ds(pl.multiple_of(j * CK, CK), CK)
            own_keys = pl.ds(pl.multiple_of(local * CK, CK), CK)
            open_ = open_to(act, bounds, rows, j, chunks)
            for h in range(pairs):
                lanes = slice(h * 128, h * 128 + 128)
                s = jnp.where(open_, dot32(k_all[keys, lanes], queries[h], NT), NEGATIVE)
                p = jnp.exp(s - lse[b, h])
                ds = p * (dot32(v_all[keys, lanes], grads[h], NT) - delta[h])
                p = p.astype(jnp.bfloat16)
                ds = ds.astype(jnp.bfloat16)
                target[0, own_keys, lanes] += dot32(ds, queries[h], NN)
                target[1, own_keys, lanes] += dot32(p, grads[h], NN)
                grad_queries[h] += dot32(k_turned[j, h], ds, NN)

        def own_chunk(j, _):
            @pl.when(act[2 + b * chunks + j] > 0)
            def _():
                one_chunk(j, grad_own, j)

            return 0

        def oth_chunk(j, _):
            @pl.when(act[2 + b * chunks + j] > 0)
            def _():
                one_chunk(j, grad_oth, j - chunks // 2)

            return 0

        lax.fori_loop(0, chunks // 2, own_chunk, 0)
        lax.fori_loop(chunks // 2, chunks, oth_chunk, 0)
        for h in range(pairs):
            grad_q[rows, h * 128 : h * 128 + 128] = (
                pair_lanes(grad_queries[h].T) * HEAD ** (-0.5)
            ).astype(grad_q.dtype)
        return 0

    lax.fori_loop(0, blocks, one_block, 0)


def attend_masks(sentence, other, start, other_start):
    n = sentence.shape[0]
    seg = jnp.concatenate([sentence, other])
    spots = start + jnp.arange(n, dtype=jnp.int32)
    pos = jnp.concatenate([spots, other_start + jnp.arange(n, dtype=jnp.int32)])
    begin = jnp.sum((seg[None, :] < sentence[:, None]).astype(jnp.int32), axis=1)
    end = jnp.sum((seg[None, :] <= sentence[:, None]).astype(jnp.int32), axis=1) - 1
    made = {}
    for causal, last, size in ((c, l, k) for c, l in ((False, end), (True, spots)) for k in (CF, CK)):
        keys = pos.reshape(-1, size)
        live = (begin.reshape(-1, BQ).min(1)[:, None] <= keys.max(1)[None, :]) & (
            last.reshape(-1, BQ).max(1)[:, None] >= keys.min(1)[None, :]
        )
        starts = jnp.stack([start, other_start]).astype(jnp.int32)
        act = jnp.concatenate([starts, live.astype(jnp.int32).reshape(-1)])
        made[causal, size] = (act, jnp.pad(jnp.stack([begin, last]), ((0, 6), (0, 0))))
    return made


def attend(masks, causal, q, kv, kv_oth):
    n, width = q.shape
    pairs = width // (2 * HEAD)
    return pl.pallas_call(
        attend_kernel,
        out_shape=[
            jax.ShapeDtypeStruct((n, width), jnp.bfloat16),
            jax.ShapeDtypeStruct((n // BQ, pairs, 1, 2 * BQ), jnp.float32),
        ],
        in_specs=[SCALAR] + [ONCHIP] * 2 + [ANY] * 2,
        out_specs=[ONCHIP, ONCHIP],
        scratch_shapes=[
            pltpu.VMEM((2 * n, width), jnp.bfloat16),
            pltpu.VMEM((2 * n, width), jnp.bfloat16),
            pltpu.VMEM((pairs, 2 * n // CF, 2 * BQ, CF), jnp.float32),
            pltpu.VMEM((pairs, 2 * BQ, 128), jnp.bfloat16),
            pltpu.VMEM((pairs, 2 * BQ, 128), jnp.float32),
            pltpu.VMEM((pairs, 2 * BQ, 128), jnp.float32),
            pltpu.VMEM((pairs, 2 * BQ, 128), jnp.float32),
            pltpu.SemaphoreType.DMA((2,)),
            pltpu.SemaphoreType.DMA((2,)),
        ],
        cost_estimate=LIGHT,
        name="attend",
    )(*masks[causal, CF], q, kv, kv_oth)


def attend_back(masks, causal, q, kv, kv_oth, o, lse, grad):
    n, width = q.shape
    pairs = width // (2 * HEAD)
    chunks = 2 * n // CK
    return pl.pallas_call(
        attend_back_kernel,
        out_shape=[
            jax.ShapeDtypeStruct((n, width), jnp.bfloat16),
            jax.ShapeDtypeStruct((2, n, width), jnp.float32),
            jax.ShapeDtypeStruct((2, n, width), jnp.float32),
        ],
        in_specs=[SCALAR] + [ONCHIP] * 2 + [ANY] * 2 + [ONCHIP] * 3,
        out_specs=[ONCHIP] * 3,
        scratch_shapes=[
            pltpu.VMEM((2 * n, width), jnp.bfloat16),
            pltpu.VMEM((2 * n, width), jnp.bfloat16),
            pltpu.VMEM((chunks, pairs, 128, CK), jnp.bfloat16),
            pltpu.VMEM((pairs, 2 * BQ, 128), jnp.bfloat16),
            pltpu.VMEM((pairs, 2 * BQ, 128), jnp.bfloat16),
            pltpu.VMEM((pairs, 1, 2 * BQ), jnp.float32),
            pltpu.VMEM((pairs, 128, 2 * BQ), jnp.float32),
            pltpu.SemaphoreType.DMA((2,)),
            pltpu.SemaphoreType.DMA((2,)),
        ],
        cost_estimate=LIGHT,
        name="attend_back",
    )(*masks[causal, CK], q, kv, kv_oth, o, lse, grad)


def rms(v, gain):
    scale = lax.rsqrt(jnp.mean(v * v, axis=-1, keepdims=True) + NORM_EPS)
    return v * scale * gain


def rms_back(v, gain, grad):
    scale = lax.rsqrt(jnp.mean(v * v, axis=-1, keepdims=True) + NORM_EPS)
    scaled = grad * gain
    lean = jnp.mean(scaled * v, axis=-1, keepdims=True) * (scale * scale * scale)
    return scaled * scale - v * lean, jnp.sum(grad * v * scale, axis=0, keepdims=True)


def project_kernel(x, gain, w, normed, q, kv):
    a = low(rms(x[...], gain[...]))
    normed[...] = a
    q[...] = low(dot32(a, w[0], NN))
    kv[0] = low(dot32(a, w[1], NN))
    kv[1] = low(dot32(a, w[2], NN))


def between_kernel(o, w_out, x, gain, w, y, normed, q):
    state = x[...] + dot32(o[...], w_out[0], NN)
    y[...] = state
    c = low(rms(state, gain[...]))
    normed[...] = c
    q[...] = low(dot32(c, w[0], NN))


def feed_kernel(o, w_out, x, gain, w_up, w_down, y, normed, hidden, z):
    state = x[...] + dot32(o[...], w_out[0], NN)
    y[...] = state
    f = low(rms(state, gain[...]))
    normed[...] = f
    for i in range(w_up.shape[0]):
        r = low(jnp.maximum(dot32(f, w_up[i], NN), 0.0))
        hidden[i] = r
        state = state + dot32(r, w_down[i], NN)
    z[...] = state


def out_back(g, o, w_out, grad_o, grad_out):
    grad_o[...] = low(dot32(g, w_out[0], NT))
    grad_out[0] = low(dot32(o[...], g, TN))


def feed_back_kernel(
    grad, y, normed, hidden, gain, w_up, w_down, o, w_out,
    grad_up, grad_down, grad_y, grad_gain, grad_o, grad_out,
):
    g = low(grad[...])
    f = normed[...]
    back = jnp.zeros(grad.shape, jnp.float32)
    for i in range(w_up.shape[0]):
        r = hidden[i]
        grad_down[i] = low(dot32(r, g, TN))
        h = low(jnp.where(r > 0, dot32(g, w_down[i], NT), 0.0))
        grad_up[i] = low(dot32(f, h, TN))
        back = back + dot32(h, w_up[i], NT)
    more, grad_gain[...] = rms_back(y[...], gain[...], back)
    total = grad[...] + more
    grad_y[...] = total
    out_back(low(total), o, w_out, grad_o, grad_out)


def between_back_kernel(
    grad_q, normed, y, gain, w, grad, o, w_out,
    grad_w, grad_x, grad_gain, grad_o, grad_out,
):
    g = grad_q[...]
    grad_w[0] = low(dot32(normed[...], g, TN))
    more, grad_gain[...] = rms_back(y[...], gain[...], dot32(g, w[0], NT))
    total = grad[...] + more
    grad_x[...] = total
    out_back(low(total), o, w_out, grad_o, grad_out)


def memory_back_kernel(own, other, memory, w, grad_w, grad_memory):
    m = memory[...]
    total = None
    for i in range(2):
        g = low(own[i] + other[i])
        grad_w[i] = low(dot32(m, g, TN))
        part = dot32(g, w[i + 1], NT)
        total = part if total is None else total + part
    grad_memory[...] = total


def project_back_kernel(
    grad_q, own, other, normed, x, gain, w, grad,
    grad_w, grad_x, grad_gain,
):
    a = normed[...]
    back = None
    for i in range(3):
        g = grad_q[...] if i == 0 else low(own[i - 1] + other[i - 1])
        grad_w[i] = low(dot32(a, g, TN))
        part = dot32(g, w[i], NT)
        back = part if back is None else back + part
    more, grad_gain[...] = rms_back(x[...], gain[...], back)
    grad_x[...] = grad[...] + more


def on_chip(kernel, name, outs, *args):
    return pl.pallas_call(
        kernel,
        out_shape=[jax.ShapeDtypeStruct(shape, kind) for shape, kind in outs],
        in_specs=[ONCHIP] * len(args),
        out_specs=[ONCHIP] * len(outs),
        cost_estimate=LIGHT,
        name=name,
    )(*args)


def shaped(lead, like, kind):
    return (lead + like.shape, kind)


HALF, FULL = jnp.bfloat16, jnp.float32


def attend_forward(masks, causal, q, kv):
    other = flip(kv, "c")
    o, lse = attend(masks, causal, q, kv, other)
    return o, (q, kv, other, o, lse)


def attend_backward(saved, masks, causal, grad):
    grad_q, own, other = attend_back(masks, causal, *saved, grad)
    return grad_q, own, flip(other, "c")


def project(x, gain, w):
    return on_chip(
        project_kernel,
        "project",
        [shaped((), x, HALF), shaped((), x, HALF), shaped((2,), x, HALF)],
        x, gain[None], w,
    )


def between(o, w_out, x, gain, w):
    return on_chip(
        between_kernel,
        "between",
        [shaped((), x, FULL), shaped((), x, HALF), shaped((), x, HALF)],
        o, w_out, x, gain[None], w,
    )


def feed(o, w_out, x, gain, w_up, w_down):
    return on_chip(
        feed_kernel,
        "feed",
        [
            shaped((), x, FULL),
            shaped((), x, HALF),
            shaped((w_up.shape[0],), x, HALF),
            shaped((), x, FULL),
        ],
        o, w_out, x, gain[None], w_up, w_down,
    )


def feed_back(grad, kept, gain, w_up, w_down, o, w_out):
    y, normed, hidden = kept
    return on_chip(
        feed_back_kernel,
        "feed_back",
        [
            (w_up.shape, HALF),
            (w_down.shape, HALF),
            shaped((), y, FULL),
            ((1, y.shape[1]), FULL),
            shaped((), y, HALF),
            (w_out.shape, HALF),
        ],
        grad, y, normed, hidden, gain[None], w_up, w_down, o, w_out,
    )


def between_back(grad_q, normed, y, gain, w, grad, o, w_out):
    return on_chip(
        between_back_kernel,
        "between_back",
        [
            (w_out.shape, HALF),
            shaped((), y, FULL),
            ((1, y.shape[1]), FULL),
            shaped((), y, HALF),
            (w_out.shape, HALF),
        ],
        grad_q, normed, y, gain[None], w, grad, o, w_out,
    )


def memory_back(own, other, memory, w):
    return on_chip(
        memory_back_kernel,
        "memory_back",
        [((2,) + w.shape[1:], HALF), shaped((), memory, FULL)],
        own, other, memory, w,
    )


def project_back(grad_q, own, other, normed, x, gain, w, grad):
    return on_chip(
        project_back_kernel,
        "project_back",
        [(w.shape, HALF), shaped((), x, FULL), ((1, x.shape[1]), FULL)],
        grad_q, own, other, normed, x, gain[None], w, grad,
    )


def shards(
    tokens,
    source,
    segments,
    loss_rows,
    targets,
    exit_depth,
    qkv_weight,
    out_weight,
    up_weight,
    down_weight,
    norm_gains,
    embed_table,
    qkv_first,
    out_first,
    up_first,
    down_first,
    gains_first,
    table_first,
    qkv_second,
    out_second,
    up_second,
    down_second,
    gains_second,
    table_second,
):
    sy, sx = lax.axis_index("sy"), lax.axis_index("sx")
    z, c = lax.axis_index("z"), lax.axis_index("c")
    s = sy * 2 + sx
    me = jnp.stack([c, z, s]).astype(jnp.int32)
    owners = lax.axis_size("z") * 2
    tok_dev = tokens.shape[2]
    loss_dev = targets.shape[2]
    voc_dev, width = embed_table.shape
    gain_count, gain_dev = norm_gains.shape
    vocabulary = voc_dev * owners
    root_width = math.sqrt(width)
    half_row = 2 * tok_dev
    unit = qkv_weight.shape[1] // 4
    fast = lax.axis_size("z") == 4 and unit % 16 == 0

    shard_of = {
        "table": embed_table[None],
        "qkv": qkv_weight,
        "out": out_weight,
        "up": up_weight,
        "down": down_weight,
    }
    shard_shapes = {name: array.shape[1:] for name, array in shard_of.items()}
    weights = {}

    def layout(entries):
        kinds = [kind for _, _, kind in entries]
        return kinds, block_counts(entries, shard_shapes, unit)

    def packed(entries):
        return jnp.concatenate(
            [owned_blocks(low(shard_of[name][i]), kind, unit) for name, i, kind in entries]
        )

    def gather(entries):
        mover = Mover()
        mover.stages = gather_stages(mover, me, packed(entries), *layout(entries), unit, owners)
        return mover

    def settle(entries, outs):
        for (name, i, kind), out in zip(entries, outs):
            weights[name, i] = out.reshape(-1, COL, COL) if kind == "blk" else out

    def gather_plainly(entries):
        everything = lax.all_gather(packed(entries), LINE)
        outs = []
        first = 0
        for kind, count in zip(*layout(entries)):
            piece = everything[:, first : first + count]
            first += count
            if kind == "row":
                outs.append(piece.transpose(1, 0, 2, 3).reshape(count, -1, COL))
            else:
                outs.append(piece.reshape(owners, count, 4, unit, COL).transpose(0, 2, 1, 3, 4))
        settle(entries, outs)

    def pieces(entries):
        arrays, kinds, counts = [], [], []
        for (name, i, kind), count in zip(entries, layout(entries)[1]):
            held = grads[name, i]
            for array in held if isinstance(held, tuple) else (held,):
                blocks = array.shape[0] if isinstance(held, tuple) else count
                arrays.append(array.reshape(natural_shape(kind, blocks, unit, owners)))
                kinds.append(kind)
                counts.append(blocks)
        return arrays, kinds, counts

    def reduce(entries, stages=reduce_stages):
        arrays, kinds, counts = pieces(entries)
        mover = Mover()
        mover.stages = stages(mover, me, arrays, kinds, counts, unit)
        return mover

    def take(entries, parts):
        first = 0
        for (name, i, kind), count in zip(entries, layout(entries)[1]):
            reduced[name, i] = owned_natural(parts[:, first : first + count], kind)
            first += count

    def reduce_plainly(entries):
        parts = []
        for array, kind, count in zip(*pieces(entries)):
            if kind == "row":
                array = array.reshape(count, owners, 4, unit, COL).transpose(1, 2, 0, 3, 4)
            parts.append(wide(array))
        total = jnp.concatenate(parts, axis=2)
        total = lax.psum_scatter(total, LINE, scatter_dimension=0, tiled=True)
        total = lax.psum(total, PLANE)[0]
        take(entries, total)
        return jnp.sum(total * total) / 4.0

    if fast:
        first = gather(GATHERED[0])
        ints = [tokens, source, segments, loss_rows, targets, exit_depth]
        ints, shard_of = step((ints, shard_of), first)
        tokens, source, segments, loss_rows, targets, exit_depth = ints
        second = gather(GATHERED[1])

        def gather_long(entries):
            return jnp.concatenate(
                [quarter_blocks(shard_of[name][i], kind, unit, s) for name, i, kind in entries]
            )

        third, fourth = gather_long(GATHERED[2]), gather_long(GATHERED[3])
    if not fast:
        for entries in GATHERED:
            gather_plainly(entries)

    numbers = jnp.concatenate(
        [array[:, 0] for array in (tokens, source, segments, loss_rows, targets, exit_depth)],
        axis=1,
    )
    plane = gathered(gathered(numbers, "c"), PLANE)
    depths_seen = plane[..., 3 * tok_dev + 2 * loss_dev :]
    reached = jnp.stack(
        [
            jnp.sum((depths_seen >= layer_id).astype(jnp.float32), axis=(0, 1, 3))
            for layer_id in range(LAYERS)
        ],
        axis=1,
    )
    if fast:
        reached, norm_gains_now, third = step((reached, norm_gains, third), first)
        third = lax.all_gather(third, PLANE + LINE).reshape(4, owners, *third.shape)
        reached, norm_gains_now = step((reached, norm_gains_now), second)
    else:
        norm_gains_now = norm_gains
    small = jnp.concatenate([norm_gains_now.reshape(-1), reached.reshape(-1)])
    small = gathered(gathered(small, "c"), "z").reshape(owners, -1)
    reach = jnp.maximum(
        jnp.sum(small[::2, gain_count * gain_dev :], axis=0).reshape(MICRO, LAYERS), 1.0
    )
    reach = lax.dynamic_index_in_dim(reach, sy, 0, False)
    gains_seen = small[:, : gain_count * gain_dev].reshape(owners, gain_count, gain_dev)
    order = jnp.arange(owners)
    rel = ((order // 2) ^ z) * 2 + ((order % 2) ^ c)
    gains_full = gains_seen[rel].transpose(1, 0, 2).reshape(gain_count, width)
    gains_full = wide(low(gains_full))

    row = lax.dynamic_index_in_dim(plane, sx ^ c, 1, False)
    row = in_order(lax.dynamic_index_in_dim(row, sy, 1, False), s)
    mine = lax.dynamic_slice_in_dim(row, 2 * c, 2, 0)
    theirs = lax.dynamic_slice_in_dim(row, 2 * (1 - c), 2, 0)
    target_ids = mine[:, :tok_dev].reshape(-1)
    source_ids = mine[:, tok_dev : 2 * tok_dev].reshape(-1)
    sentence = mine[:, 2 * tok_dev : 3 * tok_dev].reshape(-1)
    other_sentence = theirs[:, 2 * tok_dev : 3 * tok_dev].reshape(-1)
    rest = 3 * tok_dev
    places = (
        mine[:, rest : rest + loss_dev] + (jnp.arange(2, dtype=jnp.int32) * tok_dev)[:, None]
    ).reshape(-1)
    wanted = mine[:, rest + loss_dev : rest + 2 * loss_dev].reshape(-1)
    depth = mine[:, rest + 2 * loss_dev :].reshape(-1)
    masks = attend_masks(sentence, other_sentence, c * half_row, (1 - c) * half_row)

    ids = jnp.concatenate([source_ids, target_ids])
    if fast:
        ids = step(ids, first)
        ids = step(ids, second, first)
        settle(GATHERED[0], first.result)
    table = weights["table", 0].reshape(vocabulary, width)
    looked_up = table[ids].astype(jnp.float32) * root_width
    xe = looked_up[:half_row]
    x = looked_up[half_row:]
    kept_enc = (xe, *project(xe, gains_full[0], weights["qkv", 0]))
    if fast:
        xe, kept_enc, x = step((xe, kept_enc, x), second)
    o, saved_enc = attend_forward(masks, False, *kept_enc[2:])
    if fast:
        o, fourth = step((o, fourth), second)
        fourth = lax.all_gather(fourth, PLANE + LINE).reshape(4, owners, *fourth.shape)
        settle(GATHERED[1], second.result)
    *kept_enc_feed, xe = feed(
        o, weights["out", 0], xe, gains_full[1], weights["up", 0], weights["down", 0]
    )
    final_gain = gains_full[2 * ENC]
    memory = low(normalize(xe, final_gain))
    kept = []
    states = []
    for layer_id in range(LAYERS):
        base = 2 * ENC + 1 + 4 * layer_id
        slot = ENC + 2 * layer_id
        if fast and layer_id == 0:
            (x, memory), third = hold((x, memory), third)
            settle(GATHERED[2], unpack(third, *layout(GATHERED[2]), unit, owners))
        if fast and layer_id == 1:
            x, fourth = hold(x, fourth)
            settle(GATHERED[3], unpack(fourth, *layout(GATHERED[3]), unit, owners))
        cross = weights["qkv", slot + 1]
        pair = jnp.stack([low(product(memory, cross[1])), low(product(memory, cross[2]))])
        kept_self = (x, *project(x, gains_full[base], weights["qkv", slot]))
        o, saved_self = attend_forward(masks, True, *kept_self[2:])
        *kept_cross, q = between(o, weights["out", slot], x, gains_full[base + 1], cross)
        o, saved_cross = attend_forward(masks, False, q, pair)
        feed_at = ENC + layer_id
        *kept_feed, x = feed(
            o,
            weights["out", slot + 1],
            kept_cross[0],
            gains_full[base + 2],
            weights["up", feed_at],
            weights["down", feed_at],
        )
        kept.append((kept_self, saved_self, kept_cross, saved_cross, kept_feed))
        states.append(x)

    pick = (places[:, None] == jnp.arange(half_row)[None, :]).astype(jnp.bfloat16)
    exit_gains = [gains_full[2 * ENC + 4 + 4 * layer_id] for layer_id in range(LAYERS)]
    exits = jnp.concatenate(
        [low(product(pick, low(normalize(states[i], exit_gains[i])))) for i in range(LAYERS)]
    )
    logits = against_rows(exits, table) * LOGIT_SCALE
    wanted_all = jnp.concatenate([wanted] * LAYERS)
    hit = jnp.arange(vocabulary)[None, :] == wanted_all[:, None]
    picked = jnp.sum(jnp.where(hit, logits, 0.0), axis=-1)
    top = jnp.max(logits, axis=-1)
    lse = top + jnp.log(jnp.sum(jnp.exp(logits - top[:, None]), axis=-1))
    shares = jnp.concatenate(
        [(depth >= i).astype(jnp.float32) / reach[i] / MICRO for i in range(LAYERS)]
    )
    loss_part = jnp.sum((lse - picked) * shares)
    grad_logits = low(
        (jnp.exp(logits - lse[:, None]) - hit.astype(jnp.float32))
        * shares[:, None]
        * LOGIT_SCALE
    )
    grad_exits = product(grad_logits, table)
    table_grad = outer_sum(grad_logits, exits)

    grads = {}
    gain_parts = [None] * gain_count
    grad_x = None
    grad_memory = None
    for layer_id in reversed(range(LAYERS)):
        slot = ENC + 2 * layer_id
        base = 2 * ENC + 1 + 4 * layer_id
        count = places.shape[0]
        grad_rows = lax.dot_general(
            wide(pick),
            grad_exits[layer_id * count : (layer_id + 1) * count],
            (((0,), (0,)), ((), ())),
            precision=lax.Precision.HIGHEST,
            preferred_element_type=jnp.float32,
        )
        grad_here, gain_parts[base + 3] = norm_back(
            states[layer_id], exit_gains[layer_id], grad_rows
        )
        grad_x = grad_here if grad_x is None else grad_x + grad_here
        kept_self, saved_self, kept_cross, saved_cross, kept_feed = kept[layer_id]
        up, down = ("up", ENC + layer_id), ("down", ENC + layer_id)
        qkv, out = ("qkv", slot + 1), ("out", slot + 1)
        grads[up], grads[down], grad_x, gain_parts[base + 2], grad_o, grads[out] = feed_back(
            grad_x,
            kept_feed,
            gains_full[base + 2],
            weights[up],
            weights[down],
            saved_cross[3],
            weights[out],
        )
        if fast and layer_id == 1:
            feed_mover = reduce(REDUCED[0], long_reduce_stages)
            grad_x, grad_o = step((grad_x, grad_o), feed_mover, feed_mover)
        if fast and layer_id == 0:
            late = reduce(REDUCED[1], long_reduce_stages)
            grad_x, grad_o = step((grad_x, grad_o), feed_mover, late, late)
        grad_q, own, other = attend_backward(saved_cross, masks, False, grad_o)
        grad_pair, more = memory_back(own, other, memory, weights[qkv])
        grad_memory = more if grad_memory is None else grad_memory + more
        out = ("out", slot)
        grad_query, grad_x, gain_parts[base + 1], grad_o, grads[out] = between_back(
            grad_q,
            kept_cross[1],
            kept_cross[0],
            gains_full[base + 1],
            weights[qkv],
            grad_x,
            saved_self[3],
            weights[out],
        )
        grads[qkv] = (grad_query, grad_pair)
        grad_q, own, other = attend_backward(saved_self, masks, True, grad_o)
        qkv = ("qkv", slot)
        grads[qkv], grad_x, gain_parts[base] = project_back(
            grad_q,
            own,
            other,
            kept_self[1],
            kept_self[0],
            gains_full[base],
            weights[qkv],
            grad_x,
        )
    if fast:
        middle = reduce(REDUCED[2], long_reduce_stages)
        grad_x, grad_memory = step((grad_x, grad_memory), middle, middle)
    grad_enc, gain_parts[2 * ENC] = norm_back(xe, final_gain, grad_memory)
    up, down, qkv, out = ("up", 0), ("down", 0), ("qkv", 0), ("out", 0)
    grads[up], grads[down], grad_enc, gain_parts[1], grad_o, grads[out] = feed_back(
        grad_enc,
        kept_enc_feed,
        gains_full[1],
        weights[up],
        weights[down],
        saved_enc[3],
        weights[out],
    )
    if fast:
        early = reduce(REDUCED[3])
        grad_enc, grad_o = step((grad_enc, grad_o), feed_mover, early)
    grad_q, own, other = attend_backward(saved_enc, masks, False, grad_o)
    if fast:
        grad_q, own, grad_enc = step((grad_q, own, grad_enc), late, early)
    grads[qkv], grad_enc, gain_parts[0] = project_back(
        grad_q, own, other, kept_enc[1], kept_enc[0], gains_full[0], weights[qkv], grad_enc
    )
    token_ids = jnp.concatenate([source_ids, target_ids])
    token_grads = low(jnp.concatenate([grad_enc, grad_x]) * root_width)
    looked = (token_ids[:, None] == jnp.arange(vocabulary)[None, :]).astype(jnp.bfloat16)
    table_grad = low(table_grad + outer_sum(looked, token_grads))
    grads["table", 0] = table_grad

    reduced = {}
    gain_grad = jnp.concatenate([part.reshape(1, -1) for part in gain_parts])
    small = jnp.concatenate([gain_grad, jnp.full((1, width), loss_part)])
    if fast:
        last = reduce(REDUCED[4])
        small = step(small, last, early)
        small = step(small, last, early)
        small = all_sum(small)
        small = step(small, last, early, late, middle)
        small = step(small, last, early)
        movers = (feed_mover, late, middle, early, last)
        squares = sum(mover.squares for mover in movers[:4])
        squares = step(squares, last)
        squares = all_sum(squares + last.squares)
        squares = step(squares, middle, last)
    else:
        small = all_sum(small)
        squares = all_sum(sum(reduce_plainly(entries) for entries in REDUCED))
    loss_total = small[-1, 0]
    gain_grad = small[:-1]
    squares = squares + jnp.sum(gain_grad * gain_grad)
    grad_norm = jnp.sqrt(squares)
    clip_factor = CLIP_NORM / jnp.maximum(grad_norm, CLIP_NORM)

    names = ("qkv", "out", "up", "down", "table")
    if fast:
        plan = []
        for bucket, entries in enumerate(REDUCED):
            first = 0
            for (name, i, kind), count in zip(entries, layout(entries)[1]):
                plan.append((bucket, first, count, kind, names.index(name), i))
                first += count
        parts = [part for mover in movers for part in mover.result]
        shapes = [shard_of[name].shape for name in names]
        placed = pl.pallas_call(
            functools.partial(settle_kernel, len(parts), tuple(plan), unit),
            out_shape=[jax.ShapeDtypeStruct(shape, jnp.bfloat16) for shape in shapes],
            in_specs=[SCALAR] + [ANY] * len(parts),
            out_specs=[ONCHIP] * len(shapes),
            scratch_shapes=[pltpu.SemaphoreType.DMA((len(shapes),))],
            cost_estimate=LIGHT,
            name="place_gradients",
        )(me, *parts)
        ready = [wide(array) for array in placed]
    else:
        ready = [
            wide(jnp.stack([reduced[name, i] for i in range(shard_of[name].shape[0])]))
            for name in names
        ]
    gradients = (
        *ready[:4],
        lax.dynamic_slice_in_dim(gain_grad, (2 * z + c) * gain_dev, gain_dev, 1),
        ready[4][0],
    )
    masters = (qkv_weight, out_weight, up_weight, down_weight, norm_gains, embed_table)
    firsts = (qkv_first, out_first, up_first, down_first, gains_first, table_first)
    seconds = (qkv_second, out_second, up_second, down_second, gains_second, table_second)
    results = [
        adam_update(masters[i], firsts[i], seconds[i], gradients[i] * clip_factor) for i in range(6)
    ]
    gains_grad = gradients[4] * clip_factor
    return (
        loss_total,
        grad_norm,
        results[0][0],
        results[1][0],
        results[2][0],
        results[3][0],
        gains_grad,
        results[5][0],
        results[0][1],
        results[1][1],
        results[2][1],
        results[3][1],
        results[4][1],
        results[5][1],
        results[0][2],
        results[1][2],
        results[2][2],
        results[3][2],
        results[4][2],
        results[5][2],
    )


def solution(mesh):
    seq, vocab = mesh.devices.shape
    fine = Mesh(mesh.devices.reshape(2, seq // 2, vocab // 2, 2), ("sy", "sx", "z", "c"))
    ints = P(None, LINE, PLANE)
    block = P(None, LINE, None)
    gains = P(None, LINE)
    rows = P(LINE, None)
    arrays = (block, block, block, block, gains, rows)
    return jax.shard_map(
        shards,
        mesh=fine,
        in_specs=(ints,) * 6 + arrays * 3,
        out_specs=(P(), P(), block, block, block, block, gains, rows) + arrays * 2,
        check_vma=False,
    )
```

time: 954 us -> 747 us (0.78)
  matrix products: 134 us -> 23.2 us
  local copies, waits for them, and re-layouts: 135 us -> 56.1 us
  Pallas kernels: 228 us -> 302 us
  starting transfers between devices: 149 us -> 102 us
  waiting for transfers between devices: 162 us -> 138 us
  other arithmetic: 111 us -> 88.5 us
    pallas_call x18 -> x38, Pallas kernels: 228 us -> 302 us  [the longest x18 113 us: on_chip(): pl.pallas_call(kernel, out_shape=[jax.ShapeDtypeStruct(shape, kind) for s...]
    ppermute x122 -> x84, starting transfers between devices: 149 us -> 102 us  [flip(): return lax.ppermute(x, axis, [(i, i ^ bit) for i in range(n)])]
    ppermute x122 -> x84, waiting for transfers between devices: 162 us -> 117 us  [flip(): return lax.ppermute(x, axis, [(i, i ^ bit) for i in range(n)])]
    dot_general x46 -> x2, matrix products: 54.7 us -> 10 us  [outer_sum(): lax.dot_general(a, b, (((0,), (0,)), ((), ())), preferred_element_type=jn...]
    dot_general x47 -> x7, matrix products: 42.2 us -> 5.28 us  [product(): return jnp.dot(a, b, preferred_element_type=jnp.float32)]
    add x35 -> x8, other arithmetic: 43.4 us -> 9.17 us  [the longest x4 3.8 us: added(): total = total + wide(array)]
    unnamed x703 -> x259, local copies, waits for them, and re-layouts: 42.4 us -> 9.89 us
    dot_general x45 -> x1, matrix products: 34.7 us -> 3.9 us  [against_rows(): lax.dot_general(a, b, (((1,), (1,)), ((), ())), preferred_element_type=jn...]
  transfers between devices with their start and end apart: 122 -> 89, of which waited for: 38 -> 30; matrix products, arithmetic and copies ran while one was open for 29% -> 14% of each run, Pallas kernels for 13% -> 33%
where the time goes in v3:
time: 747 us; the launch traced here: 736 us
  Pallas kernels  302 us (40%)
  waiting for transfers between devices  138 us (18%)
  starting transfers between devices  102 us (14%)
  other arithmetic  88.5 us (12%)
  local copies, waits for them, and re-layouts  56.1 us (8%)
  between operations  26.3 us (4%)
  matrix products  23.2 us (3%)
    ppermute x84, waiting for transfers between devices, flip(): return lax.ppermute(x, axis, [(i, i ^ bit) for i in range(n)])  117 us
    pallas_call x18, Pallas kernels, on_chip(): pl.pallas_call(kernel, out_shape=[jax.ShapeDtypeStruct(shape, kind) for s...  113 us
    ppermute x84, starting transfers between devices, flip(): return lax.ppermute(x, axis, [(i, i ^ bit) for i in range(n)])  102 us
    pallas_call x5, Pallas kernels, attend_back(): pl.pallas_call(attend_back_kernel, out_shape=[jax.ShapeDtypeStruct((n, wi...  75.9 us
    pallas_call x5, Pallas kernels, attend(): pl.pallas_call(attend_kernel, out_shape=[jax.ShapeDtypeStruct((n, width),...  53.9 us
    pallas_call x5, Pallas kernels, collect(): pl.pallas_call(functools.partial(collect_kernel, plan, unit, ordered), ou...  28.8 us
    convert_element_type x11, other arithmetic, low(): return v.astype(jnp.bfloat16)  27.6 us
    sub x5, other arithmetic, adam_update(): master - LEARN_RATE * (fixed_first / (jnp.sqrt(fixed_second) + ADAM_EPS)...  16.2 us
  transfers between devices with their start and end apart: 89, of which 30 were waited for; matrix products, arithmetic and copies ran while one was open for 14% of the time, Pallas kernels for 33%

profile of v3, /device:TPU:0, one launch (start us, length us, event | category | flops | bytes accessed | tf_op | source)
XLA Modules:
  0.0 736.3 jit_solution(894126021191874055)
XLA Ops:
  47.4 10.4 %collective-permute-done.7.refs_2_ = bf16[3,12,16,512]{3,2,1,0:T(8,128)(2,1)S(1)} collective-permute-done((bf16[3,12,16,512]{3,2,1,0:T(8,128)(2,1)S(1)}, bf16[3,12,16,512]{3,2,1,0:T(8,128)(2,1)S(1)}, u32[]{:S(2)}, u32[]{:S(2)}) %collective-permute-start.7) | collective-permute-done | bytes 589856 | tf_op jit(solution)/shard_map/ppermute | solution.py:64
  58.0 10.7 %collective-permute-done.8.refs_3_ = bf16[3,12,16,512]{3,2,1,0:T(8,128)(2,1)} collective-permute-done((bf16[3,12,16,512]{3,2,1,0:T(8,128)(2,1)S(1)}, bf16[3,12,16,512]{3,2,1,0:T(8,128)(2,1)}, u32[]{:S(2)}, u32[]{:S(2)}) %collective-permute-start.8) | collective-permute-done | bytes 589856 | tf_op jit(solution)/shard_map/ppermute | solution.py:64
  88.5 7.3 place_weights.2
  95.9 6.7 gather_fusion
  108.3 8.3 %collective-permute-done.24.refs_4_ = bf16[3,8,16,512]{3,2,1,0:T(8,128)(2,1)} collective-permute-done((bf16[3,8,16,512]{3,2,1,0:T(8,128)(2,1)S(1)}, bf16[3,8,16,512]{3,2,1,0:T(8,128)(2,1)}, u32[]{:S(2)}, u32[]{:S(2)}) %collective-permute-start.24) | collective-permute-done | bytes 393248 | tf_op jit(solution)/shard_map/ppermute | solution.py:64
  122.0 11.2 %attend.5 = (bf16[512,512]{1,0:T(8,128)(2,1)}, f32[4,4,1,256]{3,2,1,0:T(1,128)}) custom-call(s32[18]{0:T(128)} %pad_add_fusion.7.act, s32[8,512]{1,0:T(8,128)} %pad.7.bounds, bf16[512,512]{1,0:T(8,128)(2,1)} %get-tuple-element.587.q, bf16[2,512,512]{2,1,0:T(8,128)(2,1)} %get-tuple-element.588.kv_own, bf16[2,512,512]{2,1,0:T(8,128)(2,1)} %copy-done.18), custom_call_target="tpu_custom_call" | custom-call | flops 1 | bytes 1 | tf_op jit(solution)/shard_map/attend/pallas_call | solution.py:658
  140.7 7.2 feed.3
  150.7 7.1 place_gathered.2
  168.9 10.0 %attend.6 = (bf16[512,512]{1,0:T(8,128)(2,1)}, f32[4,4,1,256]{3,2,1,0:T(1,128)}) custom-call(s32[18]{0:T(128)} %pad_add_fusion.10.act, s32[8,512]{1,0:T(8,128)} %pad.8.bounds, bf16[512,512]{1,0:T(8,128)(2,1)} %get-tuple-element.624.q, bf16[2,512,512]{2,1,0:T(8,128)(2,1)} %get-tuple-element.625.kv_own, bf16[2,512,512]{2,1,0:T(8,128)(2,1)} %copy-done.19), custom_call_target="tpu_custom_call" | custom-call | flops 1 | bytes 1 | tf_op jit(solution)/shard_map/attend/pallas_call | solution.py:658
  182.8 11.3 %attend.7 = (bf16[512,512]{1,0:T(8,128)(2,1)}, f32[4,4,1,256]{3,2,1,0:T(1,128)}) custom-call(s32[18]{0:T(128)} %pad_add_fusion.7.act, s32[8,512]{1,0:T(8,128)} %pad.7.bounds, bf16[512,512]{1,0:T(8,128)(2,1)} %get-tuple-element.630.q, bf16[2,512,512]{2,1,0:T(8,128)(2,1)} %copy-done.11, bf16[2,512,512]{2,1,0:T(8,128)(2,1)} %collective-permute-done.32.kv_oth), custom_call_target="tpu_custom_call" | custom-call | flops 1 | bytes 1 | tf_op jit(solution)/shard_map/attend/pallas_call | solution.py:658
  194.1 7.0 feed.4
  201.2 10.6 %all-gather.7.cloned.1.call-done = bf16[512,16,512]{2,1,0:T(8,128)(2,1)} async-done(((bf16[16,16,512]{2,1,0:T(8,128)(2,1)}), bf16[512,16,512]{2,1,0:T(8,128)(2,1)}) %all-gather.7.cloned.1.call-update) | async-done | bytes 8388624 | tf_op jit(solution)/shard_map/all_gather | solution.py:1120
  211.7 6.8 place_gathered.3
  229.5 10.0 %attend.8 = (bf16[512,512]{1,0:T(8,128)(2,1)}, f32[4,4,1,256]{3,2,1,0:T(1,128)}) custom-call(s32[18]{0:T(128)} %pad_add_fusion.10.act, s32[8,512]{1,0:T(8,128)} %pad.8.bounds, bf16[512,512]{1,0:T(8,128)(2,1)} %get-tuple-element.643.q, bf16[2,512,512]{2,1,0:T(8,128)(2,1)} %get-tuple-element.644.kv_own, bf16[2,512,512]{2,1,0:T(8,128)(2,1)} %copy-done.20), custom_call_target="tpu_custom_call" | custom-call | flops 1 | bytes 1 | tf_op jit(solution)/shard_map/attend/pallas_call | solution.py:658
  243.4 11.5 %attend.9 = (bf16[512,512]{1,0:T(8,128)(2,1)}, f32[4,4,1,256]{3,2,1,0:T(1,128)}) custom-call(s32[18]{0:T(128)} %pad_add_fusion.7.act, s32[8,512]{1,0:T(8,128)} %pad.7.bounds, bf16[512,512]{1,0:T(8,128)(2,1)} %get-tuple-element.649.q, bf16[2,512,512]{2,1,0:T(8,128)(2,1)} %copy-done.12, bf16[2,512,512]{2,1,0:T(8,128)(2,1)} %collective-permute-done.34.kv_oth), custom_call_target="tpu_custom_call" | custom-call | flops 1 | bytes 1 | tf_op jit(solution)/shard_map/attend/pallas_call | solution.py:658
  254.8 7.0 feed.5
  274.6 10.5 %feed_back.3 = (bf16[4,512,512]{2,1,0:T(8,128)(2,1)}, bf16[4,512,512]{2,1,0:T(8,128)(2,1)}, f32[512,512]{1,0:T(8,128)}, f32[1,512]{1,0:T(1,128)}, bf16[512,512]{...) custom-call(f32[512,512]{1,0:T(8,128)} %add_add_fusion.2.grad, f32[512,512]{1,0:T(8,128)} %get-tuple-element.657.y, ...), custom_call_target="tpu_custom_call" | custom-call | flops 1 | bytes 1 | tf_op jit(solution)/shard_map/feed_back/pallas_call | solution.py:814
  298.3 16.0 %attend_back.5 = (bf16[512,512]{1,0:T(8,128)(2,1)}, f32[2,512,512]{2,1,0:T(8,128)}, f32[2,512,512]{2,1,0:T(8,128)}) custom-call(s32[18]{0:T(128)} %pad_add_fusion.7.act, s32[8,512]{1,0:T(8,128)} %pad.7.bounds, bf16[512,512]{1,0:T(8,128)(2,1)} %get-tuple-element.649.q, bf16[2,512,512]{2,1,0:T(8,128)(2,1)} %copy-done.12, ...), custom_call_target="tpu_custom_call" | custom-call | flops 1 | bytes 1 | tf_op jit(solution)/shard_map/attend_back/pallas_call | solution.py:686
  319.5 13.8 %attend_back.6 = (bf16[512,512]{1,0:T(8,128)(2,1)}, f32[2,512,512]{2,1,0:T(8,128)}, f32[2,512,512]{2,1,0:T(8,128)}) custom-call(s32[18]{0:T(128)} %pad_add_fusion.10.act, s32[8,512]{1,0:T(8,128)} %pad.8.bounds, bf16[512,512]{1,0:T(8,128)(2,1)} %get-tuple-element.643.q, bf16[2,512,512]{2,1,0:T(8,128)(2,1)} %get-tuple-element.644.kv_own, ...), custom_call_target="tpu_custom_call" | custom-call | flops 1 | bytes 1 | tf_op jit(solution)/shard_map/attend_back/pallas_call | solution.py:686
  341.3 6.7 project_back.3
  350.9 10.5 %feed_back.4 = (bf16[4,512,512]{2,1,0:T(8,128)(2,1)}, bf16[4,512,512]{2,1,0:T(8,128)(2,1)}, f32[512,512]{1,0:T(8,128)}, f32[1,512]{1,0:T(1,128)}, bf16[512,512]{...) custom-call(f32[512,512]{1,0:T(8,128)} %fusion.10.grad, f32[512,512]{1,0:T(8,128)} %get-tuple-element.687.y, ...), custom_call_target="tpu_custom_call" | custom-call | flops 1 | bytes 1 | tf_op jit(solution)/shard_map/feed_back/pallas_call | solution.py:814
  366.6 7.7 %collect_gradients.6 = (bf16[4,4,16,16,512]{4,3,2,1,0:T(8,128)(2,1)}, bf16[4,4,16,16,512]{4,3,2,1,0:T(8,128)(2,1)}) custom-call(s32[3]{0:T(128)} %pad_add_fusion.9.me_ref, bf16[3,512,512]{2,1,0:T(8,128)(2,1)} %get-tuple-element.700.refs_0_, bf16[1,512,512]{2,1,0:T(8,128)(2,1)} %get-tuple-element.701.refs_1_, ...), custom_call_target="tpu_custom_call" | custom-call | flops 1 | bytes 1 | tf_op jit(solution)/shard_map/collect_gradients/pallas_call | solution.py:328
  374.2 10.7 %reduce-scatter.4.cloned.1.call-done = bf16[1,8,16,512]{3,2,1,0:T(8,128)(2,1)} async-done(((bf16[16,8,16,512]{3,2,1,0:T(8,128)(2,1)}), bf16[1,8,16,512]{3,2,1,0:T(8,128)(2,1)}) %reduce-scatter.4.cloned.1.call-update) | async-done | bytes 131088 | tf_op jit(solution)/shard_map/reduce_scatter | solution.py:108
  385.0 7.4 %collective-permute-done.38 = bf16[4,4,16,16,512]{4,3,2,1,0:T(8,128)(2,1)S(1)} collective-permute-done((bf16[4,4,16,16,512]{4,3,2,1,0:T(8,128)(2,1)}, bf16[4,4,16,16,512]{4,3,2,1,0:T(8,128)(2,1)S(1)}, u32[]{:S(2)}, u32[]{:S(2)}) %collective-permute-start.38) | collective-permute-done | bytes 4194336 | tf_op jit(solution)/shard_map/ppermute | solution.py:64
  398.8 16.3 %attend_back.7 = (bf16[512,512]{1,0:T(8,128)(2,1)}, f32[2,512,512]{2,1,0:T(8,128)}, f32[2,512,512]{2,1,0:T(8,128)}) custom-call(s32[18]{0:T(128)} %pad_add_fusion.7.act, s32[8,512]{1,0:T(8,128)} %pad.7.bounds, bf16[512,512]{1,0:T(8,128)(2,1)} %get-tuple-element.630.q, bf16[2,512,512]{2,1,0:T(8,128)(2,1)} %copy-done.11, ...), custom_call_target="tpu_custom_call" | custom-call | flops 1 | bytes 1 | tf_op jit(solution)/shard_map/attend_back/pallas_call | solution.py:686
  420.4 13.8 %attend_back.8 = (bf16[512,512]{1,0:T(8,128)(2,1)}, f32[2,512,512]{2,1,0:T(8,128)}, f32[2,512,512]{2,1,0:T(8,128)}) custom-call(s32[18]{0:T(128)} %pad_add_fusion.10.act, s32[8,512]{1,0:T(8,128)} %pad.8.bounds, bf16[512,512]{1,0:T(8,128)(2,1)} %get-tuple-element.624.q, bf16[2,512,512]{2,1,0:T(8,128)(2,1)} %get-tuple-element.625.kv_own, ...), custom_call_target="tpu_custom_call" | custom-call | flops 1 | bytes 1 | tf_op jit(solution)/shard_map/attend_back/pallas_call | solution.py:686
  454.2 13.1 %collective-permute-start.43 = (bf16[8,16,512]{2,1,0:T(8,128)(2,1)S(1)}, bf16[8,16,512]{2,1,0:T(8,128)(2,1)}, u32[]{:S(2)}, u32[]{:S(2)}) collective-permute-start(bf16[8,16,512]{2,1,0:T(8,128)(2,1)S(1)} %bitcast.369), channel_id=1, source_target_pairs={{0,16},{8,24},{16,0},{24,8},{1,17},{9,25},{17,1},{25,9},{2,18},{10... | collective-permute-start | bytes 393224 | tf_op jit(solution)/shard_map/ppermute | solution.py:64
  474.1 10.5 %feed_back.5 = (bf16[4,512,512]{2,1,0:T(8,128)(2,1)}, bf16[4,512,512]{2,1,0:T(8,128)(2,1)}, f32[512,512]{1,0:T(8,128)}, f32[1,512]{1,0:T(1,128)}, bf16[512,512]{...) custom-call(f32[512,512]{1,0:T(8,128)} %add_add_fusion.grad, f32[512,512]{1,0:T(8,128)} %get-tuple-element.752.y, ...), custom_call_target="tpu_custom_call" | custom-call | flops 1 | bytes 1 | tf_op jit(solution)/shard_map/feed_back/pallas_call | solution.py:814
  489.7 15.9 %attend_back.9 = (bf16[512,512]{1,0:T(8,128)(2,1)}, f32[2,512,512]{2,1,0:T(8,128)}, f32[2,512,512]{2,1,0:T(8,128)}) custom-call(s32[18]{0:T(128)} %pad_add_fusion.7.act, s32[8,512]{1,0:T(8,128)} %pad.7.bounds, bf16[512,512]{1,0:T(8,128)(2,1)} %get-tuple-element.587.q, bf16[2,512,512]{2,1,0:T(8,128)(2,1)} %get-tuple-element.588.kv_own, ...), custom_call_target="tpu_custom_call" | custom-call | flops 1 | bytes 1 | tf_op jit(solution)/shard_map/attend_back/pallas_call | solution.py:686
  543.8 6.8 collective-permute-done.47
  550.7 8.3 %collective-permute-done.48 = bf16[2,4,4,16,512]{4,3,2,1,0:T(8,128)(2,1)} collective-permute-done((bf16[2,4,4,16,512]{4,3,2,1,0:T(8,128)(2,1)}, bf16[2,4,4,16,512]{4,3,2,1,0:T(8,128)(2,1)}, u32[]{:S(2)}, u32[]{:S(2)}) %collective-permute-start.48) | collective-permute-done | bytes 524320 | tf_op jit(solution)/shard_map/ppermute | solution.py:64
  583.4 17.5 %collective-permute-done.53 = f32[12,512]{1,0:T(8,128)S(1)} collective-permute-done((f32[12,512]{1,0:T(8,128)S(1)}, f32[12,512]{1,0:T(8,128)S(1)}, u32[]{:S(2)}, u32[]{:S(2)}) %collective-permute-start.53) | collective-permute-done | bytes 24608 | tf_op jit(solution)/shard_map/ppermute | solution.py:64
  (653 shorter events, 381.4 us)
Async XLA Ops:
  7.2 143.5 %all-gather.5.cloned.1.call-start = ((), (), s32[]{:S(2)}) async-start(), calls=%async_computation.6 | async-start | bytes 8650752 | tf_op jit(solution)/shard_map/all_gather | solution.py:1073
  37.0 174.8 %all-gather.7.cloned.1.call-start = ((), (), s32[]{:S(2)}) async-start(), calls=%async_computation.7 | async-start | bytes 8650752 | tf_op jit(solution)/shard_map/all_gather | solution.py:1120
  41.1 27.7 %collective-permute-start.8 = (bf16[3,12,16,512]{3,2,1,0:T(8,128)(2,1)S(1)}, bf16[3,12,16,512]{3,2,1,0:T(8,128)(2,1)}, u32[]{:S(2)}, u32[]{:S(2)}) collective-permute-start(bf16[3,12,16,512]{3,2,1,0:T(8,128)(2,1)S(1)} %pad_maximum_fusion.4.refs_1_), channel_id=1, source_target_pairs={{0,16},{8,24},{16,0},{24,8},{1,17},{9,25},{17,1},{25,9},{2,18},{10... | collective-permute-start | bytes 1769480 | tf_op jit(solution)/shard_map/ppermute | solution.py:64
  42.6 26.5 %collective-permute-start.9 = (bf16[3,12,16,512]{3,2,1,0:T(8,128)(2,1)S(1)}, bf16[3,12,16,512]{3,2,1,0:T(8,128)(2,1)}, u32[]{:S(2)}, u32[]{:S(2)}) collective-permute-start(bf16[3,12,16,512]{3,2,1,0:T(8,128)(2,1)S(1)} %pad_maximum_fusion.4.refs_1_), channel_id=1, source_target_pairs={{0,24},{8,16},{16,8},{24,0},{1,25},{9,17},{17,9},{25,1},{2,26},{10... | collective-permute-start | bytes 1769480 | tf_op jit(solution)/shard_map/ppermute | solution.py:64
  43.6 34.3 %collective-permute-start.10 = (bf16[8,16,512]{2,1,0:T(8,128)(2,1)}, bf16[8,16,512]{2,1,0:T(8,128)(2,1)S(1)}, u32[]{:S(2)}, u32[]{:S(2)}) collective-permute-start(bf16[8,16,512]{2,1,0:T(8,128)(2,1)} %fusion.38), channel_id=1, source_target_pairs={{0,2},{2,0},{4,6},{6,4},{1,3},{3,1},{5,7},{7,5},{8,10},{10,8},{12,... | collective-permute-start | bytes 393224 | tf_op jit(solution)/shard_map/ppermute | solution.py:64
  46.4 32.0 %collective-permute-start.11 = (bf16[8,16,512]{2,1,0:T(8,128)(2,1)}, bf16[8,16,512]{2,1,0:T(8,128)(2,1)S(1)}, u32[]{:S(2)}, u32[]{:S(2)}) collective-permute-start(bf16[8,16,512]{2,1,0:T(8,128)(2,1)} %fusion.38), channel_id=1, source_target_pairs={{0,4},{2,6},{4,0},{6,2},{1,5},{3,7},{5,1},{7,3},{8,12},{10,14},{12... | collective-permute-start | bytes 393224 | tf_op jit(solution)/shard_map/ppermute | solution.py:64
  57.8 20.8 %collective-permute-start.12 = (bf16[8,16,512]{2,1,0:T(8,128)(2,1)}, bf16[8,16,512]{2,1,0:T(8,128)(2,1)}, u32[]{:S(2)}, u32[]{:S(2)}) collective-permute-start(bf16[8,16,512]{2,1,0:T(8,128)(2,1)} %fusion.38), channel_id=1, source_target_pairs={{0,6},{2,4},{4,2},{6,0},{1,7},{3,5},{5,3},{7,1},{8,14},{10,12},{12... | collective-permute-start | bytes 393224 | tf_op jit(solution)/shard_map/ppermute | solution.py:64
  84.1 24.1 %collective-permute-start.22 = (bf16[3,8,16,512]{3,2,1,0:T(8,128)(2,1)S(1)}, bf16[3,8,16,512]{3,2,1,0:T(8,128)(2,1)}, u32[]{:S(2)}, u32[]{:S(2)}) collective-permute-start(bf16[3,8,16,512]{3,2,1,0:T(8,128)(2,1)S(1)} %pad_maximum_fusion.5.refs_1_), channel_id=1, source_target_pairs={{0,8},{8,0},{16,24},{24,16},{1,9},{9,1},{17,25},{25,17},{2,10},{10... | collective-permute-start | bytes 1179656 | tf_op jit(solution)/shard_map/ppermute | solution.py:64
  84.2 24.1 %collective-permute-start.23 = (bf16[3,8,16,512]{3,2,1,0:T(8,128)(2,1)S(1)}, bf16[3,8,16,512]{3,2,1,0:T(8,128)(2,1)}, u32[]{:S(2)}, u32[]{:S(2)}) collective-permute-start(bf16[3,8,16,512]{3,2,1,0:T(8,128)(2,1)S(1)} %pad_maximum_fusion.5.refs_1_), channel_id=1, source_target_pairs={{0,16},{8,24},{16,0},{24,8},{1,17},{9,25},{17,1},{25,9},{2,18},{10... | collective-permute-start | bytes 1179656 | tf_op jit(solution)/shard_map/ppermute | solution.py:64
  86.5 30.1 %collective-permute-start.24 = (bf16[3,8,16,512]{3,2,1,0:T(8,128)(2,1)S(1)}, bf16[3,8,16,512]{3,2,1,0:T(8,128)(2,1)}, u32[]{:S(2)}, u32[]{:S(2)}) collective-permute-start(bf16[3,8,16,512]{3,2,1,0:T(8,128)(2,1)S(1)} %pad_maximum_fusion.5.refs_1_), channel_id=1, source_target_pairs={{0,24},{8,16},{16,8},{24,0},{1,25},{9,17},{17,9},{25,1},{2,26},{10... | collective-permute-start | bytes 1179656 | tf_op jit(solution)/shard_map/ppermute | solution.py:64
  134.2 250.8 %reduce-scatter.4.cloned.1.call-start = ((), (), s32[]{:S(2)}) async-start(), calls=%async_computation.3 | async-start | bytes 2228224 | tf_op jit(solution)/shard_map/reduce_scatter | solution.py:108
  162.9 19.9 %collective-permute-start.32 = (bf16[2,512,512]{2,1,0:T(8,128)(2,1)S(1)}, bf16[2,512,512]{2,1,0:T(8,128)(2,1)}, u32[]{:S(2)}, u32[]{:S(2)}) collective-permute-start(bf16[2,512,512]{2,1,0:T(8,128)(2,1)S(1)} %pad_maximum_fusion.kv_own), channel_id=1, source_target_pairs={{0,1},{1,0},{2,3},{3,2},{4,5},{5,4},{6,7},{7,6},{8,9},{9,8},{10,11... | collective-permute-start | bytes 3145736 | tf_op jit(solution)/shard_map/ppermute | solution.py:64
  223.9 19.5 %collective-permute-start.34 = (bf16[2,512,512]{2,1,0:T(8,128)(2,1)S(1)}, bf16[2,512,512]{2,1,0:T(8,128)(2,1)}, u32[]{:S(2)}, u32[]{:S(2)}) collective-permute-start(bf16[2,512,512]{2,1,0:T(8,128)(2,1)S(1)} %pad_maximum_fusion.1.kv_own), channel_id=1, source_target_pairs={{0,1},{1,0},{2,3},{3,2},{4,5},{5,4},{6,7},{7,6},{8,9},{9,8},{10,11... | collective-permute-start | bytes 3145736 | tf_op jit(solution)/shard_map/ppermute | solution.py:64
  298.3 207.5 %reduce-scatter.6.cloned.1.call-start = ((), (), s32[]{:S(2)}) async-start(), calls=%async_computation.4 | async-start | bytes 4456448 | tf_op jit(solution)/shard_map/reduce_scatter | solution.py:108
  333.4 27.9 %collective-permute-start.37 = (f32[2,512,512]{2,1,0:T(8,128)}, f32[2,512,512]{2,1,0:T(8,128)}, u32[]{:S(2)}, u32[]{:S(2)}) collective-permute-start(f32[2,512,512]{2,1,0:T(8,128)} %get-tuple-element.704), channel_id=1, source_target_pairs={{0,1},{1,0},{2,3},{3,2},{4,5},{5,4},{6,7},{7,6},{8,9},{9,8},{10,11... | collective-permute-start | bytes 6291464 | tf_op jit(solution)/shard_map/ppermute | solution.py:64
  398.8 239.2 %reduce-scatter.8.cloned.1.call-start = ((), (), s32[]{:S(2)}) async-start(), calls=%async_computation.5 | async-start | bytes 2228224 | tf_op jit(solution)/shard_map/reduce_scatter | solution.py:108
  454.2 35.4 %collective-permute-start.42 = (bf16[8,16,512]{2,1,0:T(8,128)(2,1)S(1)}, bf16[8,16,512]{2,1,0:T(8,128)(2,1)S(1)}, u32[]{:S(2)}, u32[]{:S(2)}) collective-permute-start(bf16[8,16,512]{2,1,0:T(8,128)(2,1)S(1)} %bitcast.368), channel_id=1, source_target_pairs={{0,8},{8,0},{16,24},{24,16},{1,9},{9,1},{17,25},{25,17},{2,10},{10... | collective-permute-start | bytes 393224 | tf_op jit(solution)/shard_map/ppermute | solution.py:64
  454.2 35.5 %collective-permute-start.43 = (bf16[8,16,512]{2,1,0:T(8,128)(2,1)S(1)}, bf16[8,16,512]{2,1,0:T(8,128)(2,1)}, u32[]{:S(2)}, u32[]{:S(2)}) collective-permute-start(bf16[8,16,512]{2,1,0:T(8,128)(2,1)S(1)} %bitcast.369), channel_id=1, source_target_pairs={{0,16},{8,24},{16,0},{24,8},{1,17},{9,25},{17,1},{25,9},{2,18},{10... | collective-permute-start | bytes 393224 | tf_op jit(solution)/shard_map/ppermute | solution.py:64
  467.3 22.4 %collective-permute-start.44 = (bf16[8,16,512]{2,1,0:T(8,128)(2,1)S(1)}, bf16[8,16,512]{2,1,0:T(8,128)(2,1)}, u32[]{:S(2)}, u32[]{:S(2)}) collective-permute-start(bf16[8,16,512]{2,1,0:T(8,128)(2,1)S(1)} %bitcast.370), channel_id=1, source_target_pairs={{0,24},{8,16},{16,8},{24,0},{1,25},{9,17},{17,9},{25,1},{2,26},{10... | collective-permute-start | bytes 393224 | tf_op jit(solution)/shard_map/ppermute | solution.py:64
  536.0 27.0 %collective-permute-start.49 = (bf16[4,4,12,16,512]{4,3,2,1,0:T(8,128)(2,1)}, bf16[4,4,12,16,512]{4,3,2,1,0:T(8,128)(2,1)}, u32[]{:S(2)}, u32[]{:S(2)}) collective-permute-start(bf16[4,4,12,16,512]{4,3,2,1,0:T(8,128)(2,1)} %get-tuple-element.820), channel_id=1, source_target_pairs={{0,1},{1,0},{2,3},{3,2},{4,5},{5,4},{6,7},{7,6},{8,9},{9,8},{10,11... | collective-permute-start | bytes 9437192 | tf_op jit(solution)/shard_map/ppermute | solution.py:64
  537.1 21.8 %collective-permute-start.48 = (bf16[2,4,4,16,512]{4,3,2,1,0:T(8,128)(2,1)}, bf16[2,4,4,16,512]{4,3,2,1,0:T(8,128)(2,1)}, u32[]{:S(2)}, u32[]{:S(2)}) collective-permute-start(bf16[2,4,4,16,512]{4,3,2,1,0:T(8,128)(2,1)} %fusion.21), channel_id=1, source_target_pairs={{0,16},{16,0},{1,17},{17,1},{2,18},{18,2},{3,19},{19,3},{4,20},{20... | collective-permute-start | bytes 1572872 | tf_op jit(solution)/shard_map/ppermute | solution.py:64
  572.8 43.7 %collective-permute-start.57 = (bf16[2,4,6,16,512]{4,3,2,1,0:T(8,128)(2,1)}, bf16[2,4,6,16,512]{4,3,2,1,0:T(8,128)(2,1)}, u32[]{:S(2)}, u32[]{:S(2)}) collective-permute-start(bf16[2,4,6,16,512]{4,3,2,1,0:T(8,128)(2,1)} %fusion.15), channel_id=1, source_target_pairs={{0,8},{8,0},{1,9},{9,1},{2,10},{10,2},{3,11},{11,3},{4,12},{12,4},... | collective-permute-start | bytes 2359304 | tf_op jit(solution)/shard_map/ppermute | solution.py:64
  573.2 43.9 %collective-permute-start.58 = (bf16[2,4,6,16,512]{4,3,2,1,0:T(8,128)(2,1)}, bf16[2,4,6,16,512]{4,3,2,1,0:T(8,128)(2,1)}, u32[]{:S(2)}, u32[]{:S(2)}) collective-permute-start(bf16[2,4,6,16,512]{4,3,2,1,0:T(8,128)(2,1)} %fusion.16), channel_id=1, source_target_pairs={{0,16},{16,0},{1,17},{17,1},{2,18},{18,2},{3,19},{19,3},{4,20},{20... | collective-permute-start | bytes 2359304 | tf_op jit(solution)/shard_map/ppermute | solution.py:64
  581.5 19.3 %collective-permute-start.53 = (f32[12,512]{1,0:T(8,128)S(1)}, f32[12,512]{1,0:T(8,128)S(1)}, u32[]{:S(2)}, u32[]{:S(2)}) collective-permute-start(f32[12,512]{1,0:T(8,128)S(1)} %add.717), channel_id=1, source_target_pairs={{0,8},{8,0},{1,9},{9,1},{2,10},{10,2},{3,11},{11,3},{4,12},{12,4},... | collective-permute-start | bytes 73736 | tf_op jit(solution)/shard_map/ppermute | solution.py:64
  611.3 25.3 %collective-permute-start.62 = (bf16[16,16,512]{2,1,0:T(8,128)(2,1)S(1)}, bf16[16,16,512]{2,1,0:T(8,128)(2,1)S(1)}, u32[]{:S(2)}, u32[]{:S(2)}) collective-permute-start(bf16[16,16,512]{2,1,0:T(8,128)(2,1)S(1)} %bitcast.362), channel_id=1, source_target_pairs={{0,8},{8,0},{16,24},{24,16},{1,9},{9,1},{17,25},{25,17},{2,10},{10... | collective-permute-start | bytes 786440 | tf_op jit(solution)/shard_map/ppermute | solution.py:64
  612.0 24.6 %collective-permute-start.63 = (bf16[16,16,512]{2,1,0:T(8,128)(2,1)S(1)}, bf16[16,16,512]{2,1,0:T(8,128)(2,1)S(1)}, u32[]{:S(2)}, u32[]{:S(2)}) collective-permute-start(bf16[16,16,512]{2,1,0:T(8,128)(2,1)S(1)} %bitcast.363), channel_id=1, source_target_pairs={{0,16},{8,24},{16,0},{24,8},{1,17},{9,25},{17,1},{25,9},{2,18},{10... | collective-permute-start | bytes 786440 | tf_op jit(solution)/shard_map/ppermute | solution.py:64
  638.7 19.2 %collective-permute-start.68 = (bf16[8,16,512]{2,1,0:T(8,128)(2,1)}, bf16[8,16,512]{2,1,0:T(8,128)(2,1)}, u32[]{:S(2)}, u32[]{:S(2)}) collective-permute-start(bf16[8,16,512]{2,1,0:T(8,128)(2,1)} %get-tuple-element.939.refs_12_), channel_id=1, source_target_pairs={{0,16},{8,24},{16,0},{24,8},{1,17},{9,25},{17,1},{25,9},{2,18},{10... | collective-permute-start | bytes 393224 | tf_op jit(solution)/shard_map/ppermute | solution.py:64
  638.8 19.8 %collective-permute-start.69 = (bf16[8,16,512]{2,1,0:T(8,128)(2,1)}, bf16[8,16,512]{2,1,0:T(8,128)(2,1)}, u32[]{:S(2)}, u32[]{:S(2)}) collective-permute-start(bf16[8,16,512]{2,1,0:T(8,128)(2,1)} %get-tuple-element.939.refs_12_), channel_id=1, source_target_pairs={{0,24},{8,16},{16,8},{24,0},{1,25},{9,17},{17,9},{25,1},{2,26},{10... | collective-permute-start | bytes 393224 | tf_op jit(solution)/shard_map/ppermute | solution.py:64
  658.0 33.9 %collective-permute-start.78 = (bf16[8,16,512]{2,1,0:T(8,128)(2,1)S(1)}, bf16[8,16,512]{2,1,0:T(8,128)(2,1)S(1)}, u32[]{:S(2)}, u32[]{:S(2)}) collective-permute-start(bf16[8,16,512]{2,1,0:T(8,128)(2,1)S(1)} %bitcast.372), channel_id=1, source_target_pairs={{0,8},{8,0},{16,24},{24,16},{1,9},{9,1},{17,25},{25,17},{2,10},{10... | collective-permute-start | bytes 393224 | tf_op jit(solution)/shard_map/ppermute | solution.py:64
  658.6 41.1 %collective-permute-start.79 = (bf16[8,16,512]{2,1,0:T(8,128)(2,1)S(1)}, bf16[8,16,512]{2,1,0:T(8,128)(2,1)S(1)}, u32[]{:S(2)}, u32[]{:S(2)}) collective-permute-start(bf16[8,16,512]{2,1,0:T(8,128)(2,1)S(1)} %bitcast.373), channel_id=1, source_target_pairs={{0,16},{8,24},{16,0},{24,8},{1,17},{9,25},{17,1},{25,9},{2,18},{10... | collective-permute-start | bytes 393224 | tf_op jit(solution)/shard_map/ppermute | solution.py:64
  660.2 39.5 %collective-permute-start.80 = (bf16[8,16,512]{2,1,0:T(8,128)(2,1)S(1)}, bf16[8,16,512]{2,1,0:T(8,128)(2,1)}, u32[]{:S(2)}, u32[]{:S(2)}) collective-permute-start(bf16[8,16,512]{2,1,0:T(8,128)(2,1)S(1)} %bitcast.374), channel_id=1, source_target_pairs={{0,24},{8,16},{16,8},{24,0},{1,25},{9,17},{17,9},{25,1},{2,26},{10... | collective-permute-start | bytes 393224 | tf_op jit(solution)/shard_map/ppermute | solution.py:64
  674.0 25.8 %collective-permute-start.81 = (bf16[12,16,512]{2,1,0:T(8,128)(2,1)S(1)}, bf16[12,16,512]{2,1,0:T(8,128)(2,1)S(1)}, u32[]{:S(2)}, u32[]{:S(2)}) collective-permute-start(bf16[12,16,512]{2,1,0:T(8,128)(2,1)S(1)} %get-tuple-element.943.refs_16_), channel_id=1, source_target_pairs={{0,8},{8,0},{16,24},{24,16},{1,9},{9,1},{17,25},{25,17},{2,10},{10... | collective-permute-start | bytes 589832 | tf_op jit(solution)/shard_map/ppermute | solution.py:64
  (180 other events, 2001.8 us)
Sparse Core Ops, SparseCore 0:
  37.1 94.3 all-gather.4
  134.5 77.1 all-gather.6
  298.4 86.5 reduce-scatter.3
  398.9 96.5 reduce-scatter.5
  544.0 84.8 reduce-scatter.7

commit v4 on v3

--- a/solution.py
+++ b/solution.py
@@ -15,6 +15,7 @@
 LAYERS = 2
 MICRO = 2
 COL = 512
+HALF, FULL = jnp.bfloat16, jnp.float32
 
 NORM_EPS = 1e-06
 CLIP_NORM = 0.01
@@ -50,9 +51,8 @@
 REDUCED = (
     feed_parts(2),
     attention_parts(3) + attention_parts(4) + feed_parts(1),
-    attention_parts(1) + attention_parts(2),
-    feed_parts(0),
-    (TABLE,) + attention_parts(0),
+    attention_parts(1) + attention_parts(2) + feed_parts(0),
+    (TABLE,) + attention_parts(0) + (("gains", 0, "row"),),
 )
 
 
@@ -321,6 +321,23 @@
     return total
 
 
+def plane_sum_kernel(keep, core, from_x, from_y, left, right, own, *sends):
+    half = left.shape[1]
+    for bit in range(4):
+        for part, (one, two) in ((slice(0, half), (from_x, left)), (slice(half, None), (from_y, right))):
+            total = added([keep[bit, part], core[bit, part], one[bit], two[bit]])
+            if bit == 0:
+                own[part] = total
+            else:
+                sends[bit - 1][part] = low(total)
+
+
+def line_sum_kernel(own, one, two, three, whole, squares):
+    total = added([own[...], one[...], two[...], three[...]])
+    whole[...] = low(total)
+    squares[0, 0] = jnp.sum(total * total)
+
+
 def collect(me, grads, kinds, counts, unit, ordered):
     starts = [sum(counts[:i]) for i in range(len(counts))]
     plan = tuple(zip(kinds, starts, counts))
@@ -376,19 +393,34 @@
     yield [(low(added([a[1] for a in left])), ("sy",)), (low(added([a[1] for a in right])), ("sx",))]
     mover.held += mover.arrived
 
-    def plane(bit):
-        left, right = sides()
-        left = [a[0, bit] for a in left] + [mover.held[4][bit]]
-        right = [a[0, bit] for a in right] + [mover.held[5][bit]]
-        return jnp.concatenate([added(left), added(right)], axis=0)
-
-    yield [(low(plane(bit)), ("z", bit)) for bit in (1, 2, 3)]
-    own = plane(0)
-    mover.arrived.insert(0, own)
-    whole = added(mover.arrived)
-    mover.squares = jnp.sum(whole * whole)
-    mover.held = [low(whole)]
-    yield [(mover.held[0], (PLANE, bit)) for bit in (1, 2, 3)]
+    block = (total, unit, COL)
+    first_part = pl.BlockSpec((None, None, 4, *block), lambda i: (0, 0, 0, 0, 0, 0))
+    half_part = [pl.BlockSpec((None, 4, n, unit, COL), lambda i: (0, 0, 0, 0, 0)) for n in (half, total - half)]
+    own, *sends = pl.pallas_call(
+        plane_sum_kernel,
+        grid=(1,),
+        out_shape=[jax.ShapeDtypeStruct(block, FULL)] + [jax.ShapeDtypeStruct(block, HALF)] * 3,
+        in_specs=[first_part, first_part, *half_part, ONCHIP, ONCHIP],
+        out_specs=[ONCHIP] * 4,
+        cost_estimate=LIGHT,
+        name="plane_sum",
+    )(*mover.held)
+    mover.held = [own]
+    yield [(send, ("z", bit)) for bit, send in zip((1, 2, 3), sends)]
+    own, squares = pl.pallas_call(
+        line_sum_kernel,
+        out_shape=[
+            jax.ShapeDtypeStruct(block, HALF),
+            jax.ShapeDtypeStruct((1, 1), FULL),
+        ],
+        in_specs=[ONCHIP] * 4,
+        out_specs=[ONCHIP, SCALAR],
+        cost_estimate=LIGHT,
+        name="line_sum",
+    )(*mover.held, *mover.arrived)
+    mover.squares = squares[0, 0]
+    mover.held = [own]
+    yield [(own, (PLANE, bit)) for bit in (1, 2, 3)]
     mover.result = mover.held + mover.arrived
     mover.held = []
     yield []
@@ -823,9 +855,6 @@
 
 def shaped(lead, like, kind):
     return (lead + like.shape, kind)
-
-
-HALF, FULL = jnp.bfloat16, jnp.float32
 
 
 def attend_forward(masks, causal, q, kv):
@@ -970,6 +999,7 @@
         "down": down_weight,
     }
     shard_shapes = {name: array.shape[1:] for name, array in shard_of.items()}
+    shard_shapes["gains"] = (gain_dev, COL)
     weights = {}
 
     def layout(entries):
@@ -1068,13 +1098,12 @@
         ],
         axis=1,
     )
+    gains_now = norm_gains
     if fast:
-        reached, norm_gains_now, third = step((reached, norm_gains, third), first)
+        reached, gains_now, third = step((reached, gains_now, third), first)
         third = lax.all_gather(third, PLANE + LINE).reshape(4, owners, *third.shape)
-        reached, norm_gains_now = step((reached, norm_gains_now), second)
-    else:
-        norm_gains_now = norm_gains
-    small = jnp.concatenate([norm_gains_now.reshape(-1), reached.reshape(-1)])
+        reached, gains_now = step((reached, gains_now), second)
+    small = jnp.concatenate([gains_now.reshape(-1), reached.reshape(-1)])
     small = gathered(gathered(small, "c"), "z").reshape(owners, -1)
     reach = jnp.maximum(
         jnp.sum(small[::2, gain_count * gain_dev :], axis=0).reshape(MICRO, LAYERS), 1.0
@@ -1099,12 +1128,12 @@
         mine[:, rest : rest + loss_dev] + (jnp.arange(2, dtype=jnp.int32) * tok_dev)[:, None]
     ).reshape(-1)
     wanted = mine[:, rest + loss_dev : rest + 2 * loss_dev].reshape(-1)
-    depth = mine[:, rest + 2 * loss_dev :].reshape(-1)
+    depth = mine[:, rest + 2 * loss_dev : rest + 3 * loss_dev].reshape(-1)
     masks = attend_masks(sentence, other_sentence, c * half_row, (1 - c) * half_row)
 
     ids = jnp.concatenate([source_ids, target_ids])
     if fast:
-        ids = step(ids, first)
+        ids, small = step((ids, small), first)
         ids = step(ids, second, first)
         settle(GATHERED[0], first.result)
     table = weights["table", 0].reshape(vocabulary, width)
@@ -1241,8 +1270,7 @@
             grad_x,
         )
     if fast:
-        middle = reduce(REDUCED[2], long_reduce_stages)
-        grad_x, grad_memory = step((grad_x, grad_memory), middle, middle)
+        grad_x, grad_memory = step((grad_x, grad_memory), feed_mover)
     grad_enc, gain_parts[2 * ENC] = norm_back(xe, final_gain, grad_memory)
     up, down, qkv, out = ("up", 0), ("down", 0), ("qkv", 0), ("out", 0)
     grads[up], grads[down], grad_enc, gain_parts[1], grad_o, grads[out] = feed_back(
@@ -1255,11 +1283,9 @@
         weights[out],
     )
     if fast:
-        early = reduce(REDUCED[3])
-        grad_enc, grad_o = step((grad_enc, grad_o), feed_mover, early)
+        middle = reduce(REDUCED[2], long_reduce_stages)
+        grad_enc, grad_o = step((grad_enc, grad_o), middle, late, middle)
     grad_q, own, other = attend_backward(saved_enc, masks, False, grad_o)
-    if fast:
-        grad_q, own, grad_enc = step((grad_q, own, grad_enc), late, early)
     grads[qkv], grad_enc, gain_parts[0] = project_back(
         grad_q, own, other, kept_enc[1], kept_enc[0], gains_full[0], weights[qkv], grad_enc
     )
@@ -1269,31 +1295,28 @@
     table_grad = low(table_grad + outer_sum(looked, token_grads))
     grads["table", 0] = table_grad
 
+    gain_grad = jnp.concatenate([part.reshape(1, -1) for part in gain_parts])
+    grads["gains", 0] = low(jnp.pad(gain_grad.T, ((0, 0), (0, COL - gain_count))))[None]
+
     reduced = {}
-    gain_grad = jnp.concatenate([part.reshape(1, -1) for part in gain_parts])
-    small = jnp.concatenate([gain_grad, jnp.full((1, width), loss_part)])
     if fast:
-        last = reduce(REDUCED[4])
-        small = step(small, last, early)
-        small = step(small, last, early)
-        small = all_sum(small)
-        small = step(small, last, early, late, middle)
-        small = step(small, last, early)
-        movers = (feed_mover, late, middle, early, last)
-        squares = sum(mover.squares for mover in movers[:4])
-        squares = step(squares, last)
-        squares = all_sum(squares + last.squares)
-        squares = step(squares, middle, last)
+        last = reduce(REDUCED[3])
+        loss_part = step(loss_part, last)
+        loss_part = step(loss_part, last)
+        loss_part = step(loss_part, last, middle)
+        loss_part = step(loss_part, last)
+        movers = (feed_mover, late, middle, last)
+        loss_part = step(loss_part, last)
+        squares = sum(mover.squares for mover in movers)
+        squares, loss_total = all_sum(jnp.stack([squares, loss_part]))
+        squares = step(squares, late, middle, last)
     else:
-        small = all_sum(small)
-        squares = all_sum(sum(reduce_plainly(entries) for entries in REDUCED))
-    loss_total = small[-1, 0]
-    gain_grad = small[:-1]
-    squares = squares + jnp.sum(gain_grad * gain_grad)
+        squares = sum(reduce_plainly(entries) for entries in REDUCED)
+        squares, loss_total = all_sum(jnp.stack([squares, loss_part]))
     grad_norm = jnp.sqrt(squares)
     clip_factor = CLIP_NORM / jnp.maximum(grad_norm, CLIP_NORM)
 
-    names = ("qkv", "out", "up", "down", "table")
+    names = ("qkv", "out", "up", "down", "table", "gains")
     if fast:
         plan = []
         for bucket, entries in enumerate(REDUCED):
@@ -1302,7 +1325,7 @@
                 plan.append((bucket, first, count, kind, names.index(name), i))
                 first += count
         parts = [part for mover in movers for part in mover.result]
-        shapes = [shard_of[name].shape for name in names]
+        shapes = [shard_of[name].shape for name in names[:-1]] + [(1, gain_dev, COL)]
         placed = pl.pallas_call(
             functools.partial(settle_kernel, len(parts), tuple(plan), unit),
             out_shape=[jax.ShapeDtypeStruct(shape, jnp.bfloat16) for shape in shapes],
@@ -1315,12 +1338,12 @@
         ready = [wide(array) for array in placed]
     else:
         ready = [
-            wide(jnp.stack([reduced[name, i] for i in range(shard_of[name].shape[0])]))
+            wide(jnp.stack([reduced[name, i] for i in range(len(shard_of.get(name, "1")))]))
             for name in names
         ]
     gradients = (
         *ready[:4],
-        lax.dynamic_slice_in_dim(gain_grad, (2 * z + c) * gain_dev, gain_dev, 1),
+        ready[5][0, :, :gain_count].T,
         ready[4][0],
     )
     masters = (qkv_weight, out_weight, up_weight, down_weight, norm_gains, embed_table)

time: 747 us -> 722 us (0.967)
  waiting for transfers between devices: 138 us -> 178 us
  other arithmetic: 88.5 us -> 67.6 us
  starting transfers between devices: 102 us -> 84.9 us
  Pallas kernels: 302 us -> 290 us
  local copies, waits for them, and re-layouts: 56.1 us -> 45 us
    reduce_scatter x3, waiting for transfers between devices: 10.8 us -> 34.7 us  [step(): lax.psum_scatter(array, PLANE + ('z',), scatter_dimension=0, tiled=True)]
    ppermute x84 -> x68, starting transfers between devices: 102 us -> 84.4 us  [flip(): return lax.ppermute(x, axis, [(i, i ^ bit) for i in range(n)])]
    all_gather x1, waiting for transfers between devices: 10.6 us -> 26.3 us  [shards(): lax.all_gather(fourth, PLANE + LINE).reshape(4, owners, *fourth.shape)]
    squeeze x16 -> x0, local copies, waits for them, and re-layouts: 9.57 us -> none  [the longest x8 4.82 us: sides(): a[:, 0, :, :half]]
    pallas_call x5, Pallas kernels: 75.9 us -> 67.3 us  [attend_back(): pl.pallas_call(attend_back_kernel, out_shape=[jax.ShapeDtypeStruct((n, wi...]
    pallas_call x5 -> x4, Pallas kernels: 28.8 us -> 26.7 us  [collect(): pl.pallas_call(functools.partial(collect_kernel, plan, unit, ordered), ou...]
    convert_element_type x11 -> x9, other arithmetic: 27.6 us -> 26.3 us  [low(): return v.astype(jnp.bfloat16)]
    ppermute x84 -> x68, waiting for transfers between devices: 117 us -> 117 us  [flip(): return lax.ppermute(x, axis, [(i, i ^ bit) for i in range(n)])]
  transfers between devices with their start and end apart: 89 -> 73, of which waited for: 30 -> 31; matrix products, arithmetic and copies ran while one was open for 14% -> 10% of each run, Pallas kernels for 33% -> 32%
where the time goes in v4:
time: 722 us; the launch traced here: 712 us
  Pallas kernels  290 us (40%)
  waiting for transfers between devices  178 us (25%)
  starting transfers between devices  84.9 us (12%)
  other arithmetic  67.6 us (9%)
  local copies, waits for them, and re-layouts  45 us (6%)
  matrix products  23.4 us (3%)
  between operations  22.3 us (3%)
    ppermute x68, waiting for transfers between devices, flip(): return lax.ppermute(x, axis, [(i, i ^ bit) for i in range(n)])  117 us
    pallas_call x18, Pallas kernels, on_chip(): pl.pallas_call(kernel, out_shape=[jax.ShapeDtypeStruct(shape, kind) for s...  113 us
    ppermute x68, starting transfers between devices, flip(): return lax.ppermute(x, axis, [(i, i ^ bit) for i in range(n)])  84.4 us
    pallas_call x5, Pallas kernels, attend_back(): pl.pallas_call(attend_back_kernel, out_shape=[jax.ShapeDtypeStruct((n, wi...  67.3 us
    pallas_call x5, Pallas kernels, attend(): pl.pallas_call(attend_kernel, out_shape=[jax.ShapeDtypeStruct((n, width),...  48.9 us
    reduce_scatter x3, waiting for transfers between devices, step(): lax.psum_scatter(array, PLANE + ('z',), scatter_dimension=0, tiled=True)  34.7 us
    pallas_call x4, Pallas kernels, collect(): pl.pallas_call(functools.partial(collect_kernel, plan, unit, ordered), ou...  26.7 us
    convert_element_type x9, other arithmetic, low(): return v.astype(jnp.bfloat16)  26.3 us
  transfers between devices with their start and end apart: 73, of which 31 were waited for; matrix products, arithmetic and copies ran while one was open for 10% of the time, Pallas kernels for 32%

profile of v4, /device:TPU:0, one launch (start us, length us, event | category | flops | bytes accessed | tf_op | source)
XLA Modules:
  0.0 711.9 jit_solution(10344544017131310684)
XLA Ops:
  57.6 10.9 %collective-permute-done.12.refs_3_ = bf16[3,12,16,512]{3,2,1,0:T(8,128)(2,1)} collective-permute-done((bf16[3,12,16,512]{3,2,1,0:T(8,128)(2,1)S(1)}, bf16[3,12,16,512]{3,2,1,0:T(8,128)(2,1)}, u32[]{:S(2)}, u32[]{:S(2)}) %collective-permute-start.12) | collective-permute-done | bytes 589856 | tf_op jit(solution)/shard_map/ppermute | solution.py:64
  103.7 10.0 %attend.5 = (bf16[512,512]{1,0:T(8,128)(2,1)}, f32[4,4,1,256]{3,2,1,0:T(1,128)}) custom-call(s32[18]{0:T(128)} %pad_add_fusion.9.act, s32[8,512]{1,0:T(8,128)} %pad.13.bounds, bf16[512,512]{1,0:T(8,128)(2,1)} %get-tuple-element.516.q, bf16[2,512,512]{2,1,0:T(8,128)(2,1)} %get-tuple-element.517.kv_own, bf16[2,512,512]{2,1,0:T(8,128)(2,1)} %copy-done.15), custom_call_target="tpu_custom_call" | custom-call | flops 1 | bytes 1 | tf_op jit(solution)/shard_map/attend/pallas_call | solution.py:690
  121.3 7.1 %feed.3 = (f32[512,512]{1,0:T(8,128)}, bf16[512,512]{1,0:T(8,128)(2,1)}, bf16[4,512,512]{2,1,0:T(8,128)(2,1)}, f32[512,512]{1,0:T(8,128)}) custom-call(bf16[512,512]{1,0:T(8,128)(2,1)} %get-tuple-element.531.o, bf16[1,512,512]{2,1,0:T(8,128)(2,1)} %get-tuple-element.532.w_out, f32[512,512]{1,0:T(8,128)} %get-tuple-element.704.x, f32[1,512]{1,0:T(1,128)} %slice.261.gain, ...), custom_call_target="tpu_custom_call" | custom-call | flops 1 | bytes 1 | tf_op jit(solution)/shard_map/feed/pallas_call | solution.py:846
  131.3 7.1 place_gathered.2
  150.4 9.4 %attend.6 = (bf16[512,512]{1,0:T(8,128)(2,1)}, f32[4,4,1,256]{3,2,1,0:T(1,128)}) custom-call(s32[18]{0:T(128)} %pad_add_fusion.7.act, s32[8,512]{1,0:T(8,128)} %pad.12.bounds, bf16[512,512]{1,0:T(8,128)(2,1)} %get-tuple-element.551.q, bf16[2,512,512]{2,1,0:T(8,128)(2,1)} %get-tuple-element.552.kv_own, bf16[2,512,512]{2,1,0:T(8,128)(2,1)} %copy-done.16), custom_call_target="tpu_custom_call" | custom-call | flops 1 | bytes 1 | tf_op jit(solution)/shard_map/attend/pallas_call | solution.py:690
  163.7 10.0 %attend.7 = (bf16[512,512]{1,0:T(8,128)(2,1)}, f32[4,4,1,256]{3,2,1,0:T(1,128)}) custom-call(s32[18]{0:T(128)} %pad_add_fusion.9.act, s32[8,512]{1,0:T(8,128)} %pad.13.bounds, bf16[512,512]{1,0:T(8,128)(2,1)} %get-tuple-element.556.q, bf16[2,512,512]{2,1,0:T(8,128)(2,1)} %copy-done.10, bf16[2,512,512]{2,1,0:T(8,128)(2,1)} %collective-permute-done.32.kv_oth), custom_call_target="tpu_custom_call" | custom-call | flops 1 | bytes 1 | tf_op jit(solution)/shard_map/attend/pallas_call | solution.py:690
  173.7 7.0 feed.4
  180.7 26.3 %all-gather.7.cloned.1.call-done = bf16[512,16,512]{2,1,0:T(8,128)(2,1)} async-done(((bf16[16,16,512]{2,1,0:T(8,128)(2,1)}), bf16[512,16,512]{2,1,0:T(8,128)(2,1)}) %all-gather.7.cloned.1.call-update) | async-done | bytes 8388624 | tf_op jit(solution)/shard_map/all_gather | solution.py:1149
  206.9 6.9 place_gathered.3
  224.7 9.4 %attend.8 = (bf16[512,512]{1,0:T(8,128)(2,1)}, f32[4,4,1,256]{3,2,1,0:T(1,128)}) custom-call(s32[18]{0:T(128)} %pad_add_fusion.7.act, s32[8,512]{1,0:T(8,128)} %pad.12.bounds, bf16[512,512]{1,0:T(8,128)(2,1)} %get-tuple-element.568.q, bf16[2,512,512]{2,1,0:T(8,128)(2,1)} %get-tuple-element.569.kv_own, bf16[2,512,512]{2,1,0:T(8,128)(2,1)} %copy-done.17), custom_call_target="tpu_custom_call" | custom-call | flops 1 | bytes 1 | tf_op jit(solution)/shard_map/attend/pallas_call | solution.py:690
  238.0 10.2 %attend.9 = (bf16[512,512]{1,0:T(8,128)(2,1)}, f32[4,4,1,256]{3,2,1,0:T(1,128)}) custom-call(s32[18]{0:T(128)} %pad_add_fusion.9.act, s32[8,512]{1,0:T(8,128)} %pad.13.bounds, bf16[512,512]{1,0:T(8,128)(2,1)} %get-tuple-element.574.q, bf16[2,512,512]{2,1,0:T(8,128)(2,1)} %copy-done.11, bf16[2,512,512]{2,1,0:T(8,128)(2,1)} %collective-permute-done.34.kv_oth), custom_call_target="tpu_custom_call" | custom-call | flops 1 | bytes 1 | tf_op jit(solution)/shard_map/attend/pallas_call | solution.py:690
  248.3 7.1 feed.5
  268.0 10.5 %feed_back.3 = (bf16[4,512,512]{2,1,0:T(8,128)(2,1)}, bf16[4,512,512]{2,1,0:T(8,128)(2,1)}, f32[512,512]{1,0:T(8,128)}, f32[1,512]{1,0:T(1,128)}, bf16[512,512]{...) custom-call(f32[512,512]{1,0:T(8,128)} %add_add_fusion.2.grad, f32[512,512]{1,0:T(8,128)} %get-tuple-element.582.y, ...), custom_call_target="tpu_custom_call" | custom-call | flops 1 | bytes 1 | tf_op jit(solution)/shard_map/feed_back/pallas_call | solution.py:846
  293.5 13.9 %attend_back.5 = (bf16[512,512]{1,0:T(8,128)(2,1)}, f32[2,512,512]{2,1,0:T(8,128)}, f32[2,512,512]{2,1,0:T(8,128)}) custom-call(s32[18]{0:T(128)} %pad_add_fusion.9.act, s32[8,512]{1,0:T(8,128)} %pad.13.bounds, bf16[512,512]{1,0:T(8,128)(2,1)} %get-tuple-element.574.q, bf16[2,512,512]{2,1,0:T(8,128)(2,1)} %copy-done.11, ...), custom_call_target="tpu_custom_call" | custom-call | flops 1 | bytes 1 | tf_op jit(solution)/shard_map/attend_back/pallas_call | solution.py:718
  312.5 12.8 %attend_back.6 = (bf16[512,512]{1,0:T(8,128)(2,1)}, f32[2,512,512]{2,1,0:T(8,128)}, f32[2,512,512]{2,1,0:T(8,128)}) custom-call(s32[18]{0:T(128)} %pad_add_fusion.7.act, s32[8,512]{1,0:T(8,128)} %pad.12.bounds, bf16[512,512]{1,0:T(8,128)(2,1)} %get-tuple-element.568.q, bf16[2,512,512]{2,1,0:T(8,128)(2,1)} %get-tuple-element.569.kv_own, ...), custom_call_target="tpu_custom_call" | custom-call | flops 1 | bytes 1 | tf_op jit(solution)/shard_map/attend_back/pallas_call | solution.py:718
  336.5 6.7 project_back.3
  346.1 10.5 %feed_back.4 = (bf16[4,512,512]{2,1,0:T(8,128)(2,1)}, bf16[4,512,512]{2,1,0:T(8,128)(2,1)}, f32[512,512]{1,0:T(8,128)}, f32[1,512]{1,0:T(1,128)}, bf16[512,512]{...) custom-call(f32[512,512]{1,0:T(8,128)} %fusion.10.grad, f32[512,512]{1,0:T(8,128)} %get-tuple-element.612.y, ...), custom_call_target="tpu_custom_call" | custom-call | flops 1 | bytes 1 | tf_op jit(solution)/shard_map/feed_back/pallas_call | solution.py:846
  361.7 7.7 %collect_gradients.5 = (bf16[4,4,16,16,512]{4,3,2,1,0:T(8,128)(2,1)}, bf16[4,4,16,16,512]{4,3,2,1,0:T(8,128)(2,1)}) custom-call(s32[3]{0:T(128)} %pad_add_fusion.10.me_ref, bf16[3,512,512]{2,1,0:T(8,128)(2,1)} %get-tuple-element.627.refs_0_, bf16[1,512,512]{2,1,0:T(8,128)(2,1)} %get-tuple-element.628.refs_1_, ...), custom_call_target="tpu_custom_call" | custom-call | flops 1 | bytes 1 | tf_op jit(solution)/shard_map/collect_gradients/pallas_call | solution.py:345
  369.5 11.8 %reduce-scatter.4.cloned.1.call-done = bf16[1,8,16,512]{3,2,1,0:T(8,128)(2,1)} async-done(((bf16[16,8,16,512]{3,2,1,0:T(8,128)(2,1)}), bf16[1,8,16,512]{3,2,1,0:T(8,128)(2,1)}) %reduce-scatter.4.cloned.1.call-update) | async-done | bytes 131088 | tf_op jit(solution)/shard_map/reduce_scatter | solution.py:108
  381.3 7.4 %collective-permute-done.38 = bf16[4,4,16,16,512]{4,3,2,1,0:T(8,128)(2,1)S(1)} collective-permute-done((bf16[4,4,16,16,512]{4,3,2,1,0:T(8,128)(2,1)}, bf16[4,4,16,16,512]{4,3,2,1,0:T(8,128)(2,1)S(1)}, u32[]{:S(2)}, u32[]{:S(2)}) %collective-permute-start.38) | collective-permute-done | bytes 4194336 | tf_op jit(solution)/shard_map/ppermute | solution.py:64
  395.1 14.1 %attend_back.7 = (bf16[512,512]{1,0:T(8,128)(2,1)}, f32[2,512,512]{2,1,0:T(8,128)}, f32[2,512,512]{2,1,0:T(8,128)}) custom-call(s32[18]{0:T(128)} %pad_add_fusion.9.act, s32[8,512]{1,0:T(8,128)} %pad.13.bounds, bf16[512,512]{1,0:T(8,128)(2,1)} %get-tuple-element.556.q, bf16[2,512,512]{2,1,0:T(8,128)(2,1)} %copy-done.10, ...), custom_call_target="tpu_custom_call" | custom-call | flops 1 | bytes 1 | tf_op jit(solution)/shard_map/attend_back/pallas_call | solution.py:718
  416.7 12.7 %attend_back.8 = (bf16[512,512]{1,0:T(8,128)(2,1)}, f32[2,512,512]{2,1,0:T(8,128)}, f32[2,512,512]{2,1,0:T(8,128)}) custom-call(s32[18]{0:T(128)} %pad_add_fusion.7.act, s32[8,512]{1,0:T(8,128)} %pad.12.bounds, bf16[512,512]{1,0:T(8,128)(2,1)} %get-tuple-element.551.q, bf16[2,512,512]{2,1,0:T(8,128)(2,1)} %get-tuple-element.552.kv_own, ...), custom_call_target="tpu_custom_call" | custom-call | flops 1 | bytes 1 | tf_op jit(solution)/shard_map/attend_back/pallas_call | solution.py:718
  431.9 11.6 %collective-permute-start.42 = (bf16[8,16,512]{2,1,0:T(8,128)(2,1)S(1)}, bf16[8,16,512]{2,1,0:T(8,128)(2,1)}, u32[]{:S(2)}, u32[]{:S(2)}) collective-permute-start(bf16[8,16,512]{2,1,0:T(8,128)(2,1)S(1)} %bitcast.261), channel_id=1, source_target_pairs={{0,16},{8,24},{16,0},{24,8},{1,17},{9,25},{17,1},{25,9},{2,18},{10... | collective-permute-start | bytes 393224 | tf_op jit(solution)/shard_map/ppermute | solution.py:64
  448.7 6.8 project_back.4
  458.7 10.5 %feed_back.5 = (bf16[4,512,512]{2,1,0:T(8,128)(2,1)}, bf16[4,512,512]{2,1,0:T(8,128)(2,1)}, f32[512,512]{1,0:T(8,128)}, f32[1,512]{1,0:T(1,128)}, bf16[512,512]{...) custom-call(f32[512,512]{1,0:T(8,128)} %add_add_fusion.grad, f32[512,512]{1,0:T(8,128)} %get-tuple-element.668.y, ...), custom_call_target="tpu_custom_call" | custom-call | flops 1 | bytes 1 | tf_op jit(solution)/shard_map/feed_back/pallas_call | solution.py:846
  469.2 7.6 %collect_gradients.6 = (bf16[4,4,16,16,512]{4,3,2,1,0:T(8,128)(2,1)}, bf16[4,4,16,16,512]{4,3,2,1,0:T(8,128)(2,1)}) custom-call(s32[3]{0:T(128)} %pad_add_fusion.10.me_ref, bf16[3,512,512]{2,1,0:T(8,128)(2,1)} %get-tuple-element.675.refs_0_, bf16[1,512,512]{2,1,0:T(8,128)(2,1)} %get-tuple-element.676.refs_1_, ...), custom_call_target="tpu_custom_call" | custom-call | flops 1 | bytes 1 | tf_op jit(solution)/shard_map/collect_gradients/pallas_call | solution.py:345
  476.8 14.8 %reduce-scatter.6.cloned.1.call-done = bf16[1,16,16,512]{3,2,1,0:T(8,128)(2,1)} async-done(((bf16[16,16,16,512]{3,2,1,0:T(8,128)(2,1)}), bf16[1,16,16,512]{3,2,1,0:T(8,128)(2,1)}) %reduce-scatter.6.cloned.1.call-update) | async-done | bytes 262160 | tf_op jit(solution)/shard_map/reduce_scatter | solution.py:108
  491.7 7.7 %add_convert_fusion.1 = bf16[4,4,16,16,512]{4,3,2,1,0:T(8,128)(2,1)} fusion(bf16[4,4,16,16,512]{4,3,2,1,0:T(8,128)(2,1)} %collective-permute-done.44, bf16[4,4,16,16,512]{4,3,2,1,0:T(8,128)(2,1)} %get-tuple-element.697), kind=kLoop, calls=%fused_computation.5 | loop fusion | flops 8388608 | bytes 12582912 | tf_op jit(solution)/shard_map/convert_element_type | solution.py:146
  499.3 13.8 %attend_back.9 = (bf16[512,512]{1,0:T(8,128)(2,1)}, f32[2,512,512]{2,1,0:T(8,128)}, f32[2,512,512]{2,1,0:T(8,128)}) custom-call(s32[18]{0:T(128)} %pad_add_fusion.9.act, s32[8,512]{1,0:T(8,128)} %pad.13.bounds, bf16[512,512]{1,0:T(8,128)(2,1)} %get-tuple-element.516.q, bf16[2,512,512]{2,1,0:T(8,128)(2,1)} %get-tuple-element.517.kv_own, ...), custom_call_target="tpu_custom_call" | custom-call | flops 1 | bytes 1 | tf_op jit(solution)/shard_map/attend_back/pallas_call | solution.py:718
  560.3 34.6 %collective-permute-done.47.from_x = bf16[2,4,6,16,512]{4,3,2,1,0:T(8,128)(2,1)S(1)} collective-permute-done((bf16[2,4,6,16,512]{4,3,2,1,0:T(8,128)(2,1)S(1)}, bf16[2,4,6,16,512]{4,3,2,1,0:T(8,128)(2,1)S(1)}, u32[]{:S(2)}, u32[]{:S(2)}) %collective-permute-start.47) | collective-permute-done | bytes 786464 | tf_op jit(solution)/shard_map/ppermute | solution.py:64
  605.1 8.1 %reduce-scatter.8.cloned.1.call-done = bf16[1,16,16,512]{3,2,1,0:T(8,128)(2,1)} async-done(((bf16[16,16,16,512]{3,2,1,0:T(8,128)(2,1)}), bf16[1,16,16,512]{3,2,1,0:T(8,128)(2,1)}) %reduce-scatter.8.cloned.1.call-update) | async-done | bytes 262160 | tf_op jit(solution)/shard_map/reduce_scatter | solution.py:108
  632.2 7.0 collective-permute-done.52.two
  (587 shorter events, 337.9 us)
Async XLA Ops:
  7.2 124.1 %all-gather.5.cloned.1.call-start = ((), (), s32[]{:S(2)}) async-start(), calls=%async_computation.6 | async-start | bytes 8650752 | tf_op jit(solution)/shard_map/all_gather | solution.py:1104
  11.1 18.0 %collective-permute-start.4 = (bf16[12,16,512]{2,1,0:T(8,128)(2,1)}, bf16[12,16,512]{2,1,0:T(8,128)(2,1)}, u32[]{:S(2)}, u32[]{:S(2)}) collective-permute-start(bf16[12,16,512]{2,1,0:T(8,128)(2,1)} %constant_dynamic-slice_fusion.10), channel_id=1, source_target_pairs={{0,2},{2,0},{4,6},{6,4},{1,3},{3,1},{5,7},{7,5},{8,10},{10,8},{12,... | collective-permute-start | bytes 589832 | tf_op jit(solution)/shard_map/ppermute | solution.py:64
  13.8 15.3 %collective-permute-start.5 = (bf16[12,16,512]{2,1,0:T(8,128)(2,1)}, bf16[12,16,512]{2,1,0:T(8,128)(2,1)}, u32[]{:S(2)}, u32[]{:S(2)}) collective-permute-start(bf16[12,16,512]{2,1,0:T(8,128)(2,1)} %constant_dynamic-slice_fusion.10), channel_id=1, source_target_pairs={{0,4},{2,6},{4,0},{6,2},{1,5},{3,7},{5,1},{7,3},{8,12},{10,14},{12... | collective-permute-start | bytes 589832 | tf_op jit(solution)/shard_map/ppermute | solution.py:64
  37.0 170.0 %all-gather.7.cloned.1.call-start = ((), (), s32[]{:S(2)}) async-start(), calls=%async_computation.7 | async-start | bytes 8650752 | tf_op jit(solution)/shard_map/all_gather | solution.py:1149
  39.1 18.2 %collective-permute-start.11 = (bf16[3,12,16,512]{3,2,1,0:T(8,128)(2,1)S(1)}, bf16[3,12,16,512]{3,2,1,0:T(8,128)(2,1)S(1)}, u32[]{:S(2)}, u32[]{:S(2)}) collective-permute-start(bf16[3,12,16,512]{3,2,1,0:T(8,128)(2,1)S(1)} %pad_maximum_fusion.4.refs_1_), channel_id=1, source_target_pairs={{0,8},{8,0},{16,24},{24,16},{1,9},{9,1},{17,25},{25,17},{2,10},{10... | collective-permute-start | bytes 1769480 | tf_op jit(solution)/shard_map/ppermute | solution.py:64
  40.9 27.7 %collective-permute-start.12 = (bf16[3,12,16,512]{3,2,1,0:T(8,128)(2,1)S(1)}, bf16[3,12,16,512]{3,2,1,0:T(8,128)(2,1)}, u32[]{:S(2)}, u32[]{:S(2)}) collective-permute-start(bf16[3,12,16,512]{3,2,1,0:T(8,128)(2,1)S(1)} %pad_maximum_fusion.4.refs_1_), channel_id=1, source_target_pairs={{0,16},{8,24},{16,0},{24,8},{1,17},{9,25},{17,1},{25,9},{2,18},{10... | collective-permute-start | bytes 1769480 | tf_op jit(solution)/shard_map/ppermute | solution.py:64
  42.4 26.2 %collective-permute-start.13 = (bf16[3,12,16,512]{3,2,1,0:T(8,128)(2,1)S(1)}, bf16[3,12,16,512]{3,2,1,0:T(8,128)(2,1)}, u32[]{:S(2)}, u32[]{:S(2)}) collective-permute-start(bf16[3,12,16,512]{3,2,1,0:T(8,128)(2,1)S(1)} %pad_maximum_fusion.4.refs_1_), channel_id=1, source_target_pairs={{0,24},{8,16},{16,8},{24,0},{1,25},{9,17},{17,9},{25,1},{2,26},{10... | collective-permute-start | bytes 1769480 | tf_op jit(solution)/shard_map/ppermute | solution.py:64
  50.7 18.6 %collective-permute-start.14 = (bf16[8,16,512]{2,1,0:T(8,128)(2,1)}, bf16[8,16,512]{2,1,0:T(8,128)(2,1)S(1)}, u32[]{:S(2)}, u32[]{:S(2)}) collective-permute-start(bf16[8,16,512]{2,1,0:T(8,128)(2,1)} %fusion.24), channel_id=1, source_target_pairs={{0,2},{2,0},{4,6},{6,4},{1,3},{3,1},{5,7},{7,5},{8,10},{10,8},{12,... | collective-permute-start | bytes 393224 | tf_op jit(solution)/shard_map/ppermute | solution.py:64
  53.3 16.1 %collective-permute-start.15 = (bf16[8,16,512]{2,1,0:T(8,128)(2,1)}, bf16[8,16,512]{2,1,0:T(8,128)(2,1)S(1)}, u32[]{:S(2)}, u32[]{:S(2)}) collective-permute-start(bf16[8,16,512]{2,1,0:T(8,128)(2,1)} %fusion.24), channel_id=1, source_target_pairs={{0,4},{2,6},{4,0},{6,2},{1,5},{3,7},{5,1},{7,3},{8,12},{10,14},{12... | collective-permute-start | bytes 393224 | tf_op jit(solution)/shard_map/ppermute | solution.py:64
  74.3 23.0 %collective-permute-start.22 = (bf16[3,8,16,512]{3,2,1,0:T(8,128)(2,1)S(1)}, bf16[3,8,16,512]{3,2,1,0:T(8,128)(2,1)}, u32[]{:S(2)}, u32[]{:S(2)}) collective-permute-start(bf16[3,8,16,512]{3,2,1,0:T(8,128)(2,1)S(1)} %pad_maximum_fusion.5.refs_1_), channel_id=1, source_target_pairs={{0,8},{8,0},{16,24},{24,16},{1,9},{9,1},{17,25},{25,17},{2,10},{10... | collective-permute-start | bytes 1179656 | tf_op jit(solution)/shard_map/ppermute | solution.py:64
  75.3 22.0 %collective-permute-start.23 = (bf16[3,8,16,512]{3,2,1,0:T(8,128)(2,1)S(1)}, bf16[3,8,16,512]{3,2,1,0:T(8,128)(2,1)}, u32[]{:S(2)}, u32[]{:S(2)}) collective-permute-start(bf16[3,8,16,512]{3,2,1,0:T(8,128)(2,1)S(1)} %pad_maximum_fusion.5.refs_1_), channel_id=1, source_target_pairs={{0,16},{8,24},{16,0},{24,8},{1,17},{9,25},{17,1},{25,9},{2,18},{10... | collective-permute-start | bytes 1179656 | tf_op jit(solution)/shard_map/ppermute | solution.py:64
  76.4 21.9 %collective-permute-start.24 = (bf16[3,8,16,512]{3,2,1,0:T(8,128)(2,1)S(1)}, bf16[3,8,16,512]{3,2,1,0:T(8,128)(2,1)}, u32[]{:S(2)}, u32[]{:S(2)}) collective-permute-start(bf16[3,8,16,512]{3,2,1,0:T(8,128)(2,1)S(1)} %pad_maximum_fusion.5.refs_1_), channel_id=1, source_target_pairs={{0,24},{8,16},{16,8},{24,0},{1,25},{9,17},{17,9},{25,1},{2,26},{10... | collective-permute-start | bytes 1179656 | tf_op jit(solution)/shard_map/ppermute | solution.py:64
  114.8 266.5 %reduce-scatter.4.cloned.1.call-start = ((), (), s32[]{:S(2)}) async-start(), calls=%async_computation.3 | async-start | bytes 2228224 | tf_op jit(solution)/shard_map/reduce_scatter | solution.py:108
  145.0 18.7 %collective-permute-start.32 = (bf16[2,512,512]{2,1,0:T(8,128)(2,1)S(1)}, bf16[2,512,512]{2,1,0:T(8,128)(2,1)}, u32[]{:S(2)}, u32[]{:S(2)}) collective-permute-start(bf16[2,512,512]{2,1,0:T(8,128)(2,1)S(1)} %pad_maximum_fusion.kv_own), channel_id=1, source_target_pairs={{0,1},{1,0},{2,3},{3,2},{4,5},{5,4},{6,7},{7,6},{8,9},{9,8},{10,11... | collective-permute-start | bytes 3145736 | tf_op jit(solution)/shard_map/ppermute | solution.py:64
  219.1 18.9 %collective-permute-start.34 = (bf16[2,512,512]{2,1,0:T(8,128)(2,1)S(1)}, bf16[2,512,512]{2,1,0:T(8,128)(2,1)}, u32[]{:S(2)}, u32[]{:S(2)}) collective-permute-start(bf16[2,512,512]{2,1,0:T(8,128)(2,1)S(1)} %pad_maximum_fusion.1.kv_own), channel_id=1, source_target_pairs={{0,1},{1,0},{2,3},{3,2},{4,5},{5,4},{6,7},{7,6},{8,9},{9,8},{10,11... | collective-permute-start | bytes 3145736 | tf_op jit(solution)/shard_map/ppermute | solution.py:64
  293.4 198.2 %reduce-scatter.6.cloned.1.call-start = ((), (), s32[]{:S(2)}) async-start(), calls=%async_computation.4 | async-start | bytes 4456448 | tf_op jit(solution)/shard_map/reduce_scatter | solution.py:108
  329.0 27.6 %collective-permute-start.37 = (f32[2,512,512]{2,1,0:T(8,128)}, f32[2,512,512]{2,1,0:T(8,128)}, u32[]{:S(2)}, u32[]{:S(2)}) collective-permute-start(f32[2,512,512]{2,1,0:T(8,128)} %get-tuple-element.631), channel_id=1, source_target_pairs={{0,1},{1,0},{2,3},{3,2},{4,5},{5,4},{6,7},{7,6},{8,9},{9,8},{10,11... | collective-permute-start | bytes 6291464 | tf_op jit(solution)/shard_map/ppermute | solution.py:64
  395.0 218.2 %reduce-scatter.8.cloned.1.call-start = ((), (), s32[]{:S(2)}) async-start(), calls=%async_computation.5 | async-start | bytes 4456448 | tf_op jit(solution)/shard_map/reduce_scatter | solution.py:108
  409.2 34.4 %collective-permute-start.40 = (f32[2,512,512]{2,1,0:T(8,128)}, f32[2,512,512]{2,1,0:T(8,128)}, u32[]{:S(2)}, u32[]{:S(2)}) collective-permute-start(f32[2,512,512]{2,1,0:T(8,128)} %get-tuple-element.659), channel_id=1, source_target_pairs={{0,1},{1,0},{2,3},{3,2},{4,5},{5,4},{6,7},{7,6},{8,9},{9,8},{10,11... | collective-permute-start | bytes 6291464 | tf_op jit(solution)/shard_map/ppermute | solution.py:64
  429.4 19.3 %collective-permute-start.39 = (f32[2,512,512]{2,1,0:T(8,128)}, f32[2,512,512]{2,1,0:T(8,128)}, u32[]{:S(2)}, u32[]{:S(2)}) collective-permute-start(f32[2,512,512]{2,1,0:T(8,128)} %get-tuple-element.653), channel_id=1, source_target_pairs={{0,1},{1,0},{2,3},{3,2},{4,5},{5,4},{6,7},{7,6},{8,9},{9,8},{10,11... | collective-permute-start | bytes 6291464 | tf_op jit(solution)/shard_map/ppermute | solution.py:64
  430.6 26.5 %collective-permute-start.41 = (bf16[8,16,512]{2,1,0:T(8,128)(2,1)S(1)}, bf16[8,16,512]{2,1,0:T(8,128)(2,1)S(1)}, u32[]{:S(2)}, u32[]{:S(2)}) collective-permute-start(bf16[8,16,512]{2,1,0:T(8,128)(2,1)S(1)} %bitcast.260), channel_id=1, source_target_pairs={{0,8},{8,0},{16,24},{24,16},{1,9},{9,1},{17,25},{25,17},{2,10},{10... | collective-permute-start | bytes 393224 | tf_op jit(solution)/shard_map/ppermute | solution.py:64
  431.9 25.1 %collective-permute-start.42 = (bf16[8,16,512]{2,1,0:T(8,128)(2,1)S(1)}, bf16[8,16,512]{2,1,0:T(8,128)(2,1)}, u32[]{:S(2)}, u32[]{:S(2)}) collective-permute-start(bf16[8,16,512]{2,1,0:T(8,128)(2,1)S(1)} %bitcast.261), channel_id=1, source_target_pairs={{0,16},{8,24},{16,0},{24,8},{1,17},{9,25},{17,1},{25,9},{2,18},{10... | collective-permute-start | bytes 393224 | tf_op jit(solution)/shard_map/ppermute | solution.py:64
  554.5 42.3 %collective-permute-start.48 = (bf16[2,4,7,16,512]{4,3,2,1,0:T(8,128)(2,1)S(1)}, bf16[2,4,7,16,512]{4,3,2,1,0:T(8,128)(2,1)S(1)}, u32[]{:S(2)}, u32[]{:S(2)}) collective-permute-start(bf16[2,4,7,16,512]{4,3,2,1,0:T(8,128)(2,1)S(1)} %fusion.15), channel_id=1, source_target_pairs={{0,16},{16,0},{1,17},{17,1},{2,18},{18,2},{3,19},{19,3},{4,20},{20... | collective-permute-start | bytes 2752520 | tf_op jit(solution)/shard_map/ppermute | solution.py:64
  555.8 39.1 %collective-permute-start.47 = (bf16[2,4,6,16,512]{4,3,2,1,0:T(8,128)(2,1)S(1)}, bf16[2,4,6,16,512]{4,3,2,1,0:T(8,128)(2,1)S(1)}, u32[]{:S(2)}, u32[]{:S(2)}) collective-permute-start(bf16[2,4,6,16,512]{4,3,2,1,0:T(8,128)(2,1)S(1)} %fusion.17), channel_id=1, source_target_pairs={{0,8},{8,0},{1,9},{9,1},{2,10},{10,2},{3,11},{11,3},{4,12},{12,4},... | collective-permute-start | bytes 2359304 | tf_op jit(solution)/shard_map/ppermute | solution.py:64
  600.3 17.3 %collective-permute-start.50 = (bf16[4,7,16,512]{3,2,1,0:T(8,128)(2,1)S(1)}, bf16[4,7,16,512]{3,2,1,0:T(8,128)(2,1)}, u32[]{:S(2)}, u32[]{:S(2)}) collective-permute-start(bf16[4,7,16,512]{3,2,1,0:T(8,128)(2,1)S(1)} %fusion.16), channel_id=1, source_target_pairs={{0,8},{8,0},{1,9},{9,1},{2,10},{10,2},{3,11},{11,3},{4,12},{12,4},... | collective-permute-start | bytes 1376264 | tf_op jit(solution)/shard_map/ppermute | solution.py:64
  600.4 16.6 %collective-permute-start.49 = (bf16[4,6,16,512]{3,2,1,0:T(8,128)(2,1)}, bf16[4,6,16,512]{3,2,1,0:T(8,128)(2,1)}, u32[]{:S(2)}, u32[]{:S(2)}) collective-permute-start(bf16[4,6,16,512]{3,2,1,0:T(8,128)(2,1)} %fusion.18), channel_id=1, source_target_pairs={{0,16},{16,0},{1,17},{17,1},{2,18},{18,2},{3,19},{19,3},{4,20},{20... | collective-permute-start | bytes 1179656 | tf_op jit(solution)/shard_map/ppermute | solution.py:64
  602.2 53.8 %collective-permute-start.59 = (bf16[16,16,512]{2,1,0:T(8,128)(2,1)S(1)}, bf16[16,16,512]{2,1,0:T(8,128)(2,1)S(1)}, u32[]{:S(2)}, u32[]{:S(2)}) collective-permute-start(bf16[16,16,512]{2,1,0:T(8,128)(2,1)S(1)} %bitcast.250), channel_id=1, source_target_pairs={{0,8},{8,0},{16,24},{24,16},{1,9},{9,1},{17,25},{25,17},{2,10},{10... | collective-permute-start | bytes 786440 | tf_op jit(solution)/shard_map/ppermute | solution.py:64
  604.1 57.2 %collective-permute-start.60 = (bf16[16,16,512]{2,1,0:T(8,128)(2,1)S(1)}, bf16[16,16,512]{2,1,0:T(8,128)(2,1)S(1)}, u32[]{:S(2)}, u32[]{:S(2)}) collective-permute-start(bf16[16,16,512]{2,1,0:T(8,128)(2,1)S(1)} %bitcast.251), channel_id=1, source_target_pairs={{0,16},{8,24},{16,0},{24,8},{1,17},{9,25},{17,1},{25,9},{2,18},{10... | collective-permute-start | bytes 786440 | tf_op jit(solution)/shard_map/ppermute | solution.py:64
  620.7 18.4 %collective-permute-start.52 = (bf16[13,16,512]{2,1,0:T(8,128)(2,1)}, bf16[13,16,512]{2,1,0:T(8,128)(2,1)S(1)}, u32[]{:S(2)}, u32[]{:S(2)}) collective-permute-start(bf16[13,16,512]{2,1,0:T(8,128)(2,1)} %get-tuple-element.761), channel_id=1, source_target_pairs={{0,4},{2,6},{4,0},{6,2},{1,5},{3,7},{5,1},{7,3},{8,12},{10,14},{12... | collective-permute-start | bytes 638984 | tf_op jit(solution)/shard_map/ppermute | solution.py:64
  623.3 17.6 %collective-permute-start.53 = (bf16[13,16,512]{2,1,0:T(8,128)(2,1)}, bf16[13,16,512]{2,1,0:T(8,128)(2,1)S(1)}, u32[]{:S(2)}, u32[]{:S(2)}) collective-permute-start(bf16[13,16,512]{2,1,0:T(8,128)(2,1)} %get-tuple-element.762), channel_id=1, source_target_pairs={{0,6},{2,4},{4,2},{6,0},{1,7},{3,5},{5,3},{7,1},{8,14},{10,12},{12... | collective-permute-start | bytes 638984 | tf_op jit(solution)/shard_map/ppermute | solution.py:64
  629.9 32.4 %collective-permute-start.61 = (bf16[16,16,512]{2,1,0:T(8,128)(2,1)S(1)}, bf16[16,16,512]{2,1,0:T(8,128)(2,1)S(1)}, u32[]{:S(2)}, u32[]{:S(2)}) collective-permute-start(bf16[16,16,512]{2,1,0:T(8,128)(2,1)S(1)} %bitcast.252), channel_id=1, source_target_pairs={{0,24},{8,16},{16,8},{24,0},{1,25},{9,17},{17,9},{25,1},{2,26},{10... | collective-permute-start | bytes 786440 | tf_op jit(solution)/shard_map/ppermute | solution.py:64
  639.1 28.5 %collective-permute-start.62 = (bf16[16,16,512]{2,1,0:T(8,128)(2,1)S(1)}, bf16[16,16,512]{2,1,0:T(8,128)(2,1)}, u32[]{:S(2)}, u32[]{:S(2)}) collective-permute-start(bf16[16,16,512]{2,1,0:T(8,128)(2,1)S(1)} %bitcast.254), channel_id=1, source_target_pairs={{0,8},{8,0},{16,24},{24,16},{1,9},{9,1},{17,25},{25,17},{2,10},{10... | collective-permute-start | bytes 786440 | tf_op jit(solution)/shard_map/ppermute | solution.py:64
  (155 other events, 1713.6 us)
Sparse Core Ops, SparseCore 0:
  37.1 90.2 all-gather.4
  130.9 75.9 all-gather.6
  293.6 87.6 reduce-scatter.3
  395.1 96.4 reduce-scatter.5
  515.2 97.9 reduce-scatter.7

commit v5 on v4

--- a/solution.py
+++ b/solution.py
@@ -45,14 +45,14 @@
 GATHERED = (
     (TABLE,) + attention_parts(0),
     feed_parts(0),
-    attention_parts(1) + attention_parts(2) + feed_parts(1),
-    attention_parts(3) + attention_parts(4) + feed_parts(2),
+    attention_parts(1) + attention_parts(2) + feed_parts(1) + attention_parts(3),
+    attention_parts(4) + feed_parts(2),
 )
 REDUCED = (
     feed_parts(2),
     attention_parts(3) + attention_parts(4) + feed_parts(1),
     attention_parts(1) + attention_parts(2) + feed_parts(0),
-    (TABLE,) + attention_parts(0) + (("gains", 0, "row"),),
+    (TABLE,) + attention_parts(0),
 )
 
 
@@ -426,6 +426,17 @@
     yield []
 
 
+def small_stages(mover, x, z):
+    for axis in ("c", "sx", "sy"):
+        mover.held = [x]
+        yield [(x, (axis,))]
+        x = mover.held[0] + mover.arrived[0]
+    mover.held = [x]
+    yield [(x, ("z", bit)) for bit in (1, 2, 3)]
+    mover.result = jnp.sum(in_order(jnp.stack(mover.held + mover.arrived), z), axis=0)
+    yield []
+
+
 def settle_kernel(sizes, plan, unit, me_ref, *refs):
     buckets, outs, sem = refs[:sizes], refs[sizes:-1], refs[-1]
     s = me_ref[2]
@@ -574,10 +585,14 @@
                 jnp.sum(total[h], axis=1, keepdims=True), total.shape[1:]
             )
             o[rows, h * 128 : h * 128 + 128] = pair_lanes(acc[h] / denom).astype(o.dtype)
-            level = top[h] + jnp.log(denom)
             for part in range(2):
-                own = jnp.where(square == along, level[part * BQ : part * BQ + BQ], 0.0)
-                lse[b, h, :, part * BQ : part * BQ + BQ] = jnp.sum(own, axis=0, keepdims=True)
+                span = slice(part * BQ, part * BQ + BQ)
+
+                def line(level, span=span):
+                    own = jnp.where(square == along, level[span], 0.0)
+                    return jnp.sum(own, axis=0, keepdims=True)
+
+                lse[b, h, :, span] = line(top[h]) + jnp.log(line(denom))
         return 0
 
     lax.fori_loop(0, blocks, one_block, 0)
@@ -760,6 +775,12 @@
     kv[1] = low(dot32(a, w[2], NN))
 
 
+def pair_kernel(memory, w, kv):
+    m = memory[...]
+    kv[0] = low(dot32(m, w[1], NN))
+    kv[1] = low(dot32(m, w[2], NN))
+
+
 def between_kernel(o, w_out, x, gain, w, y, normed, q):
     state = x[...] + dot32(o[...], w_out[0], NN)
     y[...] = state
@@ -875,6 +896,10 @@
         [shaped((), x, HALF), shaped((), x, HALF), shaped((2,), x, HALF)],
         x, gain[None], w,
     )
+
+
+def memory_pair(memory, w):
+    return on_chip(pair_kernel, "memory_pair", [shaped((2,), memory, HALF)], memory, w)[0]
 
 
 def between(o, w_out, x, gain, w):
@@ -999,7 +1024,6 @@
         "down": down_weight,
     }
     shard_shapes = {name: array.shape[1:] for name, array in shard_of.items()}
-    shard_shapes["gains"] = (gain_dev, COL)
     weights = {}
 
     def layout(entries):
@@ -1161,13 +1185,13 @@
         if fast and layer_id == 0:
             (x, memory), third = hold((x, memory), third)
             settle(GATHERED[2], unpack(third, *layout(GATHERED[2]), unit, owners))
+        kept_self = (x, *project(x, gains_full[base], weights["qkv", slot]))
+        o, saved_self = attend_forward(masks, True, *kept_self[2:])
         if fast and layer_id == 1:
-            x, fourth = hold(x, fourth)
+            o, fourth = hold(o, fourth)
             settle(GATHERED[3], unpack(fourth, *layout(GATHERED[3]), unit, owners))
         cross = weights["qkv", slot + 1]
-        pair = jnp.stack([low(product(memory, cross[1])), low(product(memory, cross[2]))])
-        kept_self = (x, *project(x, gains_full[base], weights["qkv", slot]))
-        o, saved_self = attend_forward(masks, True, *kept_self[2:])
+        pair = memory_pair(memory, cross)
         *kept_cross, q = between(o, weights["out", slot], x, gains_full[base + 1], cross)
         o, saved_cross = attend_forward(masks, False, q, pair)
         feed_at = ENC + layer_id
@@ -1296,27 +1320,31 @@
     grads["table", 0] = table_grad
 
     gain_grad = jnp.concatenate([part.reshape(1, -1) for part in gain_parts])
-    grads["gains", 0] = low(jnp.pad(gain_grad.T, ((0, 0), (0, COL - gain_count))))[None]
+    small = jnp.concatenate([gain_grad, jnp.full((1, width), loss_part)])
 
     reduced = {}
     if fast:
         last = reduce(REDUCED[3])
-        loss_part = step(loss_part, last)
-        loss_part = step(loss_part, last)
-        loss_part = step(loss_part, last, middle)
-        loss_part = step(loss_part, last)
+        tiny = Mover()
+        tiny.stages = small_stages(tiny, small, z)
+        loss_part = step(loss_part, last, tiny)
+        loss_part = step(loss_part, last, tiny)
+        loss_part = step(loss_part, last, tiny, middle)
+        loss_part = step(loss_part, last, tiny)
         movers = (feed_mover, late, middle, last)
-        loss_part = step(loss_part, last)
-        squares = sum(mover.squares for mover in movers)
-        squares, loss_total = all_sum(jnp.stack([squares, loss_part]))
+        loss_part = step(loss_part, last, tiny)
+        gain_grad, loss_total = tiny.result[:-1], tiny.result[-1, 0]
+        squares = all_sum(sum(mover.squares for mover in movers))
         squares = step(squares, late, middle, last)
     else:
-        squares = sum(reduce_plainly(entries) for entries in REDUCED)
-        squares, loss_total = all_sum(jnp.stack([squares, loss_part]))
+        small = all_sum(small)
+        gain_grad, loss_total = small[:-1], small[-1, 0]
+        squares = all_sum(sum(reduce_plainly(entries) for entries in REDUCED))
+    squares = squares + jnp.sum(gain_grad * gain_grad)
     grad_norm = jnp.sqrt(squares)
     clip_factor = CLIP_NORM / jnp.maximum(grad_norm, CLIP_NORM)
 
-    names = ("qkv", "out", "up", "down", "table", "gains")
+    names = ("qkv", "out", "up", "down", "table")
     if fast:
         plan = []
         for bucket, entries in enumerate(REDUCED):
@@ -1325,7 +1353,7 @@
                 plan.append((bucket, first, count, kind, names.index(name), i))
                 first += count
         parts = [part for mover in movers for part in mover.result]
-        shapes = [shard_of[name].shape for name in names[:-1]] + [(1, gain_dev, COL)]
+        shapes = [shard_of[name].shape for name in names]
         placed = pl.pallas_call(
             functools.partial(settle_kernel, len(parts), tuple(plan), unit),
             out_shape=[jax.ShapeDtypeStruct(shape, jnp.bfloat16) for shape in shapes],
@@ -1338,12 +1366,12 @@
         ready = [wide(array) for array in placed]
     else:
         ready = [
-            wide(jnp.stack([reduced[name, i] for i in range(len(shard_of.get(name, "1")))]))
+            wide(jnp.stack([reduced[name, i] for i in range(shard_of[name].shape[0])]))
             for name in names
         ]
     gradients = (
         *ready[:4],
-        ready[5][0, :, :gain_count].T,
+        lax.dynamic_slice_in_dim(gain_grad, (2 * z + c) * gain_dev, gain_dev, 1),
         ready[4][0],
     )
     masters = (qkv_weight, out_weight, up_weight, down_weight, norm_gains, embed_table)

time: 722 us -> 722 us (level)
  Pallas kernels: 290 us -> 310 us
  waiting for transfers between devices: 178 us -> 166 us
    all_gather x1, waiting for transfers between devices: 26.3 us -> 0.02 us  [shards(): lax.all_gather(fourth, PLANE + LINE).reshape(4, owners, *fourth.shape)]
    pallas_call x5, Pallas kernels: 67.3 us -> 76 us  [attend_back(): pl.pallas_call(attend_back_kernel, out_shape=[jax.ShapeDtypeStruct((n, wi...]
    pallas_call x18 -> x20, Pallas kernels: 113 us -> 120 us  [on_chip(): pl.pallas_call(kernel, out_shape=[jax.ShapeDtypeStruct(shape, kind) for s...]
    ppermute x68 -> x74, waiting for transfers between devices: 117 us -> 125 us  [flip(): return lax.ppermute(x, axis, [(i, i ^ bit) for i in range(n)])]
    ppermute x68 -> x74, starting transfers between devices: 84.4 us -> 77.4 us  [flip(): return lax.ppermute(x, axis, [(i, i ^ bit) for i in range(n)])]
    convert_element_type x9 -> x8, other arithmetic: 26.3 us -> 26.3 us  [low(): return v.astype(jnp.bfloat16)]
  transfers between devices with their start and end apart: 73 -> 79, of which waited for: 31 -> 30; matrix products, arithmetic and copies ran while one was open for 10% -> 9% of each run, Pallas kernels for 32% -> 35%
where the time goes in v5:
time: 722 us; the launch traced here: 713 us
  Pallas kernels  310 us (43%)
  waiting for transfers between devices  166 us (23%)
  starting transfers between devices  77.8 us (11%)
  other arithmetic  67.1 us (9%)
  local copies, waits for them, and re-layouts  44.4 us (6%)
  between operations  25.2 us (3%)
  matrix products  22 us (3%)
    ppermute x74, waiting for transfers between devices, flip(): return lax.ppermute(x, axis, [(i, i ^ bit) for i in range(n)])  125 us
    pallas_call x20, Pallas kernels, on_chip(): pl.pallas_call(kernel, out_shape=[jax.ShapeDtypeStruct(shape, kind) for s...  120 us
    ppermute x74, starting transfers between devices, flip(): return lax.ppermute(x, axis, [(i, i ^ bit) for i in range(n)])  77.4 us
    pallas_call x5, Pallas kernels, attend_back(): pl.pallas_call(attend_back_kernel, out_shape=[jax.ShapeDtypeStruct((n, wi...  76 us
    pallas_call x5, Pallas kernels, attend(): pl.pallas_call(attend_kernel, out_shape=[jax.ShapeDtypeStruct((n, width),...  53.4 us
    reduce_scatter x3, waiting for transfers between devices, step(): lax.psum_scatter(array, PLANE + ('z',), scatter_dimension=0, tiled=True)  36.4 us
    pallas_call x4, Pallas kernels, collect(): pl.pallas_call(functools.partial(collect_kernel, plan, unit, ordered), ou...  26.5 us
    convert_element_type x8, other arithmetic, low(): return v.astype(jnp.bfloat16)  26.3 us
  transfers between devices with their start and end apart: 79, of which 30 were waited for; matrix products, arithmetic and copies ran while one was open for 9% of the time, Pallas kernels for 35%

profile of v5, /device:TPU:0, one launch (start us, length us, event | category | flops | bytes accessed | tf_op | source)
XLA Modules:
  0.0 712.6 jit_solution(14398280486537322954)
XLA Ops:
  58.6 11.0 %collective-permute-done.12.refs_3_ = bf16[3,12,16,512]{3,2,1,0:T(8,128)(2,1)} collective-permute-done((bf16[3,12,16,512]{3,2,1,0:T(8,128)(2,1)S(1)}, bf16[3,12,16,512]{3,2,1,0:T(8,128)(2,1)}, u32[]{:S(2)}, u32[]{:S(2)}) %collective-permute-start.12) | collective-permute-done | bytes 589856 | tf_op jit(solution)/shard_map/ppermute | solution.py:64
  85.0 6.7 gather_fusion
  107.3 11.1 %attend.5 = (bf16[512,512]{1,0:T(8,128)(2,1)}, f32[4,4,1,256]{3,2,1,0:T(1,128)}) custom-call(s32[18]{0:T(128)} %pad_add_fusion.7.act, s32[8,512]{1,0:T(8,128)} %pad.7.bounds, bf16[512,512]{1,0:T(8,128)(2,1)} %get-tuple-element.527.q, bf16[2,512,512]{2,1,0:T(8,128)(2,1)} %get-tuple-element.528.kv_own, bf16[2,512,512]{2,1,0:T(8,128)(2,1)} %copy-done.10), custom_call_target="tpu_custom_call" | custom-call | flops 1 | bytes 1 | tf_op jit(solution)/shard_map/attend/pallas_call | solution.py:705
  126.0 7.2 %feed.3 = (f32[512,512]{1,0:T(8,128)}, bf16[512,512]{1,0:T(8,128)(2,1)}, bf16[4,512,512]{2,1,0:T(8,128)(2,1)}, f32[512,512]{1,0:T(8,128)}) custom-call(bf16[512,512]{1,0:T(8,128)(2,1)} %get-tuple-element.542.o, bf16[1,512,512]{2,1,0:T(8,128)(2,1)} %get-tuple-element.543.w_out, f32[512,512]{1,0:T(8,128)} %get-tuple-element.715.x, f32[1,512]{1,0:T(1,128)} %slice.247.gain, ...), custom_call_target="tpu_custom_call" | custom-call | flops 1 | bytes 1 | tf_op jit(solution)/shard_map/feed/pallas_call | solution.py:867
  141.9 8.1 %place_gathered.2 = (bf16[3,8,4,16,512]{4,3,2,1,0:T(8,128)(2,1)}, bf16[1,8,4,16,512]{4,3,2,1,0:T(8,128)(2,1)}, bf16[3,8,4,16,512]{4,3,2,1,0:T(8,128)(2,1)}, bf16...) custom-call(bf16[4,8,20,16,512]{4,3,2,1,0:T(8,128)(2,1)} %bitcast.181), custom_call_target="tpu_custom_call" | custom-call | flops 1 | bytes 1 | tf_op jit(solution)/shard_map/place_gathered/pallas_call | solution.py:302
  162.0 9.9 %attend.6 = (bf16[512,512]{1,0:T(8,128)(2,1)}, f32[4,4,1,256]{3,2,1,0:T(1,128)}) custom-call(s32[18]{0:T(128)} %pad_add_fusion.10.act, s32[8,512]{1,0:T(8,128)} %pad.8.bounds, bf16[512,512]{1,0:T(8,128)(2,1)} %get-tuple-element.562.q, bf16[2,512,512]{2,1,0:T(8,128)(2,1)} %get-tuple-element.563.kv_own, bf16[2,512,512]{2,1,0:T(8,128)(2,1)} %copy-done.11), custom_call_target="tpu_custom_call" | custom-call | flops 1 | bytes 1 | tf_op jit(solution)/shard_map/attend/pallas_call | solution.py:705
  176.8 11.1 %attend.7 = (bf16[512,512]{1,0:T(8,128)(2,1)}, f32[4,4,1,256]{3,2,1,0:T(1,128)}) custom-call(s32[18]{0:T(128)} %pad_add_fusion.7.act, s32[8,512]{1,0:T(8,128)} %pad.7.bounds, bf16[512,512]{1,0:T(8,128)(2,1)} %get-tuple-element.567.q, bf16[2,512,512]{2,1,0:T(8,128)(2,1)} %memory_pair.2.kv_own, bf16[2,512,512]{2,1,0:T(8,128)(2,1)} %copy-done.12), custom_call_target="tpu_custom_call" | custom-call | flops 1 | bytes 1 | tf_op jit(solution)/shard_map/attend/pallas_call | solution.py:705
  187.9 7.8 %feed.4 = (f32[512,512]{1,0:T(8,128)}, bf16[512,512]{1,0:T(8,128)(2,1)}, bf16[4,512,512]{2,1,0:T(8,128)(2,1)}, f32[512,512]{1,0:T(8,128)}) custom-call(bf16[512,512]{1,0:T(8,128)(2,1)} %get-tuple-element.569.o, bf16[1,512,512]{2,1,0:T(8,128)(2,1)} %bitcast.219, f32[512,512]{1,0:T(8,128)} %get-tuple-element.571.x.y, f32[1,512]{1,0:T(1,128)} %slice.254.gain, ...), custom_call_target="tpu_custom_call" | custom-call | flops 1 | bytes 1 | tf_op jit(solution)/shard_map/feed/pallas_call | solution.py:867
  203.3 9.9 %attend.8 = (bf16[512,512]{1,0:T(8,128)(2,1)}, f32[4,4,1,256]{3,2,1,0:T(1,128)}) custom-call(s32[18]{0:T(128)} %pad_add_fusion.10.act, s32[8,512]{1,0:T(8,128)} %pad.8.bounds, bf16[512,512]{1,0:T(8,128)(2,1)} %get-tuple-element.576.q, bf16[2,512,512]{2,1,0:T(8,128)(2,1)} %get-tuple-element.577.kv_own, bf16[2,512,512]{2,1,0:T(8,128)(2,1)} %copy-done.13), custom_call_target="tpu_custom_call" | custom-call | flops 1 | bytes 1 | tf_op jit(solution)/shard_map/attend/pallas_call | solution.py:705
  231.8 11.4 %attend.9 = (bf16[512,512]{1,0:T(8,128)(2,1)}, f32[4,4,1,256]{3,2,1,0:T(1,128)}) custom-call(s32[18]{0:T(128)} %pad_add_fusion.7.act, s32[8,512]{1,0:T(8,128)} %pad.7.bounds, bf16[512,512]{1,0:T(8,128)(2,1)} %get-tuple-element.584.q, bf16[2,512,512]{2,1,0:T(8,128)(2,1)} %memory_pair.3.kv_own, bf16[2,512,512]{2,1,0:T(8,128)(2,1)} %copy-done.14), custom_call_target="tpu_custom_call" | custom-call | flops 1 | bytes 1 | tf_op jit(solution)/shard_map/attend/pallas_call | solution.py:705
  243.2 7.0 feed.5
  263.0 10.5 %feed_back.3 = (bf16[4,512,512]{2,1,0:T(8,128)(2,1)}, bf16[4,512,512]{2,1,0:T(8,128)(2,1)}, f32[512,512]{1,0:T(8,128)}, f32[1,512]{1,0:T(1,128)}, bf16[512,512]{...) custom-call(f32[512,512]{1,0:T(8,128)} %add_add_fusion.2.grad, f32[512,512]{1,0:T(8,128)} %get-tuple-element.596.y, ...), custom_call_target="tpu_custom_call" | custom-call | flops 1 | bytes 1 | tf_op jit(solution)/shard_map/feed_back/pallas_call | solution.py:867
  286.6 16.0 %attend_back.5 = (bf16[512,512]{1,0:T(8,128)(2,1)}, f32[2,512,512]{2,1,0:T(8,128)}, f32[2,512,512]{2,1,0:T(8,128)}) custom-call(s32[18]{0:T(128)} %pad_add_fusion.7.act, s32[8,512]{1,0:T(8,128)} %pad.7.bounds, bf16[512,512]{1,0:T(8,128)(2,1)} %get-tuple-element.584.q, bf16[2,512,512]{2,1,0:T(8,128)(2,1)} %memory_pair.3.kv_own, ...), custom_call_target="tpu_custom_call" | custom-call | flops 1 | bytes 1 | tf_op jit(solution)/shard_map/attend_back/pallas_call | solution.py:733
  307.8 13.9 %attend_back.6 = (bf16[512,512]{1,0:T(8,128)(2,1)}, f32[2,512,512]{2,1,0:T(8,128)}, f32[2,512,512]{2,1,0:T(8,128)}) custom-call(s32[18]{0:T(128)} %pad_add_fusion.10.act, s32[8,512]{1,0:T(8,128)} %pad.8.bounds, bf16[512,512]{1,0:T(8,128)(2,1)} %get-tuple-element.576.q, bf16[2,512,512]{2,1,0:T(8,128)(2,1)} %get-tuple-element.577.kv_own, ...), custom_call_target="tpu_custom_call" | custom-call | flops 1 | bytes 1 | tf_op jit(solution)/shard_map/attend_back/pallas_call | solution.py:733
  329.7 6.8 project_back.3
  339.3 10.5 %feed_back.4 = (bf16[4,512,512]{2,1,0:T(8,128)(2,1)}, bf16[4,512,512]{2,1,0:T(8,128)(2,1)}, f32[512,512]{1,0:T(8,128)}, f32[1,512]{1,0:T(1,128)}, bf16[512,512]{...) custom-call(f32[512,512]{1,0:T(8,128)} %fusion.6.grad, f32[512,512]{1,0:T(8,128)} %get-tuple-element.626.y, ...), custom_call_target="tpu_custom_call" | custom-call | flops 1 | bytes 1 | tf_op jit(solution)/shard_map/feed_back/pallas_call | solution.py:867
  355.0 7.6 %collect_gradients.5 = (bf16[4,4,16,16,512]{4,3,2,1,0:T(8,128)(2,1)}, bf16[4,4,16,16,512]{4,3,2,1,0:T(8,128)(2,1)}) custom-call(s32[3]{0:T(128)} %pad_add_fusion.9.me_ref, bf16[3,512,512]{2,1,0:T(8,128)(2,1)} %get-tuple-element.639.refs_0_, bf16[1,512,512]{2,1,0:T(8,128)(2,1)} %get-tuple-element.640.refs_1_, ...), custom_call_target="tpu_custom_call" | custom-call | flops 1 | bytes 1 | tf_op jit(solution)/shard_map/collect_gradients/pallas_call | solution.py:345
  362.7 16.1 %reduce-scatter.4.cloned.1.call-done = bf16[1,8,16,512]{3,2,1,0:T(8,128)(2,1)} async-done(((bf16[16,8,16,512]{3,2,1,0:T(8,128)(2,1)}), bf16[1,8,16,512]{3,2,1,0:T(8,128)(2,1)}) %reduce-scatter.4.cloned.1.call-update) | async-done | bytes 131088 | tf_op jit(solution)/shard_map/reduce_scatter | solution.py:108
  378.7 7.4 %collective-permute-done.38 = bf16[4,4,16,16,512]{4,3,2,1,0:T(8,128)(2,1)S(1)} collective-permute-done((bf16[4,4,16,16,512]{4,3,2,1,0:T(8,128)(2,1)}, bf16[4,4,16,16,512]{4,3,2,1,0:T(8,128)(2,1)S(1)}, u32[]{:S(2)}, u32[]{:S(2)}) %collective-permute-start.38) | collective-permute-done | bytes 4194336 | tf_op jit(solution)/shard_map/ppermute | solution.py:64
  386.1 6.4 add_convert_fusion.2
  392.5 16.3 %attend_back.7 = (bf16[512,512]{1,0:T(8,128)(2,1)}, f32[2,512,512]{2,1,0:T(8,128)}, f32[2,512,512]{2,1,0:T(8,128)}) custom-call(s32[18]{0:T(128)} %pad_add_fusion.7.act, s32[8,512]{1,0:T(8,128)} %pad.7.bounds, bf16[512,512]{1,0:T(8,128)(2,1)} %get-tuple-element.567.q, bf16[2,512,512]{2,1,0:T(8,128)(2,1)} %memory_pair.2.kv_own, ...), custom_call_target="tpu_custom_call" | custom-call | flops 1 | bytes 1 | tf_op jit(solution)/shard_map/attend_back/pallas_call | solution.py:733
  414.0 13.8 %attend_back.8 = (bf16[512,512]{1,0:T(8,128)(2,1)}, f32[2,512,512]{2,1,0:T(8,128)}, f32[2,512,512]{2,1,0:T(8,128)}) custom-call(s32[18]{0:T(128)} %pad_add_fusion.10.act, s32[8,512]{1,0:T(8,128)} %pad.8.bounds, bf16[512,512]{1,0:T(8,128)(2,1)} %get-tuple-element.562.q, bf16[2,512,512]{2,1,0:T(8,128)(2,1)} %get-tuple-element.563.kv_own, ...), custom_call_target="tpu_custom_call" | custom-call | flops 1 | bytes 1 | tf_op jit(solution)/shard_map/attend_back/pallas_call | solution.py:733
  440.7 6.8 project_back.4
  450.7 10.5 %feed_back.5 = (bf16[4,512,512]{2,1,0:T(8,128)(2,1)}, bf16[4,512,512]{2,1,0:T(8,128)(2,1)}, f32[512,512]{1,0:T(8,128)}, f32[1,512]{1,0:T(1,128)}, bf16[512,512]{...) custom-call(f32[512,512]{1,0:T(8,128)} %add_add_fusion.grad, f32[512,512]{1,0:T(8,128)} %get-tuple-element.680.y, ...), custom_call_target="tpu_custom_call" | custom-call | flops 1 | bytes 1 | tf_op jit(solution)/shard_map/feed_back/pallas_call | solution.py:867
  461.2 7.6 %collect_gradients.6 = (bf16[4,4,16,16,512]{4,3,2,1,0:T(8,128)(2,1)}, bf16[4,4,16,16,512]{4,3,2,1,0:T(8,128)(2,1)}) custom-call(s32[3]{0:T(128)} %pad_add_fusion.9.me_ref, bf16[3,512,512]{2,1,0:T(8,128)(2,1)} %get-tuple-element.687.refs_0_, bf16[1,512,512]{2,1,0:T(8,128)(2,1)} %get-tuple-element.688.refs_1_, ...), custom_call_target="tpu_custom_call" | custom-call | flops 1 | bytes 1 | tf_op jit(solution)/shard_map/collect_gradients/pallas_call | solution.py:345
  468.9 20.3 %reduce-scatter.6.cloned.1.call-done = bf16[1,16,16,512]{3,2,1,0:T(8,128)(2,1)} async-done(((bf16[16,16,16,512]{3,2,1,0:T(8,128)(2,1)}), bf16[1,16,16,512]{3,2,1,0:T(8,128)(2,1)}) %reduce-scatter.6.cloned.1.call-update) | async-done | bytes 262160 | tf_op jit(solution)/shard_map/reduce_scatter | solution.py:108
  489.2 7.7 %add_convert_fusion.1 = bf16[4,4,16,16,512]{4,3,2,1,0:T(8,128)(2,1)} fusion(bf16[4,4,16,16,512]{4,3,2,1,0:T(8,128)(2,1)} %collective-permute-done.44, bf16[4,4,16,16,512]{4,3,2,1,0:T(8,128)(2,1)} %get-tuple-element.708), kind=kLoop, calls=%fused_computation.5 | loop fusion | flops 8388608 | bytes 12582912 | tf_op jit(solution)/shard_map/convert_element_type | solution.py:146
  496.9 15.9 %attend_back.9 = (bf16[512,512]{1,0:T(8,128)(2,1)}, f32[2,512,512]{2,1,0:T(8,128)}, f32[2,512,512]{2,1,0:T(8,128)}) custom-call(s32[18]{0:T(128)} %pad_add_fusion.7.act, s32[8,512]{1,0:T(8,128)} %pad.7.bounds, bf16[512,512]{1,0:T(8,128)(2,1)} %get-tuple-element.527.q, bf16[2,512,512]{2,1,0:T(8,128)(2,1)} %get-tuple-element.528.kv_own, ...), custom_call_target="tpu_custom_call" | custom-call | flops 1 | bytes 1 | tf_op jit(solution)/shard_map/attend_back/pallas_call | solution.py:733
  517.4 6.8 project_back.5
  534.3 6.4 collect_gradients.7
  555.3 31.3 %collective-permute-done.53.from_x = bf16[2,4,6,16,512]{4,3,2,1,0:T(8,128)(2,1)S(1)} collective-permute-done((bf16[2,4,6,16,512]{4,3,2,1,0:T(8,128)(2,1)S(1)}, bf16[2,4,6,16,512]{4,3,2,1,0:T(8,128)(2,1)S(1)}, u32[]{:S(2)}, u32[]{:S(2)}) %collective-permute-start.53) | collective-permute-done | bytes 786464 | tf_op jit(solution)/shard_map/ppermute | solution.py:64
  598.7 13.7 %collective-permute-done.48 = f32[12,512]{1,0:T(8,128)S(1)} collective-permute-done((f32[12,512]{1,0:T(8,128)S(1)}, f32[12,512]{1,0:T(8,128)S(1)}, u32[]{:S(2)}, u32[]{:S(2)}) %collective-permute-start.48) | collective-permute-done | bytes 24608 | tf_op jit(solution)/shard_map/ppermute | solution.py:64
  (550 shorter events, 334.0 us)
Async XLA Ops:
  7.2 134.7 %all-gather.5.cloned.1.call-start = ((), (), s32[]{:S(2)}) async-start(), calls=%async_computation.6 | async-start | bytes 10813440 | tf_op jit(solution)/shard_map/all_gather | solution.py:1128
  11.7 18.5 %collective-permute-start.4 = (bf16[12,16,512]{2,1,0:T(8,128)(2,1)}, bf16[12,16,512]{2,1,0:T(8,128)(2,1)}, u32[]{:S(2)}, u32[]{:S(2)}) collective-permute-start(bf16[12,16,512]{2,1,0:T(8,128)(2,1)} %constant_dynamic-slice_fusion.10), channel_id=1, source_target_pairs={{0,2},{2,0},{4,6},{6,4},{1,3},{3,1},{5,7},{7,5},{8,10},{10,8},{12,... | collective-permute-start | bytes 589832 | tf_op jit(solution)/shard_map/ppermute | solution.py:64
  14.3 15.9 %collective-permute-start.5 = (bf16[12,16,512]{2,1,0:T(8,128)(2,1)}, bf16[12,16,512]{2,1,0:T(8,128)(2,1)}, u32[]{:S(2)}, u32[]{:S(2)}) collective-permute-start(bf16[12,16,512]{2,1,0:T(8,128)(2,1)} %constant_dynamic-slice_fusion.10), channel_id=1, source_target_pairs={{0,4},{2,6},{4,0},{6,2},{1,5},{3,7},{5,1},{7,3},{8,12},{10,14},{12... | collective-permute-start | bytes 589832 | tf_op jit(solution)/shard_map/ppermute | solution.py:64
  38.4 174.9 %all-gather.7.cloned.1.call-start = ((), (), s32[]{:S(2)}) async-start(), calls=%async_computation.7 | async-start | bytes 6488064 | tf_op jit(solution)/shard_map/all_gather | solution.py:1173
  39.6 18.7 %collective-permute-start.11 = (bf16[3,12,16,512]{3,2,1,0:T(8,128)(2,1)S(1)}, bf16[3,12,16,512]{3,2,1,0:T(8,128)(2,1)S(1)}, u32[]{:S(2)}, u32[]{:S(2)}) collective-permute-start(bf16[3,12,16,512]{3,2,1,0:T(8,128)(2,1)S(1)} %pad_maximum_fusion.2.refs_1_), channel_id=1, source_target_pairs={{0,8},{8,0},{16,24},{24,16},{1,9},{9,1},{17,25},{25,17},{2,10},{10... | collective-permute-start | bytes 1769480 | tf_op jit(solution)/shard_map/ppermute | solution.py:64
  41.4 28.2 %collective-permute-start.12 = (bf16[3,12,16,512]{3,2,1,0:T(8,128)(2,1)S(1)}, bf16[3,12,16,512]{3,2,1,0:T(8,128)(2,1)}, u32[]{:S(2)}, u32[]{:S(2)}) collective-permute-start(bf16[3,12,16,512]{3,2,1,0:T(8,128)(2,1)S(1)} %pad_maximum_fusion.2.refs_1_), channel_id=1, source_target_pairs={{0,16},{8,24},{16,0},{24,8},{1,17},{9,25},{17,1},{25,9},{2,18},{10... | collective-permute-start | bytes 1769480 | tf_op jit(solution)/shard_map/ppermute | solution.py:64
  42.9 26.7 %collective-permute-start.13 = (bf16[3,12,16,512]{3,2,1,0:T(8,128)(2,1)S(1)}, bf16[3,12,16,512]{3,2,1,0:T(8,128)(2,1)}, u32[]{:S(2)}, u32[]{:S(2)}) collective-permute-start(bf16[3,12,16,512]{3,2,1,0:T(8,128)(2,1)S(1)} %pad_maximum_fusion.2.refs_1_), channel_id=1, source_target_pairs={{0,24},{8,16},{16,8},{24,0},{1,25},{9,17},{17,9},{25,1},{2,26},{10... | collective-permute-start | bytes 1769480 | tf_op jit(solution)/shard_map/ppermute | solution.py:64
  51.1 19.2 %collective-permute-start.14 = (bf16[8,16,512]{2,1,0:T(8,128)(2,1)}, bf16[8,16,512]{2,1,0:T(8,128)(2,1)S(1)}, u32[]{:S(2)}, u32[]{:S(2)}) collective-permute-start(bf16[8,16,512]{2,1,0:T(8,128)(2,1)} %fusion.20), channel_id=1, source_target_pairs={{0,2},{2,0},{4,6},{6,4},{1,3},{3,1},{5,7},{7,5},{8,10},{10,8},{12,... | collective-permute-start | bytes 393224 | tf_op jit(solution)/shard_map/ppermute | solution.py:64
  53.8 16.6 %collective-permute-start.15 = (bf16[8,16,512]{2,1,0:T(8,128)(2,1)}, bf16[8,16,512]{2,1,0:T(8,128)(2,1)S(1)}, u32[]{:S(2)}, u32[]{:S(2)}) collective-permute-start(bf16[8,16,512]{2,1,0:T(8,128)(2,1)} %fusion.20), channel_id=1, source_target_pairs={{0,4},{2,6},{4,0},{6,2},{1,5},{3,7},{5,1},{7,3},{8,12},{10,14},{12... | collective-permute-start | bytes 393224 | tf_op jit(solution)/shard_map/ppermute | solution.py:64
  74.3 23.0 %collective-permute-start.22 = (bf16[3,8,16,512]{3,2,1,0:T(8,128)(2,1)S(1)}, bf16[3,8,16,512]{3,2,1,0:T(8,128)(2,1)}, u32[]{:S(2)}, u32[]{:S(2)}) collective-permute-start(bf16[3,8,16,512]{3,2,1,0:T(8,128)(2,1)S(1)} %pad_maximum_fusion.3.refs_1_), channel_id=1, source_target_pairs={{0,8},{8,0},{16,24},{24,16},{1,9},{9,1},{17,25},{25,17},{2,10},{10... | collective-permute-start | bytes 1179656 | tf_op jit(solution)/shard_map/ppermute | solution.py:64
  75.5 21.8 %collective-permute-start.23 = (bf16[3,8,16,512]{3,2,1,0:T(8,128)(2,1)S(1)}, bf16[3,8,16,512]{3,2,1,0:T(8,128)(2,1)}, u32[]{:S(2)}, u32[]{:S(2)}) collective-permute-start(bf16[3,8,16,512]{3,2,1,0:T(8,128)(2,1)S(1)} %pad_maximum_fusion.3.refs_1_), channel_id=1, source_target_pairs={{0,16},{8,24},{16,0},{24,8},{1,17},{9,25},{17,1},{25,9},{2,18},{10... | collective-permute-start | bytes 1179656 | tf_op jit(solution)/shard_map/ppermute | solution.py:64
  76.5 25.7 %collective-permute-start.24 = (bf16[3,8,16,512]{3,2,1,0:T(8,128)(2,1)S(1)}, bf16[3,8,16,512]{3,2,1,0:T(8,128)(2,1)}, u32[]{:S(2)}, u32[]{:S(2)}) collective-permute-start(bf16[3,8,16,512]{3,2,1,0:T(8,128)(2,1)S(1)} %pad_maximum_fusion.3.refs_1_), channel_id=1, source_target_pairs={{0,24},{8,16},{16,8},{24,0},{1,25},{9,17},{17,9},{25,1},{2,26},{10... | collective-permute-start | bytes 1179656 | tf_op jit(solution)/shard_map/ppermute | solution.py:64
  119.5 259.2 %reduce-scatter.4.cloned.1.call-start = ((), (), s32[]{:S(2)}) async-start(), calls=%async_computation.3 | async-start | bytes 2228224 | tf_op jit(solution)/shard_map/reduce_scatter | solution.py:108
  157.4 18.3 %collective-permute-start.32 = (bf16[2,512,512]{2,1,0:T(8,128)(2,1)}, bf16[2,512,512]{2,1,0:T(8,128)(2,1)S(1)}, u32[]{:S(2)}, u32[]{:S(2)}) collective-permute-start(bf16[2,512,512]{2,1,0:T(8,128)(2,1)} %memory_pair.2.kv_own), channel_id=1, source_target_pairs={{0,1},{1,0},{2,3},{3,2},{4,5},{5,4},{6,7},{7,6},{8,9},{9,8},{10,11... | collective-permute-start | bytes 3145736 | tf_op jit(solution)/shard_map/ppermute | solution.py:64
  286.6 202.6 %reduce-scatter.6.cloned.1.call-start = ((), (), s32[]{:S(2)}) async-start(), calls=%async_computation.4 | async-start | bytes 4456448 | tf_op jit(solution)/shard_map/reduce_scatter | solution.py:108
  321.8 28.1 %collective-permute-start.37 = (f32[2,512,512]{2,1,0:T(8,128)}, f32[2,512,512]{2,1,0:T(8,128)}, u32[]{:S(2)}, u32[]{:S(2)}) collective-permute-start(f32[2,512,512]{2,1,0:T(8,128)} %get-tuple-element.643), channel_id=1, source_target_pairs={{0,1},{1,0},{2,3},{3,2},{4,5},{5,4},{6,7},{7,6},{8,9},{9,8},{10,11... | collective-permute-start | bytes 6291464 | tf_op jit(solution)/shard_map/ppermute | solution.py:64
  392.5 240.4 %reduce-scatter.8.cloned.1.call-start = ((), (), s32[]{:S(2)}) async-start(), calls=%async_computation.5 | async-start | bytes 4456448 | tf_op jit(solution)/shard_map/reduce_scatter | solution.py:108
  408.8 26.8 %collective-permute-start.40 = (f32[2,512,512]{2,1,0:T(8,128)}, f32[2,512,512]{2,1,0:T(8,128)}, u32[]{:S(2)}, u32[]{:S(2)}) collective-permute-start(f32[2,512,512]{2,1,0:T(8,128)} %get-tuple-element.671), channel_id=1, source_target_pairs={{0,1},{1,0},{2,3},{3,2},{4,5},{5,4},{6,7},{7,6},{8,9},{9,8},{10,11... | collective-permute-start | bytes 6291464 | tf_op jit(solution)/shard_map/ppermute | solution.py:64
  428.0 21.1 %collective-permute-start.41 = (bf16[8,16,512]{2,1,0:T(8,128)(2,1)S(1)}, bf16[8,16,512]{2,1,0:T(8,128)(2,1)S(1)}, u32[]{:S(2)}, u32[]{:S(2)}) collective-permute-start(bf16[8,16,512]{2,1,0:T(8,128)(2,1)S(1)} %bitcast.234), channel_id=1, source_target_pairs={{0,8},{8,0},{16,24},{24,16},{1,9},{9,1},{17,25},{25,17},{2,10},{10... | collective-permute-start | bytes 393224 | tf_op jit(solution)/shard_map/ppermute | solution.py:64
  428.1 21.0 %collective-permute-start.42 = (bf16[8,16,512]{2,1,0:T(8,128)(2,1)S(1)}, bf16[8,16,512]{2,1,0:T(8,128)(2,1)}, u32[]{:S(2)}, u32[]{:S(2)}) collective-permute-start(bf16[8,16,512]{2,1,0:T(8,128)(2,1)S(1)} %bitcast.235), channel_id=1, source_target_pairs={{0,16},{8,24},{16,0},{24,8},{1,17},{9,25},{17,1},{25,9},{2,18},{10... | collective-permute-start | bytes 393224 | tf_op jit(solution)/shard_map/ppermute | solution.py:64
  468.8 20.4 %collective-permute-start.44 = (bf16[4,4,16,16,512]{4,3,2,1,0:T(8,128)(2,1)}, bf16[4,4,16,16,512]{4,3,2,1,0:T(8,128)(2,1)}, u32[]{:S(2)}, u32[]{:S(2)}) collective-permute-start(bf16[4,4,16,16,512]{4,3,2,1,0:T(8,128)(2,1)} %get-tuple-element.705), channel_id=1, source_target_pairs={{0,1},{1,0},{2,3},{3,2},{4,5},{5,4},{6,7},{7,6},{8,9},{9,8},{10,11... | collective-permute-start | bytes 12582920 | tf_op jit(solution)/shard_map/ppermute | solution.py:64
  550.2 36.3 %collective-permute-start.53 = (bf16[2,4,6,16,512]{4,3,2,1,0:T(8,128)(2,1)S(1)}, bf16[2,4,6,16,512]{4,3,2,1,0:T(8,128)(2,1)S(1)}, u32[]{:S(2)}, u32[]{:S(2)}) collective-permute-start(bf16[2,4,6,16,512]{4,3,2,1,0:T(8,128)(2,1)S(1)} %fusion.11), channel_id=1, source_target_pairs={{0,8},{8,0},{1,9},{9,1},{2,10},{10,2},{3,11},{11,3},{4,12},{12,4},... | collective-permute-start | bytes 2359304 | tf_op jit(solution)/shard_map/ppermute | solution.py:64
  550.3 39.7 %collective-permute-start.54 = (bf16[2,4,6,16,512]{4,3,2,1,0:T(8,128)(2,1)S(1)}, bf16[2,4,6,16,512]{4,3,2,1,0:T(8,128)(2,1)S(1)}, u32[]{:S(2)}, u32[]{:S(2)}) collective-permute-start(bf16[2,4,6,16,512]{4,3,2,1,0:T(8,128)(2,1)S(1)} %fusion.12), channel_id=1, source_target_pairs={{0,16},{16,0},{1,17},{17,1},{2,18},{18,2},{3,19},{19,3},{4,20},{20... | collective-permute-start | bytes 2359304 | tf_op jit(solution)/shard_map/ppermute | solution.py:64
  592.5 28.3 %collective-permute-start.55 = (bf16[4,6,16,512]{3,2,1,0:T(8,128)(2,1)}, bf16[4,6,16,512]{3,2,1,0:T(8,128)(2,1)S(1)}, u32[]{:S(2)}, u32[]{:S(2)}) collective-permute-start(bf16[4,6,16,512]{3,2,1,0:T(8,128)(2,1)} %get-tuple-element.772), channel_id=1, source_target_pairs={{0,16},{16,0},{1,17},{17,1},{2,18},{18,2},{3,19},{19,3},{4,20},{20... | collective-permute-start | bytes 1179656 | tf_op jit(solution)/shard_map/ppermute | solution.py:64
  594.6 26.2 %collective-permute-start.56 = (bf16[4,6,16,512]{3,2,1,0:T(8,128)(2,1)S(1)}, bf16[4,6,16,512]{3,2,1,0:T(8,128)(2,1)S(1)}, u32[]{:S(2)}, u32[]{:S(2)}) collective-permute-start(bf16[4,6,16,512]{3,2,1,0:T(8,128)(2,1)S(1)} %get-tuple-element.773), channel_id=1, source_target_pairs={{0,8},{8,0},{1,9},{9,1},{2,10},{10,2},{3,11},{11,3},{4,12},{12,4},... | collective-permute-start | bytes 1179656 | tf_op jit(solution)/shard_map/ppermute | solution.py:64
  596.9 15.5 %collective-permute-start.48 = (f32[12,512]{1,0:T(8,128)S(1)}, f32[12,512]{1,0:T(8,128)S(1)}, u32[]{:S(2)}, u32[]{:S(2)}) collective-permute-start(f32[12,512]{1,0:T(8,128)S(1)} %add.437), channel_id=1, source_target_pairs={{0,8},{8,0},{1,9},{9,1},{2,10},{10,2},{3,11},{11,3},{4,12},{12,4},... | collective-permute-start | bytes 73736 | tf_op jit(solution)/shard_map/ppermute | solution.py:64
  625.2 15.9 %collective-permute-start.58 = (bf16[12,16,512]{2,1,0:T(8,128)(2,1)}, bf16[12,16,512]{2,1,0:T(8,128)(2,1)S(1)}, u32[]{:S(2)}, u32[]{:S(2)}) collective-permute-start(bf16[12,16,512]{2,1,0:T(8,128)(2,1)} %get-tuple-element.786), channel_id=1, source_target_pairs={{0,4},{2,6},{4,0},{6,2},{1,5},{3,7},{5,1},{7,3},{8,12},{10,14},{12... | collective-permute-start | bytes 589832 | tf_op jit(solution)/shard_map/ppermute | solution.py:64
  628.6 30.2 %collective-permute-start.65 = (bf16[16,16,512]{2,1,0:T(8,128)(2,1)S(1)}, bf16[16,16,512]{2,1,0:T(8,128)(2,1)S(1)}, u32[]{:S(2)}, u32[]{:S(2)}) collective-permute-start(bf16[16,16,512]{2,1,0:T(8,128)(2,1)S(1)} %bitcast.224), channel_id=1, source_target_pairs={{0,8},{8,0},{16,24},{24,16},{1,9},{9,1},{17,25},{25,17},{2,10},{10... | collective-permute-start | bytes 786440 | tf_op jit(solution)/shard_map/ppermute | solution.py:64
  630.5 35.4 %collective-permute-start.66 = (bf16[16,16,512]{2,1,0:T(8,128)(2,1)S(1)}, bf16[16,16,512]{2,1,0:T(8,128)(2,1)S(1)}, u32[]{:S(2)}, u32[]{:S(2)}) collective-permute-start(bf16[16,16,512]{2,1,0:T(8,128)(2,1)S(1)} %bitcast.225), channel_id=1, source_target_pairs={{0,16},{8,24},{16,0},{24,8},{1,17},{9,25},{17,1},{25,9},{2,18},{10... | collective-permute-start | bytes 786440 | tf_op jit(solution)/shard_map/ppermute | solution.py:64
  632.9 33.7 %collective-permute-start.67 = (bf16[16,16,512]{2,1,0:T(8,128)(2,1)S(1)}, bf16[16,16,512]{2,1,0:T(8,128)(2,1)S(1)}, u32[]{:S(2)}, u32[]{:S(2)}) collective-permute-start(bf16[16,16,512]{2,1,0:T(8,128)(2,1)S(1)} %bitcast.226), channel_id=1, source_target_pairs={{0,24},{8,16},{16,8},{24,0},{1,25},{9,17},{17,9},{25,1},{2,26},{10... | collective-permute-start | bytes 786440 | tf_op jit(solution)/shard_map/ppermute | solution.py:64
  641.1 30.8 %collective-permute-start.68 = (bf16[16,16,512]{2,1,0:T(8,128)(2,1)}, bf16[16,16,512]{2,1,0:T(8,128)(2,1)S(1)}, u32[]{:S(2)}, u32[]{:S(2)}) collective-permute-start(bf16[16,16,512]{2,1,0:T(8,128)(2,1)} %bitcast.227), channel_id=1, source_target_pairs={{0,8},{8,0},{16,24},{24,16},{1,9},{9,1},{17,25},{25,17},{2,10},{10... | collective-permute-start | bytes 786440 | tf_op jit(solution)/shard_map/ppermute | solution.py:64
  657.5 17.8 %collective-permute-start.69 = (bf16[16,16,512]{2,1,0:T(8,128)(2,1)}, bf16[16,16,512]{2,1,0:T(8,128)(2,1)}, u32[]{:S(2)}, u32[]{:S(2)}) collective-permute-start(bf16[16,16,512]{2,1,0:T(8,128)(2,1)} %bitcast.228), channel_id=1, source_target_pairs={{0,16},{8,24},{16,0},{24,8},{1,17},{9,25},{17,1},{25,9},{2,18},{10... | collective-permute-start | bytes 786440 | tf_op jit(solution)/shard_map/ppermute | solution.py:64
  (147 other events, 1791.9 us)
Sparse Core Ops, SparseCore 0:
  38.5 103.3 all-gather.4
  144.9 67.8 all-gather.6
  286.7 91.9 reduce-scatter.3
  392.6 96.5 reduce-scatter.5
  513.1 98.2 reduce-scatter.7

commit v6 on v5

--- a/solution.py
+++ b/solution.py
@@ -861,6 +861,35 @@
         back = part if back is None else back + part
     more, grad_gain[...] = rms_back(x[...], gain[...], back)
     grad_x[...] = grad[...] + more
+
+
+def table_back_kernel(ids, token_grads, grad_logits, exits, grad):
+    first = pl.program_id(0) * grad.shape[0]
+    spot = first + lax.broadcasted_iota(jnp.int32, (grad.shape[0], ids.shape[1]), 0)
+    looked = jnp.where(spot == ids[0:1, :], 1.0, 0.0).astype(HALF)
+    total = dot32(looked, token_grads[...], NN) + dot32(grad_logits[...], exits[...], TN)
+    grad[...] = low(total)
+
+
+def table_back(ids, token_grads, grad_logits, exits):
+    rows, vocabulary = grad_logits.shape
+    count, width = token_grads.shape
+    ids = jnp.broadcast_to(ids[None], (8, count))
+    return pl.pallas_call(
+        table_back_kernel,
+        grid=(vocabulary // COL,),
+        out_shape=jax.ShapeDtypeStruct((vocabulary, width), HALF),
+        in_specs=[
+            pl.BlockSpec((8, count), lambda i: (0, 0)),
+            pl.BlockSpec((count, width), lambda i: (0, 0)),
+            pl.BlockSpec((rows, COL), lambda i: (0, i)),
+            pl.BlockSpec((rows, width), lambda i: (0, 0)),
+        ],
+        out_specs=pl.BlockSpec((COL, width), lambda i: (i, 0)),
+        cost_estimate=LIGHT,
+        compiler_params=pltpu.CompilerParams(vmem_limit_bytes=24 << 20),
+        name="table_back",
+    )(ids, token_grads, grad_logits, exits)
 
 
 def on_chip(kernel, name, outs, *args):
@@ -1124,7 +1153,8 @@
     )
     gains_now = norm_gains
     if fast:
-        reached, gains_now, third = step((reached, gains_now, third), first)
+        reached, gains_now = step((reached, gains_now), first)
+        (reached, gains_now), third = hold((reached, gains_now), third)
         third = lax.all_gather(third, PLANE + LINE).reshape(4, owners, *third.shape)
         reached, gains_now = step((reached, gains_now), second)
     small = jnp.concatenate([gains_now.reshape(-1), reached.reshape(-1)])
@@ -1227,7 +1257,6 @@
         * LOGIT_SCALE
     )
     grad_exits = product(grad_logits, table)
-    table_grad = outer_sum(grad_logits, exits)
 
     grads = {}
     gain_parts = [None] * gain_count
@@ -1315,10 +1344,7 @@
     )
     token_ids = jnp.concatenate([source_ids, target_ids])
     token_grads = low(jnp.concatenate([grad_enc, grad_x]) * root_width)
-    looked = (token_ids[:, None] == jnp.arange(vocabulary)[None, :]).astype(jnp.bfloat16)
-    table_grad = low(table_grad + outer_sum(looked, token_grads))
-    grads["table", 0] = table_grad
-
+    grads["table", 0] = table_back(token_ids, token_grads, grad_logits, exits)
     gain_grad = jnp.concatenate([part.reshape(1, -1) for part in gain_parts])
     small = jnp.concatenate([gain_grad, jnp.full((1, width), loss_part)])
 
@@ -1328,8 +1354,8 @@
         tiny = Mover()
         tiny.stages = small_stages(tiny, small, z)
         loss_part = step(loss_part, last, tiny)
+        loss_part = step(loss_part, last, tiny, middle)
         loss_part = step(loss_part, last, tiny)
-        loss_part = step(loss_part, last, tiny, middle)
         loss_part = step(loss_part, last, tiny)
         movers = (feed_mover, late, middle, last)
         loss_part = step(loss_part, last, tiny)

time: 722 us -> 719 us (level)
  waiting for transfers between devices: 166 us -> 140 us
  Pallas kernels: 310 us -> 327 us
  matrix products: 22 us -> 9.25 us
  local copies, waits for them, and re-layouts: 44.4 us -> 56.9 us
    reduce_scatter x3, waiting for transfers between devices: 36.4 us -> 24.9 us  [step(): lax.psum_scatter(array, PLANE + ('z',), scatter_dimension=0, tiled=True)]
    dot_general x2 -> x0, matrix products: 10 us -> none  [outer_sum(): lax.dot_general(a, b, (((0,), (0,)), ((), ())), preferred_element_type=jn...]
    ppermute x74, waiting for transfers between devices: 125 us -> 115 us  [flip(): return lax.ppermute(x, axis, [(i, i ^ bit) for i in range(n)])]
    unnamed x213 -> x241, local copies, waits for them, and re-layouts: 12.6 us -> 18.8 us
    convert_element_type x8 -> x10, other arithmetic: 26.3 us -> 28.7 us  [low(): return v.astype(jnp.bfloat16)]
  transfers between devices with their start and end apart: 79 -> 79, of which waited for: 30 -> 29; matrix products, arithmetic and copies ran while one was open for 9% -> 9% of each run, Pallas kernels for 35% -> 39%
where the time goes in v6:
time: 719 us; the launch traced here: 709 us
  Pallas kernels  327 us (45%)
  waiting for transfers between devices  140 us (19%)
  starting transfers between devices  81.7 us (11%)
  other arithmetic  70.1 us (10%)
  local copies, waits for them, and re-layouts  56.9 us (8%)
  between operations  24.8 us (3%)
  matrix products  9.25 us (1%)
    pallas_call x20, Pallas kernels, on_chip(): pl.pallas_call(kernel, out_shape=[jax.ShapeDtypeStruct(shape, kind) for s...  120 us
    ppermute x74, waiting for transfers between devices, flip(): return lax.ppermute(x, axis, [(i, i ^ bit) for i in range(n)])  115 us
    pallas_call x5, Pallas kernels, attend_back(): pl.pallas_call(attend_back_kernel, out_shape=[jax.ShapeDtypeStruct((n, wi...  82.5 us
    ppermute x74, starting transfers between devices, flip(): return lax.ppermute(x, axis, [(i, i ^ bit) for i in range(n)])  81.3 us
    pallas_call x5, Pallas kernels, attend(): pl.pallas_call(attend_kernel, out_shape=[jax.ShapeDtypeStruct((n, width),...  57 us
    convert_element_type x10, other arithmetic, low(): return v.astype(jnp.bfloat16)  28.7 us
    pallas_call x4, Pallas kernels, collect(): pl.pallas_call(functools.partial(collect_kernel, plan, unit, ordered), ou...  26.5 us
    reduce_scatter x3, waiting for transfers between devices, step(): lax.psum_scatter(array, PLANE + ('z',), scatter_dimension=0, tiled=True)  24.9 us
  transfers between devices with their start and end apart: 79, of which 29 were waited for; matrix products, arithmetic and copies ran while one was open for 9% of the time, Pallas kernels for 39%

profile of v6, /device:TPU:0, one launch (start us, length us, event | category | flops | bytes accessed | tf_op | source)
XLA Modules:
  0.0 709.3 jit_solution(5334172238190535720)
XLA Ops:
  58.5 10.9 %collective-permute-done.12.refs_3_ = bf16[3,12,16,512]{3,2,1,0:T(8,128)(2,1)} collective-permute-done((bf16[3,12,16,512]{3,2,1,0:T(8,128)(2,1)S(1)}, bf16[3,12,16,512]{3,2,1,0:T(8,128)(2,1)}, u32[]{:S(2)}, u32[]{:S(2)}) %collective-permute-start.12) | collective-permute-done | bytes 589856 | tf_op jit(solution)/shard_map/ppermute | solution.py:64
  87.5 6.8 gather_fusion
  111.1 12.3 %attend.5 = (bf16[512,512]{1,0:T(8,128)(2,1)}, f32[4,4,1,256]{3,2,1,0:T(1,128)}) custom-call(s32[18]{0:T(128)} %pad_add_fusion.7.act, s32[8,512]{1,0:T(8,128)} %pad.7.bounds, bf16[512,512]{1,0:T(8,128)(2,1)} %get-tuple-element.529.q, bf16[2,512,512]{2,1,0:T(8,128)(2,1)} %get-tuple-element.530.kv_own, bf16[2,512,512]{2,1,0:T(8,128)(2,1)} %copy-done.11), custom_call_target="tpu_custom_call" | custom-call | flops 1 | bytes 1 | tf_op jit(solution)/shard_map/attend/pallas_call | solution.py:705
  133.2 7.2 %feed.3 = (f32[512,512]{1,0:T(8,128)}, bf16[512,512]{1,0:T(8,128)(2,1)}, bf16[4,512,512]{2,1,0:T(8,128)(2,1)}, f32[512,512]{1,0:T(8,128)}) custom-call(bf16[512,512]{1,0:T(8,128)(2,1)} %get-tuple-element.544.o, bf16[1,512,512]{2,1,0:T(8,128)(2,1)} %get-tuple-element.545.w_out, f32[512,512]{1,0:T(8,128)} %get-tuple-element.717.x, f32[1,512]{1,0:T(1,128)} %slice.247.gain, ...), custom_call_target="tpu_custom_call" | custom-call | flops 1 | bytes 1 | tf_op jit(solution)/shard_map/feed/pallas_call | solution.py:896
  143.9 8.2 %place_gathered.2 = (bf16[3,8,4,16,512]{4,3,2,1,0:T(8,128)(2,1)}, bf16[1,8,4,16,512]{4,3,2,1,0:T(8,128)(2,1)}, bf16[3,8,4,16,512]{4,3,2,1,0:T(8,128)(2,1)}, bf16...) custom-call(bf16[4,8,20,16,512]{4,3,2,1,0:T(8,128)(2,1)} %bitcast.182), custom_call_target="tpu_custom_call" | custom-call | flops 1 | bytes 1 | tf_op jit(solution)/shard_map/place_gathered/pallas_call | solution.py:302
  164.1 9.9 %attend.6 = (bf16[512,512]{1,0:T(8,128)(2,1)}, f32[4,4,1,256]{3,2,1,0:T(1,128)}) custom-call(s32[18]{0:T(128)} %pad_add_fusion.10.act, s32[8,512]{1,0:T(8,128)} %pad.8.bounds, bf16[512,512]{1,0:T(8,128)(2,1)} %get-tuple-element.564.q, bf16[2,512,512]{2,1,0:T(8,128)(2,1)} %get-tuple-element.565.kv_own, bf16[2,512,512]{2,1,0:T(8,128)(2,1)} %copy-done.12), custom_call_target="tpu_custom_call" | custom-call | flops 1 | bytes 1 | tf_op jit(solution)/shard_map/attend/pallas_call | solution.py:705
  178.8 12.3 %attend.7 = (bf16[512,512]{1,0:T(8,128)(2,1)}, f32[4,4,1,256]{3,2,1,0:T(1,128)}) custom-call(s32[18]{0:T(128)} %pad_add_fusion.7.act, s32[8,512]{1,0:T(8,128)} %pad.7.bounds, bf16[512,512]{1,0:T(8,128)(2,1)} %get-tuple-element.569.q, bf16[2,512,512]{2,1,0:T(8,128)(2,1)} %memory_pair.2.kv_own, bf16[2,512,512]{2,1,0:T(8,128)(2,1)} %copy-done.13), custom_call_target="tpu_custom_call" | custom-call | flops 1 | bytes 1 | tf_op jit(solution)/shard_map/attend/pallas_call | solution.py:705
  191.1 7.1 %feed.4 = (f32[512,512]{1,0:T(8,128)}, bf16[512,512]{1,0:T(8,128)(2,1)}, bf16[4,512,512]{2,1,0:T(8,128)(2,1)}, f32[512,512]{1,0:T(8,128)}) custom-call(bf16[512,512]{1,0:T(8,128)(2,1)} %get-tuple-element.571.o, bf16[1,512,512]{2,1,0:T(8,128)(2,1)} %bitcast.220, f32[512,512]{1,0:T(8,128)} %get-tuple-element.573.x.y, f32[1,512]{1,0:T(1,128)} %slice.254.gain, ...), custom_call_target="tpu_custom_call" | custom-call | flops 1 | bytes 1 | tf_op jit(solution)/shard_map/feed/pallas_call | solution.py:896
  207.4 9.9 %attend.8 = (bf16[512,512]{1,0:T(8,128)(2,1)}, f32[4,4,1,256]{3,2,1,0:T(1,128)}) custom-call(s32[18]{0:T(128)} %pad_add_fusion.10.act, s32[8,512]{1,0:T(8,128)} %pad.8.bounds, bf16[512,512]{1,0:T(8,128)(2,1)} %get-tuple-element.578.q, bf16[2,512,512]{2,1,0:T(8,128)(2,1)} %get-tuple-element.579.kv_own, bf16[2,512,512]{2,1,0:T(8,128)(2,1)} %copy-done.14), custom_call_target="tpu_custom_call" | custom-call | flops 1 | bytes 1 | tf_op jit(solution)/shard_map/attend/pallas_call | solution.py:705
  237.7 12.5 %attend.9 = (bf16[512,512]{1,0:T(8,128)(2,1)}, f32[4,4,1,256]{3,2,1,0:T(1,128)}) custom-call(s32[18]{0:T(128)} %pad_add_fusion.7.act, s32[8,512]{1,0:T(8,128)} %pad.7.bounds, bf16[512,512]{1,0:T(8,128)(2,1)} %get-tuple-element.586.q, bf16[2,512,512]{2,1,0:T(8,128)(2,1)} %memory_pair.3.kv_own, bf16[2,512,512]{2,1,0:T(8,128)(2,1)} %copy-done.15), custom_call_target="tpu_custom_call" | custom-call | flops 1 | bytes 1 | tf_op jit(solution)/shard_map/attend/pallas_call | solution.py:705
  250.2 7.1 feed.5
  270.1 10.5 %feed_back.3 = (bf16[4,512,512]{2,1,0:T(8,128)(2,1)}, bf16[4,512,512]{2,1,0:T(8,128)(2,1)}, f32[512,512]{1,0:T(8,128)}, f32[1,512]{1,0:T(1,128)}, bf16[512,512]{...) custom-call(f32[512,512]{1,0:T(8,128)} %add_add_fusion.2.grad, f32[512,512]{1,0:T(8,128)} %get-tuple-element.598.y, ...), custom_call_target="tpu_custom_call" | custom-call | flops 1 | bytes 1 | tf_op jit(solution)/shard_map/feed_back/pallas_call | solution.py:896
  293.9 18.3 %attend_back.5 = (bf16[512,512]{1,0:T(8,128)(2,1)}, f32[2,512,512]{2,1,0:T(8,128)}, f32[2,512,512]{2,1,0:T(8,128)}) custom-call(s32[18]{0:T(128)} %pad_add_fusion.7.act, s32[8,512]{1,0:T(8,128)} %pad.7.bounds, bf16[512,512]{1,0:T(8,128)(2,1)} %get-tuple-element.586.q, bf16[2,512,512]{2,1,0:T(8,128)(2,1)} %memory_pair.3.kv_own, ...), custom_call_target="tpu_custom_call" | custom-call | flops 1 | bytes 1 | tf_op jit(solution)/shard_map/attend_back/pallas_call | solution.py:733
  317.3 13.8 %attend_back.6 = (bf16[512,512]{1,0:T(8,128)(2,1)}, f32[2,512,512]{2,1,0:T(8,128)}, f32[2,512,512]{2,1,0:T(8,128)}) custom-call(s32[18]{0:T(128)} %pad_add_fusion.10.act, s32[8,512]{1,0:T(8,128)} %pad.8.bounds, bf16[512,512]{1,0:T(8,128)(2,1)} %get-tuple-element.578.q, bf16[2,512,512]{2,1,0:T(8,128)(2,1)} %get-tuple-element.579.kv_own, ...), custom_call_target="tpu_custom_call" | custom-call | flops 1 | bytes 1 | tf_op jit(solution)/shard_map/attend_back/pallas_call | solution.py:733
  342.3 6.8 project_back.3
  351.5 10.5 %feed_back.4 = (bf16[4,512,512]{2,1,0:T(8,128)(2,1)}, bf16[4,512,512]{2,1,0:T(8,128)(2,1)}, f32[512,512]{1,0:T(8,128)}, f32[1,512]{1,0:T(1,128)}, bf16[512,512]{...) custom-call(f32[512,512]{1,0:T(8,128)} %fusion.4.grad, f32[512,512]{1,0:T(8,128)} %get-tuple-element.628.y, ...), custom_call_target="tpu_custom_call" | custom-call | flops 1 | bytes 1 | tf_op jit(solution)/shard_map/feed_back/pallas_call | solution.py:896
  367.2 7.7 %collect_gradients.5 = (bf16[4,4,16,16,512]{4,3,2,1,0:T(8,128)(2,1)}, bf16[4,4,16,16,512]{4,3,2,1,0:T(8,128)(2,1)}) custom-call(s32[3]{0:T(128)} %pad_add_fusion.9.me_ref, bf16[3,512,512]{2,1,0:T(8,128)(2,1)} %get-tuple-element.641.refs_0_, bf16[1,512,512]{2,1,0:T(8,128)(2,1)} %get-tuple-element.642.refs_1_, ...), custom_call_target="tpu_custom_call" | custom-call | flops 1 | bytes 1 | tf_op jit(solution)/shard_map/collect_gradients/pallas_call | solution.py:345
  374.9 7.6 %reduce-scatter.4.cloned.1.call-done = bf16[1,8,16,512]{3,2,1,0:T(8,128)(2,1)} async-done(((bf16[16,8,16,512]{3,2,1,0:T(8,128)(2,1)}), bf16[1,8,16,512]{3,2,1,0:T(8,128)(2,1)}) %reduce-scatter.4.cloned.1.call-update) | async-done | bytes 131088 | tf_op jit(solution)/shard_map/reduce_scatter | solution.py:108
  382.5 7.4 %collective-permute-done.38 = bf16[4,4,16,16,512]{4,3,2,1,0:T(8,128)(2,1)S(1)} collective-permute-done((bf16[4,4,16,16,512]{4,3,2,1,0:T(8,128)(2,1)}, bf16[4,4,16,16,512]{4,3,2,1,0:T(8,128)(2,1)S(1)}, u32[]{:S(2)}, u32[]{:S(2)}) %collective-permute-start.38) | collective-permute-done | bytes 4194336 | tf_op jit(solution)/shard_map/ppermute | solution.py:64
  389.9 6.3 add_convert_fusion.1
  396.3 18.3 %attend_back.7 = (bf16[512,512]{1,0:T(8,128)(2,1)}, f32[2,512,512]{2,1,0:T(8,128)}, f32[2,512,512]{2,1,0:T(8,128)}) custom-call(s32[18]{0:T(128)} %pad_add_fusion.7.act, s32[8,512]{1,0:T(8,128)} %pad.7.bounds, bf16[512,512]{1,0:T(8,128)(2,1)} %get-tuple-element.569.q, bf16[2,512,512]{2,1,0:T(8,128)(2,1)} %memory_pair.2.kv_own, ...), custom_call_target="tpu_custom_call" | custom-call | flops 1 | bytes 1 | tf_op jit(solution)/shard_map/attend_back/pallas_call | solution.py:733
  420.0 13.8 %attend_back.8 = (bf16[512,512]{1,0:T(8,128)(2,1)}, f32[2,512,512]{2,1,0:T(8,128)}, f32[2,512,512]{2,1,0:T(8,128)}) custom-call(s32[18]{0:T(128)} %pad_add_fusion.10.act, s32[8,512]{1,0:T(8,128)} %pad.8.bounds, bf16[512,512]{1,0:T(8,128)(2,1)} %get-tuple-element.564.q, bf16[2,512,512]{2,1,0:T(8,128)(2,1)} %get-tuple-element.565.kv_own, ...), custom_call_target="tpu_custom_call" | custom-call | flops 1 | bytes 1 | tf_op jit(solution)/shard_map/attend_back/pallas_call | solution.py:733
  447.6 6.8 project_back.4
  457.3 10.5 %feed_back.5 = (bf16[4,512,512]{2,1,0:T(8,128)(2,1)}, bf16[4,512,512]{2,1,0:T(8,128)(2,1)}, f32[512,512]{1,0:T(8,128)}, f32[1,512]{1,0:T(1,128)}, bf16[512,512]{...) custom-call(f32[512,512]{1,0:T(8,128)} %add_add_fusion.grad, f32[512,512]{1,0:T(8,128)} %get-tuple-element.682.y, ...), custom_call_target="tpu_custom_call" | custom-call | flops 1 | bytes 1 | tf_op jit(solution)/shard_map/feed_back/pallas_call | solution.py:896
  467.8 7.6 %collect_gradients.6 = (bf16[4,4,16,16,512]{4,3,2,1,0:T(8,128)(2,1)}, bf16[4,4,16,16,512]{4,3,2,1,0:T(8,128)(2,1)}) custom-call(s32[3]{0:T(128)} %pad_add_fusion.9.me_ref, bf16[3,512,512]{2,1,0:T(8,128)(2,1)} %get-tuple-element.689.refs_0_, bf16[1,512,512]{2,1,0:T(8,128)(2,1)} %get-tuple-element.690.refs_1_, ...), custom_call_target="tpu_custom_call" | custom-call | flops 1 | bytes 1 | tf_op jit(solution)/shard_map/collect_gradients/pallas_call | solution.py:345
  475.5 17.3 %reduce-scatter.6.cloned.1.call-done = bf16[1,16,16,512]{3,2,1,0:T(8,128)(2,1)} async-done(((bf16[16,16,16,512]{3,2,1,0:T(8,128)(2,1)}), bf16[1,16,16,512]{3,2,1,0:T(8,128)(2,1)}) %reduce-scatter.6.cloned.1.call-update) | async-done | bytes 262160 | tf_op jit(solution)/shard_map/reduce_scatter | solution.py:108
  492.8 7.6 %add_convert_fusion = bf16[4,4,16,16,512]{4,3,2,1,0:T(8,128)(2,1)} fusion(bf16[4,4,16,16,512]{4,3,2,1,0:T(8,128)(2,1)} %collective-permute-done.44, bf16[4,4,16,16,512]{4,3,2,1,0:T(8,128)(2,1)} %get-tuple-element.710), kind=kLoop, calls=%fused_computation.2 | loop fusion | flops 8388608 | bytes 12582912 | tf_op jit(solution)/shard_map/convert_element_type | solution.py:146
  500.4 18.3 %attend_back.9 = (bf16[512,512]{1,0:T(8,128)(2,1)}, f32[2,512,512]{2,1,0:T(8,128)}, f32[2,512,512]{2,1,0:T(8,128)}) custom-call(s32[18]{0:T(128)} %pad_add_fusion.7.act, s32[8,512]{1,0:T(8,128)} %pad.7.bounds, bf16[512,512]{1,0:T(8,128)(2,1)} %get-tuple-element.529.q, bf16[2,512,512]{2,1,0:T(8,128)(2,1)} %get-tuple-element.530.kv_own, ...), custom_call_target="tpu_custom_call" | custom-call | flops 1 | bytes 1 | tf_op jit(solution)/shard_map/attend_back/pallas_call | solution.py:733
  524.4 6.7 project_back.5
  533.0 7.1 table_back.1
  559.0 34.8 %collective-permute-done.53.from_x = bf16[2,4,6,16,512]{4,3,2,1,0:T(8,128)(2,1)S(1)} collective-permute-done((bf16[2,4,6,16,512]{4,3,2,1,0:T(8,128)(2,1)S(1)}, bf16[2,4,6,16,512]{4,3,2,1,0:T(8,128)(2,1)S(1)}, u32[]{:S(2)}, u32[]{:S(2)}) %collective-permute-start.53) | collective-permute-done | bytes 786464 | tf_op jit(solution)/shard_map/ppermute | solution.py:64
  601.8 6.9 collective-permute-done.48
  (581 shorter events, 335.7 us)
Async XLA Ops:
  7.2 136.7 %all-gather.5.cloned.1.call-start = ((), (), s32[]{:S(2)}) async-start(), calls=%async_computation.6 | async-start | bytes 10813440 | tf_op jit(solution)/shard_map/all_gather | solution.py:1158
  11.1 18.1 %collective-permute-start.4 = (bf16[12,16,512]{2,1,0:T(8,128)(2,1)}, bf16[12,16,512]{2,1,0:T(8,128)(2,1)}, u32[]{:S(2)}, u32[]{:S(2)}) collective-permute-start(bf16[12,16,512]{2,1,0:T(8,128)(2,1)} %constant_dynamic-slice_fusion.10), channel_id=1, source_target_pairs={{0,2},{2,0},{4,6},{6,4},{1,3},{3,1},{5,7},{7,5},{8,10},{10,8},{12,... | collective-permute-start | bytes 589832 | tf_op jit(solution)/shard_map/ppermute | solution.py:64
  37.3 180.0 %all-gather.7.cloned.1.call-start = ((), (), s32[]{:S(2)}) async-start(), calls=%async_computation.7 | async-start | bytes 6488064 | tf_op jit(solution)/shard_map/all_gather | solution.py:1203
  39.4 18.8 %collective-permute-start.11 = (bf16[3,12,16,512]{3,2,1,0:T(8,128)(2,1)S(1)}, bf16[3,12,16,512]{3,2,1,0:T(8,128)(2,1)}, u32[]{:S(2)}, u32[]{:S(2)}) collective-permute-start(bf16[3,12,16,512]{3,2,1,0:T(8,128)(2,1)S(1)} %pad_maximum_fusion.2.refs_1_), channel_id=1, source_target_pairs={{0,8},{8,0},{16,24},{24,16},{1,9},{9,1},{17,25},{25,17},{2,10},{10... | collective-permute-start | bytes 1769480 | tf_op jit(solution)/shard_map/ppermute | solution.py:64
  41.2 28.2 %collective-permute-start.12 = (bf16[3,12,16,512]{3,2,1,0:T(8,128)(2,1)S(1)}, bf16[3,12,16,512]{3,2,1,0:T(8,128)(2,1)}, u32[]{:S(2)}, u32[]{:S(2)}) collective-permute-start(bf16[3,12,16,512]{3,2,1,0:T(8,128)(2,1)S(1)} %pad_maximum_fusion.2.refs_1_), channel_id=1, source_target_pairs={{0,16},{8,24},{16,0},{24,8},{1,17},{9,25},{17,1},{25,9},{2,18},{10... | collective-permute-start | bytes 1769480 | tf_op jit(solution)/shard_map/ppermute | solution.py:64
  42.7 26.6 %collective-permute-start.13 = (bf16[3,12,16,512]{3,2,1,0:T(8,128)(2,1)S(1)}, bf16[3,12,16,512]{3,2,1,0:T(8,128)(2,1)}, u32[]{:S(2)}, u32[]{:S(2)}) collective-permute-start(bf16[3,12,16,512]{3,2,1,0:T(8,128)(2,1)S(1)} %pad_maximum_fusion.2.refs_1_), channel_id=1, source_target_pairs={{0,24},{8,16},{16,8},{24,0},{1,25},{9,17},{17,9},{25,1},{2,26},{10... | collective-permute-start | bytes 1769480 | tf_op jit(solution)/shard_map/ppermute | solution.py:64
  50.9 19.1 %collective-permute-start.14 = (bf16[8,16,512]{2,1,0:T(8,128)(2,1)S(1)}, bf16[8,16,512]{2,1,0:T(8,128)(2,1)S(1)}, u32[]{:S(2)}, u32[]{:S(2)}) collective-permute-start(bf16[8,16,512]{2,1,0:T(8,128)(2,1)S(1)} %fusion.16), channel_id=1, source_target_pairs={{0,2},{2,0},{4,6},{6,4},{1,3},{3,1},{5,7},{7,5},{8,10},{10,8},{12,... | collective-permute-start | bytes 393224 | tf_op jit(solution)/shard_map/ppermute | solution.py:64
  76.8 23.1 %collective-permute-start.22 = (bf16[3,8,16,512]{3,2,1,0:T(8,128)(2,1)S(1)}, bf16[3,8,16,512]{3,2,1,0:T(8,128)(2,1)}, u32[]{:S(2)}, u32[]{:S(2)}) collective-permute-start(bf16[3,8,16,512]{3,2,1,0:T(8,128)(2,1)S(1)} %pad_maximum_fusion.3.refs_1_), channel_id=1, source_target_pairs={{0,8},{8,0},{16,24},{24,16},{1,9},{9,1},{17,25},{25,17},{2,10},{10... | collective-permute-start | bytes 1179656 | tf_op jit(solution)/shard_map/ppermute | solution.py:64
  77.8 22.1 %collective-permute-start.23 = (bf16[3,8,16,512]{3,2,1,0:T(8,128)(2,1)S(1)}, bf16[3,8,16,512]{3,2,1,0:T(8,128)(2,1)}, u32[]{:S(2)}, u32[]{:S(2)}) collective-permute-start(bf16[3,8,16,512]{3,2,1,0:T(8,128)(2,1)S(1)} %pad_maximum_fusion.3.refs_1_), channel_id=1, source_target_pairs={{0,16},{8,24},{16,0},{24,8},{1,17},{9,25},{17,1},{25,9},{2,18},{10... | collective-permute-start | bytes 1179656 | tf_op jit(solution)/shard_map/ppermute | solution.py:64
  79.0 22.7 %collective-permute-start.24 = (bf16[3,8,16,512]{3,2,1,0:T(8,128)(2,1)S(1)}, bf16[3,8,16,512]{3,2,1,0:T(8,128)(2,1)}, u32[]{:S(2)}, u32[]{:S(2)}) collective-permute-start(bf16[3,8,16,512]{3,2,1,0:T(8,128)(2,1)S(1)} %pad_maximum_fusion.3.refs_1_), channel_id=1, source_target_pairs={{0,24},{8,16},{16,8},{24,0},{1,25},{9,17},{17,9},{25,1},{2,26},{10... | collective-permute-start | bytes 1179656 | tf_op jit(solution)/shard_map/ppermute | solution.py:64
  103.5 20.0 %collective-permute-start.26 = (bf16[8,64,512]{2,1,0:T(8,128)(2,1)S(1)}, bf16[8,64,512]{2,1,0:T(8,128)(2,1)S(1)}, u32[]{:S(2)}, u32[]{:S(2)}) collective-permute-start(bf16[8,64,512]{2,1,0:T(8,128)(2,1)S(1)} %pad_maximum_fusion.1.refs_0_), channel_id=1, source_target_pairs={{0,1},{1,0},{2,3},{3,2},{4,5},{5,4},{6,7},{7,6},{8,9},{9,8},{10,11... | collective-permute-start | bytes 1572872 | tf_op jit(solution)/shard_map/ppermute | solution.py:64
  106.2 17.3 %collective-permute-start.27 = (bf16[3,8,16,512]{3,2,1,0:T(8,128)(2,1)S(1)}, bf16[3,8,16,512]{3,2,1,0:T(8,128)(2,1)S(1)}, u32[]{:S(2)}, u32[]{:S(2)}) collective-permute-start(bf16[3,8,16,512]{3,2,1,0:T(8,128)(2,1)S(1)} %pad_maximum_fusion.3.refs_1_), channel_id=1, source_target_pairs={{0,1},{1,0},{2,3},{3,2},{4,5},{5,4},{6,7},{7,6},{8,9},{9,8},{10,11... | collective-permute-start | bytes 1179656 | tf_op jit(solution)/shard_map/ppermute | solution.py:64
  106.2 17.3 %collective-permute-start.28 = (bf16[3,8,16,512]{3,2,1,0:T(8,128)(2,1)}, bf16[3,8,16,512]{3,2,1,0:T(8,128)(2,1)S(1)}, u32[]{:S(2)}, u32[]{:S(2)}) collective-permute-start(bf16[3,8,16,512]{3,2,1,0:T(8,128)(2,1)} %collective-permute-done.22.refs_2_), channel_id=1, source_target_pairs={{0,1},{1,0},{2,3},{3,2},{4,5},{5,4},{6,7},{7,6},{8,9},{9,8},{10,11... | collective-permute-start | bytes 1179656 | tf_op jit(solution)/shard_map/ppermute | solution.py:64
  124.5 258.0 %reduce-scatter.4.cloned.1.call-start = ((), (), s32[]{:S(2)}) async-start(), calls=%async_computation.3 | async-start | bytes 2228224 | tf_op jit(solution)/shard_map/reduce_scatter | solution.py:108
  159.3 18.5 %collective-permute-start.32 = (bf16[2,512,512]{2,1,0:T(8,128)(2,1)}, bf16[2,512,512]{2,1,0:T(8,128)(2,1)S(1)}, u32[]{:S(2)}, u32[]{:S(2)}) collective-permute-start(bf16[2,512,512]{2,1,0:T(8,128)(2,1)} %memory_pair.2.kv_own), channel_id=1, source_target_pairs={{0,1},{1,0},{2,3},{3,2},{4,5},{5,4},{6,7},{7,6},{8,9},{9,8},{10,11... | collective-permute-start | bytes 3145736 | tf_op jit(solution)/shard_map/ppermute | solution.py:64
  293.9 198.9 %reduce-scatter.6.cloned.1.call-start = ((), (), s32[]{:S(2)}) async-start(), calls=%async_computation.4 | async-start | bytes 4456448 | tf_op jit(solution)/shard_map/reduce_scatter | solution.py:108
  334.7 27.3 %collective-permute-start.37 = (f32[2,512,512]{2,1,0:T(8,128)}, f32[2,512,512]{2,1,0:T(8,128)}, u32[]{:S(2)}, u32[]{:S(2)}) collective-permute-start(f32[2,512,512]{2,1,0:T(8,128)} %get-tuple-element.645), channel_id=1, source_target_pairs={{0,1},{1,0},{2,3},{3,2},{4,5},{5,4},{6,7},{7,6},{8,9},{9,8},{10,11... | collective-permute-start | bytes 6291464 | tf_op jit(solution)/shard_map/ppermute | solution.py:64
  396.3 233.8 %reduce-scatter.8.cloned.1.call-start = ((), (), s32[]{:S(2)}) async-start(), calls=%async_computation.5 | async-start | bytes 4456448 | tf_op jit(solution)/shard_map/reduce_scatter | solution.py:108
  414.6 26.4 %collective-permute-start.40 = (f32[2,512,512]{2,1,0:T(8,128)}, f32[2,512,512]{2,1,0:T(8,128)S(1)}, u32[]{:S(2)}, u32[]{:S(2)}) collective-permute-start(f32[2,512,512]{2,1,0:T(8,128)} %get-tuple-element.673), channel_id=1, source_target_pairs={{0,1},{1,0},{2,3},{3,2},{4,5},{5,4},{6,7},{7,6},{8,9},{9,8},{10,11... | collective-permute-start | bytes 6291464 | tf_op jit(solution)/shard_map/ppermute | solution.py:64
  437.5 17.2 %collective-permute-start.41 = (bf16[8,16,512]{2,1,0:T(8,128)(2,1)S(1)}, bf16[8,16,512]{2,1,0:T(8,128)(2,1)S(1)}, u32[]{:S(2)}, u32[]{:S(2)}) collective-permute-start(bf16[8,16,512]{2,1,0:T(8,128)(2,1)S(1)} %bitcast.235), channel_id=1, source_target_pairs={{0,8},{8,0},{16,24},{24,16},{1,9},{9,1},{17,25},{25,17},{2,10},{10... | collective-permute-start | bytes 393224 | tf_op jit(solution)/shard_map/ppermute | solution.py:64
  437.5 17.2 %collective-permute-start.42 = (bf16[8,16,512]{2,1,0:T(8,128)(2,1)S(1)}, bf16[8,16,512]{2,1,0:T(8,128)(2,1)}, u32[]{:S(2)}, u32[]{:S(2)}) collective-permute-start(bf16[8,16,512]{2,1,0:T(8,128)(2,1)S(1)} %bitcast.236), channel_id=1, source_target_pairs={{0,16},{8,24},{16,0},{24,8},{1,17},{9,25},{17,1},{25,9},{2,18},{10... | collective-permute-start | bytes 393224 | tf_op jit(solution)/shard_map/ppermute | solution.py:64
  437.5 17.2 %collective-permute-start.43 = (bf16[8,16,512]{2,1,0:T(8,128)(2,1)S(1)}, bf16[8,16,512]{2,1,0:T(8,128)(2,1)}, u32[]{:S(2)}, u32[]{:S(2)}) collective-permute-start(bf16[8,16,512]{2,1,0:T(8,128)(2,1)S(1)} %bitcast.237), channel_id=1, source_target_pairs={{0,24},{8,16},{16,8},{24,0},{1,25},{9,17},{17,9},{25,1},{2,26},{10... | collective-permute-start | bytes 393224 | tf_op jit(solution)/shard_map/ppermute | solution.py:64
  475.4 17.4 %collective-permute-start.44 = (bf16[4,4,16,16,512]{4,3,2,1,0:T(8,128)(2,1)}, bf16[4,4,16,16,512]{4,3,2,1,0:T(8,128)(2,1)}, u32[]{:S(2)}, u32[]{:S(2)}) collective-permute-start(bf16[4,4,16,16,512]{4,3,2,1,0:T(8,128)(2,1)} %get-tuple-element.707), channel_id=1, source_target_pairs={{0,1},{1,0},{2,3},{3,2},{4,5},{5,4},{6,7},{7,6},{8,9},{9,8},{10,11... | collective-permute-start | bytes 12582920 | tf_op jit(solution)/shard_map/ppermute | solution.py:64
  557.9 36.0 %collective-permute-start.53 = (bf16[2,4,6,16,512]{4,3,2,1,0:T(8,128)(2,1)S(1)}, bf16[2,4,6,16,512]{4,3,2,1,0:T(8,128)(2,1)S(1)}, u32[]{:S(2)}, u32[]{:S(2)}) collective-permute-start(bf16[2,4,6,16,512]{4,3,2,1,0:T(8,128)(2,1)S(1)} %fusion.7), channel_id=1, source_target_pairs={{0,8},{8,0},{1,9},{9,1},{2,10},{10,2},{3,11},{11,3},{4,12},{12,4},... | collective-permute-start | bytes 2359304 | tf_op jit(solution)/shard_map/ppermute | solution.py:64
  557.9 36.5 %collective-permute-start.54 = (bf16[2,4,6,16,512]{4,3,2,1,0:T(8,128)(2,1)S(1)}, bf16[2,4,6,16,512]{4,3,2,1,0:T(8,128)(2,1)S(1)}, u32[]{:S(2)}, u32[]{:S(2)}) collective-permute-start(bf16[2,4,6,16,512]{4,3,2,1,0:T(8,128)(2,1)S(1)} %fusion.8), channel_id=1, source_target_pairs={{0,16},{16,0},{1,17},{17,1},{2,18},{18,2},{3,19},{19,3},{4,20},{20... | collective-permute-start | bytes 2359304 | tf_op jit(solution)/shard_map/ppermute | solution.py:64
  597.0 20.1 %collective-permute-start.55 = (bf16[4,6,16,512]{3,2,1,0:T(8,128)(2,1)}, bf16[4,6,16,512]{3,2,1,0:T(8,128)(2,1)S(1)}, u32[]{:S(2)}, u32[]{:S(2)}) collective-permute-start(bf16[4,6,16,512]{3,2,1,0:T(8,128)(2,1)} %get-tuple-element.774), channel_id=1, source_target_pairs={{0,16},{16,0},{1,17},{17,1},{2,18},{18,2},{3,19},{19,3},{4,20},{20... | collective-permute-start | bytes 1179656 | tf_op jit(solution)/shard_map/ppermute | solution.py:64
  597.7 19.4 %collective-permute-start.56 = (bf16[4,6,16,512]{3,2,1,0:T(8,128)(2,1)S(1)}, bf16[4,6,16,512]{3,2,1,0:T(8,128)(2,1)S(1)}, u32[]{:S(2)}, u32[]{:S(2)}) collective-permute-start(bf16[4,6,16,512]{3,2,1,0:T(8,128)(2,1)S(1)} %get-tuple-element.775), channel_id=1, source_target_pairs={{0,8},{8,0},{1,9},{9,1},{2,10},{10,2},{3,11},{11,3},{4,12},{12,4},... | collective-permute-start | bytes 1179656 | tf_op jit(solution)/shard_map/ppermute | solution.py:64
  626.6 28.6 %collective-permute-start.65 = (bf16[16,16,512]{2,1,0:T(8,128)(2,1)S(1)}, bf16[16,16,512]{2,1,0:T(8,128)(2,1)S(1)}, u32[]{:S(2)}, u32[]{:S(2)}) collective-permute-start(bf16[16,16,512]{2,1,0:T(8,128)(2,1)S(1)} %bitcast.225), channel_id=1, source_target_pairs={{0,8},{8,0},{16,24},{24,16},{1,9},{9,1},{17,25},{25,17},{2,10},{10... | collective-permute-start | bytes 786440 | tf_op jit(solution)/shard_map/ppermute | solution.py:64
  628.4 33.7 %collective-permute-start.66 = (bf16[16,16,512]{2,1,0:T(8,128)(2,1)S(1)}, bf16[16,16,512]{2,1,0:T(8,128)(2,1)S(1)}, u32[]{:S(2)}, u32[]{:S(2)}) collective-permute-start(bf16[16,16,512]{2,1,0:T(8,128)(2,1)S(1)} %bitcast.226), channel_id=1, source_target_pairs={{0,16},{8,24},{16,0},{24,8},{1,17},{9,25},{17,1},{25,9},{2,18},{10... | collective-permute-start | bytes 786440 | tf_op jit(solution)/shard_map/ppermute | solution.py:64
  630.0 33.5 %collective-permute-start.67 = (bf16[16,16,512]{2,1,0:T(8,128)(2,1)S(1)}, bf16[16,16,512]{2,1,0:T(8,128)(2,1)S(1)}, u32[]{:S(2)}, u32[]{:S(2)}) collective-permute-start(bf16[16,16,512]{2,1,0:T(8,128)(2,1)S(1)} %bitcast.227), channel_id=1, source_target_pairs={{0,24},{8,16},{16,8},{24,0},{1,25},{9,17},{17,9},{25,1},{2,26},{10... | collective-permute-start | bytes 786440 | tf_op jit(solution)/shard_map/ppermute | solution.py:64
  634.5 33.7 %collective-permute-start.68 = (bf16[16,16,512]{2,1,0:T(8,128)(2,1)}, bf16[16,16,512]{2,1,0:T(8,128)(2,1)S(1)}, u32[]{:S(2)}, u32[]{:S(2)}) collective-permute-start(bf16[16,16,512]{2,1,0:T(8,128)(2,1)} %bitcast.228), channel_id=1, source_target_pairs={{0,8},{8,0},{16,24},{24,16},{1,9},{9,1},{17,25},{25,17},{2,10},{10... | collective-permute-start | bytes 786440 | tf_op jit(solution)/shard_map/ppermute | solution.py:64
  654.5 16.9 %collective-permute-start.69 = (bf16[16,16,512]{2,1,0:T(8,128)(2,1)}, bf16[16,16,512]{2,1,0:T(8,128)(2,1)}, u32[]{:S(2)}, u32[]{:S(2)}) collective-permute-start(bf16[16,16,512]{2,1,0:T(8,128)(2,1)} %bitcast.229), channel_id=1, source_target_pairs={{0,16},{8,24},{16,0},{24,8},{1,17},{9,25},{17,1},{25,9},{2,18},{10... | collective-permute-start | bytes 786440 | tf_op jit(solution)/shard_map/ppermute | solution.py:64
  (161 other events, 1827.4 us)
Sparse Core Ops, SparseCore 0:
  37.4 100.6 all-gather.4
  141.2 67.9 all-gather.6
  294.0 88.4 reduce-scatter.3
  396.4 96.3 reduce-scatter.5
  500.5 94.7 reduce-scatter.7

commit v7 on v6

--- a/solution.py
+++ b/solution.py
@@ -246,6 +246,7 @@
 
 
 LIGHT = pl.CostEstimate(flops=1, bytes_accessed=1, transcendentals=0)
+SMALL = pltpu.CompilerParams(vmem_limit_bytes=32 << 20)
 ANY = pl.BlockSpec(memory_space=pl.ANY)
 ONCHIP = pl.BlockSpec(memory_space=pltpu.VMEM)
 SCALAR = pl.BlockSpec(memory_space=pltpu.SMEM)
@@ -272,6 +273,7 @@
         out_specs=[ONCHIP] * len(plan),
         scratch_shapes=[pltpu.SemaphoreType.DMA((len(plan),))],
         cost_estimate=LIGHT,
+        compiler_params=SMALL,
         name="place_weights",
     )(me, *mover.held, *mover.arrived)
     mover.held = []
@@ -306,6 +308,7 @@
         out_specs=[ONCHIP] * len(shapes),
         scratch_shapes=[pltpu.SemaphoreType.DMA((len(shapes),))],
         cost_estimate=LIGHT,
+        compiler_params=SMALL,
         name="place_gathered",
     )(pieces)
     return [
@@ -349,6 +352,7 @@
         out_specs=[ONCHIP, ONCHIP],
         scratch_shapes=[pltpu.SemaphoreType.DMA((2,))],
         cost_estimate=LIGHT,
+        compiler_params=SMALL,
         name="collect_gradients",
     )(me, *grads)
 
@@ -403,6 +407,7 @@
         in_specs=[first_part, first_part, *half_part, ONCHIP, ONCHIP],
         out_specs=[ONCHIP] * 4,
         cost_estimate=LIGHT,
+        compiler_params=SMALL,
         name="plane_sum",
     )(*mover.held)
     mover.held = [own]
@@ -416,6 +421,7 @@
         in_specs=[ONCHIP] * 4,
         out_specs=[ONCHIP, SCALAR],
         cost_estimate=LIGHT,
+        compiler_params=SMALL,
         name="line_sum",
     )(*mover.held, *mover.arrived)
     mover.squares = squares[0, 0]
@@ -722,6 +728,7 @@
             pltpu.SemaphoreType.DMA((2,)),
         ],
         cost_estimate=LIGHT,
+        compiler_params=SMALL,
         name="attend",
     )(*masks[causal, CF], q, kv, kv_oth)
 
@@ -751,6 +758,7 @@
             pltpu.SemaphoreType.DMA((2,)),
         ],
         cost_estimate=LIGHT,
+        compiler_params=SMALL,
         name="attend_back",
     )(*masks[causal, CK], q, kv, kv_oth, o, lse, grad)
 
@@ -899,6 +907,7 @@
         in_specs=[ONCHIP] * len(args),
         out_specs=[ONCHIP] * len(outs),
         cost_estimate=LIGHT,
+        compiler_params=SMALL,
         name=name,
     )(*args)
 
@@ -1387,6 +1396,7 @@
             out_specs=[ONCHIP] * len(shapes),
             scratch_shapes=[pltpu.SemaphoreType.DMA((len(shapes),))],
             cost_estimate=LIGHT,
+            compiler_params=SMALL,
             name="place_gradients",
         )(me, *parts)
         ready = [wide(array) for array in placed]

time: 719 us -> 688 us (0.957)
  Pallas kernels: 327 us -> 225 us
  local copies, waits for them, and re-layouts: 56.9 us -> 118 us
  waiting for transfers between devices: 140 us -> 161 us
  other arithmetic: 70.1 us -> 59 us
    pallas_call x20, Pallas kernels: 120 us -> 48.8 us  [on_chip(): pl.pallas_call(kernel, out_shape=[jax.ShapeDtypeStruct(shape, kind) for s...]
    unnamed x241 -> x501, local copies, waits for them, and re-layouts: 18.8 us -> 83.7 us
    reduce_scatter x3, waiting for transfers between devices: 24.9 us -> 41.5 us  [step(): lax.psum_scatter(array, PLANE + ('z',), scatter_dimension=0, tiled=True)]
    pallas_call x5, Pallas kernels: 82.5 us -> 69.3 us  [attend_back(): pl.pallas_call(attend_back_kernel, out_shape=[jax.ShapeDtypeStruct((n, wi...]
    pallas_call x2, Pallas kernels: 13.8 us -> 2.7 us  [unpack(): pl.pallas_call(functools.partial(unpack_kernel, tuple(zip(kinds, starts,...]
    convert_element_type x10, other arithmetic: 28.7 us -> 19.6 us  [low(): return v.astype(jnp.bfloat16)]
  transfers between devices with their start and end apart: 79 -> 79, of which waited for: 29 -> 32; matrix products, arithmetic and copies ran while one was open for 9% -> 8% of each run, Pallas kernels for 39% -> 28%
where the time goes in v7:
time: 688 us; the launch traced here: 678 us
  Pallas kernels  225 us (33%)
  waiting for transfers between devices  161 us (23%)
  local copies, waits for them, and re-layouts  118 us (17%)
  starting transfers between devices  83.5 us (12%)
  other arithmetic  59 us (9%)
  between operations  25.9 us (4%)
    ppermute x74, waiting for transfers between devices, flip(): return lax.ppermute(x, axis, [(i, i ^ bit) for i in range(n)])  120 us
    unnamed x501, local copies, waits for them, and re-layouts  83.7 us
    ppermute x74, starting transfers between devices, flip(): return lax.ppermute(x, axis, [(i, i ^ bit) for i in range(n)])  82.6 us
    pallas_call x5, Pallas kernels, attend_back(): pl.pallas_call(attend_back_kernel, out_shape=[jax.ShapeDtypeStruct((n, wi...  69.3 us
    pallas_call x5, Pallas kernels, attend(): pl.pallas_call(attend_kernel, out_shape=[jax.ShapeDtypeStruct((n, width),...  51.4 us
    pallas_call x20, Pallas kernels, on_chip(): pl.pallas_call(kernel, out_shape=[jax.ShapeDtypeStruct(shape, kind) for s...  48.8 us
    reduce_scatter x3, waiting for transfers between devices, step(): lax.psum_scatter(array, PLANE + ('z',), scatter_dimension=0, tiled=True)  41.5 us
    pallas_call x4, Pallas kernels, collect(): pl.pallas_call(functools.partial(collect_kernel, plan, unit, ordered), ou...  30.6 us
  transfers between devices with their start and end apart: 79, of which 32 were waited for; matrix products, arithmetic and copies ran while one was open for 8% of the time, Pallas kernels for 28%

profile of v7, /device:TPU:0, one launch (start us, length us, event | category | flops | bytes accessed | tf_op | source)
XLA Modules:
  0.0 678.0 jit_solution(18207287368086232623)
XLA Ops:
  30.2 6.9 %collective-permute-done.6 = bf16[12,16,512]{2,1,0:T(8,128)(2,1)S(1)} collective-permute-done((bf16[12,16,512]{2,1,0:T(8,128)(2,1)}, bf16[12,16,512]{2,1,0:T(8,128)(2,1)S(1)}, u32[]{:S(2)}, u32[]{:S(2)}) %collective-permute-start.6) | collective-permute-done | bytes 196640 | tf_op jit(solution)/shard_map/ppermute | solution.py:64
  60.0 11.0 %collective-permute-done.12.refs_3_ = bf16[3,12,16,512]{3,2,1,0:T(8,128)(2,1)} collective-permute-done((bf16[3,12,16,512]{3,2,1,0:T(8,128)(2,1)S(1)}, bf16[3,12,16,512]{3,2,1,0:T(8,128)(2,1)}, u32[]{:S(2)}, u32[]{:S(2)}) %collective-permute-start.12) | collective-permute-done | bytes 589856 | tf_op jit(solution)/shard_map/ppermute | solution.py:64
  88.4 6.7 gather_fusion
  116.9 10.7 %attend.5 = (bf16[512,512]{1,0:T(8,128)(2,1)S(1)}, f32[4,4,1,256]{3,2,1,0:T(1,128)S(1)}) custom-call(s32[18]{0:T(128)S(1)} %pad_add_fusion.7.act, s32[8,512]{1,0:T(8,128)S(1)} %pad.7.bounds, bf16[512,512]{1,0:T(8,128)(2,1)S(1)} %copy-done.66, bf16[2,512,512]{2,1,0:T(8,128)(2,1)S(1)} %copy-done.54, bf16[2,512,512]{2,1,0:T(8,128)(2,1)} %collective-permute-done.25.kv_oth), custom_call_target="tpu_custom_call" | custom-call | flops 1 | bytes 1 | tf_op jit(solution)/shard_map/attend/pallas_call | solution.py:711
  169.8 8.6 %attend.6 = (bf16[512,512]{1,0:T(8,128)(2,1)S(1)}, f32[4,4,1,256]{3,2,1,0:T(1,128)S(1)}) custom-call(s32[18]{0:T(128)S(1)} %pad_add_fusion.10.act, s32[8,512]{1,0:T(8,128)S(1)} %pad.8.bounds, bf16[512,512]{1,0:T(8,128)(2,1)S(1)} %copy-done.69, bf16[2,512,512]{2,1,0:T(8,128)(2,1)} %get-tuple-element.565.kv_own, ...), custom_call_target="tpu_custom_call" | custom-call | flops 1 | bytes 1 | tf_op jit(solution)/shard_map/attend/pallas_call | solution.py:711
  180.1 11.8 %attend.7 = (bf16[512,512]{1,0:T(8,128)(2,1)S(1)}, f32[4,4,1,256]{3,2,1,0:T(1,128)S(1)}) custom-call(s32[18]{0:T(128)S(1)} %copy-done.159, s32[8,512]{1,0:T(8,128)S(1)} %pad.7.bounds, bf16[512,512]{1,0:T(8,128)(2,1)S(1)} %get-tuple-element.569.q, bf16[2,512,512]{2,1,0:T(8,128)(2,1)} %memory_pair.2.kv_own, bf16[2,512,512]{2,1,0:T(8,128)(2,1)} %collective-permute-done.32.kv_oth), custom_call_target="tpu_custom_call" | custom-call | flops 1 | bytes 1 | tf_op jit(solution)/shard_map/attend/pallas_call | solution.py:711
  205.0 8.6 %attend.8 = (bf16[512,512]{1,0:T(8,128)(2,1)S(1)}, f32[4,4,1,256]{3,2,1,0:T(1,128)S(1)}) custom-call(s32[18]{0:T(128)S(1)} %pad_add_fusion.10.act, s32[8,512]{1,0:T(8,128)S(1)} %pad.8.bounds, bf16[512,512]{1,0:T(8,128)(2,1)S(1)} %copy-done.80, bf16[2,512,512]{2,1,0:T(8,128)(2,1)} %get-tuple-element.579.kv_own, ...), custom_call_target="tpu_custom_call" | custom-call | flops 1 | bytes 1 | tf_op jit(solution)/shard_map/attend/pallas_call | solution.py:711
  232.3 11.8 %attend.9 = (bf16[512,512]{1,0:T(8,128)(2,1)S(1)}, f32[4,4,1,256]{3,2,1,0:T(1,128)S(1)}) custom-call(s32[18]{0:T(128)S(1)} %copy-done.159, s32[8,512]{1,0:T(8,128)S(1)} %pad.7.bounds, bf16[512,512]{1,0:T(8,128)(2,1)S(1)} %get-tuple-element.586.q, bf16[2,512,512]{2,1,0:T(8,128)(2,1)} %memory_pair.3.kv_own, bf16[2,512,512]{2,1,0:T(8,128)(2,1)} %collective-permute-done.34.kv_oth), custom_call_target="tpu_custom_call" | custom-call | flops 1 | bytes 1 | tf_op jit(solution)/shard_map/attend/pallas_call | solution.py:711
  253.8 5.8 feed_back.3
  274.0 16.4 %attend_back.5 = (bf16[512,512]{1,0:T(8,128)(2,1)S(1)}, f32[2,512,512]{2,1,0:T(8,128)S(1)}, f32[2,512,512]{2,1,0:T(8,128)}) custom-call(s32[18]{0:T(128)S(1)} %copy-done.159, s32[8,512]{1,0:T(8,128)S(1)} %pad.7.bounds, bf16[512,512]{1,0:T(8,128)(2,1)S(1)} %copy-done.83, bf16[2,512,512]{2,1,0:T(8,128)(2,1)} %memory_pair.3.kv_own, ...), custom_call_target="tpu_custom_call" | custom-call | flops 1 | bytes 1 | tf_op jit(solution)/shard_map/attend_back/pallas_call | solution.py:740
  294.4 11.3 %attend_back.6 = (bf16[512,512]{1,0:T(8,128)(2,1)S(1)}, f32[2,512,512]{2,1,0:T(8,128)S(1)}, f32[2,512,512]{2,1,0:T(8,128)S(1)}) custom-call(s32[18]{0:T(128)S(1)} %pad_add_fusion.10.act, s32[8,512]{1,0:T(8,128)S(1)} %pad.8.bounds, bf16[512,512]{1,0:T(8,128)(2,1)S(1)} %copy-done.81, bf16[2,512,512]{2,1,0:T(8,128)(2,1)} %get-tuple-element.579.kv_own, ...), custom_call_target="tpu_custom_call" | custom-call | flops 1 | bytes 1 | tf_op jit(solution)/shard_map/attend_back/pallas_call | solution.py:740
  310.7 4.5 collective-permute-done.36.other
  319.6 5.8 feed_back.4
  327.8 7.8 %collect_gradients.5 = (bf16[4,4,16,16,512]{4,3,2,1,0:T(8,128)(2,1)S(1)}, bf16[4,4,16,16,512]{4,3,2,1,0:T(8,128)(2,1)S(1)}) custom-call(s32[3]{0:T(128)S(1)} %copy-done.155, bf16[3,512,512]{2,1,0:T(8,128)(2,1)S(1)} %get-tuple-element.641.refs_0_, bf16[1,512,512]{2,1,0:T(8,128)(2,1)S(1)} %get-tuple-element.642.refs_1_, ...), custom_call_target="tpu_custom_call" | custom-call | flops 1 | bytes 1 | tf_op jit(solution)/shard_map/collect_gradients/pallas_call | solution.py:348
  339.7 19.3 %reduce-scatter.4.cloned.1.call-done = bf16[1,8,16,512]{3,2,1,0:T(8,128)(2,1)} async-done(((bf16[16,8,16,512]{3,2,1,0:T(8,128)(2,1)}), bf16[1,8,16,512]{3,2,1,0:T(8,128)(2,1)}) %reduce-scatter.4.cloned.1.call-update) | async-done | bytes 131088 | tf_op jit(solution)/shard_map/reduce_scatter | solution.py:108
  359.0 7.4 %collective-permute-done.38 = bf16[4,4,16,16,512]{4,3,2,1,0:T(8,128)(2,1)S(1)} collective-permute-done((bf16[4,4,16,16,512]{4,3,2,1,0:T(8,128)(2,1)}, bf16[4,4,16,16,512]{4,3,2,1,0:T(8,128)(2,1)S(1)}, u32[]{:S(2)}, u32[]{:S(2)}) %collective-permute-start.38) | collective-permute-done | bytes 4194336 | tf_op jit(solution)/shard_map/ppermute | solution.py:64
  366.4 6.4 add_convert_fusion.1
  375.9 15.2 %attend_back.7 = (bf16[512,512]{1,0:T(8,128)(2,1)S(1)}, f32[2,512,512]{2,1,0:T(8,128)S(1)}, f32[2,512,512]{2,1,0:T(8,128)S(1)}) custom-call(s32[18]{0:T(128)S(1)} %copy-done.159, s32[8,512]{1,0:T(8,128)S(1)} %pad.7.bounds, bf16[512,512]{1,0:T(8,128)(2,1)S(1)} %copy-done.75, bf16[2,512,512]{2,1,0:T(8,128)(2,1)} %memory_pair.2.kv_own, ...), custom_call_target="tpu_custom_call" | custom-call | flops 1 | bytes 1 | tf_op jit(solution)/shard_map/attend_back/pallas_call | solution.py:740
  393.2 11.1 %attend_back.8 = (bf16[512,512]{1,0:T(8,128)(2,1)S(1)}, f32[2,512,512]{2,1,0:T(8,128)S(1)}, f32[2,512,512]{2,1,0:T(8,128)S(1)}) custom-call(s32[18]{0:T(128)S(1)} %pad_add_fusion.10.act, s32[8,512]{1,0:T(8,128)S(1)} %pad.8.bounds, bf16[512,512]{1,0:T(8,128)(2,1)S(1)} %copy-done.70, bf16[2,512,512]{2,1,0:T(8,128)(2,1)} %get-tuple-element.565.kv_own, ...), custom_call_target="tpu_custom_call" | custom-call | flops 1 | bytes 1 | tf_op jit(solution)/shard_map/attend_back/pallas_call | solution.py:740
  417.3 4.6 collective-permute-done.42.refs_2_
  424.9 5.7 feed_back.5
  431.6 10.0 %collect_gradients.6 = (bf16[4,4,16,16,512]{4,3,2,1,0:T(8,128)(2,1)S(1)}, bf16[4,4,16,16,512]{4,3,2,1,0:T(8,128)(2,1)}) custom-call(s32[3]{0:T(128)S(1)} %copy-done.156, bf16[3,512,512]{2,1,0:T(8,128)(2,1)S(1)} %get-tuple-element.689.refs_0_, bf16[1,512,512]{2,1,0:T(8,128)(2,1)S(1)} %get-tuple-element.690.refs_1_, ...), custom_call_target="tpu_custom_call" | custom-call | flops 1 | bytes 1 | tf_op jit(solution)/shard_map/collect_gradients/pallas_call | solution.py:348
  443.6 22.2 %reduce-scatter.6.cloned.1.call-done = bf16[1,16,16,512]{3,2,1,0:T(8,128)(2,1)} async-done(((bf16[16,16,16,512]{3,2,1,0:T(8,128)(2,1)}), bf16[1,16,16,512]{3,2,1,0:T(8,128)(2,1)}) %reduce-scatter.6.cloned.1.call-update) | async-done | bytes 262160 | tf_op jit(solution)/shard_map/reduce_scatter | solution.py:108
  465.8 7.7 %add_convert_fusion = bf16[4,4,16,16,512]{4,3,2,1,0:T(8,128)(2,1)} fusion(bf16[4,4,16,16,512]{4,3,2,1,0:T(8,128)(2,1)} %collective-permute-done.44, bf16[4,4,16,16,512]{4,3,2,1,0:T(8,128)(2,1)} %copy-done.52), kind=kLoop, calls=%fused_computation.2 | loop fusion | flops 8388608 | bytes 12582912 | tf_op jit(solution)/shard_map/convert_element_type | solution.py:146
  476.0 15.3 %attend_back.9 = (bf16[512,512]{1,0:T(8,128)(2,1)S(1)}, f32[2,512,512]{2,1,0:T(8,128)S(1)}, f32[2,512,512]{2,1,0:T(8,128)S(1)}) custom-call(s32[18]{0:T(128)S(1)} %copy-done.160, s32[8,512]{1,0:T(8,128)S(1)} %pad.7.bounds, bf16[512,512]{1,0:T(8,128)(2,1)S(1)} %copy-done.67, bf16[2,512,512]{2,1,0:T(8,128)(2,1)S(1)} %copy-done.55, ...), custom_call_target="tpu_custom_call" | custom-call | flops 1 | bytes 1 | tf_op jit(solution)/shard_map/attend_back/pallas_call | solution.py:740
  500.0 7.1 %table_back.1 = bf16[4096,512]{1,0:T(8,128)(2,1)S(1)} custom-call(s32[8,1024]{1,0:T(8,128)S(1)} %broadcast_in_dim.17.ids, bf16[1024,512]{1,0:T(8,128)(2,1)S(1)} %fusion.token_grads, bf16[128,4096]{1,0:T(8,128)(2,1)S(1)} %copy-done.15, bf16[128,512]{1,0:T(8,128)(2,1)S(1)} %pad_maximum_fusion.5.exits), custom_call_target="tpu_custom_call" | custom-call | flops 1 | bytes 1 | tf_op jit(solution)/shard_map/table_back/pallas_call | solution.py:886
  507.1 8.7 %collect_gradients.7 = (bf16[4,4,12,16,512]{4,3,2,1,0:T(8,128)(2,1)S(1)}, bf16[4,4,12,16,512]{4,3,2,1,0:T(8,128)(2,1)S(1)}) custom-call(s32[3]{0:T(128)S(1)} %copy-done.156, bf16[8,4,8,16,512]{4,3,2,1,0:T(8,128)(2,1)S(1)} %bitcast.179, bf16[3,512,512]{2,1,0:T(8,128)(2,1)S(1)} %get-tuple-element.721.refs_1_, bf16[1,512,512]{2,1,0:T(8,128)(2,1)S(1)} %copy-done.121), custom_call_target="tpu_custom_call" | custom-call | flops 1 | bytes 1 | tf_op jit(solution)/shard_map/collect_gradients/pallas_call | solution.py:348
  515.9 5.5 collective-permute-done.46
  524.4 34.3 %collective-permute-done.53.from_x = bf16[2,4,6,16,512]{4,3,2,1,0:T(8,128)(2,1)S(1)} collective-permute-done((bf16[2,4,6,16,512]{4,3,2,1,0:T(8,128)(2,1)S(1)}, bf16[2,4,6,16,512]{4,3,2,1,0:T(8,128)(2,1)S(1)}, u32[]{:S(2)}, u32[]{:S(2)}) %collective-permute-start.53) | collective-permute-done | bytes 786464 | tf_op jit(solution)/shard_map/ppermute | solution.py:64
  566.2 8.0 %collective-permute-done.48 = f32[12,512]{1,0:T(8,128)S(1)} collective-permute-done((f32[12,512]{1,0:T(8,128)S(1)}, f32[12,512]{1,0:T(8,128)S(1)}, u32[]{:S(2)}, u32[]{:S(2)}) %collective-permute-start.48) | collective-permute-done | bytes 24608 | tf_op jit(solution)/shard_map/ppermute | solution.py:64
  647.0 5.1 place_gradients.1
  652.2 5.9 multiply_subtract_fusion
  (841 shorter events, 324.9 us)
Async XLA Ops:
  7.2 144.9 %all-gather.5.cloned.1.call-start = ((), (), s32[]{:S(2)}) async-start(), calls=%async_computation.6 | async-start | bytes 10813440 | tf_op jit(solution)/shard_map/all_gather | solution.py:1167
  11.7 18.5 %collective-permute-start.4 = (bf16[12,16,512]{2,1,0:T(8,128)(2,1)}, bf16[12,16,512]{2,1,0:T(8,128)(2,1)}, u32[]{:S(2)}, u32[]{:S(2)}) collective-permute-start(bf16[12,16,512]{2,1,0:T(8,128)(2,1)} %constant_dynamic-slice_fusion.10), channel_id=1, source_target_pairs={{0,2},{2,0},{4,6},{6,4},{1,3},{3,1},{5,7},{7,5},{8,10},{10,8},{12,... | collective-permute-start | bytes 589832 | tf_op jit(solution)/shard_map/ppermute | solution.py:64
  39.0 175.4 %all-gather.7.cloned.1.call-start = ((), (), s32[]{:S(2)}) async-start(), calls=%async_computation.7 | async-start | bytes 6488064 | tf_op jit(solution)/shard_map/all_gather | solution.py:1212
  41.0 18.7 %collective-permute-start.11 = (bf16[3,12,16,512]{3,2,1,0:T(8,128)(2,1)S(1)}, bf16[3,12,16,512]{3,2,1,0:T(8,128)(2,1)S(1)}, u32[]{:S(2)}, u32[]{:S(2)}) collective-permute-start(bf16[3,12,16,512]{3,2,1,0:T(8,128)(2,1)S(1)} %pad_maximum_fusion.2.refs_1_), channel_id=1, source_target_pairs={{0,8},{8,0},{16,24},{24,16},{1,9},{9,1},{17,25},{25,17},{2,10},{10... | collective-permute-start | bytes 1769480 | tf_op jit(solution)/shard_map/ppermute | solution.py:64
  42.8 28.2 %collective-permute-start.12 = (bf16[3,12,16,512]{3,2,1,0:T(8,128)(2,1)S(1)}, bf16[3,12,16,512]{3,2,1,0:T(8,128)(2,1)}, u32[]{:S(2)}, u32[]{:S(2)}) collective-permute-start(bf16[3,12,16,512]{3,2,1,0:T(8,128)(2,1)S(1)} %pad_maximum_fusion.2.refs_1_), channel_id=1, source_target_pairs={{0,16},{8,24},{16,0},{24,8},{1,17},{9,25},{17,1},{25,9},{2,18},{10... | collective-permute-start | bytes 1769480 | tf_op jit(solution)/shard_map/ppermute | solution.py:64
  44.3 26.7 %collective-permute-start.13 = (bf16[3,12,16,512]{3,2,1,0:T(8,128)(2,1)S(1)}, bf16[3,12,16,512]{3,2,1,0:T(8,128)(2,1)}, u32[]{:S(2)}, u32[]{:S(2)}) collective-permute-start(bf16[3,12,16,512]{3,2,1,0:T(8,128)(2,1)S(1)} %pad_maximum_fusion.2.refs_1_), channel_id=1, source_target_pairs={{0,24},{8,16},{16,8},{24,0},{1,25},{9,17},{17,9},{25,1},{2,26},{10... | collective-permute-start | bytes 1769480 | tf_op jit(solution)/shard_map/ppermute | solution.py:64
  52.5 19.1 %collective-permute-start.14 = (bf16[8,16,512]{2,1,0:T(8,128)(2,1)S(1)}, bf16[8,16,512]{2,1,0:T(8,128)(2,1)S(1)}, u32[]{:S(2)}, u32[]{:S(2)}) collective-permute-start(bf16[8,16,512]{2,1,0:T(8,128)(2,1)S(1)} %fusion.16), channel_id=1, source_target_pairs={{0,2},{2,0},{4,6},{6,4},{1,3},{3,1},{5,7},{7,5},{8,10},{10,8},{12,... | collective-permute-start | bytes 393224 | tf_op jit(solution)/shard_map/ppermute | solution.py:64
  55.2 16.5 %collective-permute-start.15 = (bf16[8,16,512]{2,1,0:T(8,128)(2,1)S(1)}, bf16[8,16,512]{2,1,0:T(8,128)(2,1)S(1)}, u32[]{:S(2)}, u32[]{:S(2)}) collective-permute-start(bf16[8,16,512]{2,1,0:T(8,128)(2,1)S(1)} %fusion.16), channel_id=1, source_target_pairs={{0,4},{2,6},{4,0},{6,2},{1,5},{3,7},{5,1},{7,3},{8,12},{10,14},{12... | collective-permute-start | bytes 393224 | tf_op jit(solution)/shard_map/ppermute | solution.py:64
  76.3 23.9 %collective-permute-start.22 = (bf16[3,8,16,512]{3,2,1,0:T(8,128)(2,1)S(1)}, bf16[3,8,16,512]{3,2,1,0:T(8,128)(2,1)}, u32[]{:S(2)}, u32[]{:S(2)}) collective-permute-start(bf16[3,8,16,512]{3,2,1,0:T(8,128)(2,1)S(1)} %pad_maximum_fusion.3.refs_1_), channel_id=1, source_target_pairs={{0,8},{8,0},{16,24},{24,16},{1,9},{9,1},{17,25},{25,17},{2,10},{10... | collective-permute-start | bytes 1179656 | tf_op jit(solution)/shard_map/ppermute | solution.py:64
  77.3 22.9 %collective-permute-start.23 = (bf16[3,8,16,512]{3,2,1,0:T(8,128)(2,1)S(1)}, bf16[3,8,16,512]{3,2,1,0:T(8,128)(2,1)}, u32[]{:S(2)}, u32[]{:S(2)}) collective-permute-start(bf16[3,8,16,512]{3,2,1,0:T(8,128)(2,1)S(1)} %pad_maximum_fusion.3.refs_1_), channel_id=1, source_target_pairs={{0,16},{8,24},{16,0},{24,8},{1,17},{9,25},{17,1},{25,9},{2,18},{10... | collective-permute-start | bytes 1179656 | tf_op jit(solution)/shard_map/ppermute | solution.py:64
  78.4 24.7 %collective-permute-start.24 = (bf16[3,8,16,512]{3,2,1,0:T(8,128)(2,1)S(1)}, bf16[3,8,16,512]{3,2,1,0:T(8,128)(2,1)}, u32[]{:S(2)}, u32[]{:S(2)}) collective-permute-start(bf16[3,8,16,512]{3,2,1,0:T(8,128)(2,1)S(1)} %pad_maximum_fusion.3.refs_1_), channel_id=1, source_target_pairs={{0,24},{8,16},{16,8},{24,0},{1,25},{9,17},{17,9},{25,1},{2,26},{10... | collective-permute-start | bytes 1179656 | tf_op jit(solution)/shard_map/ppermute | solution.py:64
  109.0 22.3 %collective-permute-start.26 = (bf16[8,64,512]{2,1,0:T(8,128)(2,1)}, bf16[8,64,512]{2,1,0:T(8,128)(2,1)}, u32[]{:S(2)}, u32[]{:S(2)}) collective-permute-start(bf16[8,64,512]{2,1,0:T(8,128)(2,1)} %pad_maximum_fusion.1.refs_0_), channel_id=1, source_target_pairs={{0,1},{1,0},{2,3},{3,2},{4,5},{5,4},{6,7},{7,6},{8,9},{9,8},{10,11... | collective-permute-start | bytes 1572872 | tf_op jit(solution)/shard_map/ppermute | solution.py:64
  112.3 16.8 %collective-permute-start.28 = (bf16[3,8,16,512]{3,2,1,0:T(8,128)(2,1)}, bf16[3,8,16,512]{3,2,1,0:T(8,128)(2,1)S(1)}, u32[]{:S(2)}, u32[]{:S(2)}) collective-permute-start(bf16[3,8,16,512]{3,2,1,0:T(8,128)(2,1)} %collective-permute-done.22.refs_2_), channel_id=1, source_target_pairs={{0,1},{1,0},{2,3},{3,2},{4,5},{5,4},{6,7},{7,6},{8,9},{9,8},{10,11... | collective-permute-start | bytes 1179656 | tf_op jit(solution)/shard_map/ppermute | solution.py:64
  112.8 17.0 %collective-permute-start.29 = (bf16[3,8,16,512]{3,2,1,0:T(8,128)(2,1)}, bf16[3,8,16,512]{3,2,1,0:T(8,128)(2,1)S(1)}, u32[]{:S(2)}, u32[]{:S(2)}) collective-permute-start(bf16[3,8,16,512]{3,2,1,0:T(8,128)(2,1)} %collective-permute-done.23.refs_3_), channel_id=1, source_target_pairs={{0,1},{1,0},{2,3},{3,2},{4,5},{5,4},{6,7},{7,6},{8,9},{9,8},{10,11... | collective-permute-start | bytes 1179656 | tf_op jit(solution)/shard_map/ppermute | solution.py:64
  112.8 17.7 %collective-permute-start.30 = (bf16[3,8,16,512]{3,2,1,0:T(8,128)(2,1)}, bf16[3,8,16,512]{3,2,1,0:T(8,128)(2,1)S(1)}, u32[]{:S(2)}, u32[]{:S(2)}) collective-permute-start(bf16[3,8,16,512]{3,2,1,0:T(8,128)(2,1)} %collective-permute-done.24.refs_4_), channel_id=1, source_target_pairs={{0,1},{1,0},{2,3},{3,2},{4,5},{5,4},{6,7},{7,6},{8,9},{9,8},{10,11... | collective-permute-start | bytes 1179656 | tf_op jit(solution)/shard_map/ppermute | solution.py:64
  132.1 226.9 %reduce-scatter.4.cloned.1.call-start = ((), (), s32[]{:S(2)}) async-start(), calls=%async_computation.3 | async-start | bytes 2228224 | tf_op jit(solution)/shard_map/reduce_scatter | solution.py:108
  270.4 195.4 %reduce-scatter.6.cloned.1.call-start = ((), (), s32[]{:S(2)}) async-start(), calls=%async_computation.4 | async-start | bytes 4456448 | tf_op jit(solution)/shard_map/reduce_scatter | solution.py:108
  372.8 227.1 %reduce-scatter.8.cloned.1.call-start = ((), (), s32[]{:S(2)}) async-start(), calls=%async_computation.5 | async-start | bytes 4456448 | tf_op jit(solution)/shard_map/reduce_scatter | solution.py:108
  391.2 20.3 %collective-permute-start.40 = (f32[2,512,512]{2,1,0:T(8,128)S(1)}, f32[2,512,512]{2,1,0:T(8,128)S(1)}, u32[]{:S(2)}, u32[]{:S(2)}) collective-permute-start(f32[2,512,512]{2,1,0:T(8,128)S(1)} %get-tuple-element.673), channel_id=1, source_target_pairs={{0,1},{1,0},{2,3},{3,2},{4,5},{5,4},{6,7},{7,6},{8,9},{9,8},{10,11... | collective-permute-start | bytes 6291464 | tf_op jit(solution)/shard_map/ppermute | solution.py:64
  443.6 22.2 %collective-permute-start.44 = (bf16[4,4,16,16,512]{4,3,2,1,0:T(8,128)(2,1)}, bf16[4,4,16,16,512]{4,3,2,1,0:T(8,128)(2,1)}, u32[]{:S(2)}, u32[]{:S(2)}) collective-permute-start(bf16[4,4,16,16,512]{4,3,2,1,0:T(8,128)(2,1)} %get-tuple-element.707), channel_id=1, source_target_pairs={{0,1},{1,0},{2,3},{3,2},{4,5},{5,4},{6,7},{7,6},{8,9},{9,8},{10,11... | collective-permute-start | bytes 12582920 | tf_op jit(solution)/shard_map/ppermute | solution.py:64
  522.2 36.5 %collective-permute-start.53 = (bf16[2,4,6,16,512]{4,3,2,1,0:T(8,128)(2,1)S(1)}, bf16[2,4,6,16,512]{4,3,2,1,0:T(8,128)(2,1)S(1)}, u32[]{:S(2)}, u32[]{:S(2)}) collective-permute-start(bf16[2,4,6,16,512]{4,3,2,1,0:T(8,128)(2,1)S(1)} %fusion.7), channel_id=1, source_target_pairs={{0,8},{8,0},{1,9},{9,1},{2,10},{10,2},{3,11},{11,3},{4,12},{12,4},... | collective-permute-start | bytes 2359304 | tf_op jit(solution)/shard_map/ppermute | solution.py:64
  522.3 36.6 %collective-permute-start.54 = (bf16[2,4,6,16,512]{4,3,2,1,0:T(8,128)(2,1)S(1)}, bf16[2,4,6,16,512]{4,3,2,1,0:T(8,128)(2,1)S(1)}, u32[]{:S(2)}, u32[]{:S(2)}) collective-permute-start(bf16[2,4,6,16,512]{4,3,2,1,0:T(8,128)(2,1)S(1)} %fusion.8), channel_id=1, source_target_pairs={{0,16},{16,0},{1,17},{17,1},{2,18},{18,2},{3,19},{19,3},{4,20},{20... | collective-permute-start | bytes 2359304 | tf_op jit(solution)/shard_map/ppermute | solution.py:64
  560.2 23.0 %collective-permute-start.55 = (bf16[4,6,16,512]{3,2,1,0:T(8,128)(2,1)}, bf16[4,6,16,512]{3,2,1,0:T(8,128)(2,1)}, u32[]{:S(2)}, u32[]{:S(2)}) collective-permute-start(bf16[4,6,16,512]{3,2,1,0:T(8,128)(2,1)} %get-tuple-element.774), channel_id=1, source_target_pairs={{0,16},{16,0},{1,17},{17,1},{2,18},{18,2},{3,19},{19,3},{4,20},{20... | collective-permute-start | bytes 1179656 | tf_op jit(solution)/shard_map/ppermute | solution.py:64
  562.1 21.1 %collective-permute-start.56 = (bf16[4,6,16,512]{3,2,1,0:T(8,128)(2,1)}, bf16[4,6,16,512]{3,2,1,0:T(8,128)(2,1)}, u32[]{:S(2)}, u32[]{:S(2)}) collective-permute-start(bf16[4,6,16,512]{3,2,1,0:T(8,128)(2,1)} %get-tuple-element.775), channel_id=1, source_target_pairs={{0,8},{8,0},{1,9},{9,1},{2,10},{10,2},{3,11},{11,3},{4,12},{12,4},... | collective-permute-start | bytes 1179656 | tf_op jit(solution)/shard_map/ppermute | solution.py:64
  578.8 16.5 %collective-permute-start.50 = (f32[12,512]{1,0:T(8,128)}, f32[12,512]{1,0:T(8,128)}, u32[]{:S(2)}, u32[]{:S(2)}) collective-permute-start(f32[12,512]{1,0:T(8,128)} %add.435), channel_id=1, source_target_pairs={{0,2},{2,0},{4,6},{6,4},{1,3},{3,1},{5,7},{7,5},{8,10},{10,8},{12,... | collective-permute-start | bytes 73736 | tf_op jit(solution)/shard_map/ppermute | solution.py:64
  578.8 18.3 %collective-permute-start.51 = (f32[12,512]{1,0:T(8,128)}, f32[12,512]{1,0:T(8,128)}, u32[]{:S(2)}, u32[]{:S(2)}) collective-permute-start(f32[12,512]{1,0:T(8,128)} %add.435), channel_id=1, source_target_pairs={{0,4},{2,6},{4,0},{6,2},{1,5},{3,7},{5,1},{7,3},{8,12},{10,14},{12... | collective-permute-start | bytes 73736 | tf_op jit(solution)/shard_map/ppermute | solution.py:64
  581.1 16.6 %collective-permute-start.52 = (f32[12,512]{1,0:T(8,128)}, f32[12,512]{1,0:T(8,128)}, u32[]{:S(2)}, u32[]{:S(2)}) collective-permute-start(f32[12,512]{1,0:T(8,128)} %add.435), channel_id=1, source_target_pairs={{0,6},{2,4},{4,2},{6,0},{1,7},{3,5},{5,3},{7,1},{8,14},{10,12},{12... | collective-permute-start | bytes 73736 | tf_op jit(solution)/shard_map/ppermute | solution.py:64
  595.3 28.4 %collective-permute-start.65 = (bf16[16,16,512]{2,1,0:T(8,128)(2,1)S(1)}, bf16[16,16,512]{2,1,0:T(8,128)(2,1)S(1)}, u32[]{:S(2)}, u32[]{:S(2)}) collective-permute-start(bf16[16,16,512]{2,1,0:T(8,128)(2,1)S(1)} %bitcast.215), channel_id=1, source_target_pairs={{0,8},{8,0},{16,24},{24,16},{1,9},{9,1},{17,25},{25,17},{2,10},{10... | collective-permute-start | bytes 786440 | tf_op jit(solution)/shard_map/ppermute | solution.py:64
  597.1 33.2 %collective-permute-start.66 = (bf16[16,16,512]{2,1,0:T(8,128)(2,1)S(1)}, bf16[16,16,512]{2,1,0:T(8,128)(2,1)S(1)}, u32[]{:S(2)}, u32[]{:S(2)}) collective-permute-start(bf16[16,16,512]{2,1,0:T(8,128)(2,1)S(1)} %bitcast.216), channel_id=1, source_target_pairs={{0,16},{8,24},{16,0},{24,8},{1,17},{9,25},{17,1},{25,9},{2,18},{10... | collective-permute-start | bytes 786440 | tf_op jit(solution)/shard_map/ppermute | solution.py:64
  600.0 31.5 %collective-permute-start.67 = (bf16[16,16,512]{2,1,0:T(8,128)(2,1)S(1)}, bf16[16,16,512]{2,1,0:T(8,128)(2,1)S(1)}, u32[]{:S(2)}, u32[]{:S(2)}) collective-permute-start(bf16[16,16,512]{2,1,0:T(8,128)(2,1)S(1)} %bitcast.217), channel_id=1, source_target_pairs={{0,24},{8,16},{16,8},{24,0},{1,25},{9,17},{17,9},{25,1},{2,26},{10... | collective-permute-start | bytes 786440 | tf_op jit(solution)/shard_map/ppermute | solution.py:64
  606.0 31.3 %collective-permute-start.68 = (bf16[16,16,512]{2,1,0:T(8,128)(2,1)}, bf16[16,16,512]{2,1,0:T(8,128)(2,1)S(1)}, u32[]{:S(2)}, u32[]{:S(2)}) collective-permute-start(bf16[16,16,512]{2,1,0:T(8,128)(2,1)} %bitcast.219), channel_id=1, source_target_pairs={{0,8},{8,0},{16,24},{24,16},{1,9},{9,1},{17,25},{25,17},{2,10},{10... | collective-permute-start | bytes 786440 | tf_op jit(solution)/shard_map/ppermute | solution.py:64
  622.4 17.4 %collective-permute-start.69 = (bf16[16,16,512]{2,1,0:T(8,128)(2,1)}, bf16[16,16,512]{2,1,0:T(8,128)(2,1)S(1)}, u32[]{:S(2)}, u32[]{:S(2)}) collective-permute-start(bf16[16,16,512]{2,1,0:T(8,128)(2,1)} %bitcast.220), channel_id=1, source_target_pairs={{0,16},{8,24},{16,0},{24,8},{1,17},{9,25},{17,1},{25,9},{2,18},{10... | collective-permute-start | bytes 786440 | tf_op jit(solution)/shard_map/ppermute | solution.py:64
  (291 other events, 2445.3 us)
Sparse Core Ops, SparseCore 0:
  39.2 102.8 all-gather.4
  145.6 68.2 all-gather.6
  270.5 88.4 reduce-scatter.3
  372.9 92.8 reduce-scatter.5
  473.7 94.6 reduce-scatter.7
